TPU v7x, 128 devices: a whole 4x4x4 slice. The times are simulated.
128 devices in a mesh: order: 2 (over core), tok: 64 (over z, y, x).
Axes of the slice: x: 4, y: 4, z: 4, core: 2. Of those that a mesh axis runs over, the one named last changes fastest.
Arguments:
- queries: bfloat16 [262144, 512], P(('order', 'tok')), may hold values from -6 to 6
- key_tokens: bfloat16 [262144, 512], P(('order', 'tok')), may hold values from -6 to 6
- value_tokens: bfloat16 [262144, 512], P(('order', 'tok')), may hold values from -6 to 6
- learn_rates: float32 [262144], P(('order', 'tok')), may hold values from 0.02 to 0.2
- fast_init: float32 [512, 1536], replicated, may hold values from -0.25 to 0.25
- out_gain: float32 [512], replicated, may hold values from 0.5 to 1.5
Outputs:
- output: bfloat16 [262144, 512], P(('order', 'tok'))
All inputs are finite; a program needn't handle non-finite values.
Results may differ from a plain program's by a relative error of at most 0.015.
Values may be sent and summed in bfloat16 or wider, within the bound.
No kernel may reach another device: no remote copies, remote signals or barrier semaphores. Data moves between devices by JAX's collectives and lax.ppermute only.
A program may use at most 128 MiB of HBM per device.

v0:
```python
import jax
import jax.numpy as jnp
from jax import lax
from jax.sharding import PartitionSpec as P


def cut_along(x, dim, count):
    lengths = x.shape
    blocks = x.reshape(*lengths[:dim], count, lengths[dim] // count, *lengths[dim + 1 :])
    return jnp.moveaxis(blocks, dim, 0)


def sum_at_owner(x, axis, dim):
    count = lax.axis_size(axis)
    blocks = lax.all_to_all(cut_along(x, dim, count), axis, 0, 0, tiled=True)
    return jnp.sum(blocks, axis=0)


def padded_to(lines, count):
    spare = -len(lines) % count
    return jnp.pad(lines, [(0, spare)] + [(0, 0)] * (lines.ndim - 1))


def in_order(blocks, dim):
    lengths = list(blocks.shape[1:])
    lengths[dim] *= blocks.shape[0]
    return jnp.moveaxis(blocks, 0, dim).reshape(lengths)


def from_everyone(x, axis):
    count = lax.axis_size(axis)
    return lax.all_to_all(jnp.broadcast_to(x[None], (count, *x.shape)), axis, 0, 0, tiled=True)


def gathered_copies(x, axis, dim):
    return in_order(from_everyone(x, axis), dim)


def nested_sum(x, axes):
    lines = x.reshape(-1, x.shape[-1])
    own = sum_at_owner(padded_to(lines, lax.axis_size(axes)), axes, 0)
    whole = gathered_copies(own, axes, 0)
    return whole[: len(lines)].reshape(x.shape)


def prefix(x, axis, join, neutral):
    place = lax.axis_index(axis)
    gathered = lax.all_gather(x.astype(jnp.bfloat16), axis)
    state = jnp.zeros_like(x) + jnp.asarray(neutral, x.dtype)

    def one(lap, state):
        return join(state, lax.dynamic_index_in_dim(gathered, lap, 0, False).astype(x.dtype))

    return lax.fori_loop(0, place, one, state)


def gate_up(rows_in, weights_bf):
    width = weights_bf.shape[0]
    both_parts = jnp.dot(rows_in, weights_bf[:, : 2 * width], preferred_element_type=jnp.float32)
    return (both_parts[:, :width], both_parts[:, width:])


def backward_terms(key_rows, target, weights_bf):
    width = weights_bf.shape[0]
    gate_pre, up_pre = gate_up(key_rows, weights_bf)
    squash = jax.nn.sigmoid(gate_pre)
    activated = gate_pre * squash
    hidden = (activated * up_pre).astype(jnp.bfloat16)
    hidden_grad = lax.dot_general(
        target,
        weights_bf[:, 2 * width :],
        (((1,), (1,)), ((), ())),
        preferred_element_type=jnp.float32,
    )
    gate_grad = (hidden_grad * up_pre * squash * (1.0 + gate_pre * (1.0 - squash))).astype(
        jnp.bfloat16
    )
    up_grad = (hidden_grad * activated).astype(jnp.bfloat16)
    return (hidden, jnp.concatenate([gate_grad, up_grad], axis=1))


def local_term(key_rows, hidden, inner_grads, target):
    upper = lax.dot_general(
        key_rows, inner_grads, (((0,), (0,)), ((), ())), preferred_element_type=jnp.float32
    )
    lower = lax.dot_general(
        hidden, target, (((0,), (0,)), ((), ())), preferred_element_type=jnp.float32
    )
    return jnp.concatenate([upper, lower], axis=1)


def summed_whole(key_rows, target, weights_bf):
    hidden, inner_grads = backward_terms(key_rows, target, weights_bf)
    return nested_sum(local_term(key_rows, hidden, inner_grads, target), "tok")


def accumulate(earlier, later):
    return earlier + later


def apply_weights(query_rows, weights_bf, out_gain):
    width = weights_bf.shape[0]
    gate_pre, up_pre = gate_up(query_rows, weights_bf)
    hidden = (jax.nn.silu(gate_pre) * up_pre).astype(jnp.bfloat16)
    result = jnp.dot(hidden, weights_bf[:, 2 * width :], preferred_element_type=jnp.float32)
    norm_inv = lax.rsqrt(jnp.mean(result * result, axis=1, keepdims=True) + 1e-06)
    return (result * norm_inv * out_gain[None, :]).astype(jnp.bfloat16)


def shards(queries, key_tokens, value_tokens, learn_rates, fast_init, out_gain):
    group_rows = key_tokens.shape[0] * lax.axis_size("tok")
    factor = group_rows ** (-0.5)
    target = (-(learn_rates[:, None] * factor) * value_tokens.astype(jnp.float32)).astype(
        jnp.bfloat16
    )
    first_step = fast_init - summed_whole(key_tokens, target, fast_init.astype(jnp.bfloat16))
    second_step = first_step - summed_whole(key_tokens, target, first_step.astype(jnp.bfloat16))
    change = second_step - fast_init
    earlier = prefix(change, "order", accumulate, jnp.zeros_like(change))
    closing_bf = (fast_init + earlier + change).astype(jnp.bfloat16)
    return apply_weights(queries, closing_bf, out_gain)


def solution(mesh):
    return jax.shard_map(
        shards,
        mesh=mesh,
        in_specs=(
            P(("order", "tok"), None),
            P(("order", "tok"), None),
            P(("order", "tok"), None),
            P(("order", "tok")),
            P(),
            P(),
        ),
        out_specs=P(("order", "tok"), None),
        check_vma=False,
    )
```

profile of v0, /device:TPU:0, one launch (start us, length us, event | category | flops | bytes accessed | tf_op | source)
XLA Modules:
  0.0 272.7 jit_solution(6422924271208722089)
XLA Ops:
  6.5 0.0 copy-start
  6.5 0.0 all-gather.3.cloned.1.call-start
  6.5 0.8 multiply_negate_fusion
  7.4 2.1 convert_element_type.50
  9.5 0.0 copy-done
  9.5 0.0 copy-start.7
  9.5 2.4 fusion.25
  11.9 0.0 copy-done.7
  11.9 2.8 %multiply_convert_fusion.6 = (bf16[2048,512]{0,1:T(8,128)(2,1)S(1)}, bf16[2048,512]{0,1:T(8,128)(2,1)S(1)}) fusion(f32[2048,1024]{0,1:T(8,128)S(1)} %fusion.25, bf16[512,1536]{1,0:T(8,128)(2,1)S(1)} %convert_element_type.50, bf16[2048,512]{1,0:T(8,128)(2,1)S(1)} %copy-done.7, f32[2048]{0:T(1024)S(1)} %multiply_negate_fusion), kind=kOutput, calls=%fused_computation.22 | convolution fusion | flops 1090519040 | bytes 15212544 | tf_op jit(solution)/shard_map/dot_general | solution.py:69
  14.8 2.1 fusion.13
  16.9 2.3 fusion.20
  19.2 2.0 pad_maximum_fusion
  21.2 3.5 %copy.8 = f32[512,1536]{1,0:T(8,128)} copy(f32[512,1536]{0,1:T(8,128)} %pad_maximum_fusion) | data formatting | bytes 6291456 | tf_op jit(solution)/shard_map/concatenate | solution.py:89
  24.8 53.0 %all_to_all.20 = f32[64,8,1536]{2,1,0:T(8,128)} all-to-all(f32[64,8,1536]{2,1,0:T(8,128)} %bitcast.40), channel_id=1, replica_groups=mesh['order'=2,'tok'=64] {'tok'}, dimensions={0} | all-to-all | bytes 6291456 | tf_op jit(solution)/shard_map/all_to_all | solution.py:15
  77.8 2.1 reduce_sum.27
  79.8 0.4 broadcast_in_dim.7
  80.2 0.0 copy-start.2
  80.2 46.7 %all_to_all.21 = f32[64,8,1536]{2,1,0:T(8,128)S(1)} all-to-all(f32[64,8,1536]{2,1,0:T(8,128)S(1)} %broadcast_in_dim.7), channel_id=1, replica_groups=mesh['order'=2,'tok'=64] {'tok'}, dimensions={0} | all-to-all | bytes 6291456 | tf_op jit(solution)/shard_map/all_to_all | solution.py:32
  126.9 0.0 copy-done.2
  126.9 0.0 copy-start.4
  126.9 0.8 fusion.12
  127.7 0.8 copy-done.4
  128.6 0.0 copy-start.8
  128.6 2.4 convolution_bitcast_fusion.1
  131.0 0.0 copy-done.8
  131.0 2.7 multiply_convert_fusion.3
  133.7 2.1 fusion.14
  135.7 2.3 fusion.17
  138.1 0.3 pad_maximum_fusion.1
  138.4 2.4 copy.9
  140.8 46.7 %all_to_all.22 = f32[64,8,1536]{2,1,0:T(8,128)S(1)} all-to-all(f32[64,8,1536]{2,1,0:T(8,128)} %bitcast.41), channel_id=1, replica_groups=mesh['order'=2,'tok'=64] {'tok'}, dimensions={0} | all-to-all | bytes 6291456 | tf_op jit(solution)/shard_map/all_to_all | solution.py:15
  187.5 0.2 reduce_sum.28
  187.6 0.4 broadcast_in_dim.8
  188.0 0.0 copy-start.3
  188.0 0.0 copy-start.5
  188.0 46.8 %all_to_all.23 = f32[64,8,1536]{2,1,0:T(8,128)} all-to-all(f32[64,8,1536]{2,1,0:T(8,128)S(1)} %broadcast_in_dim.8), channel_id=1, replica_groups=mesh['order'=2,'tok'=64] {'tok'}, dimensions={0} | all-to-all | bytes 6291456 | tf_op jit(solution)/shard_map/all_to_all | solution.py:32
  234.8 0.0 copy-done.3
  234.8 0.0 copy-done.5
  234.8 4.2 %fusion.27 = bf16[512,1536]{1,0:T(8,128)(2,1)} fusion(f32[512,1536]{1,0:T(8,128)S(1)} %copy-done.3, f32[64,8,1536]{2,1,0:T(8,128)} %all_to_all.23, f32[64,8,1536]{2,1,0:T(8,128)S(1)} %copy-done.5), kind=kLoop, calls=%fused_computation.42 | loop fusion | flops 3145728 | bytes 11010048 | tf_op jit(solution)/shard_map/convert_element_type | solution.py:48
  239.1 0.0 all-gather.3.cloned.1.call-update
  239.1 11.0 %all-gather.3.cloned.1.call-done = bf16[1024,1536]{1,0:T(8,128)(2,1)} async-done(((bf16[512,1536]{1,0:T(8,128)(2,1)}), bf16[1024,1536]{1,0:T(8,128)(2,1)}) %all-gather.3.cloned.1.call-update) | async-done | bytes 3145744 | tf_op jit(solution)/shard_map/all_gather | solution.py:48
  250.1 0.4 broadcast_in_dim.6
  250.5 0.0 copy-start.9
  250.5 5.4 %add_convert_fusion = bf16[512,1536]{1,0:T(8,128)(2,1)S(1)} fusion(f32[512,1536]{1,0:T(8,128)} %param.12, f32[512,1536]{1,0:T(8,128)S(1)} %get-tuple-element.28, f32[64,8,1536]{2,1,0:T(8,128)} %all_to_all.23, f32[64,8,1536]{2,1,0:T(8,128)} %copy-done.4), kind=kLoop, calls=%fused_computation.31 | loop fusion | flops 4718592 | bytes 14155776 | tf_op jit(solution)/shard_map/convert_element_type | solution.py:120
  256.0 0.0 copy-done.9
  256.0 2.4 convolution_bitcast_fusion
  258.4 0.0 copy-start.6
  258.4 1.8 multiply_reduce_fusion
  260.2 0.0 copy-done.6
  260.2 0.0 copy-start.1
  260.2 1.8 multiply_convert_fusion
  262.0 3.9 %copy.10 = bf16[2048,512]{1,0:T(8,128)(2,1)} copy(bf16[2048,512]{0,1:T(8,128)(2,1)} %multiply_convert_fusion) | data formatting | bytes 4194304 | tf_op jit(solution)/shard_map/convert_element_type | solution.py:107
  265.9 0.0 copy-done.1
  (2 shorter events, 0.0 us)
Async XLA Ops:
  6.5 2.9 %copy-start = (bf16[2048,512]{1,0:T(8,128)(2,1)S(1)}, bf16[2048,512]{1,0:T(8,128)(2,1)}, u32[]{:S(2)}) copy-start(bf16[2048,512]{1,0:T(8,128)(2,1)} %param.9) | copy-start | bytes 6291460
  6.5 243.6 %all-gather.3.cloned.1.call-start = ((), (), s32[]{:S(2)}) async-start(), calls=%async_computation.4 | async-start | bytes 4718592 | tf_op jit(solution)/shard_map/all_gather | solution.py:48
  9.5 2.5 copy-start.7
  80.2 46.7 %copy-start.2 = (f32[512,1536]{1,0:T(8,128)S(1)}, f32[512,1536]{1,0:T(8,128)}, u32[]{:S(2)}) copy-start(f32[512,1536]{1,0:T(8,128)} %param.12) | copy-start | bytes 9437188
  126.9 1.6 copy-start.4
  128.6 2.4 copy-start.8
  188.0 46.8 %copy-start.3 = (f32[512,1536]{1,0:T(8,128)S(1)}, f32[512,1536]{1,0:T(8,128)}, u32[]{:S(2)}) copy-start(f32[512,1536]{1,0:T(8,128)} %param.12) | copy-start | bytes 9437188
  188.0 46.8 %copy-start.5 = (f32[64,8,1536]{2,1,0:T(8,128)S(1)}, f32[64,8,1536]{2,1,0:T(8,128)}, u32[]{:S(2)}) copy-start(f32[64,8,1536]{2,1,0:T(8,128)} %copy-done.4) | copy-start | bytes 9437188
  250.5 5.4 %copy-start.9 = (bf16[2048,512]{1,0:T(8,128)(2,1)S(1)}, bf16[2048,512]{1,0:T(8,128)(2,1)}, u32[]{:S(2)}) copy-start(bf16[2048,512]{1,0:T(8,128)(2,1)} %param.8) | copy-start | bytes 6291460
  258.4 1.8 copy-start.6
  260.2 5.7 %copy-start.1 = (bf16[2048,512]{1,0:T(8,128)(2,1)S(1)}, bf16[2048,512]{1,0:T(8,128)(2,1)}, u32[]{:S(2)}) copy-start(bf16[2048,512]{1,0:T(8,128)(2,1)} %param.9) | copy-start | bytes 6291460
Sparse Core Ops, SparseCore 0:
  239.2 10.8 all-gather.2
where the time goes:
time: 277 us; the launch traced here: 273 us
  blocking collectives  193 us (70%)
  matrix products  23.4 us (8%)
  other arithmetic  19.7 us (7%)
  between operations  13.6 us (5%)
  local copies, waits for them, and re-layouts  11.8 us (4%)
  waiting for transfers between devices  11 us (4%)
    all_to_all x2, blocking collectives, sum_at_owner(): blocks = lax.all_to_all(cut_along(x, dim, count), axis, 0, 0, tiled=True)  99.7 us
    all_to_all x2, blocking collectives, from_everyone(): lax.all_to_all(jnp.broadcast_to(x[None], (count, *x.shape)), axis, 0, 0,...  93.5 us
    all_gather x1, waiting for transfers between devices, prefix(): gathered = lax.all_gather(x.astype(jnp.bfloat16), axis)  11 us
    dot_general x3, matrix products, gate_up(): jnp.dot(rows_in, weights_bf[:, :2 * width], preferred_element_type=jnp.fl...  7.2 us
    concatenate x2, local copies, waits for them, and re-layouts, local_term(): return jnp.concatenate([upper, lower], axis=1)  5.91 us
    dot_general x2, matrix products, backward_terms(): lax.dot_general(target, weights_bf[:, 2 * width:], (((1,), (1,)), ((), ()...  5.56 us
  transfers between devices with their start and end apart: 1, of which 1 were waited for; matrix products, arithmetic and copies ran while one was open for 0% of the time, Pallas kernels for 0%

commit v1 on v0

v1 whole, which is shorter than its diff:
```python
import functools
import itertools

import jax
import jax.numpy as jnp
from jax import lax
from jax.experimental import pallas as pl
from jax.experimental.pallas import tpu as pltpu
from jax.sharding import PartitionSpec as P

SIDE = 4
AXES = ("order", "tok")
BF = jnp.bfloat16
F32 = jnp.float32
NT = (((1,), (1,)), ((), ()))
NN = (((1,), (0,)), ((), ()))
VMEM = pl.BlockSpec(memory_space=pltpu.VMEM)
SMEM = pl.BlockSpec(memory_space=pltpu.SMEM)


def flat(core, z, y, x):
    return ((core * SIDE + z % SIDE) * SIDE + y % SIDE) * SIDE + x % SIDE


def hop_pairs(level, step):
    pairs = []
    for core, z, y, x in itertools.product(range(2), *[range(SIDE)] * 3):
        dz = dy = dx = 0
        if level == 2:
            dz = step
        elif (level == 0) == (core == 0):
            dx = step
        else:
            dy = step
        pairs.append((flat(core, z, y, x), flat(core, z + dz, y + dy, x + dx)))
    return pairs


def hop(x, level, step):
    return lax.ppermute(x, AXES, hop_pairs(level, step % SIDE))


def call(kernel, outs, n_smem, args, cost, scratch=(), limit=24 << 20):
    return pl.pallas_call(
        kernel,
        out_shape=outs,
        in_specs=[SMEM] * n_smem + [VMEM] * (len(args) - n_smem),
        out_specs=jax.tree.map(lambda _: VMEM, outs),
        scratch_shapes=scratch,
        compiler_params=pltpu.CompilerParams(vmem_limit_bytes=limit),
        cost_estimate=pl.CostEstimate(flops=cost[0], bytes_accessed=cost[1], transcendentals=0),
    )(*args)


def arr(shape, dtype):
    return jax.ShapeDtypeStruct(shape, dtype)


def layout_kernel(place, w_ref, b0, b1, b2, b3, own, turned, slab):
    width = w_ref.shape[0]
    lines = width // (SIDE * SIDE)
    for m in range(2):
        part = w_ref[:, m * width : (m + 1) * width].astype(BF)
        turned[m] = part.T.reshape(SIDE * SIDE, lines, width)
    turned[2] = w_ref[:, 2 * width :].astype(BF).reshape(SIDE * SIDE, lines, width)
    for r, block in enumerate((b0, b1, b2, b3)):
        for s in range(SIDE):
            group = place[r * SIDE + s]
            for m in range(3):
                block[s, m] = turned[m, group]
    mine = place[0]
    for m in range(2):
        start = pl.multiple_of(m * width + (mine // SIDE) * 128, 128)
        slab[...] = w_ref[:, pl.ds(start, 128)].T.reshape(SIDE, lines, width)
        own[m] = slab[mine % SIDE]
    own[2] = w_ref[pl.ds(pl.multiple_of(mine * lines, lines), lines), 2 * width :]


def gradient_kernel(factor, tile, w_ref, k_ref, v_ref, rate_ref, out_ref, acc):
    units = w_ref.shape[0] * w_ref.shape[2]
    width = w_ref.shape[3]
    lines = w_ref.shape[2]
    wgu = jnp.concatenate([w_ref[:, m].reshape(units, width) for m in range(2)], axis=0)
    wd = w_ref[:, 2].reshape(units, width)
    tokens = k_ref.shape[0]

    def one(i, first):
        rows = pl.ds(i * tile, tile) if first else pl.ds(pl.multiple_of(i * tile, tile), tile)
        k = k_ref[rows, :]
        v = v_ref[rows, :]
        scale = -(rate_ref[:, rows] * factor)
        gu = lax.dot_general(wgu, k, NT, preferred_element_type=F32)
        hidden_grad = lax.dot_general(wd, v, NT, preferred_element_type=F32) * scale
        gate = gu[:units]
        up = gu[units:]
        sig = 0.5 * jnp.tanh(0.5 * gate) + 0.5
        act = gate * sig
        hidden = (act * up * scale).astype(BF)
        gate_grad = (hidden_grad * up * (sig + act * (1.0 - sig))).astype(BF)
        up_grad = (hidden_grad * act).astype(BF)
        both = jnp.concatenate([gate_grad, up_grad], axis=0)
        upper = lax.dot_general(both, k, NN, preferred_element_type=F32)
        lower = lax.dot_general(hidden, v, NN, preferred_element_type=F32)
        if first:
            acc[: 2 * units] = upper
            acc[2 * units :] = lower
        else:
            acc[: 2 * units] += upper
            acc[2 * units :] += lower

    one(0, True)

    @pl.loop(1, tokens // tile)
    def _(i):
        one(i, False)

    for m in range(3):
        part = acc[m * units : (m + 1) * units]
        out_ref[:, m] = part.reshape(SIDE, lines, width).astype(out_ref.dtype)


def gradient_block(weights, keys, values, rates, factor, dtype, tile=512):
    units = weights.shape[0] * weights.shape[2]
    width = weights.shape[3]
    tokens = keys.shape[0]
    return call(
        functools.partial(gradient_kernel, factor, tile),
        arr(weights.shape, dtype),
        0,
        (weights, keys, values, rates),
        (12 * tokens * width * units, 4 * tokens * width),
        [pltpu.VMEM((3 * units, width), F32)],
    )


def scatter_kernel(own, r1, r2, r3, keep, s1, s2, s3):
    for s, out in enumerate((keep, s1, s2, s3)):
        total = own[s] + r1[s].astype(F32) + r2[s].astype(F32) + r3[s].astype(F32)
        out[...] = total.astype(out.dtype)


def add_kernel(own, r1, r2, r3, out):
    out[...] = (
        own[...] + r1[...].astype(F32) + r2[...].astype(F32) + r3[...].astype(F32)
    ).astype(out.dtype)


def update_kernel(weights, own, r1, r2, r3, new, new_bf):
    total = (
        own[...].astype(F32) + r1[...].astype(F32) + r2[...].astype(F32) + r3[...].astype(F32)
    )
    value = weights[...] - total
    new[...] = value
    new_bf[...] = value.astype(BF)


def change_kernel(start, weights, own, r1, r2, r3, change, change_bf):
    total = (
        own[...].astype(F32) + r1[...].astype(F32) + r2[...].astype(F32) + r3[...].astype(F32)
    )
    value = (weights[...] - total) - start[...]
    change[...] = value
    change_bf[...] = value.astype(BF)


def closing_kernel(start, earlier, change, out):
    out[...] = ((start[...] + earlier[...].astype(F32)) + change[...]).astype(BF)


def join_kernel(own, r1, r2, r3, out):
    for s, part in enumerate((own, r1, r2, r3)):
        out[s] = part[...]


def apply_kernel(tile, first, last, *refs):
    refs = list(refs)
    w_ref, q_ref = refs[:2]
    refs = refs[2:]
    gain = refs.pop(0) if last else None
    so_far = None if first else refs.pop(0)
    out = refs.pop(0)
    units = w_ref.shape[0] * w_ref.shape[2]
    width = w_ref.shape[3]
    wgu = jnp.concatenate([w_ref[:, m].reshape(units, width) for m in range(2)], axis=0)
    wd = w_ref[:, 2].reshape(units, width)

    @pl.loop(0, q_ref.shape[0] // tile)
    def _(i):
        rows = pl.ds(pl.multiple_of(i * tile, tile), tile)
        gu = lax.dot_general(q_ref[rows, :], wgu, NT, preferred_element_type=F32)
        gate = gu[:, :units]
        up = gu[:, units:]
        act = gate * (0.5 * jnp.tanh(0.5 * gate) + 0.5)
        y = lax.dot_general((act * up).astype(BF), wd, NN, preferred_element_type=F32)
        if so_far is not None:
            y = y + so_far[rows, :]
        if last:
            scale = lax.rsqrt(jnp.mean(y * y, axis=1, keepdims=True) + 1e-06)
            y = y * scale * gain[...]
        out[rows, :] = y.astype(out.dtype)


def apply_block(weights, queries, so_far, gain, tile=512):
    units = weights.shape[0] * weights.shape[2]
    tokens, width = queries.shape
    first, last = so_far is None, gain is not None
    args = (weights, queries) + ((gain,) if last else ()) + (() if first else (so_far,))
    return call(
        functools.partial(apply_kernel, tile, first, last),
        arr((tokens, width), BF if last else F32),
        0,
        args,
        (6 * tokens * width * units, 6 * tokens * width),
    )


def ring_parts(x, level):
    return [hop(x, level, -r) for r in range(1, SIDE)]


def total_parts(blocks, keys, values, rates, factor):
    sent = {}
    for r in (2, 1, 3):
        sent[r] = hop(gradient_block(blocks[r], keys, values, rates, factor, BF), 0, r)
    own = gradient_block(blocks[0], keys, values, rates, factor, F32)
    shard = own.shape[1:]
    size = own.size
    keep, *out = call(
        scatter_kernel,
        [arr(shard, F32)] + [arr(shard, BF)] * 3,
        0,
        (own, sent[1], sent[2], sent[3]),
        (3 * size, 12 * size),
    )
    got = [hop(x, 1, r + 1) for r, x in enumerate(out)]
    part = call(add_kernel, arr(shard, BF), 0, (keep, *got), (size, 3 * size))
    return [part] + ring_parts(part, 2)


def gathered(shard):
    parts = [shard] + ring_parts(shard, 1)
    block = call(join_kernel, arr((SIDE, *shard.shape), BF), 0, parts, (0, 16 * shard.size))
    return [block] + ring_parts(block, 0)


def shards(queries, key_tokens, value_tokens, learn_rates, fast_init, out_gain):
    tokens, width = key_tokens.shape
    factor = (tokens * lax.axis_size("tok")) ** (-0.5)
    lines = width // (SIDE * SIDE)
    core = lax.axis_index("order")
    tok = lax.axis_index("tok")
    x, y = tok % SIDE, (tok // SIDE) % SIDE
    ring = jnp.arange(SIDE, dtype=jnp.int32)
    r1, r2 = ring[:, None], ring[None, :]
    along_x = (x + jnp.where(core == 0, r1, r2)) % SIDE
    along_y = (y + jnp.where(core == 0, r2, r1)) % SIDE
    place = (along_x * SIDE + along_y).reshape(-1).astype(jnp.int32)
    rates = learn_rates.reshape(1, tokens)
    gain = out_gain.reshape(1, width)

    shard = (3, lines, width)
    *blocks, start = call(
        layout_kernel,
        [arr((SIDE, *shard), BF)] * SIDE + [arr(shard, F32)],
        1,
        (place, fast_init),
        (0, 6 * fast_init.size),
        [
            pltpu.VMEM((3, SIDE * SIDE, lines, width), BF),
            pltpu.VMEM((SIDE, lines, width), F32),
        ],
    )
    size = start.size
    parts = total_parts(blocks, key_tokens, value_tokens, rates, factor)
    first_step, first_bf = call(
        update_kernel, [arr(shard, F32), arr(shard, BF)], 0, (start, *parts), (size, 8 * size)
    )
    blocks = gathered(first_bf)
    parts = total_parts(blocks, key_tokens, value_tokens, rates, factor)
    change, change_bf = call(
        change_kernel,
        [arr(shard, F32), arr(shard, BF)],
        0,
        (start, first_step, *parts),
        (size, 8 * size),
    )
    pairs = [(flat(0, *c), flat(1, *c)) for c in itertools.product(*[range(SIDE)] * 3)]
    earlier = lax.ppermute(change_bf, AXES, pairs)
    closing = call(closing_kernel, arr(shard, BF), 0, (start, earlier, change), (size, 8 * size))
    blocks = gathered(closing)
    result = apply_block(blocks[0], queries, None, None)
    for r in (1, 3):
        result = apply_block(blocks[r], queries, result, None)
    return apply_block(blocks[2], queries, result, gain)


def solution(mesh):
    rows = P(AXES, None)
    return jax.shard_map(
        shards,
        mesh=mesh,
        in_specs=(rows, rows, rows, P(AXES), P(), P()),
        out_specs=rows,
        check_vma=False,
    )
```

time: 277 us -> 146 us (0.53); the launches traced: 273 us -> 146 us
  blocking collectives: 193 us -> 0 us
  starting transfers between devices: 0.01 us -> 54.5 us
  Pallas kernels: 0 us -> 40.8 us
  waiting for transfers between devices: 11 us -> 46.1 us
  matrix products: 23.4 us -> 0 us
  other arithmetic: 19.7 us -> 0.02 us
  between operations: 13.6 us -> 0.26 us
  local copies, waits for them, and re-layouts: 11.8 us -> 4.11 us
    all_to_all x4 -> x0, blocking collectives: 193 us -> none  [the longest x2 99.7 us: sum_at_owner(): blocks = lax.all_to_all(cut_along(x, dim, count), axis, 0, 0, tiled=True)]
    ppermute x0 -> x31, starting transfers between devices: none -> 54.5 us  [the longest x30 53.2 us: hop(): return lax.ppermute(x, AXES, hop_pairs(level, step % SIDE))]
    ppermute x0 -> x31, waiting for transfers between devices: none -> 46.1 us  [the longest x30 45.2 us: hop(): return lax.ppermute(x, AXES, hop_pairs(level, step % SIDE))]
    pallas_call x0 -> x22, Pallas kernels: none -> 40.8 us  [call(): pl.pallas_call(kernel, out_shape=outs, in_specs=[SMEM] * n_smem + [VMEM]...]
    dot_general x10 -> x0, matrix products: 23.4 us -> none  [the longest x3 7.2 us: gate_up(): jnp.dot(rows_in, weights_bf[:, :2 * width], preferred_element_type=jnp.fl...]
    convert_element_type x5 -> x0, other arithmetic: 14.3 us -> none  [the longest x1 5.42 us: shards(): closing_bf = (fast_init + earlier + change).astype(jnp.bfloat16)]
    all_gather x1 -> x0, waiting for transfers between devices: 11 us -> none  [prefix(): gathered = lax.all_gather(x.astype(jnp.bfloat16), axis)]
    concatenate x2 -> x0, local copies, waits for them, and re-layouts: 5.91 us -> none  [local_term(): return jnp.concatenate([upper, lower], axis=1)]
  transfers between devices with their start and end apart: 1 -> 31, of which waited for: 1 -> 24; matrix products, arithmetic and copies ran while one was open for 0% -> 0% of each run, Pallas kernels for 0% -> 21%
where the time goes in v1:
time: 146 us
  starting transfers between devices  54.5 us (37%)
  waiting for transfers between devices  46.1 us (32%)
  Pallas kernels  40.8 us (28%)
  local copies, waits for them, and re-layouts  4.11 us (3%)
    ppermute x30, starting transfers between devices, hop(): return lax.ppermute(x, AXES, hop_pairs(level, step % SIDE))  53.2 us
    ppermute x30, waiting for transfers between devices, hop(): return lax.ppermute(x, AXES, hop_pairs(level, step % SIDE))  45.2 us
    pallas_call x22, Pallas kernels, call(): pl.pallas_call(kernel, out_shape=outs, in_specs=[SMEM] * n_smem + [VMEM]...  40.8 us
    unnamed x14, local copies, waits for them, and re-layouts  3.95 us
  transfers between devices with their start and end apart: 31, of which 24 were waited for; matrix products, arithmetic and copies ran while one was open for 0% of the time, Pallas kernels for 21%

profile of v1, /device:TPU:0, one launch (start us, length us, event | category | flops | bytes accessed | tf_op | source)
XLA Modules:
  0.0 145.7 jit_solution(3577400939722101834)
XLA Ops:
  0.2 1.9 %copy-done.1 = f32[512,1536]{1,0:T(8,128)S(1)} copy-done((f32[512,1536]{1,0:T(8,128)S(1)}, f32[512,1536]{1,0:T(8,128)}, u32[]{:S(2)}) %copy-start.1) | copy-done | bytes 3145752
  2.1 1.1 shard_map.64
  3.7 1.6 %copy-done.4 = bf16[2048,512]{1,0:T(8,128)(2,1)S(1)} copy-done((bf16[2048,512]{1,0:T(8,128)(2,1)S(1)}, bf16[2048,512]{1,0:T(8,128)(2,1)}, u32[]{:S(2)}) %copy-start.4) | copy-done | bytes 2097176
  5.3 3.2 %shard_map.66 = bf16[4,3,32,512]{3,2,1,0:T(8,128)(2,1)S(1)} custom-call(bf16[4,3,32,512]{3,2,1,0:T(8,128)(2,1)S(1)} %get-tuple-element.24.w_ref, bf16[2048,512]{1,0:T(8,128)(2,1)S(1)} %copy-done.3, bf16[2048,512]{1,0:T(8,128)(2,1)S(1)} %copy-done.4, f32[1,2048]{1,0:T(1,128)S(1)} %bitcast.3), custom_call_target="tpu_custom_call" | custom-call | flops 1610612736 | bytes 4194304 | tf_op jit(solution)/shard_map/pallas_call | solution.py:44
  8.5 1.6 %collective-permute-start = (bf16[4,3,32,512]{3,2,1,0:T(8,128)(2,1)S(1)}, bf16[4,3,32,512]{3,2,1,0:T(8,128)(2,1)S(1)}, u32[]{:S(2)}, u32[]{:S(2)}) collective-permute-start(bf16[4,3,32,512]{3,2,1,0:T(8,128)(2,1)S(1)} %shard_map.66), channel_id=1, source_target_pairs={{0,1},{1,2},{2,3},{3,0},{4,5},{5,6},{6,7},{7,4},{8,9},{9,10},{10,1... | collective-permute-start | bytes 1179656 | tf_op jit(solution)/shard_map/ppermute | solution.py:40
  10.1 3.2 %shard_map.67 = bf16[4,3,32,512]{3,2,1,0:T(8,128)(2,1)S(1)} custom-call(bf16[4,3,32,512]{3,2,1,0:T(8,128)(2,1)S(1)} %get-tuple-element.25.w_ref, bf16[2048,512]{1,0:T(8,128)(2,1)S(1)} %copy-done.3, bf16[2048,512]{1,0:T(8,128)(2,1)S(1)} %copy-done.4, f32[1,2048]{1,0:T(1,128)S(1)} %bitcast.4), custom_call_target="tpu_custom_call" | custom-call | flops 1610612736 | bytes 4194304 | tf_op jit(solution)/shard_map/pallas_call | solution.py:44
  13.3 2.8 %collective-permute-start.1 = (bf16[4,3,32,512]{3,2,1,0:T(8,128)(2,1)S(1)}, bf16[4,3,32,512]{3,2,1,0:T(8,128)(2,1)S(1)}, u32[]{:S(2)}, u32[]{:S(2)}) collective-permute-start(bf16[4,3,32,512]{3,2,1,0:T(8,128)(2,1)S(1)} %shard_map.67), channel_id=1, source_target_pairs={{0,2},{1,3},{2,0},{3,1},{4,6},{5,7},{6,4},{7,5},{8,10},{9,11},{10,... | collective-permute-start | bytes 1179656 | tf_op jit(solution)/shard_map/ppermute | solution.py:40
  16.1 3.2 %shard_map.68 = bf16[4,3,32,512]{3,2,1,0:T(8,128)(2,1)S(1)} custom-call(bf16[4,3,32,512]{3,2,1,0:T(8,128)(2,1)S(1)} %get-tuple-element.26.w_ref, bf16[2048,512]{1,0:T(8,128)(2,1)S(1)} %copy-done.3, bf16[2048,512]{1,0:T(8,128)(2,1)S(1)} %copy-done.4, f32[1,2048]{1,0:T(1,128)S(1)} %bitcast.5), custom_call_target="tpu_custom_call" | custom-call | flops 1610612736 | bytes 4194304 | tf_op jit(solution)/shard_map/pallas_call | solution.py:44
  19.4 1.5 %collective-permute-start.2 = (bf16[4,3,32,512]{3,2,1,0:T(8,128)(2,1)S(1)}, bf16[4,3,32,512]{3,2,1,0:T(8,128)(2,1)S(1)}, u32[]{:S(2)}, u32[]{:S(2)}) collective-permute-start(bf16[4,3,32,512]{3,2,1,0:T(8,128)(2,1)S(1)} %shard_map.68), channel_id=1, source_target_pairs={{0,3},{1,0},{2,1},{3,2},{4,7},{5,4},{6,5},{7,6},{8,11},{9,8},{10,9... | collective-permute-start | bytes 1179656 | tf_op jit(solution)/shard_map/ppermute | solution.py:40
  20.8 3.2 %shard_map.65.own = f32[4,3,32,512]{3,2,1,0:T(8,128)S(1)} custom-call(bf16[4,3,32,512]{3,2,1,0:T(8,128)(2,1)S(1)} %get-tuple-element.23.w_ref, bf16[2048,512]{1,0:T(8,128)(2,1)S(1)} %copy-done.3, bf16[2048,512]{1,0:T(8,128)(2,1)S(1)} %copy-done.4, f32[1,2048]{1,0:T(1,128)S(1)} %bitcast.6), custom_call_target="tpu_custom_call" | custom-call | flops 1610612736 | bytes 4194304 | tf_op jit(solution)/shard_map/pallas_call | solution.py:44
  24.1 3.1 %collective-permute-done.2.r3 = bf16[4,3,32,512]{3,2,1,0:T(8,128)(2,1)S(1)} collective-permute-done((bf16[4,3,32,512]{3,2,1,0:T(8,128)(2,1)S(1)}, bf16[4,3,32,512]{3,2,1,0:T(8,128)(2,1)S(1)}, u32[]{:S(2)}, u32[]{:S(2)}) %collective-permute-start.2) | collective-permute-done | bytes 393248 | tf_op jit(solution)/shard_map/ppermute | solution.py:40
  27.4 1.6 %collective-permute-start.3 = (bf16[3,32,512]{2,1,0:T(8,128)(2,1)S(1)}, bf16[3,32,512]{2,1,0:T(8,128)(2,1)S(1)}, u32[]{:S(2)}, u32[]{:S(2)}) collective-permute-start(bf16[3,32,512]{2,1,0:T(8,128)(2,1)S(1)} %get-tuple-element.28), channel_id=1, source_target_pairs={{0,4},{1,5},{2,6},{3,7},{4,8},{5,9},{6,10},{7,11},{8,12},{9,13},{1... | collective-permute-start | bytes 294920 | tf_op jit(solution)/shard_map/ppermute | solution.py:40
  29.0 2.9 %collective-permute-start.4 = (bf16[3,32,512]{2,1,0:T(8,128)(2,1)S(1)}, bf16[3,32,512]{2,1,0:T(8,128)(2,1)S(1)}, u32[]{:S(2)}, u32[]{:S(2)}) collective-permute-start(bf16[3,32,512]{2,1,0:T(8,128)(2,1)S(1)} %get-tuple-element.29), channel_id=1, source_target_pairs={{0,8},{1,9},{2,10},{3,11},{4,12},{5,13},{6,14},{7,15},{8,0},{9,1},... | collective-permute-start | bytes 294920 | tf_op jit(solution)/shard_map/ppermute | solution.py:40
  31.9 1.3 collective-permute-start.5
  33.3 2.3 %collective-permute-done.4.r2 = bf16[3,32,512]{2,1,0:T(8,128)(2,1)S(1)} collective-permute-done((bf16[3,32,512]{2,1,0:T(8,128)(2,1)S(1)}, bf16[3,32,512]{2,1,0:T(8,128)(2,1)S(1)}, u32[]{:S(2)}, u32[]{:S(2)}) %collective-permute-start.4) | collective-permute-done | bytes 98336 | tf_op jit(solution)/shard_map/ppermute | solution.py:40
  35.6 1.0 collective-permute-done.5.r3
  36.6 4.1 %collective-permute-start.6 = (bf16[3,32,512]{2,1,0:T(8,128)(2,1)S(1)}, bf16[3,32,512]{2,1,0:T(8,128)(2,1)S(1)}, u32[]{:S(2)}, u32[]{:S(2)}) collective-permute-start(bf16[3,32,512]{2,1,0:T(8,128)(2,1)S(1)} %shard_map.70.own), channel_id=1, source_target_pairs={{0,48},{1,49},{2,50},{3,51},{4,52},{5,53},{6,54},{7,55},{8,56},{9,... | collective-permute-start | bytes 294920 | tf_op jit(solution)/shard_map/ppermute | solution.py:40
  40.7 1.3 collective-permute-start.8
  41.9 2.0 %collective-permute-done.6.r1 = bf16[3,32,512]{2,1,0:T(8,128)(2,1)S(1)} collective-permute-done((bf16[3,32,512]{2,1,0:T(8,128)(2,1)S(1)}, bf16[3,32,512]{2,1,0:T(8,128)(2,1)S(1)}, u32[]{:S(2)}, u32[]{:S(2)}) %collective-permute-start.6) | collective-permute-done | bytes 98336 | tf_op jit(solution)/shard_map/ppermute | solution.py:40
  43.9 3.0 %collective-permute-done.7.r2 = bf16[3,32,512]{2,1,0:T(8,128)(2,1)S(1)} collective-permute-done((bf16[3,32,512]{2,1,0:T(8,128)(2,1)S(1)}, bf16[3,32,512]{2,1,0:T(8,128)(2,1)S(1)}, u32[]{:S(2)}, u32[]{:S(2)}) %collective-permute-start.7) | collective-permute-done | bytes 98336 | tf_op jit(solution)/shard_map/ppermute | solution.py:40
  46.9 0.7 collective-permute-done.8.r3
  47.6 2.0 %collective-permute-start.10 = (bf16[3,32,512]{2,1,0:T(8,128)(2,1)S(1)}, bf16[3,32,512]{2,1,0:T(8,128)(2,1)S(1)}, u32[]{:S(2)}, u32[]{:S(2)}) collective-permute-start(bf16[3,32,512]{2,1,0:T(8,128)(2,1)S(1)} %get-tuple-element.32.own), channel_id=1, source_target_pairs={{0,8},{1,9},{2,10},{3,11},{4,12},{5,13},{6,14},{7,15},{8,0},{9,1},... | collective-permute-start | bytes 294920 | tf_op jit(solution)/shard_map/ppermute | solution.py:40
  49.6 1.5 %collective-permute-start.11 = (bf16[3,32,512]{2,1,0:T(8,128)(2,1)S(1)}, bf16[3,32,512]{2,1,0:T(8,128)(2,1)S(1)}, u32[]{:S(2)}, u32[]{:S(2)}) collective-permute-start(bf16[3,32,512]{2,1,0:T(8,128)(2,1)S(1)} %get-tuple-element.32.own), channel_id=1, source_target_pairs={{0,4},{1,5},{2,6},{3,7},{4,8},{5,9},{6,10},{7,11},{8,12},{9,13},{1... | collective-permute-start | bytes 294920 | tf_op jit(solution)/shard_map/ppermute | solution.py:40
  51.1 1.7 %collective-permute-start.9 = (bf16[3,32,512]{2,1,0:T(8,128)(2,1)S(1)}, bf16[3,32,512]{2,1,0:T(8,128)(2,1)S(1)}, u32[]{:S(2)}, u32[]{:S(2)}) collective-permute-start(bf16[3,32,512]{2,1,0:T(8,128)(2,1)S(1)} %get-tuple-element.32.own), channel_id=1, source_target_pairs={{0,12},{1,13},{2,14},{3,15},{4,0},{5,1},{6,2},{7,3},{8,4},{9,5},{1... | collective-permute-start | bytes 294920 | tf_op jit(solution)/shard_map/ppermute | solution.py:40
  52.8 1.0 collective-permute-done.10.r2
  53.8 1.6 %collective-permute-done.11.r3 = bf16[3,32,512]{2,1,0:T(8,128)(2,1)S(1)} collective-permute-done((bf16[3,32,512]{2,1,0:T(8,128)(2,1)S(1)}, bf16[3,32,512]{2,1,0:T(8,128)(2,1)S(1)}, u32[]{:S(2)}, u32[]{:S(2)}) %collective-permute-start.11) | collective-permute-done | bytes 98336 | tf_op jit(solution)/shard_map/ppermute | solution.py:40
  55.4 1.5 collective-permute-done.9.r1
  56.9 2.7 %collective-permute-start.12 = (bf16[4,3,32,512]{3,2,1,0:T(8,128)(2,1)S(1)}, bf16[4,3,32,512]{3,2,1,0:T(8,128)(2,1)S(1)}, u32[]{:S(2)}, u32[]{:S(2)}) collective-permute-start(bf16[4,3,32,512]{3,2,1,0:T(8,128)(2,1)S(1)} %shard_map.72.w_ref), channel_id=1, source_target_pairs={{0,3},{1,0},{2,1},{3,2},{4,7},{5,4},{6,5},{7,6},{8,11},{9,8},{10,9... | collective-permute-start | bytes 1179656 | tf_op jit(solution)/shard_map/ppermute | solution.py:40
  59.6 3.6 %collective-permute-start.14 = (bf16[4,3,32,512]{3,2,1,0:T(8,128)(2,1)S(1)}, bf16[4,3,32,512]{3,2,1,0:T(8,128)(2,1)S(1)}, u32[]{:S(2)}, u32[]{:S(2)}) collective-permute-start(bf16[4,3,32,512]{3,2,1,0:T(8,128)(2,1)S(1)} %shard_map.72.w_ref), channel_id=1, source_target_pairs={{0,2},{1,3},{2,0},{3,1},{4,6},{5,7},{6,4},{7,5},{8,10},{9,11},{10,... | collective-permute-start | bytes 1179656 | tf_op jit(solution)/shard_map/ppermute | solution.py:40
  63.1 3.7 %collective-permute-done.12.w_ref = bf16[4,3,32,512]{3,2,1,0:T(8,128)(2,1)S(1)} collective-permute-done((bf16[4,3,32,512]{3,2,1,0:T(8,128)(2,1)S(1)}, bf16[4,3,32,512]{3,2,1,0:T(8,128)(2,1)S(1)}, u32[]{:S(2)}, u32[]{:S(2)}) %collective-permute-start.12) | collective-permute-done | bytes 393248 | tf_op jit(solution)/shard_map/ppermute | solution.py:40
  66.8 3.2 %shard_map.74 = bf16[4,3,32,512]{3,2,1,0:T(8,128)(2,1)S(1)} custom-call(bf16[4,3,32,512]{3,2,1,0:T(8,128)(2,1)S(1)} %collective-permute-done.12.w_ref, bf16[2048,512]{1,0:T(8,128)(2,1)S(1)} %copy-done.3, bf16[2048,512]{1,0:T(8,128)(2,1)S(1)} %copy-done.5, f32[1,2048]{1,0:T(1,128)S(1)} %bitcast.7), custom_call_target="tpu_custom_call" | custom-call | flops 1610612736 | bytes 4194304 | tf_op jit(solution)/shard_map/pallas_call | solution.py:44
  70.0 6.3 %collective-permute-start.13 = (bf16[4,3,32,512]{3,2,1,0:T(8,128)(2,1)S(1)}, bf16[4,3,32,512]{3,2,1,0:T(8,128)(2,1)S(1)}, u32[]{:S(2)}, u32[]{:S(2)}) collective-permute-start(bf16[4,3,32,512]{3,2,1,0:T(8,128)(2,1)S(1)} %shard_map.74), channel_id=1, source_target_pairs={{0,1},{1,2},{2,3},{3,0},{4,5},{5,6},{6,7},{7,4},{8,9},{9,10},{10,1... | collective-permute-start | bytes 1179656 | tf_op jit(solution)/shard_map/ppermute | solution.py:40
  76.3 3.2 %shard_map.75 = bf16[4,3,32,512]{3,2,1,0:T(8,128)(2,1)S(1)} custom-call(bf16[4,3,32,512]{3,2,1,0:T(8,128)(2,1)S(1)} %collective-permute-done.14.w_ref, bf16[2048,512]{1,0:T(8,128)(2,1)S(1)} %copy-done.3, bf16[2048,512]{1,0:T(8,128)(2,1)S(1)} %copy-done.5, f32[1,2048]{1,0:T(1,128)S(1)} %bitcast.8), custom_call_target="tpu_custom_call" | custom-call | flops 1610612736 | bytes 4194304 | tf_op jit(solution)/shard_map/pallas_call | solution.py:44
  79.7 3.2 %shard_map.76 = bf16[4,3,32,512]{3,2,1,0:T(8,128)(2,1)S(1)} custom-call(bf16[4,3,32,512]{3,2,1,0:T(8,128)(2,1)S(1)} %collective-permute-done.16.w_ref, bf16[2048,512]{1,0:T(8,128)(2,1)S(1)} %copy-done.3, bf16[2048,512]{1,0:T(8,128)(2,1)S(1)} %copy-done.5, f32[1,2048]{1,0:T(1,128)S(1)} %bitcast.9), custom_call_target="tpu_custom_call" | custom-call | flops 1610612736 | bytes 4194304 | tf_op jit(solution)/shard_map/pallas_call | solution.py:44
  82.9 2.7 %collective-permute-start.17 = (bf16[4,3,32,512]{3,2,1,0:T(8,128)(2,1)S(1)}, bf16[4,3,32,512]{3,2,1,0:T(8,128)(2,1)S(1)}, u32[]{:S(2)}, u32[]{:S(2)}) collective-permute-start(bf16[4,3,32,512]{3,2,1,0:T(8,128)(2,1)S(1)} %shard_map.76), channel_id=1, source_target_pairs={{0,3},{1,0},{2,1},{3,2},{4,7},{5,4},{6,5},{7,6},{8,11},{9,8},{10,9... | collective-permute-start | bytes 1179656 | tf_op jit(solution)/shard_map/ppermute | solution.py:40
  85.6 3.2 %shard_map.73.own = f32[4,3,32,512]{3,2,1,0:T(8,128)S(1)} custom-call(bf16[4,3,32,512]{3,2,1,0:T(8,128)(2,1)S(1)} %shard_map.72.w_ref, bf16[2048,512]{1,0:T(8,128)(2,1)S(1)} %copy-done.3, bf16[2048,512]{1,0:T(8,128)(2,1)S(1)} %copy-done.5, f32[1,2048]{1,0:T(1,128)S(1)} %bitcast.10), custom_call_target="tpu_custom_call" | custom-call | flops 1610612736 | bytes 4194304 | tf_op jit(solution)/shard_map/pallas_call | solution.py:44
  89.0 4.0 %collective-permute-done.17.r3 = bf16[4,3,32,512]{3,2,1,0:T(8,128)(2,1)S(1)} collective-permute-done((bf16[4,3,32,512]{3,2,1,0:T(8,128)(2,1)S(1)}, bf16[4,3,32,512]{3,2,1,0:T(8,128)(2,1)S(1)}, u32[]{:S(2)}, u32[]{:S(2)}) %collective-permute-start.17) | collective-permute-done | bytes 393248 | tf_op jit(solution)/shard_map/ppermute | solution.py:40
  93.2 1.0 collective-permute-start.18
  94.2 3.9 %collective-permute-start.19 = (bf16[3,32,512]{2,1,0:T(8,128)(2,1)S(1)}, bf16[3,32,512]{2,1,0:T(8,128)(2,1)S(1)}, u32[]{:S(2)}, u32[]{:S(2)}) collective-permute-start(bf16[3,32,512]{2,1,0:T(8,128)(2,1)S(1)} %get-tuple-element.35), channel_id=1, source_target_pairs={{0,8},{1,9},{2,10},{3,11},{4,12},{5,13},{6,14},{7,15},{8,0},{9,1},... | collective-permute-start | bytes 294920 | tf_op jit(solution)/shard_map/ppermute | solution.py:40
  98.2 1.1 collective-permute-done.18.r1
  99.3 2.5 %collective-permute-done.19.r2 = bf16[3,32,512]{2,1,0:T(8,128)(2,1)S(1)} collective-permute-done((bf16[3,32,512]{2,1,0:T(8,128)(2,1)S(1)}, bf16[3,32,512]{2,1,0:T(8,128)(2,1)S(1)}, u32[]{:S(2)}, u32[]{:S(2)}) %collective-permute-start.19) | collective-permute-done | bytes 98336 | tf_op jit(solution)/shard_map/ppermute | solution.py:40
  101.8 1.0 collective-permute-done.20.r3
  102.8 1.0 collective-permute-start.21
  103.8 0.5 collective-permute-start.22
  104.3 1.3 collective-permute-start.23
  105.6 1.9 %collective-permute-done.21.r1 = bf16[3,32,512]{2,1,0:T(8,128)(2,1)S(1)} collective-permute-done((bf16[3,32,512]{2,1,0:T(8,128)(2,1)S(1)}, bf16[3,32,512]{2,1,0:T(8,128)(2,1)S(1)}, u32[]{:S(2)}, u32[]{:S(2)}) %collective-permute-start.21) | collective-permute-done | bytes 98336 | tf_op jit(solution)/shard_map/ppermute | solution.py:40
  107.5 2.5 %collective-permute-done.22.r2 = bf16[3,32,512]{2,1,0:T(8,128)(2,1)S(1)} collective-permute-done((bf16[3,32,512]{2,1,0:T(8,128)(2,1)S(1)}, bf16[3,32,512]{2,1,0:T(8,128)(2,1)S(1)}, u32[]{:S(2)}, u32[]{:S(2)}) %collective-permute-start.22) | collective-permute-done | bytes 98336 | tf_op jit(solution)/shard_map/ppermute | solution.py:40
  110.0 1.0 collective-permute-done.23.r3
  111.0 1.3 collective-permute-start.24
  112.3 0.9 collective-permute-done.24.earlier
  113.3 1.3 collective-permute-start.25
  114.6 0.6 collective-permute-start.26
  115.2 1.1 collective-permute-start.27
  116.3 1.7 %collective-permute-done.25.r1 = bf16[3,32,512]{2,1,0:T(8,128)(2,1)S(1)} collective-permute-done((bf16[3,32,512]{2,1,0:T(8,128)(2,1)S(1)}, bf16[3,32,512]{2,1,0:T(8,128)(2,1)S(1)}, u32[]{:S(2)}, u32[]{:S(2)}) %collective-permute-start.25) | collective-permute-done | bytes 98336 | tf_op jit(solution)/shard_map/ppermute | solution.py:40
  118.0 2.8 %collective-permute-done.26.r2 = bf16[3,32,512]{2,1,0:T(8,128)(2,1)S(1)} collective-permute-done((bf16[3,32,512]{2,1,0:T(8,128)(2,1)S(1)}, bf16[3,32,512]{2,1,0:T(8,128)(2,1)S(1)}, u32[]{:S(2)}, u32[]{:S(2)}) %collective-permute-start.26) | collective-permute-done | bytes 98336 | tf_op jit(solution)/shard_map/ppermute | solution.py:40
  120.8 1.0 collective-permute-done.27.r3
  121.8 3.2 %collective-permute-start.30 = (bf16[4,3,32,512]{3,2,1,0:T(8,128)(2,1)S(1)}, bf16[4,3,32,512]{3,2,1,0:T(8,128)(2,1)S(1)}, u32[]{:S(2)}, u32[]{:S(2)}) collective-permute-start(bf16[4,3,32,512]{3,2,1,0:T(8,128)(2,1)S(1)} %shard_map.81.refs_0_), channel_id=1, source_target_pairs={{0,3},{1,0},{2,1},{3,2},{4,7},{5,4},{6,5},{7,6},{8,11},{9,8},{10,9... | collective-permute-start | bytes 1179656 | tf_op jit(solution)/shard_map/ppermute | solution.py:40
  125.0 1.5 %collective-permute-start.28 = (bf16[4,3,32,512]{3,2,1,0:T(8,128)(2,1)S(1)}, bf16[4,3,32,512]{3,2,1,0:T(8,128)(2,1)S(1)}, u32[]{:S(2)}, u32[]{:S(2)}) collective-permute-start(bf16[4,3,32,512]{3,2,1,0:T(8,128)(2,1)S(1)} %shard_map.81.refs_0_), channel_id=1, source_target_pairs={{0,2},{1,3},{2,0},{3,1},{4,6},{5,7},{6,4},{7,5},{8,10},{9,11},{10,... | collective-permute-start | bytes 1179656 | tf_op jit(solution)/shard_map/ppermute | solution.py:40
  126.5 2.9 %shard_map.82.refs_2_ = f32[2048,512]{1,0:T(8,128)S(1)} custom-call(bf16[4,3,32,512]{3,2,1,0:T(8,128)(2,1)S(1)} %shard_map.81.refs_0_, bf16[2048,512]{1,0:T(8,128)(2,1)S(1)} %copy-done), custom_call_target="tpu_custom_call" | custom-call | flops 805306368 | bytes 6291456 | tf_op jit(solution)/shard_map/pallas_call | solution.py:44
  129.4 5.1 %collective-permute-done.30.refs_0_ = bf16[4,3,32,512]{3,2,1,0:T(8,128)(2,1)S(1)} collective-permute-done((bf16[4,3,32,512]{3,2,1,0:T(8,128)(2,1)S(1)}, bf16[4,3,32,512]{3,2,1,0:T(8,128)(2,1)S(1)}, u32[]{:S(2)}, u32[]{:S(2)}) %collective-permute-start.30) | collective-permute-done | bytes 393248 | tf_op jit(solution)/shard_map/ppermute | solution.py:40
  134.5 2.9 %shard_map.83.refs_2_ = f32[2048,512]{1,0:T(8,128)S(1)} custom-call(bf16[4,3,32,512]{3,2,1,0:T(8,128)(2,1)S(1)} %collective-permute-done.30.refs_0_, bf16[2048,512]{1,0:T(8,128)(2,1)S(1)} %copy-done, f32[2048,512]{1,0:T(8,128)S(1)} %shard_map.82.refs_2_), custom_call_target="tpu_custom_call" | custom-call | flops 805306368 | bytes 6291456 | tf_op jit(solution)/shard_map/pallas_call | solution.py:44
  137.4 0.7 collective-permute-done.29.refs_0_
  138.2 2.9 %shard_map.84.refs_3_ = f32[2048,512]{1,0:T(8,128)S(1)} custom-call(bf16[4,3,32,512]{3,2,1,0:T(8,128)(2,1)S(1)} %collective-permute-done.29.refs_0_, bf16[2048,512]{1,0:T(8,128)(2,1)S(1)} %copy-done, f32[2048,512]{1,0:T(8,128)S(1)} %shard_map.83.refs_2_), custom_call_target="tpu_custom_call" | custom-call | flops 805306368 | bytes 6291456 | tf_op jit(solution)/shard_map/pallas_call | solution.py:44
  141.1 4.7 %shard_map.85 = bf16[2048,512]{1,0:T(8,128)(2,1)} custom-call(bf16[4,3,32,512]{3,2,1,0:T(8,128)(2,1)S(1)} %collective-permute-done.28.refs_0_, bf16[2048,512]{1,0:T(8,128)(2,1)S(1)} %copy-done, f32[1,512]{1,0:T(1,128)S(1)} %bitcast.2, f32[2048,512]{1,0:T(8,128)S(1)} %shard_map.84.refs_3_), custom_call_target="tpu_custom_call" | custom-call | flops 805306368 | bytes 6291456 | tf_op jit(solution)/shard_map/pallas_call | solution.py:44
  (38 shorter events, 1.6 us)
Async XLA Ops:
  0.0 3.2 %copy-start.6 = (f32[2048]{0:T(1024)S(1)}, f32[2048]{0:T(1024)}, u32[]{:S(2)}) copy-start(f32[2048]{0:T(1024)} %param.9) | copy-start | bytes 24580
  0.2 1.9 %copy-start.1 = (f32[512,1536]{1,0:T(8,128)S(1)}, f32[512,1536]{1,0:T(8,128)}, u32[]{:S(2)}) copy-start(f32[512,1536]{1,0:T(8,128)} %w_ref.1) | copy-start | bytes 9437188
  2.1 1.6 %copy-start.3 = (bf16[2048,512]{1,0:T(8,128)(2,1)S(1)}, bf16[2048,512]{1,0:T(8,128)(2,1)}, u32[]{:S(2)}) copy-start(bf16[2048,512]{1,0:T(8,128)(2,1)} %k_ref.15) | copy-start | bytes 6291460
  3.7 1.6 %copy-start.4 = (bf16[2048,512]{1,0:T(8,128)(2,1)S(1)}, bf16[2048,512]{1,0:T(8,128)(2,1)}, u32[]{:S(2)}) copy-start(bf16[2048,512]{1,0:T(8,128)(2,1)} %v_ref.15) | copy-start | bytes 6291460
  8.5 15.6 %collective-permute-start = (bf16[4,3,32,512]{3,2,1,0:T(8,128)(2,1)S(1)}, bf16[4,3,32,512]{3,2,1,0:T(8,128)(2,1)S(1)}, u32[]{:S(2)}, u32[]{:S(2)}) collective-permute-start(bf16[4,3,32,512]{3,2,1,0:T(8,128)(2,1)S(1)} %shard_map.66), channel_id=1, source_target_pairs={{0,1},{1,2},{2,3},{3,0},{4,5},{5,6},{6,7},{7,4},{8,9},{9,10},{10,1... | collective-permute-start | bytes 1179656 | tf_op jit(solution)/shard_map/ppermute | solution.py:40
  13.3 10.8 %collective-permute-start.1 = (bf16[4,3,32,512]{3,2,1,0:T(8,128)(2,1)S(1)}, bf16[4,3,32,512]{3,2,1,0:T(8,128)(2,1)S(1)}, u32[]{:S(2)}, u32[]{:S(2)}) collective-permute-start(bf16[4,3,32,512]{3,2,1,0:T(8,128)(2,1)S(1)} %shard_map.67), channel_id=1, source_target_pairs={{0,2},{1,3},{2,0},{3,1},{4,6},{5,7},{6,4},{7,5},{8,10},{9,11},{10,... | collective-permute-start | bytes 1179656 | tf_op jit(solution)/shard_map/ppermute | solution.py:40
  19.4 7.8 %collective-permute-start.2 = (bf16[4,3,32,512]{3,2,1,0:T(8,128)(2,1)S(1)}, bf16[4,3,32,512]{3,2,1,0:T(8,128)(2,1)S(1)}, u32[]{:S(2)}, u32[]{:S(2)}) collective-permute-start(bf16[4,3,32,512]{3,2,1,0:T(8,128)(2,1)S(1)} %shard_map.68), channel_id=1, source_target_pairs={{0,3},{1,0},{2,1},{3,2},{4,7},{5,4},{6,5},{7,6},{8,11},{9,8},{10,9... | collective-permute-start | bytes 1179656 | tf_op jit(solution)/shard_map/ppermute | solution.py:40
  24.1 42.8 %copy-start.5 = (bf16[2048,512]{1,0:T(8,128)(2,1)S(1)}, bf16[2048,512]{1,0:T(8,128)(2,1)}, u32[]{:S(2)}) copy-start(bf16[2048,512]{1,0:T(8,128)(2,1)} %v_ref.15) | copy-start | bytes 6291460
  27.4 5.9 %collective-permute-start.3 = (bf16[3,32,512]{2,1,0:T(8,128)(2,1)S(1)}, bf16[3,32,512]{2,1,0:T(8,128)(2,1)S(1)}, u32[]{:S(2)}, u32[]{:S(2)}) collective-permute-start(bf16[3,32,512]{2,1,0:T(8,128)(2,1)S(1)} %get-tuple-element.28), channel_id=1, source_target_pairs={{0,4},{1,5},{2,6},{3,7},{4,8},{5,9},{6,10},{7,11},{8,12},{9,13},{1... | collective-permute-start | bytes 294920 | tf_op jit(solution)/shard_map/ppermute | solution.py:40
  29.0 6.5 %collective-permute-start.4 = (bf16[3,32,512]{2,1,0:T(8,128)(2,1)S(1)}, bf16[3,32,512]{2,1,0:T(8,128)(2,1)S(1)}, u32[]{:S(2)}, u32[]{:S(2)}) collective-permute-start(bf16[3,32,512]{2,1,0:T(8,128)(2,1)S(1)} %get-tuple-element.29), channel_id=1, source_target_pairs={{0,8},{1,9},{2,10},{3,11},{4,12},{5,13},{6,14},{7,15},{8,0},{9,1},... | collective-permute-start | bytes 294920 | tf_op jit(solution)/shard_map/ppermute | solution.py:40
  31.9 4.6 %collective-permute-start.5 = (bf16[3,32,512]{2,1,0:T(8,128)(2,1)S(1)}, bf16[3,32,512]{2,1,0:T(8,128)(2,1)S(1)}, u32[]{:S(2)}, u32[]{:S(2)}) collective-permute-start(bf16[3,32,512]{2,1,0:T(8,128)(2,1)S(1)} %get-tuple-element.30), channel_id=1, source_target_pairs={{0,12},{1,13},{2,14},{3,15},{4,0},{5,1},{6,2},{7,3},{8,4},{9,5},{1... | collective-permute-start | bytes 294920 | tf_op jit(solution)/shard_map/ppermute | solution.py:40
  36.6 7.3 %collective-permute-start.6 = (bf16[3,32,512]{2,1,0:T(8,128)(2,1)S(1)}, bf16[3,32,512]{2,1,0:T(8,128)(2,1)S(1)}, u32[]{:S(2)}, u32[]{:S(2)}) collective-permute-start(bf16[3,32,512]{2,1,0:T(8,128)(2,1)S(1)} %shard_map.70.own), channel_id=1, source_target_pairs={{0,48},{1,49},{2,50},{3,51},{4,52},{5,53},{6,54},{7,55},{8,56},{9,... | collective-permute-start | bytes 294920 | tf_op jit(solution)/shard_map/ppermute | solution.py:40
  40.7 6.2 %collective-permute-start.7 = (bf16[3,32,512]{2,1,0:T(8,128)(2,1)S(1)}, bf16[3,32,512]{2,1,0:T(8,128)(2,1)S(1)}, u32[]{:S(2)}, u32[]{:S(2)}) collective-permute-start(bf16[3,32,512]{2,1,0:T(8,128)(2,1)S(1)} %shard_map.70.own), channel_id=1, source_target_pairs={{0,32},{1,33},{2,34},{3,35},{4,36},{5,37},{6,38},{7,39},{8,40},{9,... | collective-permute-start | bytes 294920 | tf_op jit(solution)/shard_map/ppermute | solution.py:40
  40.7 6.9 %collective-permute-start.8 = (bf16[3,32,512]{2,1,0:T(8,128)(2,1)S(1)}, bf16[3,32,512]{2,1,0:T(8,128)(2,1)S(1)}, u32[]{:S(2)}, u32[]{:S(2)}) collective-permute-start(bf16[3,32,512]{2,1,0:T(8,128)(2,1)S(1)} %shard_map.70.own), channel_id=1, source_target_pairs={{0,16},{1,17},{2,18},{3,19},{4,20},{5,21},{6,22},{7,23},{8,24},{9,... | collective-permute-start | bytes 294920 | tf_op jit(solution)/shard_map/ppermute | solution.py:40
  47.6 6.2 %collective-permute-start.10 = (bf16[3,32,512]{2,1,0:T(8,128)(2,1)S(1)}, bf16[3,32,512]{2,1,0:T(8,128)(2,1)S(1)}, u32[]{:S(2)}, u32[]{:S(2)}) collective-permute-start(bf16[3,32,512]{2,1,0:T(8,128)(2,1)S(1)} %get-tuple-element.32.own), channel_id=1, source_target_pairs={{0,8},{1,9},{2,10},{3,11},{4,12},{5,13},{6,14},{7,15},{8,0},{9,1},... | collective-permute-start | bytes 294920 | tf_op jit(solution)/shard_map/ppermute | solution.py:40
  49.6 5.8 %collective-permute-start.11 = (bf16[3,32,512]{2,1,0:T(8,128)(2,1)S(1)}, bf16[3,32,512]{2,1,0:T(8,128)(2,1)S(1)}, u32[]{:S(2)}, u32[]{:S(2)}) collective-permute-start(bf16[3,32,512]{2,1,0:T(8,128)(2,1)S(1)} %get-tuple-element.32.own), channel_id=1, source_target_pairs={{0,4},{1,5},{2,6},{3,7},{4,8},{5,9},{6,10},{7,11},{8,12},{9,13},{1... | collective-permute-start | bytes 294920 | tf_op jit(solution)/shard_map/ppermute | solution.py:40
  51.1 5.8 %collective-permute-start.9 = (bf16[3,32,512]{2,1,0:T(8,128)(2,1)S(1)}, bf16[3,32,512]{2,1,0:T(8,128)(2,1)S(1)}, u32[]{:S(2)}, u32[]{:S(2)}) collective-permute-start(bf16[3,32,512]{2,1,0:T(8,128)(2,1)S(1)} %get-tuple-element.32.own), channel_id=1, source_target_pairs={{0,12},{1,13},{2,14},{3,15},{4,0},{5,1},{6,2},{7,3},{8,4},{9,5},{1... | collective-permute-start | bytes 294920 | tf_op jit(solution)/shard_map/ppermute | solution.py:40
  56.9 9.9 %collective-permute-start.12 = (bf16[4,3,32,512]{3,2,1,0:T(8,128)(2,1)S(1)}, bf16[4,3,32,512]{3,2,1,0:T(8,128)(2,1)S(1)}, u32[]{:S(2)}, u32[]{:S(2)}) collective-permute-start(bf16[4,3,32,512]{3,2,1,0:T(8,128)(2,1)S(1)} %shard_map.72.w_ref), channel_id=1, source_target_pairs={{0,3},{1,0},{2,1},{3,2},{4,7},{5,4},{6,5},{7,6},{8,11},{9,8},{10,9... | collective-permute-start | bytes 1179656 | tf_op jit(solution)/shard_map/ppermute | solution.py:40
  59.6 16.8 %collective-permute-start.14 = (bf16[4,3,32,512]{3,2,1,0:T(8,128)(2,1)S(1)}, bf16[4,3,32,512]{3,2,1,0:T(8,128)(2,1)S(1)}, u32[]{:S(2)}, u32[]{:S(2)}) collective-permute-start(bf16[4,3,32,512]{3,2,1,0:T(8,128)(2,1)S(1)} %shard_map.72.w_ref), channel_id=1, source_target_pairs={{0,2},{1,3},{2,0},{3,1},{4,6},{5,7},{6,4},{7,5},{8,10},{9,11},{10,... | collective-permute-start | bytes 1179656 | tf_op jit(solution)/shard_map/ppermute | solution.py:40
  63.1 16.5 %collective-permute-start.16 = (bf16[4,3,32,512]{3,2,1,0:T(8,128)(2,1)S(1)}, bf16[4,3,32,512]{3,2,1,0:T(8,128)(2,1)S(1)}, u32[]{:S(2)}, u32[]{:S(2)}) collective-permute-start(bf16[4,3,32,512]{3,2,1,0:T(8,128)(2,1)S(1)} %shard_map.72.w_ref), channel_id=1, source_target_pairs={{0,1},{1,2},{2,3},{3,0},{4,5},{5,6},{6,7},{7,4},{8,9},{9,10},{10,1... | collective-permute-start | bytes 1179656 | tf_op jit(solution)/shard_map/ppermute | solution.py:40
  70.0 18.8 %collective-permute-start.13 = (bf16[4,3,32,512]{3,2,1,0:T(8,128)(2,1)S(1)}, bf16[4,3,32,512]{3,2,1,0:T(8,128)(2,1)S(1)}, u32[]{:S(2)}, u32[]{:S(2)}) collective-permute-start(bf16[4,3,32,512]{3,2,1,0:T(8,128)(2,1)S(1)} %shard_map.74), channel_id=1, source_target_pairs={{0,1},{1,2},{2,3},{3,0},{4,5},{5,6},{6,7},{7,4},{8,9},{9,10},{10,1... | collective-permute-start | bytes 1179656 | tf_op jit(solution)/shard_map/ppermute | solution.py:40
  79.6 9.5 %collective-permute-start.15 = (bf16[4,3,32,512]{3,2,1,0:T(8,128)(2,1)S(1)}, bf16[4,3,32,512]{3,2,1,0:T(8,128)(2,1)S(1)}, u32[]{:S(2)}, u32[]{:S(2)}) collective-permute-start(bf16[4,3,32,512]{3,2,1,0:T(8,128)(2,1)S(1)} %shard_map.75), channel_id=1, source_target_pairs={{0,2},{1,3},{2,0},{3,1},{4,6},{5,7},{6,4},{7,5},{8,10},{9,11},{10,... | collective-permute-start | bytes 1179656 | tf_op jit(solution)/shard_map/ppermute | solution.py:40
  82.9 10.1 %collective-permute-start.17 = (bf16[4,3,32,512]{3,2,1,0:T(8,128)(2,1)S(1)}, bf16[4,3,32,512]{3,2,1,0:T(8,128)(2,1)S(1)}, u32[]{:S(2)}, u32[]{:S(2)}) collective-permute-start(bf16[4,3,32,512]{3,2,1,0:T(8,128)(2,1)S(1)} %shard_map.76), channel_id=1, source_target_pairs={{0,3},{1,0},{2,1},{3,2},{4,7},{5,4},{6,5},{7,6},{8,11},{9,8},{10,9... | collective-permute-start | bytes 1179656 | tf_op jit(solution)/shard_map/ppermute | solution.py:40
  88.8 37.7 %copy-start = (bf16[2048,512]{1,0:T(8,128)(2,1)S(1)}, bf16[2048,512]{1,0:T(8,128)(2,1)}, u32[]{:S(2)}) copy-start(bf16[2048,512]{1,0:T(8,128)(2,1)} %refs_1_.7) | copy-start | bytes 6291460
  93.2 6.1 %collective-permute-start.18 = (bf16[3,32,512]{2,1,0:T(8,128)(2,1)S(1)}, bf16[3,32,512]{2,1,0:T(8,128)(2,1)S(1)}, u32[]{:S(2)}, u32[]{:S(2)}) collective-permute-start(bf16[3,32,512]{2,1,0:T(8,128)(2,1)S(1)} %get-tuple-element.34), channel_id=1, source_target_pairs={{0,4},{1,5},{2,6},{3,7},{4,8},{5,9},{6,10},{7,11},{8,12},{9,13},{1... | collective-permute-start | bytes 294920 | tf_op jit(solution)/shard_map/ppermute | solution.py:40
  94.2 7.6 %collective-permute-start.19 = (bf16[3,32,512]{2,1,0:T(8,128)(2,1)S(1)}, bf16[3,32,512]{2,1,0:T(8,128)(2,1)S(1)}, u32[]{:S(2)}, u32[]{:S(2)}) collective-permute-start(bf16[3,32,512]{2,1,0:T(8,128)(2,1)S(1)} %get-tuple-element.35), channel_id=1, source_target_pairs={{0,8},{1,9},{2,10},{3,11},{4,12},{5,13},{6,14},{7,15},{8,0},{9,1},... | collective-permute-start | bytes 294920 | tf_op jit(solution)/shard_map/ppermute | solution.py:40
  98.2 4.6 %collective-permute-start.20 = (bf16[3,32,512]{2,1,0:T(8,128)(2,1)S(1)}, bf16[3,32,512]{2,1,0:T(8,128)(2,1)S(1)}, u32[]{:S(2)}, u32[]{:S(2)}) collective-permute-start(bf16[3,32,512]{2,1,0:T(8,128)(2,1)S(1)} %get-tuple-element.36), channel_id=1, source_target_pairs={{0,12},{1,13},{2,14},{3,15},{4,0},{5,1},{6,2},{7,3},{8,4},{9,5},{1... | collective-permute-start | bytes 294920 | tf_op jit(solution)/shard_map/ppermute | solution.py:40
  102.8 4.7 %collective-permute-start.21 = (bf16[3,32,512]{2,1,0:T(8,128)(2,1)S(1)}, bf16[3,32,512]{2,1,0:T(8,128)(2,1)S(1)}, u32[]{:S(2)}, u32[]{:S(2)}) collective-permute-start(bf16[3,32,512]{2,1,0:T(8,128)(2,1)S(1)} %shard_map.78.own), channel_id=1, source_target_pairs={{0,48},{1,49},{2,50},{3,51},{4,52},{5,53},{6,54},{7,55},{8,56},{9,... | collective-permute-start | bytes 294920 | tf_op jit(solution)/shard_map/ppermute | solution.py:40
  103.8 6.2 %collective-permute-start.22 = (bf16[3,32,512]{2,1,0:T(8,128)(2,1)S(1)}, bf16[3,32,512]{2,1,0:T(8,128)(2,1)S(1)}, u32[]{:S(2)}, u32[]{:S(2)}) collective-permute-start(bf16[3,32,512]{2,1,0:T(8,128)(2,1)S(1)} %shard_map.78.own), channel_id=1, source_target_pairs={{0,32},{1,33},{2,34},{3,35},{4,36},{5,37},{6,38},{7,39},{8,40},{9,... | collective-permute-start | bytes 294920 | tf_op jit(solution)/shard_map/ppermute | solution.py:40
  104.3 6.7 %collective-permute-start.23 = (bf16[3,32,512]{2,1,0:T(8,128)(2,1)S(1)}, bf16[3,32,512]{2,1,0:T(8,128)(2,1)S(1)}, u32[]{:S(2)}, u32[]{:S(2)}) collective-permute-start(bf16[3,32,512]{2,1,0:T(8,128)(2,1)S(1)} %shard_map.78.own), channel_id=1, source_target_pairs={{0,16},{1,17},{2,18},{3,19},{4,20},{5,21},{6,22},{7,23},{8,24},{9,... | collective-permute-start | bytes 294920 | tf_op jit(solution)/shard_map/ppermute | solution.py:40
  111.0 2.2 %collective-permute-start.24 = (bf16[3,32,512]{2,1,0:T(8,128)(2,1)S(1)}, bf16[3,32,512]{2,1,0:T(8,128)(2,1)S(1)}, u32[]{:S(2)}, u32[]{:S(2)}) collective-permute-start(bf16[3,32,512]{2,1,0:T(8,128)(2,1)S(1)} %get-tuple-element.37), channel_id=1, source_target_pairs={{0,64},{1,65},{2,66},{3,67},{4,68},{5,69},{6,70},{7,71},{8,72},{9,... | collective-permute-start | bytes 294920 | tf_op jit(solution)/shard_map/ppermute | solution.py:288
  113.3 4.7 %collective-permute-start.25 = (bf16[3,32,512]{2,1,0:T(8,128)(2,1)S(1)}, bf16[3,32,512]{2,1,0:T(8,128)(2,1)S(1)}, u32[]{:S(2)}, u32[]{:S(2)}) collective-permute-start(bf16[3,32,512]{2,1,0:T(8,128)(2,1)S(1)} %shard_map.80.own), channel_id=1, source_target_pairs={{0,12},{1,13},{2,14},{3,15},{4,0},{5,1},{6,2},{7,3},{8,4},{9,5},{1... | collective-permute-start | bytes 294920 | tf_op jit(solution)/shard_map/ppermute | solution.py:40
  114.6 6.2 %collective-permute-start.26 = (bf16[3,32,512]{2,1,0:T(8,128)(2,1)S(1)}, bf16[3,32,512]{2,1,0:T(8,128)(2,1)S(1)}, u32[]{:S(2)}, u32[]{:S(2)}) collective-permute-start(bf16[3,32,512]{2,1,0:T(8,128)(2,1)S(1)} %shard_map.80.own), channel_id=1, source_target_pairs={{0,8},{1,9},{2,10},{3,11},{4,12},{5,13},{6,14},{7,15},{8,0},{9,1},... | collective-permute-start | bytes 294920 | tf_op jit(solution)/shard_map/ppermute | solution.py:40
  115.2 6.5 %collective-permute-start.27 = (bf16[3,32,512]{2,1,0:T(8,128)(2,1)S(1)}, bf16[3,32,512]{2,1,0:T(8,128)(2,1)S(1)}, u32[]{:S(2)}, u32[]{:S(2)}) collective-permute-start(bf16[3,32,512]{2,1,0:T(8,128)(2,1)S(1)} %shard_map.80.own), channel_id=1, source_target_pairs={{0,4},{1,5},{2,6},{3,7},{4,8},{5,9},{6,10},{7,11},{8,12},{9,13},{1... | collective-permute-start | bytes 294920 | tf_op jit(solution)/shard_map/ppermute | solution.py:40
  121.8 12.7 %collective-permute-start.30 = (bf16[4,3,32,512]{3,2,1,0:T(8,128)(2,1)S(1)}, bf16[4,3,32,512]{3,2,1,0:T(8,128)(2,1)S(1)}, u32[]{:S(2)}, u32[]{:S(2)}) collective-permute-start(bf16[4,3,32,512]{3,2,1,0:T(8,128)(2,1)S(1)} %shard_map.81.refs_0_), channel_id=1, source_target_pairs={{0,3},{1,0},{2,1},{3,2},{4,7},{5,4},{6,5},{7,6},{8,11},{9,8},{10,9... | collective-permute-start | bytes 1179656 | tf_op jit(solution)/shard_map/ppermute | solution.py:40
  125.0 13.2 %collective-permute-start.29 = (bf16[4,3,32,512]{3,2,1,0:T(8,128)(2,1)S(1)}, bf16[4,3,32,512]{3,2,1,0:T(8,128)(2,1)S(1)}, u32[]{:S(2)}, u32[]{:S(2)}) collective-permute-start(bf16[4,3,32,512]{3,2,1,0:T(8,128)(2,1)S(1)} %shard_map.81.refs_0_), channel_id=1, source_target_pairs={{0,1},{1,2},{2,3},{3,0},{4,5},{5,6},{6,7},{7,4},{8,9},{9,10},{10,1... | collective-permute-start | bytes 1179656 | tf_op jit(solution)/shard_map/ppermute | solution.py:40
  125.0 16.1 %collective-permute-start.28 = (bf16[4,3,32,512]{3,2,1,0:T(8,128)(2,1)S(1)}, bf16[4,3,32,512]{3,2,1,0:T(8,128)(2,1)S(1)}, u32[]{:S(2)}, u32[]{:S(2)}) collective-permute-start(bf16[4,3,32,512]{3,2,1,0:T(8,128)(2,1)S(1)} %shard_map.81.refs_0_), channel_id=1, source_target_pairs={{0,2},{1,3},{2,0},{3,1},{4,6},{5,7},{6,4},{7,5},{8,10},{9,11},{10,... | collective-permute-start | bytes 1179656 | tf_op jit(solution)/shard_map/ppermute | solution.py:40
  137.4 3.7 %copy-start.2 = (f32[512]{0:T(512)S(1)}, f32[512]{0:T(512)}, u32[]{:S(2)}) copy-start(f32[512]{0:T(512)} %param.11) | copy-start | bytes 6148

commit v2 on v1

v2 whole, which is shorter than its diff:
```python
import functools
import itertools

import jax
import jax.numpy as jnp
from jax import lax
from jax.experimental import pallas as pl
from jax.experimental.pallas import tpu as pltpu
from jax.sharding import PartitionSpec as P

SIDE = 4
AXES = ("order", "tok")
BF = jnp.bfloat16
F32 = jnp.float32
NT = (((1,), (1,)), ((), ()))
NN = (((1,), (0,)), ((), ()))
VMEM = pl.BlockSpec(memory_space=pltpu.VMEM)
SMEM = pl.BlockSpec(memory_space=pltpu.SMEM)


def flat(core, z, y, x):
    return ((core * SIDE + z % SIDE) * SIDE + y % SIDE) * SIDE + x % SIDE


def hop_pairs(level, step):
    pairs = []
    for core, z, y, x in itertools.product(range(2), *[range(SIDE)] * 3):
        dz = dy = dx = 0
        if level == 2:
            dz = step
        elif (level == 0) == (core == 0):
            dx = step
        else:
            dy = step
        pairs.append((flat(core, z, y, x), flat(core, z + dz, y + dy, x + dx)))
    return pairs


def hop(x, level, step):
    return lax.ppermute(x, AXES, hop_pairs(level, step % SIDE))


HBM = pl.BlockSpec(memory_space=pltpu.HBM)


def call(kernel, outs, specs, args, cost, scratch=(), out_spec=VMEM, limit=24 << 20):
    return pl.pallas_call(
        kernel,
        out_shape=outs,
        in_specs=specs or [VMEM] * len(args),
        out_specs=jax.tree.map(lambda _: out_spec, outs),
        scratch_shapes=scratch,
        compiler_params=pltpu.CompilerParams(vmem_limit_bytes=limit),
        cost_estimate=pl.CostEstimate(flops=cost[0], bytes_accessed=cost[1], transcendentals=0),
    )(*args)


def arr(shape, dtype):
    return jax.ShapeDtypeStruct(shape, dtype)


def first_kernel(factor, tile, place, *refs):
    sources, (b0, b2, own, g1, g3), scratch = refs[:4], refs[4:9], refs[9:]
    w_ref, k_ref, v_ref, rate_ref, turned, slab, b1, b3, grads, hiddens, sems = scratch
    copies = [
        pltpu.make_async_copy(src, dst, sems.at[i])
        for i, (src, dst) in enumerate(zip(sources, scratch[:4]))
    ]
    for copy in copies:
        copy.start()
    copies[0].wait()
    width = w_ref.shape[0]
    lines = width // (SIDE * SIDE)
    for m in range(2):
        part = w_ref[:, m * width : (m + 1) * width].astype(BF)
        turned[m] = part.T.reshape(SIDE * SIDE, lines, width)
    turned[2] = w_ref[:, 2 * width :].astype(BF).reshape(SIDE * SIDE, lines, width)
    for r, block in enumerate((b0, b1, b2, b3)):
        for s in range(SIDE):
            group = place[r * SIDE + s]
            for m in range(3):
                block[s, m] = turned[m, group]
    mine = place[0]
    for m in range(2):
        start = pl.multiple_of(m * width + (mine // SIDE) * 128, 128)
        slab[...] = w_ref[:, pl.ds(start, 128)].T.reshape(SIDE, lines, width)
        own[m] = slab[mine % SIDE]
    own[2] = w_ref[pl.ds(pl.multiple_of(mine * lines, lines), lines), 2 * width :]
    for copy in copies[1:]:
        copy.wait()
    gradient_kernel(factor, tile, 2, b1, b3, k_ref, v_ref, rate_ref, g1, g3, grads, hiddens)


def rows_of(w_refs, m):
    parts = [w[:, m].reshape(-1, w.shape[3]) for w in w_refs]
    return parts[0] if len(parts) == 1 else jnp.concatenate(parts, axis=0)


def gradient_kernel(factor, tile, count, *refs):
    w_refs, (k_ref, v_ref, rate_ref) = refs[:count], refs[count : count + 3]
    outs, (grads, hiddens) = refs[count + 3 : 2 * count + 3], refs[2 * count + 3 :]
    wgu = jnp.concatenate([rows_of(w_refs, 0), rows_of(w_refs, 1)], axis=0)
    wd = rows_of(w_refs, 2)
    units, width = wd.shape
    for i in range(k_ref.shape[0] // tile):
        rows = slice(i * tile, (i + 1) * tile)
        scale = -(rate_ref[:, rows] * factor)
        gu = lax.dot_general(wgu, k_ref[rows, :], NT, preferred_element_type=F32)
        hidden_grad = lax.dot_general(wd, v_ref[rows, :], NT, preferred_element_type=F32) * scale
        gate = gu[:units]
        up = gu[units:]
        sig = 0.5 * jnp.tanh(0.5 * gate) + 0.5
        act = gate * sig
        hiddens[:, rows] = (act * up * scale).astype(BF)
        grads[:units, rows] = (hidden_grad * up * (sig + act * (1.0 - sig))).astype(BF)
        grads[units:, rows] = (hidden_grad * act).astype(BF)
    upper = lax.dot_general(grads[...], k_ref[...], NN, preferred_element_type=F32)
    lower = lax.dot_general(hiddens[...], v_ref[...], NN, preferred_element_type=F32)
    lines = outs[0].shape[2]
    per = units // count
    for b, out in enumerate(outs):
        own = slice(b * per, (b + 1) * per)
        for m, part in enumerate((upper[:units], upper[units:], lower)):
            out[:, m] = part[own].reshape(SIDE, lines, width).astype(out.dtype)


def gradient_blocks(weights, keys, values, rates, factor, dtype, tile=256):
    count = len(weights)
    units = count * weights[0].shape[0] * weights[0].shape[2]
    tokens, width = keys.shape
    return call(
        functools.partial(gradient_kernel, factor, tile, count),
        [arr(w.shape, dtype) for w in weights],
        None,
        (*weights, keys, values, rates),
        (12 * tokens * width * units, 4 * tokens * width),
        [pltpu.VMEM((2 * units, tokens), BF), pltpu.VMEM((units, tokens), BF)],
    )


def near_kernel(own, r1, r3, out):
    out[...] = own[...] + r1[...].astype(F32) + r3[...].astype(F32)


def scatter_kernel(near, r2, keep, s1, s2, s3):
    for s, out in enumerate((keep, s1, s2, s3)):
        out[...] = (near[s] + r2[s].astype(F32)).astype(out.dtype)


def add_kernel(own, r1, r2, r3, out):
    out[...] = (
        own[...] + r1[...].astype(F32) + r2[...].astype(F32) + r3[...].astype(F32)
    ).astype(out.dtype)


def update_kernel(weights, own, r1, r2, r3, new, new_bf):
    total = (
        own[...].astype(F32) + r1[...].astype(F32) + r2[...].astype(F32) + r3[...].astype(F32)
    )
    value = weights[...] - total
    new[...] = value
    new_bf[...] = value.astype(BF)


def change_kernel(start, weights, own, r1, r2, r3, change, change_bf):
    total = (
        own[...].astype(F32) + r1[...].astype(F32) + r2[...].astype(F32) + r3[...].astype(F32)
    )
    value = (weights[...] - total) - start[...]
    change[...] = value
    change_bf[...] = value.astype(BF)


def closing_kernel(start, earlier, change, out):
    out[...] = ((start[...] + earlier[...].astype(F32)) + change[...]).astype(BF)


def join_kernel(own, r1, r2, r3, out):
    for s, part in enumerate((own, r1, r2, r3)):
        out[s] = part[...]


def apply_kernel(tile, count, first, last, *refs):
    refs = list(refs)
    w_refs, q_ref = refs[:count], refs[count]
    refs = refs[count + 1 :]
    gain = refs.pop(0) if last else None
    so_far = None if first else refs.pop(0)
    out = refs.pop(0)
    wgu = jnp.concatenate([rows_of(w_refs, 0), rows_of(w_refs, 1)], axis=0)
    wd = rows_of(w_refs, 2)
    units = wd.shape[0]
    copies = []
    for i in range(q_ref.shape[0] // tile):
        rows = slice(i * tile, (i + 1) * tile)
        gu = lax.dot_general(q_ref[rows, :], wgu, NT, preferred_element_type=F32)
        gate = gu[:, :units]
        up = gu[:, units:]
        act = gate * (0.5 * jnp.tanh(0.5 * gate) + 0.5)
        y = lax.dot_general((act * up).astype(BF), wd, NN, preferred_element_type=F32)
        if so_far is not None:
            y = y + so_far[rows, :]
        if last:
            held, sems = refs
            scale = lax.rsqrt(jnp.mean(y * y, axis=1, keepdims=True) + 1e-06)
            held[rows, :] = (y * scale * gain[...]).astype(BF)
            copies.append(pltpu.make_async_copy(held.at[rows], out.at[rows], sems.at[i]))
            copies[-1].start()
        else:
            out[rows, :] = y
    for copy in copies:
        copy.wait()


def apply_blocks(weights, queries, so_far, gain, tile=256):
    count = len(weights)
    units = count * weights[0].shape[0] * weights[0].shape[2]
    tokens, width = queries.shape
    first, last = so_far is None, gain is not None
    args = (*weights, queries) + ((gain,) if last else ()) + (() if first else (so_far,))
    scratch = ()
    if last:
        scratch = [pltpu.VMEM((tokens, width), BF), pltpu.SemaphoreType.DMA((tokens // tile,))]
    return call(
        functools.partial(apply_kernel, tile, count, first, last),
        arr((tokens, width), BF if last else F32),
        None,
        args,
        (6 * tokens * width * units, 6 * tokens * width),
        scratch,
        out_spec=HBM if last else VMEM,
    )


def ring_parts(x, level):
    parts = {r: hop(x, level, -r) for r in (1, 3, 2)}
    return [parts[r] for r in range(1, SIDE)]


def in_turn(first, *later):
    return lax.optimization_barrier((first, *later))


def combined(own, sent):
    shard = own.shape[1:]
    size = own.size
    near = call(near_kernel, arr(own.shape, F32), None, (own, sent[1], sent[3]), (2 * size, 8 * size))
    keep, *out = call(
        scatter_kernel,
        [arr(shard, F32)] + [arr(shard, BF)] * 3,
        None,
        (near, sent[2]),
        (size, 8 * size),
    )
    got = {r: hop(out[r - 1], 1, r) for r in (1, 3, 2)}
    part = call(add_kernel, arr(shard, BF), None, (keep, got[1], got[2], got[3]), (size, 3 * size))
    return [part] + ring_parts(part, 2)


def first_totals(place, weights, keys, values, rates, factor, tile=256):
    tokens, width = keys.shape
    lines = width // (SIDE * SIDE)
    block = (SIDE, 3, lines, width)
    units = 2 * SIDE * lines
    b0, b2, start, g1, g3 = call(
        functools.partial(first_kernel, factor, tile),
        [arr(block, BF)] * 2 + [arr(block[1:], F32)] + [arr(block, BF)] * 2,
        [SMEM] + [HBM] * 4,
        (place, weights, keys, values, rates),
        (12 * tokens * width * units, 4 * tokens * width),
        [
            pltpu.VMEM(weights.shape, F32),
            pltpu.VMEM(keys.shape, BF),
            pltpu.VMEM(values.shape, BF),
            pltpu.VMEM(rates.shape, F32),
            pltpu.VMEM((3, SIDE * SIDE, lines, width), BF),
            pltpu.VMEM((SIDE, lines, width), F32),
            pltpu.VMEM(block, BF),
            pltpu.VMEM(block, BF),
            pltpu.VMEM((2 * units, tokens), BF),
            pltpu.VMEM((units, tokens), BF),
            pltpu.SemaphoreType.DMA((4,)),
        ],
        limit=52 << 20,
    )
    sent = {1: hop(g1, 0, 1), 3: hop(g3, 0, 3)}
    (g2,) = gradient_blocks([b2], keys, values, rates, factor, BF)
    sent[2] = hop(g2, 0, 2)
    (own,) = gradient_blocks([b0], keys, values, rates, factor, F32)
    return start, combined(own, sent)


def second_totals(blocks, keys, values, rates, factor):
    sent = {}
    (own,) = gradient_blocks([blocks[0]], keys, values, rates, factor, F32)
    own, keys = in_turn(own, keys)
    g1, g3 = gradient_blocks([blocks[1], blocks[3]], keys, values, rates, factor, BF)
    sent[1], sent[3] = hop(g1, 0, 1), hop(g3, 0, 3)
    g1, keys = in_turn(g1, keys)
    (g2,) = gradient_blocks([blocks[2]], keys, values, rates, factor, BF)
    sent[2] = hop(g2, 0, 2)
    return combined(own, sent)


def gathered(shard):
    parts = [shard] + ring_parts(shard, 1)
    block = call(join_kernel, arr((SIDE, *shard.shape), BF), None, parts, (0, 16 * shard.size))
    return [block] + ring_parts(block, 0)


def shards(queries, key_tokens, value_tokens, learn_rates, fast_init, out_gain):
    tokens, width = key_tokens.shape
    factor = (tokens * lax.axis_size("tok")) ** (-0.5)
    core = lax.axis_index("order")
    tok = lax.axis_index("tok")
    x, y = tok % SIDE, (tok // SIDE) % SIDE
    ring = jnp.arange(SIDE, dtype=jnp.int32)
    r1, r2 = ring[:, None], ring[None, :]
    along_x = (x + jnp.where(core == 0, r1, r2)) % SIDE
    along_y = (y + jnp.where(core == 0, r2, r1)) % SIDE
    place = (along_x * SIDE + along_y).reshape(-1).astype(jnp.int32)
    rates = learn_rates.reshape(1, tokens)
    gain = out_gain.reshape(1, width)

    start, parts = first_totals(place, fast_init, key_tokens, value_tokens, rates, factor)
    shard = start.shape
    size = start.size
    first_step, first_bf = call(
        update_kernel, [arr(shard, F32), arr(shard, BF)], None, (start, *parts), (size, 8 * size)
    )
    blocks = gathered(first_bf)
    parts = second_totals(blocks, key_tokens, value_tokens, rates, factor)
    change, change_bf = call(
        change_kernel,
        [arr(shard, F32), arr(shard, BF)],
        None,
        (start, first_step, *parts),
        (size, 8 * size),
    )
    pairs = [(flat(0, *c), flat(1, *c)) for c in itertools.product(*[range(SIDE)] * 3)]
    earlier = lax.ppermute(change_bf, AXES, pairs)
    closing = call(closing_kernel, arr(shard, BF), None, (start, earlier, change), (size, 8 * size))
    blocks = gathered(closing)
    result = apply_blocks([blocks[0]], queries, None, None)
    result = apply_blocks([blocks[1], blocks[3]], queries, result, None)
    return apply_blocks([blocks[2]], queries, result, gain)


def solution(mesh):
    rows = P(AXES, None)
    return jax.shard_map(
        shards,
        mesh=mesh,
        in_specs=(rows, rows, rows, P(AXES), P(), P()),
        out_specs=rows,
        check_vma=False,
    )
```

time: 146 us -> 133 us (0.911)
  Pallas kernels: 40.8 us -> 27.9 us
  waiting for transfers between devices: 46.1 us -> 54.6 us
  starting transfers between devices: 54.5 us -> 48.8 us
  local copies, waits for them, and re-layouts: 4.11 us -> 0.88 us
    pallas_call x22 -> x20, Pallas kernels: 40.8 us -> 27.9 us  [call(): pl.pallas_call(kernel, out_shape=outs, in_specs=specs or [VMEM] * len(arg...]
    ppermute x30, waiting for transfers between devices: 45.2 us -> 53.7 us  [hop(): return lax.ppermute(x, AXES, hop_pairs(level, step % SIDE))]
    ppermute x30, starting transfers between devices: 53.2 us -> 47.5 us  [hop(): return lax.ppermute(x, AXES, hop_pairs(level, step % SIDE))]
    unnamed x14 -> x10, local copies, waits for them, and re-layouts: 3.95 us -> 0.71 us
  transfers between devices with their start and end apart: 31 -> 31, of which waited for: 24 -> 25; matrix products, arithmetic and copies ran while one was open for 0% -> 0% of each run, Pallas kernels for 21% -> 13%
where the time goes in v2:
time: 133 us; the launch traced here: 132 us
  waiting for transfers between devices  54.6 us (41%)
  starting transfers between devices  48.8 us (37%)
  Pallas kernels  27.9 us (21%)
    ppermute x30, waiting for transfers between devices, hop(): return lax.ppermute(x, AXES, hop_pairs(level, step % SIDE))  53.7 us
    ppermute x30, starting transfers between devices, hop(): return lax.ppermute(x, AXES, hop_pairs(level, step % SIDE))  47.5 us
    pallas_call x20, Pallas kernels, call(): pl.pallas_call(kernel, out_shape=outs, in_specs=specs or [VMEM] * len(arg...  27.9 us
  transfers between devices with their start and end apart: 31, of which 25 were waited for; matrix products, arithmetic and copies ran while one was open for 0% of the time, Pallas kernels for 13%

profile of v2, /device:TPU:0, one launch (start us, length us, event | category | flops | bytes accessed | tf_op | source)
XLA Modules:
  0.0 132.5 jit_solution(14062671452021710535)
XLA Ops:
  0.2 0.7 copy-done.4
  0.9 7.5 %shard_map.64 = (bf16[4,3,32,512]{3,2,1,0:T(8,128)(2,1)S(1)}, bf16[4,3,32,512]{3,2,1,0:T(8,128)(2,1)S(1)}, f32[3,32,512]{2,1,0:T(8,128)S(1)}, bf16[4,3,32,512]{3...) custom-call(s32[16]{0:T(128)S(1)} %fusion.place, f32[512,1536]{1,0:T(8,128)} %refs_0_.1, bf16[2048,512]{1,0:T(8,128)(2,1)} %refs_1_.10, ...), custom_call_target="tpu_custom_call" | custom-call | flops 3221225472 | bytes 4194304 | tf_op jit(solution)/shard_map/pallas_call | solution.py:47
  8.4 1.6 %collective-permute-start = (bf16[4,3,32,512]{3,2,1,0:T(8,128)(2,1)S(1)}, bf16[4,3,32,512]{3,2,1,0:T(8,128)(2,1)S(1)}, u32[]{:S(2)}, u32[]{:S(2)}) collective-permute-start(bf16[4,3,32,512]{3,2,1,0:T(8,128)(2,1)S(1)} %get-tuple-element.29), channel_id=1, source_target_pairs={{0,1},{1,2},{2,3},{3,0},{4,5},{5,6},{6,7},{7,4},{8,9},{9,10},{10,1... | collective-permute-start | bytes 1179656 | tf_op jit(solution)/shard_map/ppermute | solution.py:40
  10.1 1.7 %collective-permute-start.1 = (bf16[4,3,32,512]{3,2,1,0:T(8,128)(2,1)S(1)}, bf16[4,3,32,512]{3,2,1,0:T(8,128)(2,1)S(1)}, u32[]{:S(2)}, u32[]{:S(2)}) collective-permute-start(bf16[4,3,32,512]{3,2,1,0:T(8,128)(2,1)S(1)} %get-tuple-element.30), channel_id=1, source_target_pairs={{0,3},{1,0},{2,1},{3,2},{4,7},{5,4},{6,5},{7,6},{8,11},{9,8},{10,9... | collective-permute-start | bytes 1179656 | tf_op jit(solution)/shard_map/ppermute | solution.py:40
  11.7 2.3 %shard_map.67 = bf16[4,3,32,512]{3,2,1,0:T(8,128)(2,1)S(1)} custom-call(bf16[4,3,32,512]{3,2,1,0:T(8,128)(2,1)S(1)} %get-tuple-element.31.refs_0_, bf16[2048,512]{1,0:T(8,128)(2,1)S(1)} %copy-done.2, bf16[2048,512]{1,0:T(8,128)(2,1)S(1)} %copy-done.3, f32[1,2048]{1,0:T(1,128)S(1)} %bitcast.4), custom_call_target="tpu_custom_call" | custom-call | flops 1610612736 | bytes 4194304 | tf_op jit(solution)/shard_map/pallas_call | solution.py:47
  14.0 2.0 %collective-permute-start.2 = (bf16[4,3,32,512]{3,2,1,0:T(8,128)(2,1)S(1)}, bf16[4,3,32,512]{3,2,1,0:T(8,128)(2,1)S(1)}, u32[]{:S(2)}, u32[]{:S(2)}) collective-permute-start(bf16[4,3,32,512]{3,2,1,0:T(8,128)(2,1)S(1)} %shard_map.67), channel_id=1, source_target_pairs={{0,2},{1,3},{2,0},{3,1},{4,6},{5,7},{6,4},{7,5},{8,10},{9,11},{10,... | collective-permute-start | bytes 1179656 | tf_op jit(solution)/shard_map/ppermute | solution.py:40
  16.0 2.3 %shard_map.65.own = f32[4,3,32,512]{3,2,1,0:T(8,128)S(1)} custom-call(bf16[4,3,32,512]{3,2,1,0:T(8,128)(2,1)S(1)} %get-tuple-element.28.refs_0_, bf16[2048,512]{1,0:T(8,128)(2,1)S(1)} %copy-done.2, bf16[2048,512]{1,0:T(8,128)(2,1)S(1)} %copy-done.3, f32[1,2048]{1,0:T(1,128)S(1)} %bitcast.5), custom_call_target="tpu_custom_call" | custom-call | flops 1610612736 | bytes 4194304 | tf_op jit(solution)/shard_map/pallas_call | solution.py:47
  18.4 5.0 %collective-permute-done.2.r2 = bf16[4,3,32,512]{3,2,1,0:T(8,128)(2,1)S(1)} collective-permute-done((bf16[4,3,32,512]{3,2,1,0:T(8,128)(2,1)S(1)}, bf16[4,3,32,512]{3,2,1,0:T(8,128)(2,1)S(1)}, u32[]{:S(2)}, u32[]{:S(2)}) %collective-permute-start.2) | collective-permute-done | bytes 393248 | tf_op jit(solution)/shard_map/ppermute | solution.py:40
  23.5 1.7 %collective-permute-start.3 = (bf16[3,32,512]{2,1,0:T(8,128)(2,1)S(1)}, bf16[3,32,512]{2,1,0:T(8,128)(2,1)S(1)}, u32[]{:S(2)}, u32[]{:S(2)}) collective-permute-start(bf16[3,32,512]{2,1,0:T(8,128)(2,1)S(1)} %get-tuple-element.33), channel_id=1, source_target_pairs={{0,4},{1,5},{2,6},{3,7},{4,8},{5,9},{6,10},{7,11},{8,12},{9,13},{1... | collective-permute-start | bytes 294920 | tf_op jit(solution)/shard_map/ppermute | solution.py:40
  25.2 2.9 %collective-permute-start.4 = (bf16[3,32,512]{2,1,0:T(8,128)(2,1)S(1)}, bf16[3,32,512]{2,1,0:T(8,128)(2,1)S(1)}, u32[]{:S(2)}, u32[]{:S(2)}) collective-permute-start(bf16[3,32,512]{2,1,0:T(8,128)(2,1)S(1)} %get-tuple-element.34), channel_id=1, source_target_pairs={{0,8},{1,9},{2,10},{3,11},{4,12},{5,13},{6,14},{7,15},{8,0},{9,1},... | collective-permute-start | bytes 294920 | tf_op jit(solution)/shard_map/ppermute | solution.py:40
  28.1 1.3 %collective-permute-start.5 = (bf16[3,32,512]{2,1,0:T(8,128)(2,1)S(1)}, bf16[3,32,512]{2,1,0:T(8,128)(2,1)S(1)}, u32[]{:S(2)}, u32[]{:S(2)}) collective-permute-start(bf16[3,32,512]{2,1,0:T(8,128)(2,1)S(1)} %get-tuple-element.35), channel_id=1, source_target_pairs={{0,12},{1,13},{2,14},{3,15},{4,0},{5,1},{6,2},{7,3},{8,4},{9,5},{1... | collective-permute-start | bytes 294920 | tf_op jit(solution)/shard_map/ppermute | solution.py:40
  29.5 2.3 %collective-permute-done.4.r2 = bf16[3,32,512]{2,1,0:T(8,128)(2,1)S(1)} collective-permute-done((bf16[3,32,512]{2,1,0:T(8,128)(2,1)S(1)}, bf16[3,32,512]{2,1,0:T(8,128)(2,1)S(1)}, u32[]{:S(2)}, u32[]{:S(2)}) %collective-permute-start.4) | collective-permute-done | bytes 98336 | tf_op jit(solution)/shard_map/ppermute | solution.py:40
  31.8 1.0 collective-permute-done.5.r3
  32.8 2.0 %collective-permute-start.8 = (bf16[3,32,512]{2,1,0:T(8,128)(2,1)S(1)}, bf16[3,32,512]{2,1,0:T(8,128)(2,1)S(1)}, u32[]{:S(2)}, u32[]{:S(2)}) collective-permute-start(bf16[3,32,512]{2,1,0:T(8,128)(2,1)S(1)} %shard_map.69.own), channel_id=1, source_target_pairs={{0,16},{1,17},{2,18},{3,19},{4,20},{5,21},{6,22},{7,23},{8,24},{9,... | collective-permute-start | bytes 294920 | tf_op jit(solution)/shard_map/ppermute | solution.py:40
  34.8 3.6 %collective-permute-start.7 = (bf16[3,32,512]{2,1,0:T(8,128)(2,1)S(1)}, bf16[3,32,512]{2,1,0:T(8,128)(2,1)S(1)}, u32[]{:S(2)}, u32[]{:S(2)}) collective-permute-start(bf16[3,32,512]{2,1,0:T(8,128)(2,1)S(1)} %shard_map.69.own), channel_id=1, source_target_pairs={{0,32},{1,33},{2,34},{3,35},{4,36},{5,37},{6,38},{7,39},{8,40},{9,... | collective-permute-start | bytes 294920 | tf_op jit(solution)/shard_map/ppermute | solution.py:40
  38.4 1.0 collective-permute-start.6
  39.5 2.5 %collective-permute-done.7.r2 = bf16[3,32,512]{2,1,0:T(8,128)(2,1)S(1)} collective-permute-done((bf16[3,32,512]{2,1,0:T(8,128)(2,1)S(1)}, bf16[3,32,512]{2,1,0:T(8,128)(2,1)S(1)}, u32[]{:S(2)}, u32[]{:S(2)}) %collective-permute-start.7) | collective-permute-done | bytes 98336 | tf_op jit(solution)/shard_map/ppermute | solution.py:40
  42.0 1.0 collective-permute-done.6.r1
  43.0 0.7 collective-permute-start.11
  43.8 3.4 %collective-permute-start.10 = (bf16[3,32,512]{2,1,0:T(8,128)(2,1)S(1)}, bf16[3,32,512]{2,1,0:T(8,128)(2,1)S(1)}, u32[]{:S(2)}, u32[]{:S(2)}) collective-permute-start(bf16[3,32,512]{2,1,0:T(8,128)(2,1)S(1)} %get-tuple-element.37.own), channel_id=1, source_target_pairs={{0,8},{1,9},{2,10},{3,11},{4,12},{5,13},{6,14},{7,15},{8,0},{9,1},... | collective-permute-start | bytes 294920 | tf_op jit(solution)/shard_map/ppermute | solution.py:40
  47.1 0.5 collective-permute-start.9
  47.6 1.3 %collective-permute-done.11.r3 = bf16[3,32,512]{2,1,0:T(8,128)(2,1)S(1)} collective-permute-done((bf16[3,32,512]{2,1,0:T(8,128)(2,1)S(1)}, bf16[3,32,512]{2,1,0:T(8,128)(2,1)S(1)}, u32[]{:S(2)}, u32[]{:S(2)}) %collective-permute-start.11) | collective-permute-done | bytes 98336 | tf_op jit(solution)/shard_map/ppermute | solution.py:40
  49.0 3.1 %collective-permute-done.10.r2 = bf16[3,32,512]{2,1,0:T(8,128)(2,1)S(1)} collective-permute-done((bf16[3,32,512]{2,1,0:T(8,128)(2,1)S(1)}, bf16[3,32,512]{2,1,0:T(8,128)(2,1)S(1)}, u32[]{:S(2)}, u32[]{:S(2)}) %collective-permute-start.10) | collective-permute-done | bytes 98336 | tf_op jit(solution)/shard_map/ppermute | solution.py:40
  52.1 0.8 collective-permute-done.9.r1
  52.9 0.8 collective-permute-start.13
  53.7 2.5 %collective-permute-start.12 = (bf16[4,3,32,512]{3,2,1,0:T(8,128)(2,1)S(1)}, bf16[4,3,32,512]{3,2,1,0:T(8,128)(2,1)S(1)}, u32[]{:S(2)}, u32[]{:S(2)}) collective-permute-start(bf16[4,3,32,512]{3,2,1,0:T(8,128)(2,1)S(1)} %shard_map.71.refs_0_), channel_id=1, source_target_pairs={{0,3},{1,0},{2,1},{3,2},{4,7},{5,4},{6,5},{7,6},{8,11},{9,8},{10,9... | collective-permute-start | bytes 1179656 | tf_op jit(solution)/shard_map/ppermute | solution.py:40
  56.2 0.6 collective-permute-start.16
  56.8 2.3 %shard_map.72.own = f32[4,3,32,512]{3,2,1,0:T(8,128)S(1)} custom-call(bf16[4,3,32,512]{3,2,1,0:T(8,128)(2,1)S(1)} %shard_map.71.refs_0_, bf16[2048,512]{1,0:T(8,128)(2,1)S(1)} %copy-done.2, bf16[2048,512]{1,0:T(8,128)(2,1)S(1)} %copy-done.3, f32[1,2048]{1,0:T(1,128)S(1)} %bitcast.6), custom_call_target="tpu_custom_call" | custom-call | flops 1610612736 | bytes 4194304 | tf_op jit(solution)/shard_map/pallas_call | solution.py:47
  59.1 7.0 %collective-permute-done.13.refs_1_ = bf16[4,3,32,512]{3,2,1,0:T(8,128)(2,1)S(1)} collective-permute-done((bf16[4,3,32,512]{3,2,1,0:T(8,128)(2,1)S(1)}, bf16[4,3,32,512]{3,2,1,0:T(8,128)(2,1)S(1)}, u32[]{:S(2)}, u32[]{:S(2)}) %collective-permute-start.13) | collective-permute-done | bytes 393248 | tf_op jit(solution)/shard_map/ppermute | solution.py:40
  66.2 3.7 %shard_map.73 = (bf16[4,3,32,512]{3,2,1,0:T(8,128)(2,1)S(1)}, bf16[4,3,32,512]{3,2,1,0:T(8,128)(2,1)S(1)}) custom-call(bf16[4,3,32,512]{3,2,1,0:T(8,128)(2,1)S(1)} %collective-permute-done.12.refs_0_, bf16[4,3,32,512]{3,2,1,0:T(8,128)(2,1)S(1)} %collective-permute-done.13.refs_1_, bf16[2048,512]{1,0:T(8,128)(2,1)S(1)} %copy-done.2, ...), custom_call_target="tpu_custom_call" | custom-call | flops 3221225472 | bytes 4194304 | tf_op jit(solution)/shard_map/pallas_call | solution.py:47
  69.9 3.3 %collective-permute-start.15 = (bf16[4,3,32,512]{3,2,1,0:T(8,128)(2,1)S(1)}, bf16[4,3,32,512]{3,2,1,0:T(8,128)(2,1)S(1)}, u32[]{:S(2)}, u32[]{:S(2)}) collective-permute-start(bf16[4,3,32,512]{3,2,1,0:T(8,128)(2,1)S(1)} %get-tuple-element.41), channel_id=1, source_target_pairs={{0,3},{1,0},{2,1},{3,2},{4,7},{5,4},{6,5},{7,6},{8,11},{9,8},{10,9... | collective-permute-start | bytes 1179656 | tf_op jit(solution)/shard_map/ppermute | solution.py:40
  73.2 2.3 %shard_map.75 = bf16[4,3,32,512]{3,2,1,0:T(8,128)(2,1)S(1)} custom-call(bf16[4,3,32,512]{3,2,1,0:T(8,128)(2,1)S(1)} %collective-permute-done.16.refs_0_, bf16[2048,512]{1,0:T(8,128)(2,1)S(1)} %copy-done.2, bf16[2048,512]{1,0:T(8,128)(2,1)S(1)} %copy-done.3, f32[1,2048]{1,0:T(1,128)S(1)} %bitcast.8), custom_call_target="tpu_custom_call" | custom-call | flops 1610612736 | bytes 4194304 | tf_op jit(solution)/shard_map/pallas_call | solution.py:47
  75.5 1.5 %collective-permute-start.17 = (bf16[4,3,32,512]{3,2,1,0:T(8,128)(2,1)S(1)}, bf16[4,3,32,512]{3,2,1,0:T(8,128)(2,1)S(1)}, u32[]{:S(2)}, u32[]{:S(2)}) collective-permute-start(bf16[4,3,32,512]{3,2,1,0:T(8,128)(2,1)S(1)} %shard_map.75), channel_id=1, source_target_pairs={{0,2},{1,3},{2,0},{3,1},{4,6},{5,7},{6,4},{7,5},{8,10},{9,11},{10,... | collective-permute-start | bytes 1179656 | tf_op jit(solution)/shard_map/ppermute | solution.py:40
  77.0 1.5 %collective-permute-done.15.r3 = bf16[4,3,32,512]{3,2,1,0:T(8,128)(2,1)S(1)} collective-permute-done((bf16[4,3,32,512]{3,2,1,0:T(8,128)(2,1)S(1)}, bf16[4,3,32,512]{3,2,1,0:T(8,128)(2,1)S(1)}, u32[]{:S(2)}, u32[]{:S(2)}) %collective-permute-start.15) | collective-permute-done | bytes 393248 | tf_op jit(solution)/shard_map/ppermute | solution.py:40
  78.5 0.4 collective-permute-done.14.r1
  79.0 7.7 %collective-permute-done.17.r2 = bf16[4,3,32,512]{3,2,1,0:T(8,128)(2,1)S(1)} collective-permute-done((bf16[4,3,32,512]{3,2,1,0:T(8,128)(2,1)S(1)}, bf16[4,3,32,512]{3,2,1,0:T(8,128)(2,1)S(1)}, u32[]{:S(2)}, u32[]{:S(2)}) %collective-permute-start.17) | collective-permute-done | bytes 393248 | tf_op jit(solution)/shard_map/ppermute | solution.py:40
  86.8 0.8 collective-permute-start.18
  87.6 2.8 %collective-permute-start.19 = (bf16[3,32,512]{2,1,0:T(8,128)(2,1)S(1)}, bf16[3,32,512]{2,1,0:T(8,128)(2,1)S(1)}, u32[]{:S(2)}, u32[]{:S(2)}) collective-permute-start(bf16[3,32,512]{2,1,0:T(8,128)(2,1)S(1)} %get-tuple-element.45), channel_id=1, source_target_pairs={{0,8},{1,9},{2,10},{3,11},{4,12},{5,13},{6,14},{7,15},{8,0},{9,1},... | collective-permute-start | bytes 294920 | tf_op jit(solution)/shard_map/ppermute | solution.py:40
  90.3 0.6 collective-permute-start.20
  91.0 1.7 %collective-permute-done.18.r1 = bf16[3,32,512]{2,1,0:T(8,128)(2,1)S(1)} collective-permute-done((bf16[3,32,512]{2,1,0:T(8,128)(2,1)S(1)}, bf16[3,32,512]{2,1,0:T(8,128)(2,1)S(1)}, u32[]{:S(2)}, u32[]{:S(2)}) %collective-permute-start.18) | collective-permute-done | bytes 98336 | tf_op jit(solution)/shard_map/ppermute | solution.py:40
  92.7 1.3 %collective-permute-done.19.r2 = bf16[3,32,512]{2,1,0:T(8,128)(2,1)S(1)} collective-permute-done((bf16[3,32,512]{2,1,0:T(8,128)(2,1)S(1)}, bf16[3,32,512]{2,1,0:T(8,128)(2,1)S(1)}, u32[]{:S(2)}, u32[]{:S(2)}) %collective-permute-start.19) | collective-permute-done | bytes 98336 | tf_op jit(solution)/shard_map/ppermute | solution.py:40
  94.0 1.0 collective-permute-done.20.r3
  95.0 0.8 collective-permute-start.23
  95.8 3.0 %collective-permute-start.22 = (bf16[3,32,512]{2,1,0:T(8,128)(2,1)S(1)}, bf16[3,32,512]{2,1,0:T(8,128)(2,1)S(1)}, u32[]{:S(2)}, u32[]{:S(2)}) collective-permute-start(bf16[3,32,512]{2,1,0:T(8,128)(2,1)S(1)} %shard_map.77.own), channel_id=1, source_target_pairs={{0,32},{1,33},{2,34},{3,35},{4,36},{5,37},{6,38},{7,39},{8,40},{9,... | collective-permute-start | bytes 294920 | tf_op jit(solution)/shard_map/ppermute | solution.py:40
  98.9 0.2 collective-permute-start.21
  99.1 1.8 %collective-permute-done.23.r3 = bf16[3,32,512]{2,1,0:T(8,128)(2,1)S(1)} collective-permute-done((bf16[3,32,512]{2,1,0:T(8,128)(2,1)S(1)}, bf16[3,32,512]{2,1,0:T(8,128)(2,1)S(1)}, u32[]{:S(2)}, u32[]{:S(2)}) %collective-permute-start.23) | collective-permute-done | bytes 98336 | tf_op jit(solution)/shard_map/ppermute | solution.py:40
  100.9 1.6 %collective-permute-done.22.r2 = bf16[3,32,512]{2,1,0:T(8,128)(2,1)S(1)} collective-permute-done((bf16[3,32,512]{2,1,0:T(8,128)(2,1)S(1)}, bf16[3,32,512]{2,1,0:T(8,128)(2,1)S(1)}, u32[]{:S(2)}, u32[]{:S(2)}) %collective-permute-start.22) | collective-permute-done | bytes 98336 | tf_op jit(solution)/shard_map/ppermute | solution.py:40
  102.5 1.0 collective-permute-done.21.r1
  103.6 1.3 collective-permute-start.24
  104.9 0.9 collective-permute-done.24.earlier
  105.8 0.7 collective-permute-start.27
  106.5 3.1 %collective-permute-start.26 = (bf16[3,32,512]{2,1,0:T(8,128)(2,1)S(1)}, bf16[3,32,512]{2,1,0:T(8,128)(2,1)S(1)}, u32[]{:S(2)}, u32[]{:S(2)}) collective-permute-start(bf16[3,32,512]{2,1,0:T(8,128)(2,1)S(1)} %shard_map.79.own), channel_id=1, source_target_pairs={{0,8},{1,9},{2,10},{3,11},{4,12},{5,13},{6,14},{7,15},{8,0},{9,1},... | collective-permute-start | bytes 294920 | tf_op jit(solution)/shard_map/ppermute | solution.py:40
  109.6 0.4 collective-permute-start.25
  110.0 1.7 %collective-permute-done.27.r3 = bf16[3,32,512]{2,1,0:T(8,128)(2,1)S(1)} collective-permute-done((bf16[3,32,512]{2,1,0:T(8,128)(2,1)S(1)}, bf16[3,32,512]{2,1,0:T(8,128)(2,1)S(1)}, u32[]{:S(2)}, u32[]{:S(2)}) %collective-permute-start.27) | collective-permute-done | bytes 98336 | tf_op jit(solution)/shard_map/ppermute | solution.py:40
  111.7 1.5 %collective-permute-done.26.r2 = bf16[3,32,512]{2,1,0:T(8,128)(2,1)S(1)} collective-permute-done((bf16[3,32,512]{2,1,0:T(8,128)(2,1)S(1)}, bf16[3,32,512]{2,1,0:T(8,128)(2,1)S(1)}, u32[]{:S(2)}, u32[]{:S(2)}) %collective-permute-start.26) | collective-permute-done | bytes 98336 | tf_op jit(solution)/shard_map/ppermute | solution.py:40
  113.3 1.0 collective-permute-done.25.r1
  114.3 1.5 %collective-permute-start.30 = (bf16[4,3,32,512]{3,2,1,0:T(8,128)(2,1)S(1)}, bf16[4,3,32,512]{3,2,1,0:T(8,128)(2,1)S(1)}, u32[]{:S(2)}, u32[]{:S(2)}) collective-permute-start(bf16[4,3,32,512]{3,2,1,0:T(8,128)(2,1)S(1)} %shard_map.80.refs_0_), channel_id=1, source_target_pairs={{0,1},{1,2},{2,3},{3,0},{4,5},{5,6},{6,7},{7,4},{8,9},{9,10},{10,1... | collective-permute-start | bytes 1179656 | tf_op jit(solution)/shard_map/ppermute | solution.py:40
  115.8 1.8 %collective-permute-start.29 = (bf16[4,3,32,512]{3,2,1,0:T(8,128)(2,1)S(1)}, bf16[4,3,32,512]{3,2,1,0:T(8,128)(2,1)S(1)}, u32[]{:S(2)}, u32[]{:S(2)}) collective-permute-start(bf16[4,3,32,512]{3,2,1,0:T(8,128)(2,1)S(1)} %shard_map.80.refs_0_), channel_id=1, source_target_pairs={{0,3},{1,0},{2,1},{3,2},{4,7},{5,4},{6,5},{7,6},{8,11},{9,8},{10,9... | collective-permute-start | bytes 1179656 | tf_op jit(solution)/shard_map/ppermute | solution.py:40
  117.6 0.5 collective-permute-start.28
  118.1 1.6 %shard_map.81.refs_3_ = f32[2048,512]{1,0:T(8,128)S(1)} custom-call(bf16[4,3,32,512]{3,2,1,0:T(8,128)(2,1)S(1)} %shard_map.80.refs_0_, bf16[2048,512]{1,0:T(8,128)(2,1)S(1)} %copy-done), custom_call_target="tpu_custom_call" | custom-call | flops 805306368 | bytes 6291456 | tf_op jit(solution)/shard_map/pallas_call | solution.py:47
  119.7 3.6 %collective-permute-done.30.refs_1_ = bf16[4,3,32,512]{3,2,1,0:T(8,128)(2,1)S(1)} collective-permute-done((bf16[4,3,32,512]{3,2,1,0:T(8,128)(2,1)S(1)}, bf16[4,3,32,512]{3,2,1,0:T(8,128)(2,1)S(1)}, u32[]{:S(2)}, u32[]{:S(2)}) %collective-permute-start.30) | collective-permute-done | bytes 393248 | tf_op jit(solution)/shard_map/ppermute | solution.py:40
  123.3 3.8 %collective-permute-done.29.refs_0_ = bf16[4,3,32,512]{3,2,1,0:T(8,128)(2,1)S(1)} collective-permute-done((bf16[4,3,32,512]{3,2,1,0:T(8,128)(2,1)S(1)}, bf16[4,3,32,512]{3,2,1,0:T(8,128)(2,1)S(1)}, u32[]{:S(2)}, u32[]{:S(2)}) %collective-permute-start.29) | collective-permute-done | bytes 393248 | tf_op jit(solution)/shard_map/ppermute | solution.py:40
  127.1 2.5 %shard_map.82.refs_3_ = f32[2048,512]{1,0:T(8,128)S(1)} custom-call(bf16[4,3,32,512]{3,2,1,0:T(8,128)(2,1)S(1)} %collective-permute-done.29.refs_0_, bf16[4,3,32,512]{3,2,1,0:T(8,128)(2,1)S(1)} %collective-permute-done.30.refs_1_, bf16[2048,512]{1,0:T(8,128)(2,1)S(1)} %copy-done, f32[2048,512]{1,0:T(8,128)S(1)} %shard_map.81.refs_3_), custom_call_target="tpu_custom_call" | custom-call | flops 1610612736 | bytes 6291456 | tf_op jit(solution)/shard_map/pallas_call | solution.py:47
  129.7 2.6 %shard_map.83 = bf16[2048,512]{1,0:T(8,128)(2,1)} custom-call(bf16[4,3,32,512]{3,2,1,0:T(8,128)(2,1)S(1)} %collective-permute-done.28.refs_0_, bf16[2048,512]{1,0:T(8,128)(2,1)S(1)} %copy-done, f32[1,512]{1,0:T(1,128)S(1)} %bitcast.2, f32[2048,512]{1,0:T(8,128)S(1)} %shard_map.82.refs_3_), custom_call_target="tpu_custom_call" | custom-call | flops 805306368 | bytes 6291456 | tf_op jit(solution)/shard_map/pallas_call | solution.py:47
  (32 shorter events, 1.1 us)
Async XLA Ops:
  0.2 0.7 copy-start.4
  0.9 10.8 %copy-start.2 = (bf16[2048,512]{1,0:T(8,128)(2,1)S(1)}, bf16[2048,512]{1,0:T(8,128)(2,1)}, u32[]{:S(2)}) copy-start(bf16[2048,512]{1,0:T(8,128)(2,1)} %refs_1_.10) | copy-start | bytes 6291460
  0.9 10.8 %copy-start.3 = (bf16[2048,512]{1,0:T(8,128)(2,1)S(1)}, bf16[2048,512]{1,0:T(8,128)(2,1)}, u32[]{:S(2)}) copy-start(bf16[2048,512]{1,0:T(8,128)(2,1)} %refs_2_.11) | copy-start | bytes 6291460
  8.4 9.9 %collective-permute-start = (bf16[4,3,32,512]{3,2,1,0:T(8,128)(2,1)S(1)}, bf16[4,3,32,512]{3,2,1,0:T(8,128)(2,1)S(1)}, u32[]{:S(2)}, u32[]{:S(2)}) collective-permute-start(bf16[4,3,32,512]{3,2,1,0:T(8,128)(2,1)S(1)} %get-tuple-element.29), channel_id=1, source_target_pairs={{0,1},{1,2},{2,3},{3,0},{4,5},{5,6},{6,7},{7,4},{8,9},{9,10},{10,1... | collective-permute-start | bytes 1179656 | tf_op jit(solution)/shard_map/ppermute | solution.py:40
  10.1 8.2 %collective-permute-start.1 = (bf16[4,3,32,512]{3,2,1,0:T(8,128)(2,1)S(1)}, bf16[4,3,32,512]{3,2,1,0:T(8,128)(2,1)S(1)}, u32[]{:S(2)}, u32[]{:S(2)}) collective-permute-start(bf16[4,3,32,512]{3,2,1,0:T(8,128)(2,1)S(1)} %get-tuple-element.30), channel_id=1, source_target_pairs={{0,3},{1,0},{2,1},{3,2},{4,7},{5,4},{6,5},{7,6},{8,11},{9,8},{10,9... | collective-permute-start | bytes 1179656 | tf_op jit(solution)/shard_map/ppermute | solution.py:40
  14.0 9.4 %collective-permute-start.2 = (bf16[4,3,32,512]{3,2,1,0:T(8,128)(2,1)S(1)}, bf16[4,3,32,512]{3,2,1,0:T(8,128)(2,1)S(1)}, u32[]{:S(2)}, u32[]{:S(2)}) collective-permute-start(bf16[4,3,32,512]{3,2,1,0:T(8,128)(2,1)S(1)} %shard_map.67), channel_id=1, source_target_pairs={{0,2},{1,3},{2,0},{3,1},{4,6},{5,7},{6,4},{7,5},{8,10},{9,11},{10,... | collective-permute-start | bytes 1179656 | tf_op jit(solution)/shard_map/ppermute | solution.py:40
  23.5 6.0 %collective-permute-start.3 = (bf16[3,32,512]{2,1,0:T(8,128)(2,1)S(1)}, bf16[3,32,512]{2,1,0:T(8,128)(2,1)S(1)}, u32[]{:S(2)}, u32[]{:S(2)}) collective-permute-start(bf16[3,32,512]{2,1,0:T(8,128)(2,1)S(1)} %get-tuple-element.33), channel_id=1, source_target_pairs={{0,4},{1,5},{2,6},{3,7},{4,8},{5,9},{6,10},{7,11},{8,12},{9,13},{1... | collective-permute-start | bytes 294920 | tf_op jit(solution)/shard_map/ppermute | solution.py:40
  25.2 6.5 %collective-permute-start.4 = (bf16[3,32,512]{2,1,0:T(8,128)(2,1)S(1)}, bf16[3,32,512]{2,1,0:T(8,128)(2,1)S(1)}, u32[]{:S(2)}, u32[]{:S(2)}) collective-permute-start(bf16[3,32,512]{2,1,0:T(8,128)(2,1)S(1)} %get-tuple-element.34), channel_id=1, source_target_pairs={{0,8},{1,9},{2,10},{3,11},{4,12},{5,13},{6,14},{7,15},{8,0},{9,1},... | collective-permute-start | bytes 294920 | tf_op jit(solution)/shard_map/ppermute | solution.py:40
  28.1 4.6 %collective-permute-start.5 = (bf16[3,32,512]{2,1,0:T(8,128)(2,1)S(1)}, bf16[3,32,512]{2,1,0:T(8,128)(2,1)S(1)}, u32[]{:S(2)}, u32[]{:S(2)}) collective-permute-start(bf16[3,32,512]{2,1,0:T(8,128)(2,1)S(1)} %get-tuple-element.35), channel_id=1, source_target_pairs={{0,12},{1,13},{2,14},{3,15},{4,0},{5,1},{6,2},{7,3},{8,4},{9,5},{1... | collective-permute-start | bytes 294920 | tf_op jit(solution)/shard_map/ppermute | solution.py:40
  32.8 6.7 %collective-permute-start.8 = (bf16[3,32,512]{2,1,0:T(8,128)(2,1)S(1)}, bf16[3,32,512]{2,1,0:T(8,128)(2,1)S(1)}, u32[]{:S(2)}, u32[]{:S(2)}) collective-permute-start(bf16[3,32,512]{2,1,0:T(8,128)(2,1)S(1)} %shard_map.69.own), channel_id=1, source_target_pairs={{0,16},{1,17},{2,18},{3,19},{4,20},{5,21},{6,22},{7,23},{8,24},{9,... | collective-permute-start | bytes 294920 | tf_op jit(solution)/shard_map/ppermute | solution.py:40
  34.8 7.2 %collective-permute-start.7 = (bf16[3,32,512]{2,1,0:T(8,128)(2,1)S(1)}, bf16[3,32,512]{2,1,0:T(8,128)(2,1)S(1)}, u32[]{:S(2)}, u32[]{:S(2)}) collective-permute-start(bf16[3,32,512]{2,1,0:T(8,128)(2,1)S(1)} %shard_map.69.own), channel_id=1, source_target_pairs={{0,32},{1,33},{2,34},{3,35},{4,36},{5,37},{6,38},{7,39},{8,40},{9,... | collective-permute-start | bytes 294920 | tf_op jit(solution)/shard_map/ppermute | solution.py:40
  38.4 4.6 %collective-permute-start.6 = (bf16[3,32,512]{2,1,0:T(8,128)(2,1)S(1)}, bf16[3,32,512]{2,1,0:T(8,128)(2,1)S(1)}, u32[]{:S(2)}, u32[]{:S(2)}) collective-permute-start(bf16[3,32,512]{2,1,0:T(8,128)(2,1)S(1)} %shard_map.69.own), channel_id=1, source_target_pairs={{0,48},{1,49},{2,50},{3,51},{4,52},{5,53},{6,54},{7,55},{8,56},{9,... | collective-permute-start | bytes 294920 | tf_op jit(solution)/shard_map/ppermute | solution.py:40
  43.0 5.9 %collective-permute-start.11 = (bf16[3,32,512]{2,1,0:T(8,128)(2,1)S(1)}, bf16[3,32,512]{2,1,0:T(8,128)(2,1)S(1)}, u32[]{:S(2)}, u32[]{:S(2)}) collective-permute-start(bf16[3,32,512]{2,1,0:T(8,128)(2,1)S(1)} %get-tuple-element.37.own), channel_id=1, source_target_pairs={{0,4},{1,5},{2,6},{3,7},{4,8},{5,9},{6,10},{7,11},{8,12},{9,13},{1... | collective-permute-start | bytes 294920 | tf_op jit(solution)/shard_map/ppermute | solution.py:40
  43.8 8.3 %collective-permute-start.10 = (bf16[3,32,512]{2,1,0:T(8,128)(2,1)S(1)}, bf16[3,32,512]{2,1,0:T(8,128)(2,1)S(1)}, u32[]{:S(2)}, u32[]{:S(2)}) collective-permute-start(bf16[3,32,512]{2,1,0:T(8,128)(2,1)S(1)} %get-tuple-element.37.own), channel_id=1, source_target_pairs={{0,8},{1,9},{2,10},{3,11},{4,12},{5,13},{6,14},{7,15},{8,0},{9,1},... | collective-permute-start | bytes 294920 | tf_op jit(solution)/shard_map/ppermute | solution.py:40
  47.1 5.7 %collective-permute-start.9 = (bf16[3,32,512]{2,1,0:T(8,128)(2,1)S(1)}, bf16[3,32,512]{2,1,0:T(8,128)(2,1)S(1)}, u32[]{:S(2)}, u32[]{:S(2)}) collective-permute-start(bf16[3,32,512]{2,1,0:T(8,128)(2,1)S(1)} %get-tuple-element.37.own), channel_id=1, source_target_pairs={{0,12},{1,13},{2,14},{3,15},{4,0},{5,1},{6,2},{7,3},{8,4},{9,5},{1... | collective-permute-start | bytes 294920 | tf_op jit(solution)/shard_map/ppermute | solution.py:40
  52.9 13.3 %collective-permute-start.13 = (bf16[4,3,32,512]{3,2,1,0:T(8,128)(2,1)S(1)}, bf16[4,3,32,512]{3,2,1,0:T(8,128)(2,1)S(1)}, u32[]{:S(2)}, u32[]{:S(2)}) collective-permute-start(bf16[4,3,32,512]{3,2,1,0:T(8,128)(2,1)S(1)} %shard_map.71.refs_0_), channel_id=1, source_target_pairs={{0,1},{1,2},{2,3},{3,0},{4,5},{5,6},{6,7},{7,4},{8,9},{9,10},{10,1... | collective-permute-start | bytes 1179656 | tf_op jit(solution)/shard_map/ppermute | solution.py:40
  53.7 12.5 %collective-permute-start.12 = (bf16[4,3,32,512]{3,2,1,0:T(8,128)(2,1)S(1)}, bf16[4,3,32,512]{3,2,1,0:T(8,128)(2,1)S(1)}, u32[]{:S(2)}, u32[]{:S(2)}) collective-permute-start(bf16[4,3,32,512]{3,2,1,0:T(8,128)(2,1)S(1)} %shard_map.71.refs_0_), channel_id=1, source_target_pairs={{0,3},{1,0},{2,1},{3,2},{4,7},{5,4},{6,5},{7,6},{8,11},{9,8},{10,9... | collective-permute-start | bytes 1179656 | tf_op jit(solution)/shard_map/ppermute | solution.py:40
  56.2 17.1 %collective-permute-start.16 = (bf16[4,3,32,512]{3,2,1,0:T(8,128)(2,1)S(1)}, bf16[4,3,32,512]{3,2,1,0:T(8,128)(2,1)S(1)}, u32[]{:S(2)}, u32[]{:S(2)}) collective-permute-start(bf16[4,3,32,512]{3,2,1,0:T(8,128)(2,1)S(1)} %shard_map.71.refs_0_), channel_id=1, source_target_pairs={{0,2},{1,3},{2,0},{3,1},{4,6},{5,7},{6,4},{7,5},{8,10},{9,11},{10,... | collective-permute-start | bytes 1179656 | tf_op jit(solution)/shard_map/ppermute | solution.py:40
  69.9 9.1 %collective-permute-start.14 = (bf16[4,3,32,512]{3,2,1,0:T(8,128)(2,1)S(1)}, bf16[4,3,32,512]{3,2,1,0:T(8,128)(2,1)S(1)}, u32[]{:S(2)}, u32[]{:S(2)}) collective-permute-start(bf16[4,3,32,512]{3,2,1,0:T(8,128)(2,1)S(1)} %get-tuple-element.40), channel_id=1, source_target_pairs={{0,1},{1,2},{2,3},{3,0},{4,5},{5,6},{6,7},{7,4},{8,9},{9,10},{10,1... | collective-permute-start | bytes 1179656 | tf_op jit(solution)/shard_map/ppermute | solution.py:40
  69.9 8.6 %collective-permute-start.15 = (bf16[4,3,32,512]{3,2,1,0:T(8,128)(2,1)S(1)}, bf16[4,3,32,512]{3,2,1,0:T(8,128)(2,1)S(1)}, u32[]{:S(2)}, u32[]{:S(2)}) collective-permute-start(bf16[4,3,32,512]{3,2,1,0:T(8,128)(2,1)S(1)} %get-tuple-element.41), channel_id=1, source_target_pairs={{0,3},{1,0},{2,1},{3,2},{4,7},{5,4},{6,5},{7,6},{8,11},{9,8},{10,9... | collective-permute-start | bytes 1179656 | tf_op jit(solution)/shard_map/ppermute | solution.py:40
  75.5 11.2 %collective-permute-start.17 = (bf16[4,3,32,512]{3,2,1,0:T(8,128)(2,1)S(1)}, bf16[4,3,32,512]{3,2,1,0:T(8,128)(2,1)S(1)}, u32[]{:S(2)}, u32[]{:S(2)}) collective-permute-start(bf16[4,3,32,512]{3,2,1,0:T(8,128)(2,1)S(1)} %shard_map.75), channel_id=1, source_target_pairs={{0,2},{1,3},{2,0},{3,1},{4,6},{5,7},{6,4},{7,5},{8,10},{9,11},{10,... | collective-permute-start | bytes 1179656 | tf_op jit(solution)/shard_map/ppermute | solution.py:40
  79.0 39.1 %copy-start = (bf16[2048,512]{1,0:T(8,128)(2,1)S(1)}, bf16[2048,512]{1,0:T(8,128)(2,1)}, u32[]{:S(2)}) copy-start(bf16[2048,512]{1,0:T(8,128)(2,1)} %refs_1_.12) | copy-start | bytes 6291460
  86.8 5.9 %collective-permute-start.18 = (bf16[3,32,512]{2,1,0:T(8,128)(2,1)S(1)}, bf16[3,32,512]{2,1,0:T(8,128)(2,1)S(1)}, u32[]{:S(2)}, u32[]{:S(2)}) collective-permute-start(bf16[3,32,512]{2,1,0:T(8,128)(2,1)S(1)} %get-tuple-element.44), channel_id=1, source_target_pairs={{0,4},{1,5},{2,6},{3,7},{4,8},{5,9},{6,10},{7,11},{8,12},{9,13},{1... | collective-permute-start | bytes 294920 | tf_op jit(solution)/shard_map/ppermute | solution.py:40
  87.6 6.4 %collective-permute-start.19 = (bf16[3,32,512]{2,1,0:T(8,128)(2,1)S(1)}, bf16[3,32,512]{2,1,0:T(8,128)(2,1)S(1)}, u32[]{:S(2)}, u32[]{:S(2)}) collective-permute-start(bf16[3,32,512]{2,1,0:T(8,128)(2,1)S(1)} %get-tuple-element.45), channel_id=1, source_target_pairs={{0,8},{1,9},{2,10},{3,11},{4,12},{5,13},{6,14},{7,15},{8,0},{9,1},... | collective-permute-start | bytes 294920 | tf_op jit(solution)/shard_map/ppermute | solution.py:40
  90.3 4.6 %collective-permute-start.20 = (bf16[3,32,512]{2,1,0:T(8,128)(2,1)S(1)}, bf16[3,32,512]{2,1,0:T(8,128)(2,1)S(1)}, u32[]{:S(2)}, u32[]{:S(2)}) collective-permute-start(bf16[3,32,512]{2,1,0:T(8,128)(2,1)S(1)} %get-tuple-element.46), channel_id=1, source_target_pairs={{0,12},{1,13},{2,14},{3,15},{4,0},{5,1},{6,2},{7,3},{8,4},{9,5},{1... | collective-permute-start | bytes 294920 | tf_op jit(solution)/shard_map/ppermute | solution.py:40
  95.0 5.9 %collective-permute-start.23 = (bf16[3,32,512]{2,1,0:T(8,128)(2,1)S(1)}, bf16[3,32,512]{2,1,0:T(8,128)(2,1)S(1)}, u32[]{:S(2)}, u32[]{:S(2)}) collective-permute-start(bf16[3,32,512]{2,1,0:T(8,128)(2,1)S(1)} %shard_map.77.own), channel_id=1, source_target_pairs={{0,16},{1,17},{2,18},{3,19},{4,20},{5,21},{6,22},{7,23},{8,24},{9,... | collective-permute-start | bytes 294920 | tf_op jit(solution)/shard_map/ppermute | solution.py:40
  95.8 6.7 %collective-permute-start.22 = (bf16[3,32,512]{2,1,0:T(8,128)(2,1)S(1)}, bf16[3,32,512]{2,1,0:T(8,128)(2,1)S(1)}, u32[]{:S(2)}, u32[]{:S(2)}) collective-permute-start(bf16[3,32,512]{2,1,0:T(8,128)(2,1)S(1)} %shard_map.77.own), channel_id=1, source_target_pairs={{0,32},{1,33},{2,34},{3,35},{4,36},{5,37},{6,38},{7,39},{8,40},{9,... | collective-permute-start | bytes 294920 | tf_op jit(solution)/shard_map/ppermute | solution.py:40
  98.9 4.6 %collective-permute-start.21 = (bf16[3,32,512]{2,1,0:T(8,128)(2,1)S(1)}, bf16[3,32,512]{2,1,0:T(8,128)(2,1)S(1)}, u32[]{:S(2)}, u32[]{:S(2)}) collective-permute-start(bf16[3,32,512]{2,1,0:T(8,128)(2,1)S(1)} %shard_map.77.own), channel_id=1, source_target_pairs={{0,48},{1,49},{2,50},{3,51},{4,52},{5,53},{6,54},{7,55},{8,56},{9,... | collective-permute-start | bytes 294920 | tf_op jit(solution)/shard_map/ppermute | solution.py:40
  103.6 2.2 %collective-permute-start.24 = (bf16[3,32,512]{2,1,0:T(8,128)(2,1)S(1)}, bf16[3,32,512]{2,1,0:T(8,128)(2,1)S(1)}, u32[]{:S(2)}, u32[]{:S(2)}) collective-permute-start(bf16[3,32,512]{2,1,0:T(8,128)(2,1)S(1)} %get-tuple-element.47), channel_id=1, source_target_pairs={{0,64},{1,65},{2,66},{3,67},{4,68},{5,69},{6,70},{7,71},{8,72},{9,... | collective-permute-start | bytes 294920 | tf_op jit(solution)/shard_map/ppermute | solution.py:341
  105.8 5.9 %collective-permute-start.27 = (bf16[3,32,512]{2,1,0:T(8,128)(2,1)S(1)}, bf16[3,32,512]{2,1,0:T(8,128)(2,1)S(1)}, u32[]{:S(2)}, u32[]{:S(2)}) collective-permute-start(bf16[3,32,512]{2,1,0:T(8,128)(2,1)S(1)} %shard_map.79.own), channel_id=1, source_target_pairs={{0,4},{1,5},{2,6},{3,7},{4,8},{5,9},{6,10},{7,11},{8,12},{9,13},{1... | collective-permute-start | bytes 294920 | tf_op jit(solution)/shard_map/ppermute | solution.py:40
  106.5 6.8 %collective-permute-start.26 = (bf16[3,32,512]{2,1,0:T(8,128)(2,1)S(1)}, bf16[3,32,512]{2,1,0:T(8,128)(2,1)S(1)}, u32[]{:S(2)}, u32[]{:S(2)}) collective-permute-start(bf16[3,32,512]{2,1,0:T(8,128)(2,1)S(1)} %shard_map.79.own), channel_id=1, source_target_pairs={{0,8},{1,9},{2,10},{3,11},{4,12},{5,13},{6,14},{7,15},{8,0},{9,1},... | collective-permute-start | bytes 294920 | tf_op jit(solution)/shard_map/ppermute | solution.py:40
  109.6 4.6 %collective-permute-start.25 = (bf16[3,32,512]{2,1,0:T(8,128)(2,1)S(1)}, bf16[3,32,512]{2,1,0:T(8,128)(2,1)S(1)}, u32[]{:S(2)}, u32[]{:S(2)}) collective-permute-start(bf16[3,32,512]{2,1,0:T(8,128)(2,1)S(1)} %shard_map.79.own), channel_id=1, source_target_pairs={{0,12},{1,13},{2,14},{3,15},{4,0},{5,1},{6,2},{7,3},{8,4},{9,5},{1... | collective-permute-start | bytes 294920 | tf_op jit(solution)/shard_map/ppermute | solution.py:40
  114.3 9.1 %collective-permute-start.30 = (bf16[4,3,32,512]{3,2,1,0:T(8,128)(2,1)S(1)}, bf16[4,3,32,512]{3,2,1,0:T(8,128)(2,1)S(1)}, u32[]{:S(2)}, u32[]{:S(2)}) collective-permute-start(bf16[4,3,32,512]{3,2,1,0:T(8,128)(2,1)S(1)} %shard_map.80.refs_0_), channel_id=1, source_target_pairs={{0,1},{1,2},{2,3},{3,0},{4,5},{5,6},{6,7},{7,4},{8,9},{9,10},{10,1... | collective-permute-start | bytes 1179656 | tf_op jit(solution)/shard_map/ppermute | solution.py:40
  115.8 11.4 %collective-permute-start.29 = (bf16[4,3,32,512]{3,2,1,0:T(8,128)(2,1)S(1)}, bf16[4,3,32,512]{3,2,1,0:T(8,128)(2,1)S(1)}, u32[]{:S(2)}, u32[]{:S(2)}) collective-permute-start(bf16[4,3,32,512]{3,2,1,0:T(8,128)(2,1)S(1)} %shard_map.80.refs_0_), channel_id=1, source_target_pairs={{0,3},{1,0},{2,1},{3,2},{4,7},{5,4},{6,5},{7,6},{8,11},{9,8},{10,9... | collective-permute-start | bytes 1179656 | tf_op jit(solution)/shard_map/ppermute | solution.py:40
  117.6 12.1 %collective-permute-start.28 = (bf16[4,3,32,512]{3,2,1,0:T(8,128)(2,1)S(1)}, bf16[4,3,32,512]{3,2,1,0:T(8,128)(2,1)S(1)}, u32[]{:S(2)}, u32[]{:S(2)}) collective-permute-start(bf16[4,3,32,512]{3,2,1,0:T(8,128)(2,1)S(1)} %shard_map.80.refs_0_), channel_id=1, source_target_pairs={{0,2},{1,3},{2,0},{3,1},{4,6},{5,7},{6,4},{7,5},{8,10},{9,11},{10,... | collective-permute-start | bytes 1179656 | tf_op jit(solution)/shard_map/ppermute | solution.py:40
  119.7 9.9 %copy-start.1 = (f32[512]{0:T(512)S(1)}, f32[512]{0:T(512)}, u32[]{:S(2)}) copy-start(f32[512]{0:T(512)} %param.11) | copy-start | bytes 6148

commit v3 on v2

--- a/solution.py
+++ b/solution.py
@@ -43,13 +43,16 @@
 HBM = pl.BlockSpec(memory_space=pltpu.HBM)
 
 
-def call(kernel, outs, specs, args, cost, scratch=(), out_spec=VMEM, limit=24 << 20):
+def call(
+    kernel, outs, specs, args, cost, scratch=(), out_spec=VMEM, limit=24 << 20, aliases={}
+):
     return pl.pallas_call(
         kernel,
         out_shape=outs,
         in_specs=specs or [VMEM] * len(args),
         out_specs=jax.tree.map(lambda _: out_spec, outs),
         scratch_shapes=scratch,
+        input_output_aliases=aliases,
         compiler_params=pltpu.CompilerParams(vmem_limit_bytes=limit),
         cost_estimate=pl.CostEstimate(flops=cost[0], bytes_accessed=cost[1], transcendentals=0),
     )(*args)
@@ -60,15 +63,16 @@
 
 
 def first_kernel(factor, tile, place, *refs):
-    sources, (b0, b2, own, g1, g3), scratch = refs[:4], refs[4:9], refs[9:]
-    w_ref, k_ref, v_ref, rate_ref, turned, slab, b1, b3, grads, hiddens, sems = scratch
+    sources, (k_ref, v_ref, rate_ref, b0, b2, own, g1, g3), scratch = refs[:4], refs[4:12], refs[12:]
+    w_ref, turned, slab, b1, b3, grads, hiddens, sems = scratch
     copies = [
         pltpu.make_async_copy(src, dst, sems.at[i])
-        for i, (src, dst) in enumerate(zip(sources, scratch[:4]))
+        for i, (src, dst) in enumerate(zip(sources, (w_ref, k_ref, v_ref, rate_ref)))
     ]
-    for copy in copies:
+    copies[0].start()
+    copies[0].wait()
+    for copy in copies[1:]:
         copy.start()
-    copies[0].wait()
     width = w_ref.shape[0]
     lines = width // (SIDE * SIDE)
     for m in range(2):
@@ -139,7 +143,7 @@
 
 
 def near_kernel(own, r1, r3, out):
-    out[...] = own[...] + r1[...].astype(F32) + r3[...].astype(F32)
+    out[...] = own[...].astype(F32) + r1[...].astype(F32) + r3[...].astype(F32)
 
 
 def scatter_kernel(near, r2, keep, s1, s2, s3):
@@ -147,26 +151,18 @@
         out[...] = (near[s] + r2[s].astype(F32)).astype(out.dtype)
 
 
-def add_kernel(own, r1, r2, r3, out):
-    out[...] = (
-        own[...] + r1[...].astype(F32) + r2[...].astype(F32) + r3[...].astype(F32)
-    ).astype(out.dtype)
-
-
-def update_kernel(weights, own, r1, r2, r3, new, new_bf):
-    total = (
-        own[...].astype(F32) + r1[...].astype(F32) + r2[...].astype(F32) + r3[...].astype(F32)
-    )
-    value = weights[...] - total
+def add_kernel(near, r2, out):
+    out[...] = (near[...] + r2[...].astype(F32)).astype(out.dtype)
+
+
+def update_kernel(weights, near, r2, new, new_bf):
+    value = weights[...] - (near[...] + r2[...].astype(F32))
     new[...] = value
     new_bf[...] = value.astype(BF)
 
 
-def change_kernel(start, weights, own, r1, r2, r3, change, change_bf):
-    total = (
-        own[...].astype(F32) + r1[...].astype(F32) + r2[...].astype(F32) + r3[...].astype(F32)
-    )
-    value = (weights[...] - total) - start[...]
+def change_kernel(start, weights, near, r2, change, change_bf):
+    value = (weights[...] - (near[...] + r2[...].astype(F32))) - start[...]
     change[...] = value
     change_bf[...] = value.astype(BF)
 
@@ -175,9 +171,14 @@
     out[...] = ((start[...] + earlier[...].astype(F32)) + change[...]).astype(BF)
 
 
-def join_kernel(own, r1, r2, r3, out):
-    for s, part in enumerate((own, r1, r2, r3)):
+def join_kernel(own, r1, r3, out):
+    for s, part in ((0, own), (1, r1), (3, r3)):
         out[s] = part[...]
+
+
+def join_last_kernel(joined, r2, out):
+    del joined
+    out[2] = r2[...]
 
 
 def apply_kernel(tile, count, first, last, *refs):
@@ -232,9 +233,9 @@
     )
 
 
-def ring_parts(x, level):
-    parts = {r: hop(x, level, -r) for r in (1, 3, 2)}
-    return [parts[r] for r in range(1, SIDE)]
+def near_sum(own, r1, r3):
+    size = own.size
+    return call(near_kernel, arr(own.shape, F32), None, (own, r1, r3), (2 * size, 12 * size))
 
 
 def in_turn(first, *later):
@@ -244,35 +245,37 @@
 def combined(own, sent):
     shard = own.shape[1:]
     size = own.size
-    near = call(near_kernel, arr(own.shape, F32), None, (own, sent[1], sent[3]), (2 * size, 8 * size))
     keep, *out = call(
         scatter_kernel,
         [arr(shard, F32)] + [arr(shard, BF)] * 3,
         None,
-        (near, sent[2]),
+        (near_sum(own, sent[1], sent[3]), sent[2]),
         (size, 8 * size),
     )
     got = {r: hop(out[r - 1], 1, r) for r in (1, 3, 2)}
-    part = call(add_kernel, arr(shard, BF), None, (keep, got[1], got[2], got[3]), (size, 3 * size))
-    return [part] + ring_parts(part, 2)
+    near = near_sum(keep, got[1], got[3])
+    part = call(add_kernel, arr(shard, BF), None, (near, got[2]), (size, 3 * size))
+    got = {r: hop(part, 2, r) for r in (1, 3, 2)}
+    return near_sum(part, got[1], got[3]), got[2]
 
 
 def first_totals(place, weights, keys, values, rates, factor, tile=256):
+    sources = (weights, keys, values, rates)
     tokens, width = keys.shape
     lines = width // (SIDE * SIDE)
     block = (SIDE, 3, lines, width)
     units = 2 * SIDE * lines
-    b0, b2, start, g1, g3 = call(
+    keys, values, rates, b0, b2, start, g1, g3 = call(
         functools.partial(first_kernel, factor, tile),
-        [arr(block, BF)] * 2 + [arr(block[1:], F32)] + [arr(block, BF)] * 2,
+        [arr(keys.shape, BF), arr(values.shape, BF), arr(rates.shape, F32)]
+        + [arr(block, BF)] * 2
+        + [arr(block[1:], F32)]
+        + [arr(block, BF)] * 2,
         [SMEM] + [HBM] * 4,
-        (place, weights, keys, values, rates),
+        (place, *(pltpu.with_memory_space_constraint(x, pltpu.HBM) for x in sources)),
         (12 * tokens * width * units, 4 * tokens * width),
         [
             pltpu.VMEM(weights.shape, F32),
-            pltpu.VMEM(keys.shape, BF),
-            pltpu.VMEM(values.shape, BF),
-            pltpu.VMEM(rates.shape, F32),
             pltpu.VMEM((3, SIDE * SIDE, lines, width), BF),
             pltpu.VMEM((SIDE, lines, width), F32),
             pltpu.VMEM(block, BF),
@@ -281,31 +284,48 @@
             pltpu.VMEM((units, tokens), BF),
             pltpu.SemaphoreType.DMA((4,)),
         ],
-        limit=52 << 20,
+        limit=32 << 20,
     )
     sent = {1: hop(g1, 0, 1), 3: hop(g3, 0, 3)}
     (g2,) = gradient_blocks([b2], keys, values, rates, factor, BF)
     sent[2] = hop(g2, 0, 2)
     (own,) = gradient_blocks([b0], keys, values, rates, factor, F32)
-    return start, combined(own, sent)
-
-
-def second_totals(blocks, keys, values, rates, factor):
+    return start, (keys, values, rates), combined(own, sent)
+
+
+def gathered(shard):
+    got = {r: hop(shard, 1, -r) for r in (1, 3, 2)}
+    block = arr((SIDE, *shard.shape), BF)
+    size = shard.size
+    joined = call(join_kernel, block, None, (shard, got[1], got[3]), (0, 12 * size))
+    return call(
+        join_last_kernel, block, None, (joined, got[2]), (0, 4 * size), aliases={0: 0}
+    )
+
+
+def second_totals(shard, keys, values, rates, factor):
+    block = gathered(shard)
+    b1, b3 = hop(block, 0, -1), hop(block, 0, -3)
+    (own,) = gradient_blocks([block], keys, values, rates, factor, F32)
+    own, keys, block = in_turn(own, keys, block)
+    b2 = hop(block, 0, -2)
     sent = {}
-    (own,) = gradient_blocks([blocks[0]], keys, values, rates, factor, F32)
-    own, keys = in_turn(own, keys)
-    g1, g3 = gradient_blocks([blocks[1], blocks[3]], keys, values, rates, factor, BF)
+    g1, g3 = gradient_blocks([b1, b3], keys, values, rates, factor, BF)
     sent[1], sent[3] = hop(g1, 0, 1), hop(g3, 0, 3)
     g1, keys = in_turn(g1, keys)
-    (g2,) = gradient_blocks([blocks[2]], keys, values, rates, factor, BF)
+    (g2,) = gradient_blocks([b2], keys, values, rates, factor, BF)
     sent[2] = hop(g2, 0, 2)
     return combined(own, sent)
 
 
-def gathered(shard):
-    parts = [shard] + ring_parts(shard, 1)
-    block = call(join_kernel, arr((SIDE, *shard.shape), BF), None, parts, (0, 16 * shard.size))
-    return [block] + ring_parts(block, 0)
+def applied(shard, queries, gain):
+    block = gathered(shard)
+    b1, b3 = hop(block, 0, -1), hop(block, 0, -3)
+    result = apply_blocks([block], queries, None, None)
+    result, block = in_turn(result, block)
+    b2 = hop(block, 0, -2)
+    result = apply_blocks([b1, b3], queries, result, None)
+    return apply_blocks([b2], queries, result, gain)
 
 
 def shards(queries, key_tokens, value_tokens, learn_rates, fast_init, out_gain):
@@ -322,14 +342,13 @@
     rates = learn_rates.reshape(1, tokens)
     gain = out_gain.reshape(1, width)
 
-    start, parts = first_totals(place, fast_init, key_tokens, value_tokens, rates, factor)
+    start, tokens_in, parts = first_totals(place, fast_init, key_tokens, value_tokens, rates, factor)
     shard = start.shape
     size = start.size
-    first_step, first_bf = call(
+    first_step, shard_bf = call(
         update_kernel, [arr(shard, F32), arr(shard, BF)], None, (start, *parts), (size, 8 * size)
     )
-    blocks = gathered(first_bf)
-    parts = second_totals(blocks, key_tokens, value_tokens, rates, factor)
+    parts = second_totals(shard_bf, *tokens_in, factor)
     change, change_bf = call(
         change_kernel,
         [arr(shard, F32), arr(shard, BF)],
@@ -340,10 +359,7 @@
     pairs = [(flat(0, *c), flat(1, *c)) for c in itertools.product(*[range(SIDE)] * 3)]
     earlier = lax.ppermute(change_bf, AXES, pairs)
     closing = call(closing_kernel, arr(shard, BF), None, (start, earlier, change), (size, 8 * size))
-    blocks = gathered(closing)
-    result = apply_blocks([blocks[0]], queries, None, None)
-    result = apply_blocks([blocks[1], blocks[3]], queries, result, None)
-    return apply_blocks([blocks[2]], queries, result, gain)
+    return applied(closing, queries, gain)
 
 
 def solution(mesh):

time: 133 us -> 139 us (1.045)
  waiting for transfers between devices: 54.6 us -> 62.1 us
  starting transfers between devices: 48.8 us -> 46 us
  Pallas kernels: 27.9 us -> 29.4 us
    ppermute x30, waiting for transfers between devices: 53.7 us -> 61.2 us  [hop(): return lax.ppermute(x, AXES, hop_pairs(level, step % SIDE))]
    ppermute x30, starting transfers between devices: 47.5 us -> 44.7 us  [hop(): return lax.ppermute(x, AXES, hop_pairs(level, step % SIDE))]
    pallas_call x20 -> x26, Pallas kernels: 27.9 us -> 29.4 us  [call(): pl.pallas_call(kernel, out_shape=outs, in_specs=specs or [VMEM] * len(arg...]
  transfers between devices with their start and end apart: 31 -> 31, of which waited for: 25 -> 24; matrix products, arithmetic and copies ran while one was open for 0% -> 0% of each run, Pallas kernels for 13% -> 13%
where the time goes in v3:
time: 139 us; the launch traced here: 138 us
  waiting for transfers between devices  62.1 us (45%)
  starting transfers between devices  46 us (33%)
  Pallas kernels  29.4 us (21%)
    ppermute x30, waiting for transfers between devices, hop(): return lax.ppermute(x, AXES, hop_pairs(level, step % SIDE))  61.2 us
    ppermute x30, starting transfers between devices, hop(): return lax.ppermute(x, AXES, hop_pairs(level, step % SIDE))  44.7 us
    pallas_call x26, Pallas kernels, call(): pl.pallas_call(kernel, out_shape=outs, in_specs=specs or [VMEM] * len(arg...  29.4 us
  transfers between devices with their start and end apart: 31, of which 24 were waited for; matrix products, arithmetic and copies ran while one was open for 0% of the time, Pallas kernels for 13%

profile of v3, /device:TPU:0, one launch (start us, length us, event | category | flops | bytes accessed | tf_op | source)
XLA Modules:
  0.0 138.1 jit_solution(14641218928053748840)
XLA Ops:
  0.0 0.1 add.52
  0.1 0.1 add.47
  0.2 8.9 %shard_map.64 = (bf16[2048,512]{1,0:T(8,128)(2,1)S(1)}, bf16[2048,512]{1,0:T(8,128)(2,1)S(1)}, f32[1,2048]{1,0:T(1,128)S(1)}, bf16[4,3,32,512]{3,2,1,0:T(8,128)(...) custom-call(s32[16]{0:T(128)S(1)} %fusion.place, ...), custom_call_target="tpu_custom_call" | custom-call | flops 3221225472 | bytes 4194304 | tf_op jit(solution)/shard_map/pallas_call | solution.py:49
  9.1 1.6 %collective-permute-start = (bf16[4,3,32,512]{3,2,1,0:T(8,128)(2,1)S(1)}, bf16[4,3,32,512]{3,2,1,0:T(8,128)(2,1)S(1)}, u32[]{:S(2)}, u32[]{:S(2)}) collective-permute-start(bf16[4,3,32,512]{3,2,1,0:T(8,128)(2,1)S(1)} %get-tuple-element.38), channel_id=1, source_target_pairs={{0,1},{1,2},{2,3},{3,0},{4,5},{5,6},{6,7},{7,4},{8,9},{9,10},{10,1... | collective-permute-start | bytes 1179656 | tf_op jit(solution)/shard_map/ppermute | solution.py:40
  10.7 1.7 %collective-permute-start.1 = (bf16[4,3,32,512]{3,2,1,0:T(8,128)(2,1)S(1)}, bf16[4,3,32,512]{3,2,1,0:T(8,128)(2,1)S(1)}, u32[]{:S(2)}, u32[]{:S(2)}) collective-permute-start(bf16[4,3,32,512]{3,2,1,0:T(8,128)(2,1)S(1)} %get-tuple-element.39), channel_id=1, source_target_pairs={{0,3},{1,0},{2,1},{3,2},{4,7},{5,4},{6,5},{7,6},{8,11},{9,8},{10,9... | collective-permute-start | bytes 1179656 | tf_op jit(solution)/shard_map/ppermute | solution.py:40
  12.4 2.3 %shard_map.67 = bf16[4,3,32,512]{3,2,1,0:T(8,128)(2,1)S(1)} custom-call(bf16[4,3,32,512]{3,2,1,0:T(8,128)(2,1)S(1)} %get-tuple-element.40.refs_0_, bf16[2048,512]{1,0:T(8,128)(2,1)S(1)} %get-tuple-element.52.refs_1_.refs_2_, bf16[2048,512]{1,0:T(8,128)(2,1)S(1)} %get-tuple-element.36.refs_2_.refs_3_, f32[1,2048]{1,0:T(1,128)S(1)} %get-tuple-element.37.refs_3_.refs_4_), custom_call_target="tpu_custom_call" | custom-call | flops 1610612736 | bytes 4194304 | tf_op jit(solution)/shard_map/pallas_call | solution.py:49
  14.7 2.0 %collective-permute-start.2 = (bf16[4,3,32,512]{3,2,1,0:T(8,128)(2,1)S(1)}, bf16[4,3,32,512]{3,2,1,0:T(8,128)(2,1)S(1)}, u32[]{:S(2)}, u32[]{:S(2)}) collective-permute-start(bf16[4,3,32,512]{3,2,1,0:T(8,128)(2,1)S(1)} %shard_map.67), channel_id=1, source_target_pairs={{0,2},{1,3},{2,0},{3,1},{4,6},{5,7},{6,4},{7,5},{8,10},{9,11},{10,... | collective-permute-start | bytes 1179656 | tf_op jit(solution)/shard_map/ppermute | solution.py:40
  16.7 2.3 %shard_map.65.own = f32[4,3,32,512]{3,2,1,0:T(8,128)S(1)} custom-call(bf16[4,3,32,512]{3,2,1,0:T(8,128)(2,1)S(1)} %get-tuple-element.34.refs_0_, bf16[2048,512]{1,0:T(8,128)(2,1)S(1)} %get-tuple-element.52.refs_1_.refs_2_, bf16[2048,512]{1,0:T(8,128)(2,1)S(1)} %get-tuple-element.36.refs_2_.refs_3_, f32[1,2048]{1,0:T(1,128)S(1)} %get-tuple-element.37.refs_3_.refs_4_), custom_call_target="tpu_custom_call" | custom-call | flops 1610612736 | bytes 4194304 | tf_op jit(solution)/shard_map/pallas_call | solution.py:49
  19.0 0.1 shard_map.66.near
  19.1 5.0 %collective-permute-done.2.r2 = bf16[4,3,32,512]{3,2,1,0:T(8,128)(2,1)S(1)} collective-permute-done((bf16[4,3,32,512]{3,2,1,0:T(8,128)(2,1)S(1)}, bf16[4,3,32,512]{3,2,1,0:T(8,128)(2,1)S(1)}, u32[]{:S(2)}, u32[]{:S(2)}) %collective-permute-start.2) | collective-permute-done | bytes 393248 | tf_op jit(solution)/shard_map/ppermute | solution.py:40
  24.0 0.1 shard_map.68
  24.1 1.7 %collective-permute-start.3 = (bf16[3,32,512]{2,1,0:T(8,128)(2,1)S(1)}, bf16[3,32,512]{2,1,0:T(8,128)(2,1)S(1)}, u32[]{:S(2)}, u32[]{:S(2)}) collective-permute-start(bf16[3,32,512]{2,1,0:T(8,128)(2,1)S(1)} %get-tuple-element.42), channel_id=1, source_target_pairs={{0,4},{1,5},{2,6},{3,7},{4,8},{5,9},{6,10},{7,11},{8,12},{9,13},{1... | collective-permute-start | bytes 294920 | tf_op jit(solution)/shard_map/ppermute | solution.py:40
  25.9 1.6 %collective-permute-start.4 = (bf16[3,32,512]{2,1,0:T(8,128)(2,1)S(1)}, bf16[3,32,512]{2,1,0:T(8,128)(2,1)S(1)}, u32[]{:S(2)}, u32[]{:S(2)}) collective-permute-start(bf16[3,32,512]{2,1,0:T(8,128)(2,1)S(1)} %get-tuple-element.43), channel_id=1, source_target_pairs={{0,12},{1,13},{2,14},{3,15},{4,0},{5,1},{6,2},{7,3},{8,4},{9,5},{1... | collective-permute-start | bytes 294920 | tf_op jit(solution)/shard_map/ppermute | solution.py:40
  27.4 2.1 %collective-permute-start.5 = (bf16[3,32,512]{2,1,0:T(8,128)(2,1)S(1)}, bf16[3,32,512]{2,1,0:T(8,128)(2,1)S(1)}, u32[]{:S(2)}, u32[]{:S(2)}) collective-permute-start(bf16[3,32,512]{2,1,0:T(8,128)(2,1)S(1)} %get-tuple-element.44), channel_id=1, source_target_pairs={{0,8},{1,9},{2,10},{3,11},{4,12},{5,13},{6,14},{7,15},{8,0},{9,1},... | collective-permute-start | bytes 294920 | tf_op jit(solution)/shard_map/ppermute | solution.py:40
  29.5 0.5 collective-permute-done.3.r1
  30.0 0.4 collective-permute-done.4.r3
  30.5 3.1 %collective-permute-done.5.r2 = bf16[3,32,512]{2,1,0:T(8,128)(2,1)S(1)} collective-permute-done((bf16[3,32,512]{2,1,0:T(8,128)(2,1)S(1)}, bf16[3,32,512]{2,1,0:T(8,128)(2,1)S(1)}, u32[]{:S(2)}, u32[]{:S(2)}) %collective-permute-start.5) | collective-permute-done | bytes 98336 | tf_op jit(solution)/shard_map/ppermute | solution.py:40
  33.6 4.2 %collective-permute-start.7 = (bf16[3,32,512]{2,1,0:T(8,128)(2,1)S(1)}, bf16[3,32,512]{2,1,0:T(8,128)(2,1)S(1)}, u32[]{:S(2)}, u32[]{:S(2)}) collective-permute-start(bf16[3,32,512]{2,1,0:T(8,128)(2,1)S(1)} %shard_map.70.own), channel_id=1, source_target_pairs={{0,48},{1,49},{2,50},{3,51},{4,52},{5,53},{6,54},{7,55},{8,56},{9,... | collective-permute-start | bytes 294920 | tf_op jit(solution)/shard_map/ppermute | solution.py:40
  37.8 1.9 %collective-permute-start.8 = (bf16[3,32,512]{2,1,0:T(8,128)(2,1)S(1)}, bf16[3,32,512]{2,1,0:T(8,128)(2,1)S(1)}, u32[]{:S(2)}, u32[]{:S(2)}) collective-permute-start(bf16[3,32,512]{2,1,0:T(8,128)(2,1)S(1)} %shard_map.70.own), channel_id=1, source_target_pairs={{0,32},{1,33},{2,34},{3,35},{4,36},{5,37},{6,38},{7,39},{8,40},{9,... | collective-permute-start | bytes 294920 | tf_op jit(solution)/shard_map/ppermute | solution.py:40
  39.7 0.3 collective-permute-done.7.r3
  40.0 4.7 %collective-permute-done.6.r1 = bf16[3,32,512]{2,1,0:T(8,128)(2,1)S(1)} collective-permute-done((bf16[3,32,512]{2,1,0:T(8,128)(2,1)S(1)}, bf16[3,32,512]{2,1,0:T(8,128)(2,1)S(1)}, u32[]{:S(2)}, u32[]{:S(2)}) %collective-permute-start.6) | collective-permute-done | bytes 98336 | tf_op jit(solution)/shard_map/ppermute | solution.py:40
  44.8 0.4 collective-permute-start.10
  45.2 2.9 %collective-permute-start.9 = (bf16[3,32,512]{2,1,0:T(8,128)(2,1)S(1)}, bf16[3,32,512]{2,1,0:T(8,128)(2,1)S(1)}, u32[]{:S(2)}, u32[]{:S(2)}) collective-permute-start(bf16[3,32,512]{2,1,0:T(8,128)(2,1)S(1)} %get-tuple-element.46.own), channel_id=1, source_target_pairs={{0,12},{1,13},{2,14},{3,15},{4,0},{5,1},{6,2},{7,3},{8,4},{9,5},{1... | collective-permute-start | bytes 294920 | tf_op jit(solution)/shard_map/ppermute | solution.py:40
  48.1 0.8 collective-permute-start.11
  48.8 1.8 %collective-permute-done.10.r3 = bf16[3,32,512]{2,1,0:T(8,128)(2,1)S(1)} collective-permute-done((bf16[3,32,512]{2,1,0:T(8,128)(2,1)S(1)}, bf16[3,32,512]{2,1,0:T(8,128)(2,1)S(1)}, u32[]{:S(2)}, u32[]{:S(2)}) %collective-permute-start.10) | collective-permute-done | bytes 98336 | tf_op jit(solution)/shard_map/ppermute | solution.py:40
  50.7 4.6 %collective-permute-done.11.r2 = bf16[3,32,512]{2,1,0:T(8,128)(2,1)S(1)} collective-permute-done((bf16[3,32,512]{2,1,0:T(8,128)(2,1)S(1)}, bf16[3,32,512]{2,1,0:T(8,128)(2,1)S(1)}, u32[]{:S(2)}, u32[]{:S(2)}) %collective-permute-start.11) | collective-permute-done | bytes 98336 | tf_op jit(solution)/shard_map/ppermute | solution.py:40
  55.3 0.8 collective-permute-start.13
  56.1 2.5 %collective-permute-start.12 = (bf16[4,3,32,512]{3,2,1,0:T(8,128)(2,1)S(1)}, bf16[4,3,32,512]{3,2,1,0:T(8,128)(2,1)S(1)}, u32[]{:S(2)}, u32[]{:S(2)}) collective-permute-start(bf16[4,3,32,512]{3,2,1,0:T(8,128)(2,1)S(1)} %shard_map.74.refs_0_), channel_id=1, source_target_pairs={{0,3},{1,0},{2,1},{3,2},{4,7},{5,4},{6,5},{7,6},{8,11},{9,8},{10,9... | collective-permute-start | bytes 1179656 | tf_op jit(solution)/shard_map/ppermute | solution.py:40
  58.6 2.3 %shard_map.75.own = f32[4,3,32,512]{3,2,1,0:T(8,128)S(1)} custom-call(bf16[4,3,32,512]{3,2,1,0:T(8,128)(2,1)S(1)} %shard_map.74.refs_0_, bf16[2048,512]{1,0:T(8,128)(2,1)S(1)} %get-tuple-element.52.refs_1_.refs_2_, bf16[2048,512]{1,0:T(8,128)(2,1)S(1)} %get-tuple-element.36.refs_2_.refs_3_, f32[1,2048]{1,0:T(1,128)S(1)} %get-tuple-element.37.refs_3_.refs_4_), custom_call_target="tpu_custom_call" | custom-call | flops 1610612736 | bytes 4194304 | tf_op jit(solution)/shard_map/pallas_call | solution.py:49
  60.9 0.7 collective-permute-start.16
  61.6 2.7 %collective-permute-done.13.refs_1_ = bf16[4,3,32,512]{3,2,1,0:T(8,128)(2,1)S(1)} collective-permute-done((bf16[4,3,32,512]{3,2,1,0:T(8,128)(2,1)S(1)}, bf16[4,3,32,512]{3,2,1,0:T(8,128)(2,1)S(1)}, u32[]{:S(2)}, u32[]{:S(2)}) %collective-permute-start.13) | collective-permute-done | bytes 393248 | tf_op jit(solution)/shard_map/ppermute | solution.py:40
  64.3 3.8 %collective-permute-done.12.refs_0_ = bf16[4,3,32,512]{3,2,1,0:T(8,128)(2,1)S(1)} collective-permute-done((bf16[4,3,32,512]{3,2,1,0:T(8,128)(2,1)S(1)}, bf16[4,3,32,512]{3,2,1,0:T(8,128)(2,1)S(1)}, u32[]{:S(2)}, u32[]{:S(2)}) %collective-permute-start.12) | collective-permute-done | bytes 393248 | tf_op jit(solution)/shard_map/ppermute | solution.py:40
  68.1 3.7 %shard_map.76 = (bf16[4,3,32,512]{3,2,1,0:T(8,128)(2,1)S(1)}, bf16[4,3,32,512]{3,2,1,0:T(8,128)(2,1)S(1)}) custom-call(bf16[4,3,32,512]{3,2,1,0:T(8,128)(2,1)S(1)} %collective-permute-done.12.refs_0_, bf16[4,3,32,512]{3,2,1,0:T(8,128)(2,1)S(1)} %collective-permute-done.13.refs_1_, bf16[2048,512]{1,0:T(8,128)(2,1)S(1)} %get-tuple-element.52.refs_1_.refs_2_, ...), custom_call_target="tpu_custom_call" | custom-call | flops 3221225472 | bytes 4194304 | tf_op jit(solution)/shard_map/pallas_call | solution.py:49
  71.8 0.1 collective-permute-start.14
  71.9 3.7 %collective-permute-start.15 = (bf16[4,3,32,512]{3,2,1,0:T(8,128)(2,1)S(1)}, bf16[4,3,32,512]{3,2,1,0:T(8,128)(2,1)S(1)}, u32[]{:S(2)}, u32[]{:S(2)}) collective-permute-start(bf16[4,3,32,512]{3,2,1,0:T(8,128)(2,1)S(1)} %get-tuple-element.50), channel_id=1, source_target_pairs={{0,3},{1,0},{2,1},{3,2},{4,7},{5,4},{6,5},{7,6},{8,11},{9,8},{10,9... | collective-permute-start | bytes 1179656 | tf_op jit(solution)/shard_map/ppermute | solution.py:40
  75.6 2.3 %shard_map.78 = bf16[4,3,32,512]{3,2,1,0:T(8,128)(2,1)S(1)} custom-call(bf16[4,3,32,512]{3,2,1,0:T(8,128)(2,1)S(1)} %collective-permute-done.16.refs_0_, bf16[2048,512]{1,0:T(8,128)(2,1)S(1)} %get-tuple-element.52.refs_1_.refs_2_, bf16[2048,512]{1,0:T(8,128)(2,1)S(1)} %get-tuple-element.36.refs_2_.refs_3_, f32[1,2048]{1,0:T(1,128)S(1)} %get-tuple-element.37.refs_3_.refs_4_), custom_call_target="tpu_custom_call" | custom-call | flops 1610612736 | bytes 4194304 | tf_op jit(solution)/shard_map/pallas_call | solution.py:49
  78.0 1.5 %collective-permute-start.17 = (bf16[4,3,32,512]{3,2,1,0:T(8,128)(2,1)S(1)}, bf16[4,3,32,512]{3,2,1,0:T(8,128)(2,1)S(1)}, u32[]{:S(2)}, u32[]{:S(2)}) collective-permute-start(bf16[4,3,32,512]{3,2,1,0:T(8,128)(2,1)S(1)} %shard_map.78), channel_id=1, source_target_pairs={{0,2},{1,3},{2,0},{3,1},{4,6},{5,7},{6,4},{7,5},{8,10},{9,11},{10,... | collective-permute-start | bytes 1179656 | tf_op jit(solution)/shard_map/ppermute | solution.py:40
  79.4 1.5 %collective-permute-done.15.r3 = bf16[4,3,32,512]{3,2,1,0:T(8,128)(2,1)S(1)} collective-permute-done((bf16[4,3,32,512]{3,2,1,0:T(8,128)(2,1)S(1)}, bf16[4,3,32,512]{3,2,1,0:T(8,128)(2,1)S(1)}, u32[]{:S(2)}, u32[]{:S(2)}) %collective-permute-start.15) | collective-permute-done | bytes 393248 | tf_op jit(solution)/shard_map/ppermute | solution.py:40
  80.9 0.4 collective-permute-done.14.r1
  81.3 0.1 shard_map.77.near
  81.4 7.7 %collective-permute-done.17.r2 = bf16[4,3,32,512]{3,2,1,0:T(8,128)(2,1)S(1)} collective-permute-done((bf16[4,3,32,512]{3,2,1,0:T(8,128)(2,1)S(1)}, bf16[4,3,32,512]{3,2,1,0:T(8,128)(2,1)S(1)}, u32[]{:S(2)}, u32[]{:S(2)}) %collective-permute-start.17) | collective-permute-done | bytes 393248 | tf_op jit(solution)/shard_map/ppermute | solution.py:40
  89.1 0.1 shard_map.79
  89.3 3.2 %collective-permute-start.19 = (bf16[3,32,512]{2,1,0:T(8,128)(2,1)S(1)}, bf16[3,32,512]{2,1,0:T(8,128)(2,1)S(1)}, u32[]{:S(2)}, u32[]{:S(2)}) collective-permute-start(bf16[3,32,512]{2,1,0:T(8,128)(2,1)S(1)} %get-tuple-element.55), channel_id=1, source_target_pairs={{0,12},{1,13},{2,14},{3,15},{4,0},{5,1},{6,2},{7,3},{8,4},{9,5},{1... | collective-permute-start | bytes 294920 | tf_op jit(solution)/shard_map/ppermute | solution.py:40
  92.5 2.6 %collective-permute-done.18.r1 = bf16[3,32,512]{2,1,0:T(8,128)(2,1)S(1)} collective-permute-done((bf16[3,32,512]{2,1,0:T(8,128)(2,1)S(1)}, bf16[3,32,512]{2,1,0:T(8,128)(2,1)S(1)}, u32[]{:S(2)}, u32[]{:S(2)}) %collective-permute-start.18) | collective-permute-done | bytes 98336 | tf_op jit(solution)/shard_map/ppermute | solution.py:40
  95.1 0.6 collective-permute-done.19.r3
  95.7 2.9 %collective-permute-done.20.r2 = bf16[3,32,512]{2,1,0:T(8,128)(2,1)S(1)} collective-permute-done((bf16[3,32,512]{2,1,0:T(8,128)(2,1)S(1)}, bf16[3,32,512]{2,1,0:T(8,128)(2,1)S(1)}, u32[]{:S(2)}, u32[]{:S(2)}) %collective-permute-start.20) | collective-permute-done | bytes 98336 | tf_op jit(solution)/shard_map/ppermute | solution.py:40
  98.6 2.5 %collective-permute-start.22 = (bf16[3,32,512]{2,1,0:T(8,128)(2,1)S(1)}, bf16[3,32,512]{2,1,0:T(8,128)(2,1)S(1)}, u32[]{:S(2)}, u32[]{:S(2)}) collective-permute-start(bf16[3,32,512]{2,1,0:T(8,128)(2,1)S(1)} %shard_map.81.own), channel_id=1, source_target_pairs={{0,48},{1,49},{2,50},{3,51},{4,52},{5,53},{6,54},{7,55},{8,56},{9,... | collective-permute-start | bytes 294920 | tf_op jit(solution)/shard_map/ppermute | solution.py:40
  101.2 1.5 %collective-permute-start.23 = (bf16[3,32,512]{2,1,0:T(8,128)(2,1)S(1)}, bf16[3,32,512]{2,1,0:T(8,128)(2,1)S(1)}, u32[]{:S(2)}, u32[]{:S(2)}) collective-permute-start(bf16[3,32,512]{2,1,0:T(8,128)(2,1)S(1)} %shard_map.81.own), channel_id=1, source_target_pairs={{0,32},{1,33},{2,34},{3,35},{4,36},{5,37},{6,38},{7,39},{8,40},{9,... | collective-permute-start | bytes 294920 | tf_op jit(solution)/shard_map/ppermute | solution.py:40
  102.7 0.7 collective-permute-done.22.r3
  103.4 4.7 %collective-permute-done.21.r1 = bf16[3,32,512]{2,1,0:T(8,128)(2,1)S(1)} collective-permute-done((bf16[3,32,512]{2,1,0:T(8,128)(2,1)S(1)}, bf16[3,32,512]{2,1,0:T(8,128)(2,1)S(1)}, u32[]{:S(2)}, u32[]{:S(2)}) %collective-permute-start.21) | collective-permute-done | bytes 98336 | tf_op jit(solution)/shard_map/ppermute | solution.py:40
  108.1 1.3 collective-permute-start.24
  109.4 0.9 collective-permute-done.24.earlier
  110.5 3.2 %collective-permute-start.25 = (bf16[3,32,512]{2,1,0:T(8,128)(2,1)S(1)}, bf16[3,32,512]{2,1,0:T(8,128)(2,1)S(1)}, u32[]{:S(2)}, u32[]{:S(2)}) collective-permute-start(bf16[3,32,512]{2,1,0:T(8,128)(2,1)S(1)} %shard_map.84.own), channel_id=1, source_target_pairs={{0,12},{1,13},{2,14},{3,15},{4,0},{5,1},{6,2},{7,3},{8,4},{9,5},{1... | collective-permute-start | bytes 294920 | tf_op jit(solution)/shard_map/ppermute | solution.py:40
  113.7 2.6 %collective-permute-done.26.r3 = bf16[3,32,512]{2,1,0:T(8,128)(2,1)S(1)} collective-permute-done((bf16[3,32,512]{2,1,0:T(8,128)(2,1)S(1)}, bf16[3,32,512]{2,1,0:T(8,128)(2,1)S(1)}, u32[]{:S(2)}, u32[]{:S(2)}) %collective-permute-start.26) | collective-permute-done | bytes 98336 | tf_op jit(solution)/shard_map/ppermute | solution.py:40
  116.3 0.6 collective-permute-done.25.r1
  117.0 2.9 %collective-permute-done.27.r2 = bf16[3,32,512]{2,1,0:T(8,128)(2,1)S(1)} collective-permute-done((bf16[3,32,512]{2,1,0:T(8,128)(2,1)S(1)}, bf16[3,32,512]{2,1,0:T(8,128)(2,1)S(1)}, u32[]{:S(2)}, u32[]{:S(2)}) %collective-permute-start.27) | collective-permute-done | bytes 98336 | tf_op jit(solution)/shard_map/ppermute | solution.py:40
  119.8 1.5 %collective-permute-start.30 = (bf16[4,3,32,512]{3,2,1,0:T(8,128)(2,1)S(1)}, bf16[4,3,32,512]{3,2,1,0:T(8,128)(2,1)S(1)}, u32[]{:S(2)}, u32[]{:S(2)}) collective-permute-start(bf16[4,3,32,512]{3,2,1,0:T(8,128)(2,1)S(1)} %shard_map.86.refs_0_), channel_id=1, source_target_pairs={{0,1},{1,2},{2,3},{3,0},{4,5},{5,6},{6,7},{7,4},{8,9},{9,10},{10,1... | collective-permute-start | bytes 1179656 | tf_op jit(solution)/shard_map/ppermute | solution.py:40
  121.3 1.8 %collective-permute-start.29 = (bf16[4,3,32,512]{3,2,1,0:T(8,128)(2,1)S(1)}, bf16[4,3,32,512]{3,2,1,0:T(8,128)(2,1)S(1)}, u32[]{:S(2)}, u32[]{:S(2)}) collective-permute-start(bf16[4,3,32,512]{3,2,1,0:T(8,128)(2,1)S(1)} %shard_map.86.refs_0_), channel_id=1, source_target_pairs={{0,3},{1,0},{2,1},{3,2},{4,7},{5,4},{6,5},{7,6},{8,11},{9,8},{10,9... | collective-permute-start | bytes 1179656 | tf_op jit(solution)/shard_map/ppermute | solution.py:40
  123.2 1.6 %shard_map.87.refs_3_ = f32[2048,512]{1,0:T(8,128)S(1)} custom-call(bf16[4,3,32,512]{3,2,1,0:T(8,128)(2,1)S(1)} %shard_map.86.refs_0_, bf16[2048,512]{1,0:T(8,128)(2,1)S(1)} %copy-done), custom_call_target="tpu_custom_call" | custom-call | flops 805306368 | bytes 6291456 | tf_op jit(solution)/shard_map/pallas_call | solution.py:49
  124.8 0.6 collective-permute-start.28
  125.4 3.5 %collective-permute-done.30.refs_1_ = bf16[4,3,32,512]{3,2,1,0:T(8,128)(2,1)S(1)} collective-permute-done((bf16[4,3,32,512]{3,2,1,0:T(8,128)(2,1)S(1)}, bf16[4,3,32,512]{3,2,1,0:T(8,128)(2,1)S(1)}, u32[]{:S(2)}, u32[]{:S(2)}) %collective-permute-start.30) | collective-permute-done | bytes 393248 | tf_op jit(solution)/shard_map/ppermute | solution.py:40
  128.9 3.8 %collective-permute-done.29.refs_0_ = bf16[4,3,32,512]{3,2,1,0:T(8,128)(2,1)S(1)} collective-permute-done((bf16[4,3,32,512]{3,2,1,0:T(8,128)(2,1)S(1)}, bf16[4,3,32,512]{3,2,1,0:T(8,128)(2,1)S(1)}, u32[]{:S(2)}, u32[]{:S(2)}) %collective-permute-start.29) | collective-permute-done | bytes 393248 | tf_op jit(solution)/shard_map/ppermute | solution.py:40
  132.7 2.5 %shard_map.88.refs_3_ = f32[2048,512]{1,0:T(8,128)S(1)} custom-call(bf16[4,3,32,512]{3,2,1,0:T(8,128)(2,1)S(1)} %collective-permute-done.29.refs_0_, bf16[4,3,32,512]{3,2,1,0:T(8,128)(2,1)S(1)} %collective-permute-done.30.refs_1_, bf16[2048,512]{1,0:T(8,128)(2,1)S(1)} %copy-done, f32[2048,512]{1,0:T(8,128)S(1)} %shard_map.87.refs_3_), custom_call_target="tpu_custom_call" | custom-call | flops 1610612736 | bytes 6291456 | tf_op jit(solution)/shard_map/pallas_call | solution.py:49
  135.2 2.6 %shard_map.89 = bf16[2048,512]{1,0:T(8,128)(2,1)} custom-call(bf16[4,3,32,512]{3,2,1,0:T(8,128)(2,1)S(1)} %collective-permute-done.28.refs_0_, bf16[2048,512]{1,0:T(8,128)(2,1)S(1)} %copy-done, f32[1,512]{1,0:T(1,128)S(1)} %bitcast.2, f32[2048,512]{1,0:T(8,128)S(1)} %shard_map.88.refs_3_), custom_call_target="tpu_custom_call" | custom-call | flops 805306368 | bytes 6291456 | tf_op jit(solution)/shard_map/pallas_call | solution.py:49
  (32 shorter events, 0.6 us)
Async XLA Ops:
  9.1 9.9 %collective-permute-start = (bf16[4,3,32,512]{3,2,1,0:T(8,128)(2,1)S(1)}, bf16[4,3,32,512]{3,2,1,0:T(8,128)(2,1)S(1)}, u32[]{:S(2)}, u32[]{:S(2)}) collective-permute-start(bf16[4,3,32,512]{3,2,1,0:T(8,128)(2,1)S(1)} %get-tuple-element.38), channel_id=1, source_target_pairs={{0,1},{1,2},{2,3},{3,0},{4,5},{5,6},{6,7},{7,4},{8,9},{9,10},{10,1... | collective-permute-start | bytes 1179656 | tf_op jit(solution)/shard_map/ppermute | solution.py:40
  10.7 8.2 %collective-permute-start.1 = (bf16[4,3,32,512]{3,2,1,0:T(8,128)(2,1)S(1)}, bf16[4,3,32,512]{3,2,1,0:T(8,128)(2,1)S(1)}, u32[]{:S(2)}, u32[]{:S(2)}) collective-permute-start(bf16[4,3,32,512]{3,2,1,0:T(8,128)(2,1)S(1)} %get-tuple-element.39), channel_id=1, source_target_pairs={{0,3},{1,0},{2,1},{3,2},{4,7},{5,4},{6,5},{7,6},{8,11},{9,8},{10,9... | collective-permute-start | bytes 1179656 | tf_op jit(solution)/shard_map/ppermute | solution.py:40
  14.7 9.4 %collective-permute-start.2 = (bf16[4,3,32,512]{3,2,1,0:T(8,128)(2,1)S(1)}, bf16[4,3,32,512]{3,2,1,0:T(8,128)(2,1)S(1)}, u32[]{:S(2)}, u32[]{:S(2)}) collective-permute-start(bf16[4,3,32,512]{3,2,1,0:T(8,128)(2,1)S(1)} %shard_map.67), channel_id=1, source_target_pairs={{0,2},{1,3},{2,0},{3,1},{4,6},{5,7},{6,4},{7,5},{8,10},{9,11},{10,... | collective-permute-start | bytes 1179656 | tf_op jit(solution)/shard_map/ppermute | solution.py:40
  24.1 5.9 %collective-permute-start.3 = (bf16[3,32,512]{2,1,0:T(8,128)(2,1)S(1)}, bf16[3,32,512]{2,1,0:T(8,128)(2,1)S(1)}, u32[]{:S(2)}, u32[]{:S(2)}) collective-permute-start(bf16[3,32,512]{2,1,0:T(8,128)(2,1)S(1)} %get-tuple-element.42), channel_id=1, source_target_pairs={{0,4},{1,5},{2,6},{3,7},{4,8},{5,9},{6,10},{7,11},{8,12},{9,13},{1... | collective-permute-start | bytes 294920 | tf_op jit(solution)/shard_map/ppermute | solution.py:40
  25.9 4.6 %collective-permute-start.4 = (bf16[3,32,512]{2,1,0:T(8,128)(2,1)S(1)}, bf16[3,32,512]{2,1,0:T(8,128)(2,1)S(1)}, u32[]{:S(2)}, u32[]{:S(2)}) collective-permute-start(bf16[3,32,512]{2,1,0:T(8,128)(2,1)S(1)} %get-tuple-element.43), channel_id=1, source_target_pairs={{0,12},{1,13},{2,14},{3,15},{4,0},{5,1},{6,2},{7,3},{8,4},{9,5},{1... | collective-permute-start | bytes 294920 | tf_op jit(solution)/shard_map/ppermute | solution.py:40
  27.4 6.1 %collective-permute-start.5 = (bf16[3,32,512]{2,1,0:T(8,128)(2,1)S(1)}, bf16[3,32,512]{2,1,0:T(8,128)(2,1)S(1)}, u32[]{:S(2)}, u32[]{:S(2)}) collective-permute-start(bf16[3,32,512]{2,1,0:T(8,128)(2,1)S(1)} %get-tuple-element.44), channel_id=1, source_target_pairs={{0,8},{1,9},{2,10},{3,11},{4,12},{5,13},{6,14},{7,15},{8,0},{9,1},... | collective-permute-start | bytes 294920 | tf_op jit(solution)/shard_map/ppermute | solution.py:40
  33.6 6.4 %collective-permute-start.7 = (bf16[3,32,512]{2,1,0:T(8,128)(2,1)S(1)}, bf16[3,32,512]{2,1,0:T(8,128)(2,1)S(1)}, u32[]{:S(2)}, u32[]{:S(2)}) collective-permute-start(bf16[3,32,512]{2,1,0:T(8,128)(2,1)S(1)} %shard_map.70.own), channel_id=1, source_target_pairs={{0,48},{1,49},{2,50},{3,51},{4,52},{5,53},{6,54},{7,55},{8,56},{9,... | collective-permute-start | bytes 294920 | tf_op jit(solution)/shard_map/ppermute | solution.py:40
  37.8 6.9 %collective-permute-start.6 = (bf16[3,32,512]{2,1,0:T(8,128)(2,1)S(1)}, bf16[3,32,512]{2,1,0:T(8,128)(2,1)S(1)}, u32[]{:S(2)}, u32[]{:S(2)}) collective-permute-start(bf16[3,32,512]{2,1,0:T(8,128)(2,1)S(1)} %shard_map.70.own), channel_id=1, source_target_pairs={{0,16},{1,17},{2,18},{3,19},{4,20},{5,21},{6,22},{7,23},{8,24},{9,... | collective-permute-start | bytes 294920 | tf_op jit(solution)/shard_map/ppermute | solution.py:40
  37.8 6.9 %collective-permute-start.8 = (bf16[3,32,512]{2,1,0:T(8,128)(2,1)S(1)}, bf16[3,32,512]{2,1,0:T(8,128)(2,1)S(1)}, u32[]{:S(2)}, u32[]{:S(2)}) collective-permute-start(bf16[3,32,512]{2,1,0:T(8,128)(2,1)S(1)} %shard_map.70.own), channel_id=1, source_target_pairs={{0,32},{1,33},{2,34},{3,35},{4,36},{5,37},{6,38},{7,39},{8,40},{9,... | collective-permute-start | bytes 294920 | tf_op jit(solution)/shard_map/ppermute | solution.py:40
  44.8 5.9 %collective-permute-start.10 = (bf16[3,32,512]{2,1,0:T(8,128)(2,1)S(1)}, bf16[3,32,512]{2,1,0:T(8,128)(2,1)S(1)}, u32[]{:S(2)}, u32[]{:S(2)}) collective-permute-start(bf16[3,32,512]{2,1,0:T(8,128)(2,1)S(1)} %get-tuple-element.46.own), channel_id=1, source_target_pairs={{0,4},{1,5},{2,6},{3,7},{4,8},{5,9},{6,10},{7,11},{8,12},{9,13},{1... | collective-permute-start | bytes 294920 | tf_op jit(solution)/shard_map/ppermute | solution.py:40
  45.2 5.5 %collective-permute-start.9 = (bf16[3,32,512]{2,1,0:T(8,128)(2,1)S(1)}, bf16[3,32,512]{2,1,0:T(8,128)(2,1)S(1)}, u32[]{:S(2)}, u32[]{:S(2)}) collective-permute-start(bf16[3,32,512]{2,1,0:T(8,128)(2,1)S(1)} %get-tuple-element.46.own), channel_id=1, source_target_pairs={{0,12},{1,13},{2,14},{3,15},{4,0},{5,1},{6,2},{7,3},{8,4},{9,5},{1... | collective-permute-start | bytes 294920 | tf_op jit(solution)/shard_map/ppermute | solution.py:40
  48.1 7.2 %collective-permute-start.11 = (bf16[3,32,512]{2,1,0:T(8,128)(2,1)S(1)}, bf16[3,32,512]{2,1,0:T(8,128)(2,1)S(1)}, u32[]{:S(2)}, u32[]{:S(2)}) collective-permute-start(bf16[3,32,512]{2,1,0:T(8,128)(2,1)S(1)} %get-tuple-element.46.own), channel_id=1, source_target_pairs={{0,8},{1,9},{2,10},{3,11},{4,12},{5,13},{6,14},{7,15},{8,0},{9,1},... | collective-permute-start | bytes 294920 | tf_op jit(solution)/shard_map/ppermute | solution.py:40
  55.3 9.1 %collective-permute-start.13 = (bf16[4,3,32,512]{3,2,1,0:T(8,128)(2,1)S(1)}, bf16[4,3,32,512]{3,2,1,0:T(8,128)(2,1)S(1)}, u32[]{:S(2)}, u32[]{:S(2)}) collective-permute-start(bf16[4,3,32,512]{3,2,1,0:T(8,128)(2,1)S(1)} %shard_map.74.refs_0_), channel_id=1, source_target_pairs={{0,1},{1,2},{2,3},{3,0},{4,5},{5,6},{6,7},{7,4},{8,9},{9,10},{10,1... | collective-permute-start | bytes 1179656 | tf_op jit(solution)/shard_map/ppermute | solution.py:40
  56.1 12.0 %collective-permute-start.12 = (bf16[4,3,32,512]{3,2,1,0:T(8,128)(2,1)S(1)}, bf16[4,3,32,512]{3,2,1,0:T(8,128)(2,1)S(1)}, u32[]{:S(2)}, u32[]{:S(2)}) collective-permute-start(bf16[4,3,32,512]{3,2,1,0:T(8,128)(2,1)S(1)} %shard_map.74.refs_0_), channel_id=1, source_target_pairs={{0,3},{1,0},{2,1},{3,2},{4,7},{5,4},{6,5},{7,6},{8,11},{9,8},{10,9... | collective-permute-start | bytes 1179656 | tf_op jit(solution)/shard_map/ppermute | solution.py:40
  60.9 14.7 %collective-permute-start.16 = (bf16[4,3,32,512]{3,2,1,0:T(8,128)(2,1)S(1)}, bf16[4,3,32,512]{3,2,1,0:T(8,128)(2,1)S(1)}, u32[]{:S(2)}, u32[]{:S(2)}) collective-permute-start(bf16[4,3,32,512]{3,2,1,0:T(8,128)(2,1)S(1)} %shard_map.74.refs_0_), channel_id=1, source_target_pairs={{0,2},{1,3},{2,0},{3,1},{4,6},{5,7},{6,4},{7,5},{8,10},{9,11},{10,... | collective-permute-start | bytes 1179656 | tf_op jit(solution)/shard_map/ppermute | solution.py:40
  71.8 9.5 %collective-permute-start.14 = (bf16[4,3,32,512]{3,2,1,0:T(8,128)(2,1)S(1)}, bf16[4,3,32,512]{3,2,1,0:T(8,128)(2,1)S(1)}, u32[]{:S(2)}, u32[]{:S(2)}) collective-permute-start(bf16[4,3,32,512]{3,2,1,0:T(8,128)(2,1)S(1)} %get-tuple-element.49), channel_id=1, source_target_pairs={{0,1},{1,2},{2,3},{3,0},{4,5},{5,6},{6,7},{7,4},{8,9},{9,10},{10,1... | collective-permute-start | bytes 1179656 | tf_op jit(solution)/shard_map/ppermute | solution.py:40
  71.9 9.0 %collective-permute-start.15 = (bf16[4,3,32,512]{3,2,1,0:T(8,128)(2,1)S(1)}, bf16[4,3,32,512]{3,2,1,0:T(8,128)(2,1)S(1)}, u32[]{:S(2)}, u32[]{:S(2)}) collective-permute-start(bf16[4,3,32,512]{3,2,1,0:T(8,128)(2,1)S(1)} %get-tuple-element.50), channel_id=1, source_target_pairs={{0,3},{1,0},{2,1},{3,2},{4,7},{5,4},{6,5},{7,6},{8,11},{9,8},{10,9... | collective-permute-start | bytes 1179656 | tf_op jit(solution)/shard_map/ppermute | solution.py:40
  78.0 11.1 %collective-permute-start.17 = (bf16[4,3,32,512]{3,2,1,0:T(8,128)(2,1)S(1)}, bf16[4,3,32,512]{3,2,1,0:T(8,128)(2,1)S(1)}, u32[]{:S(2)}, u32[]{:S(2)}) collective-permute-start(bf16[4,3,32,512]{3,2,1,0:T(8,128)(2,1)S(1)} %shard_map.78), channel_id=1, source_target_pairs={{0,2},{1,3},{2,0},{3,1},{4,6},{5,7},{6,4},{7,5},{8,10},{9,11},{10,... | collective-permute-start | bytes 1179656 | tf_op jit(solution)/shard_map/ppermute | solution.py:40
  89.2 5.9 %collective-permute-start.18 = (bf16[3,32,512]{2,1,0:T(8,128)(2,1)S(1)}, bf16[3,32,512]{2,1,0:T(8,128)(2,1)S(1)}, u32[]{:S(2)}, u32[]{:S(2)}) collective-permute-start(bf16[3,32,512]{2,1,0:T(8,128)(2,1)S(1)} %get-tuple-element.54), channel_id=1, source_target_pairs={{0,4},{1,5},{2,6},{3,7},{4,8},{5,9},{6,10},{7,11},{8,12},{9,13},{1... | collective-permute-start | bytes 294920 | tf_op jit(solution)/shard_map/ppermute | solution.py:40
  89.3 6.4 %collective-permute-start.19 = (bf16[3,32,512]{2,1,0:T(8,128)(2,1)S(1)}, bf16[3,32,512]{2,1,0:T(8,128)(2,1)S(1)}, u32[]{:S(2)}, u32[]{:S(2)}) collective-permute-start(bf16[3,32,512]{2,1,0:T(8,128)(2,1)S(1)} %get-tuple-element.55), channel_id=1, source_target_pairs={{0,12},{1,13},{2,14},{3,15},{4,0},{5,1},{6,2},{7,3},{8,4},{9,5},{1... | collective-permute-start | bytes 294920 | tf_op jit(solution)/shard_map/ppermute | solution.py:40
  92.5 6.1 %collective-permute-start.20 = (bf16[3,32,512]{2,1,0:T(8,128)(2,1)S(1)}, bf16[3,32,512]{2,1,0:T(8,128)(2,1)S(1)}, u32[]{:S(2)}, u32[]{:S(2)}) collective-permute-start(bf16[3,32,512]{2,1,0:T(8,128)(2,1)S(1)} %get-tuple-element.56), channel_id=1, source_target_pairs={{0,8},{1,9},{2,10},{3,11},{4,12},{5,13},{6,14},{7,15},{8,0},{9,1},... | collective-permute-start | bytes 294920 | tf_op jit(solution)/shard_map/ppermute | solution.py:40
  95.7 27.5 %copy-start = (bf16[2048,512]{1,0:T(8,128)(2,1)S(1)}, bf16[2048,512]{1,0:T(8,128)(2,1)}, u32[]{:S(2)}) copy-start(bf16[2048,512]{1,0:T(8,128)(2,1)} %refs_1_.5) | copy-start | bytes 6291460
  98.6 4.7 %collective-permute-start.22 = (bf16[3,32,512]{2,1,0:T(8,128)(2,1)S(1)}, bf16[3,32,512]{2,1,0:T(8,128)(2,1)S(1)}, u32[]{:S(2)}, u32[]{:S(2)}) collective-permute-start(bf16[3,32,512]{2,1,0:T(8,128)(2,1)S(1)} %shard_map.81.own), channel_id=1, source_target_pairs={{0,48},{1,49},{2,50},{3,51},{4,52},{5,53},{6,54},{7,55},{8,56},{9,... | collective-permute-start | bytes 294920 | tf_op jit(solution)/shard_map/ppermute | solution.py:40
  101.2 6.9 %collective-permute-start.21 = (bf16[3,32,512]{2,1,0:T(8,128)(2,1)S(1)}, bf16[3,32,512]{2,1,0:T(8,128)(2,1)S(1)}, u32[]{:S(2)}, u32[]{:S(2)}) collective-permute-start(bf16[3,32,512]{2,1,0:T(8,128)(2,1)S(1)} %shard_map.81.own), channel_id=1, source_target_pairs={{0,16},{1,17},{2,18},{3,19},{4,20},{5,21},{6,22},{7,23},{8,24},{9,... | collective-permute-start | bytes 294920 | tf_op jit(solution)/shard_map/ppermute | solution.py:40
  101.2 6.9 %collective-permute-start.23 = (bf16[3,32,512]{2,1,0:T(8,128)(2,1)S(1)}, bf16[3,32,512]{2,1,0:T(8,128)(2,1)S(1)}, u32[]{:S(2)}, u32[]{:S(2)}) collective-permute-start(bf16[3,32,512]{2,1,0:T(8,128)(2,1)S(1)} %shard_map.81.own), channel_id=1, source_target_pairs={{0,32},{1,33},{2,34},{3,35},{4,36},{5,37},{6,38},{7,39},{8,40},{9,... | collective-permute-start | bytes 294920 | tf_op jit(solution)/shard_map/ppermute | solution.py:40
  108.1 2.2 %collective-permute-start.24 = (bf16[3,32,512]{2,1,0:T(8,128)(2,1)S(1)}, bf16[3,32,512]{2,1,0:T(8,128)(2,1)S(1)}, u32[]{:S(2)}, u32[]{:S(2)}) collective-permute-start(bf16[3,32,512]{2,1,0:T(8,128)(2,1)S(1)} %get-tuple-element.57), channel_id=1, source_target_pairs={{0,64},{1,65},{2,66},{3,67},{4,68},{5,69},{6,70},{7,71},{8,72},{9,... | collective-permute-start | bytes 294920 | tf_op jit(solution)/shard_map/ppermute | solution.py:360
  110.4 5.9 %collective-permute-start.26 = (bf16[3,32,512]{2,1,0:T(8,128)(2,1)S(1)}, bf16[3,32,512]{2,1,0:T(8,128)(2,1)S(1)}, u32[]{:S(2)}, u32[]{:S(2)}) collective-permute-start(bf16[3,32,512]{2,1,0:T(8,128)(2,1)S(1)} %shard_map.84.own), channel_id=1, source_target_pairs={{0,4},{1,5},{2,6},{3,7},{4,8},{5,9},{6,10},{7,11},{8,12},{9,13},{1... | collective-permute-start | bytes 294920 | tf_op jit(solution)/shard_map/ppermute | solution.py:40
  110.5 6.4 %collective-permute-start.25 = (bf16[3,32,512]{2,1,0:T(8,128)(2,1)S(1)}, bf16[3,32,512]{2,1,0:T(8,128)(2,1)S(1)}, u32[]{:S(2)}, u32[]{:S(2)}) collective-permute-start(bf16[3,32,512]{2,1,0:T(8,128)(2,1)S(1)} %shard_map.84.own), channel_id=1, source_target_pairs={{0,12},{1,13},{2,14},{3,15},{4,0},{5,1},{6,2},{7,3},{8,4},{9,5},{1... | collective-permute-start | bytes 294920 | tf_op jit(solution)/shard_map/ppermute | solution.py:40
  113.7 6.1 %collective-permute-start.27 = (bf16[3,32,512]{2,1,0:T(8,128)(2,1)S(1)}, bf16[3,32,512]{2,1,0:T(8,128)(2,1)S(1)}, u32[]{:S(2)}, u32[]{:S(2)}) collective-permute-start(bf16[3,32,512]{2,1,0:T(8,128)(2,1)S(1)} %shard_map.84.own), channel_id=1, source_target_pairs={{0,8},{1,9},{2,10},{3,11},{4,12},{5,13},{6,14},{7,15},{8,0},{9,1},... | collective-permute-start | bytes 294920 | tf_op jit(solution)/shard_map/ppermute | solution.py:40
  119.8 9.1 %collective-permute-start.30 = (bf16[4,3,32,512]{3,2,1,0:T(8,128)(2,1)S(1)}, bf16[4,3,32,512]{3,2,1,0:T(8,128)(2,1)S(1)}, u32[]{:S(2)}, u32[]{:S(2)}) collective-permute-start(bf16[4,3,32,512]{3,2,1,0:T(8,128)(2,1)S(1)} %shard_map.86.refs_0_), channel_id=1, source_target_pairs={{0,1},{1,2},{2,3},{3,0},{4,5},{5,6},{6,7},{7,4},{8,9},{9,10},{10,1... | collective-permute-start | bytes 1179656 | tf_op jit(solution)/shard_map/ppermute | solution.py:40
  121.3 11.4 %collective-permute-start.29 = (bf16[4,3,32,512]{3,2,1,0:T(8,128)(2,1)S(1)}, bf16[4,3,32,512]{3,2,1,0:T(8,128)(2,1)S(1)}, u32[]{:S(2)}, u32[]{:S(2)}) collective-permute-start(bf16[4,3,32,512]{3,2,1,0:T(8,128)(2,1)S(1)} %shard_map.86.refs_0_), channel_id=1, source_target_pairs={{0,3},{1,0},{2,1},{3,2},{4,7},{5,4},{6,5},{7,6},{8,11},{9,8},{10,9... | collective-permute-start | bytes 1179656 | tf_op jit(solution)/shard_map/ppermute | solution.py:40
  124.8 10.4 %copy-start.1 = (f32[512]{0:T(512)S(1)}, f32[512]{0:T(512)}, u32[]{:S(2)}) copy-start(f32[512]{0:T(512)} %param.11) | copy-start | bytes 6148
  124.8 10.4 %collective-permute-start.28 = (bf16[4,3,32,512]{3,2,1,0:T(8,128)(2,1)S(1)}, bf16[4,3,32,512]{3,2,1,0:T(8,128)(2,1)S(1)}, u32[]{:S(2)}, u32[]{:S(2)}) collective-permute-start(bf16[4,3,32,512]{3,2,1,0:T(8,128)(2,1)S(1)} %shard_map.86.refs_0_), channel_id=1, source_target_pairs={{0,2},{1,3},{2,0},{3,1},{4,6},{5,7},{6,4},{7,5},{8,10},{9,11},{10,... | collective-permute-start | bytes 1179656 | tf_op jit(solution)/shard_map/ppermute | solution.py:40

commit v4 on v3

--- a/solution.py
+++ b/solution.py
@@ -63,16 +63,20 @@
 
 
 def first_kernel(factor, tile, place, *refs):
-    sources, (k_ref, v_ref, rate_ref, b0, b2, own, g1, g3), scratch = refs[:4], refs[4:12], refs[12:]
-    w_ref, turned, slab, b1, b3, grads, hiddens, sems = scratch
-    copies = [
-        pltpu.make_async_copy(src, dst, sems.at[i])
-        for i, (src, dst) in enumerate(zip(sources, (w_ref, k_ref, v_ref, rate_ref)))
-    ]
-    copies[0].start()
-    copies[0].wait()
-    for copy in copies[1:]:
-        copy.start()
+    sources, outs, scratch = refs[:4], refs[4:12], refs[12:]
+    k_ref, v_ref, rate_ref, b0, b1, b3, own, g2 = outs
+    w_ref, turned, slab, b2, grads, hiddens, sems = scratch
+    copies = []
+    for src, dst in zip(sources, (w_ref, k_ref, v_ref, rate_ref)):
+        count = sems.shape[1] if src.shape[0] > 1 else 1
+        rows = src.shape[0] // count
+        for j in range(count):
+            part = pl.ds(j * rows, rows)
+            sem = sems.at[len(copies) // sems.shape[1], j]
+            copies.append(pltpu.make_async_copy(src.at[part], dst.at[part], sem))
+            copies[-1].start()
+    for copy in copies[: sems.shape[1]]:
+        copy.wait()
     width = w_ref.shape[0]
     lines = width // (SIDE * SIDE)
     for m in range(2):
@@ -90,9 +94,9 @@
         slab[...] = w_ref[:, pl.ds(start, 128)].T.reshape(SIDE, lines, width)
         own[m] = slab[mine % SIDE]
     own[2] = w_ref[pl.ds(pl.multiple_of(mine * lines, lines), lines), 2 * width :]
-    for copy in copies[1:]:
+    for copy in copies[sems.shape[1] :]:
         copy.wait()
-    gradient_kernel(factor, tile, 2, b1, b3, k_ref, v_ref, rate_ref, g1, g3, grads, hiddens)
+    gradient_kernel(factor, tile, 1, b2, k_ref, v_ref, rate_ref, g2, grads, hiddens)
 
 
 def rows_of(w_refs, m):
@@ -142,27 +146,31 @@
     )
 
 
-def near_kernel(own, r1, r3, out):
-    out[...] = own[...].astype(F32) + r1[...].astype(F32) + r3[...].astype(F32)
-
-
-def scatter_kernel(near, r2, keep, s1, s2, s3):
+def far_kernel(own, r2, out):
+    out[...] = own[...] + r2[...].astype(F32)
+
+
+def scatter_kernel(far, r1, r3, keep, s1, s2, s3):
     for s, out in enumerate((keep, s1, s2, s3)):
-        out[...] = (near[s] + r2[s].astype(F32)).astype(out.dtype)
-
-
-def add_kernel(near, r2, out):
-    out[...] = (near[...] + r2[...].astype(F32)).astype(out.dtype)
-
-
-def update_kernel(weights, near, r2, new, new_bf):
-    value = weights[...] - (near[...] + r2[...].astype(F32))
+        out[...] = (far[s] + r1[s].astype(F32) + r3[s].astype(F32)).astype(out.dtype)
+
+
+def grow_kernel(own, part, out):
+    out[...] = own[...].astype(F32) + part[...].astype(F32)
+
+
+def add_kernel(own, part, out):
+    out[...] = (own[...] + part[...].astype(F32)).astype(out.dtype)
+
+
+def update_kernel(weights, own, part, new, new_bf):
+    value = weights[...] - (own[...] + part[...].astype(F32))
     new[...] = value
     new_bf[...] = value.astype(BF)
 
 
-def change_kernel(start, weights, near, r2, change, change_bf):
-    value = (weights[...] - (near[...] + r2[...].astype(F32))) - start[...]
+def change_kernel(start, weights, own, part, change, change_bf):
+    value = (weights[...] - (own[...] + part[...].astype(F32))) - start[...]
     change[...] = value
     change_bf[...] = value.astype(BF)
 
@@ -171,14 +179,14 @@
     out[...] = ((start[...] + earlier[...].astype(F32)) + change[...]).astype(BF)
 
 
-def join_kernel(own, r1, r3, out):
-    for s, part in ((0, own), (1, r1), (3, r3)):
-        out[s] = part[...]
-
-
-def join_last_kernel(joined, r2, out):
+def join_kernel(slot, joined, part, out):
     del joined
-    out[2] = r2[...]
+    out[slot] = part[...]
+
+
+def join_first_kernel(own, part, out):
+    out[0] = own[...]
+    out[1] = part[...]
 
 
 def apply_kernel(tile, count, first, last, *refs):
@@ -233,30 +241,36 @@
     )
 
 
-def near_sum(own, r1, r3):
-    size = own.size
-    return call(near_kernel, arr(own.shape, F32), None, (own, r1, r3), (2 * size, 12 * size))
-
-
 def in_turn(first, *later):
     return lax.optimization_barrier((first, *later))
+
+
+def ring_parts(x, level):
+    return [hop(x, level, -r) for r in range(1, SIDE)]
+
+
+def grown(total, parts):
+    size = total.size
+    for part in parts:
+        total = call(grow_kernel, arr(total.shape, F32), None, (total, part), (size, 8 * size))
+    return total
 
 
 def combined(own, sent):
     shard = own.shape[1:]
     size = own.size
+    far = call(far_kernel, arr(own.shape, F32), None, (own, sent[2]), (size, 10 * size))
     keep, *out = call(
         scatter_kernel,
         [arr(shard, F32)] + [arr(shard, BF)] * 3,
         None,
-        (near_sum(own, sent[1], sent[3]), sent[2]),
-        (size, 8 * size),
-    )
-    got = {r: hop(out[r - 1], 1, r) for r in (1, 3, 2)}
-    near = near_sum(keep, got[1], got[3])
-    part = call(add_kernel, arr(shard, BF), None, (near, got[2]), (size, 3 * size))
-    got = {r: hop(part, 2, r) for r in (1, 3, 2)}
-    return near_sum(part, got[1], got[3]), got[2]
+        (far, sent[1], sent[3]),
+        (2 * size, 10 * size),
+    )
+    got = [hop(x, 1, r + 1) for r, x in enumerate(out)]
+    part = call(add_kernel, arr(shard, BF), None, (grown(keep, got[:2]), got[2]), (size, 3 * size))
+    got = ring_parts(part, 2)
+    return grown(part, got[:2]), got[2]
 
 
 def first_totals(place, weights, keys, values, rates, factor, tile=256):
@@ -264,13 +278,12 @@
     tokens, width = keys.shape
     lines = width // (SIDE * SIDE)
     block = (SIDE, 3, lines, width)
-    units = 2 * SIDE * lines
-    keys, values, rates, b0, b2, start, g1, g3 = call(
+    units = SIDE * lines
+    keys, values, rates, b0, b1, b3, start, g2 = call(
         functools.partial(first_kernel, factor, tile),
         [arr(keys.shape, BF), arr(values.shape, BF), arr(rates.shape, F32)]
-        + [arr(block, BF)] * 2
-        + [arr(block[1:], F32)]
-        + [arr(block, BF)] * 2,
+        + [arr(block, BF)] * 3
+        + [arr(block[1:], F32), arr(block, BF)],
         [SMEM] + [HBM] * 4,
         (place, *(pltpu.with_memory_space_constraint(x, pltpu.HBM) for x in sources)),
         (12 * tokens * width * units, 4 * tokens * width),
@@ -279,53 +292,49 @@
             pltpu.VMEM((3, SIDE * SIDE, lines, width), BF),
             pltpu.VMEM((SIDE, lines, width), F32),
             pltpu.VMEM(block, BF),
-            pltpu.VMEM(block, BF),
             pltpu.VMEM((2 * units, tokens), BF),
             pltpu.VMEM((units, tokens), BF),
-            pltpu.SemaphoreType.DMA((4,)),
+            pltpu.SemaphoreType.DMA((4, 4)),
         ],
         limit=32 << 20,
     )
-    sent = {1: hop(g1, 0, 1), 3: hop(g3, 0, 3)}
-    (g2,) = gradient_blocks([b2], keys, values, rates, factor, BF)
-    sent[2] = hop(g2, 0, 2)
+    sent = {2: hop(g2, 0, 2)}
+    g1, g3 = gradient_blocks([b1, b3], keys, values, rates, factor, BF)
+    sent[1], sent[3] = hop(g1, 0, 1), hop(g3, 0, 3)
     (own,) = gradient_blocks([b0], keys, values, rates, factor, F32)
     return start, (keys, values, rates), combined(own, sent)
 
 
 def gathered(shard):
-    got = {r: hop(shard, 1, -r) for r in (1, 3, 2)}
+    parts = ring_parts(shard, 1)
     block = arr((SIDE, *shard.shape), BF)
-    size = shard.size
-    joined = call(join_kernel, block, None, (shard, got[1], got[3]), (0, 12 * size))
-    return call(
-        join_last_kernel, block, None, (joined, got[2]), (0, 4 * size), aliases={0: 0}
-    )
+    cost = (0, 4 * shard.size)
+    joined = call(join_first_kernel, block, None, (shard, parts[0]), cost)
+    for r in (2, 3):
+        kernel = functools.partial(join_kernel, r)
+        joined = call(kernel, block, None, (joined, parts[r - 1]), cost, aliases={0: 0})
+    return joined
 
 
 def second_totals(shard, keys, values, rates, factor):
     block = gathered(shard)
-    b1, b3 = hop(block, 0, -1), hop(block, 0, -3)
+    b2, b1, b3 = hop(block, 0, -2), hop(block, 0, -1), hop(block, 0, -3)
     (own,) = gradient_blocks([block], keys, values, rates, factor, F32)
-    own, keys, block = in_turn(own, keys, block)
-    b2 = hop(block, 0, -2)
-    sent = {}
+    own, keys = in_turn(own, keys)
+    (g2,) = gradient_blocks([b2], keys, values, rates, factor, BF)
+    sent = {2: hop(g2, 0, 2)}
+    g2, keys = in_turn(g2, keys)
     g1, g3 = gradient_blocks([b1, b3], keys, values, rates, factor, BF)
     sent[1], sent[3] = hop(g1, 0, 1), hop(g3, 0, 3)
-    g1, keys = in_turn(g1, keys)
-    (g2,) = gradient_blocks([b2], keys, values, rates, factor, BF)
-    sent[2] = hop(g2, 0, 2)
     return combined(own, sent)
 
 
 def applied(shard, queries, gain):
     block = gathered(shard)
-    b1, b3 = hop(block, 0, -1), hop(block, 0, -3)
+    b2, b1, b3 = hop(block, 0, -2), hop(block, 0, -1), hop(block, 0, -3)
     result = apply_blocks([block], queries, None, None)
-    result, block = in_turn(result, block)
-    b2 = hop(block, 0, -2)
-    result = apply_blocks([b1, b3], queries, result, None)
-    return apply_blocks([b2], queries, result, gain)
+    result = apply_blocks([b2], queries, result, None)
+    return apply_blocks([b1, b3], queries, result, gain)
 
 
 def shards(queries, key_tokens, value_tokens, learn_rates, fast_init, out_gain):

time: 139 us -> 130 us (0.935)
  waiting for transfers between devices: 62.1 us -> 56 us
    ppermute x30, waiting for transfers between devices: 61.2 us -> 55 us  [hop(): return lax.ppermute(x, AXES, hop_pairs(level, step % SIDE))]
    pallas_call x26 -> x32, Pallas kernels: 29.4 us -> 28.1 us  [call(): pl.pallas_call(kernel, out_shape=outs, in_specs=specs or [VMEM] * len(arg...]
  transfers between devices with their start and end apart: 31 -> 31, of which waited for: 24 -> 25; matrix products, arithmetic and copies ran while one was open for 0% -> 0% of each run, Pallas kernels for 13% -> 14%
where the time goes in v4:
time: 130 us
  waiting for transfers between devices  56 us (43%)
  starting transfers between devices  45.6 us (35%)
  Pallas kernels  28.1 us (22%)
    ppermute x30, waiting for transfers between devices, hop(): return lax.ppermute(x, AXES, hop_pairs(level, step % SIDE))  55 us
    ppermute x30, starting transfers between devices, hop(): return lax.ppermute(x, AXES, hop_pairs(level, step % SIDE))  44.3 us
    pallas_call x32, Pallas kernels, call(): pl.pallas_call(kernel, out_shape=outs, in_specs=specs or [VMEM] * len(arg...  28.1 us
  transfers between devices with their start and end apart: 31, of which 25 were waited for; matrix products, arithmetic and copies ran while one was open for 0% of the time, Pallas kernels for 14%

profile of v4, /device:TPU:0, one launch (start us, length us, event | category | flops | bytes accessed | tf_op | source)
XLA Modules:
  0.0 130.2 jit_solution(10767960231329317110)
XLA Ops:
  0.2 6.1 %shard_map.64 = (bf16[2048,512]{1,0:T(8,128)(2,1)S(1)}, bf16[2048,512]{1,0:T(8,128)(2,1)S(1)}, f32[1,2048]{1,0:T(1,128)S(1)}, bf16[4,3,32,512]{3,2,1,0:T(8,128)(...) custom-call(s32[16]{0:T(128)S(1)} %fusion.place, ...), custom_call_target="tpu_custom_call" | custom-call | flops 1610612736 | bytes 4194304 | tf_op jit(solution)/shard_map/pallas_call | solution.py:49
  6.3 3.2 %collective-permute-start = (bf16[4,3,32,512]{3,2,1,0:T(8,128)(2,1)S(1)}, bf16[4,3,32,512]{3,2,1,0:T(8,128)(2,1)S(1)}, u32[]{:S(2)}, u32[]{:S(2)}) collective-permute-start(bf16[4,3,32,512]{3,2,1,0:T(8,128)(2,1)S(1)} %get-tuple-element.37), channel_id=1, source_target_pairs={{0,2},{1,3},{2,0},{3,1},{4,6},{5,7},{6,4},{7,5},{8,10},{9,11},{10,... | collective-permute-start | bytes 1179656 | tf_op jit(solution)/shard_map/ppermute | solution.py:40
  9.5 3.7 %shard_map.67 = (bf16[4,3,32,512]{3,2,1,0:T(8,128)(2,1)S(1)}, bf16[4,3,32,512]{3,2,1,0:T(8,128)(2,1)S(1)}) custom-call(bf16[4,3,32,512]{3,2,1,0:T(8,128)(2,1)S(1)} %get-tuple-element.38.refs_0_, bf16[4,3,32,512]{3,2,1,0:T(8,128)(2,1)S(1)} %get-tuple-element.39.refs_1_, bf16[2048,512]{1,0:T(8,128)(2,1)S(1)} %get-tuple-element.50.refs_1_.refs_2_, ...), custom_call_target="tpu_custom_call" | custom-call | flops 3221225472 | bytes 4194304 | tf_op jit(solution)/shard_map/pallas_call | solution.py:49
  13.2 0.7 collective-permute-start.1
  13.9 2.6 %collective-permute-start.2 = (bf16[4,3,32,512]{3,2,1,0:T(8,128)(2,1)S(1)}, bf16[4,3,32,512]{3,2,1,0:T(8,128)(2,1)S(1)}, u32[]{:S(2)}, u32[]{:S(2)}) collective-permute-start(bf16[4,3,32,512]{3,2,1,0:T(8,128)(2,1)S(1)} %get-tuple-element.41), channel_id=1, source_target_pairs={{0,3},{1,0},{2,1},{3,2},{4,7},{5,4},{6,5},{7,6},{8,11},{9,8},{10,9... | collective-permute-start | bytes 1179656 | tf_op jit(solution)/shard_map/ppermute | solution.py:40
  16.5 2.3 %shard_map.65.own = f32[4,3,32,512]{3,2,1,0:T(8,128)S(1)} custom-call(bf16[4,3,32,512]{3,2,1,0:T(8,128)(2,1)S(1)} %get-tuple-element.33.refs_0_, bf16[2048,512]{1,0:T(8,128)(2,1)S(1)} %get-tuple-element.50.refs_1_.refs_2_, bf16[2048,512]{1,0:T(8,128)(2,1)S(1)} %get-tuple-element.35.refs_2_.refs_3_, f32[1,2048]{1,0:T(1,128)S(1)} %get-tuple-element.36.refs_3_.refs_4_), custom_call_target="tpu_custom_call" | custom-call | flops 1610612736 | bytes 4194304 | tf_op jit(solution)/shard_map/pallas_call | solution.py:49
  18.9 3.4 %collective-permute-done.1.r1 = bf16[4,3,32,512]{3,2,1,0:T(8,128)(2,1)S(1)} collective-permute-done((bf16[4,3,32,512]{3,2,1,0:T(8,128)(2,1)S(1)}, bf16[4,3,32,512]{3,2,1,0:T(8,128)(2,1)S(1)}, u32[]{:S(2)}, u32[]{:S(2)}) %collective-permute-start.1) | collective-permute-done | bytes 393248 | tf_op jit(solution)/shard_map/ppermute | solution.py:40
  22.3 0.1 shard_map.68
  22.4 1.7 %collective-permute-start.3 = (bf16[3,32,512]{2,1,0:T(8,128)(2,1)S(1)}, bf16[3,32,512]{2,1,0:T(8,128)(2,1)S(1)}, u32[]{:S(2)}, u32[]{:S(2)}) collective-permute-start(bf16[3,32,512]{2,1,0:T(8,128)(2,1)S(1)} %get-tuple-element.43), channel_id=1, source_target_pairs={{0,4},{1,5},{2,6},{3,7},{4,8},{5,9},{6,10},{7,11},{8,12},{9,13},{1... | collective-permute-start | bytes 294920 | tf_op jit(solution)/shard_map/ppermute | solution.py:40
  24.1 2.9 %collective-permute-start.4 = (bf16[3,32,512]{2,1,0:T(8,128)(2,1)S(1)}, bf16[3,32,512]{2,1,0:T(8,128)(2,1)S(1)}, u32[]{:S(2)}, u32[]{:S(2)}) collective-permute-start(bf16[3,32,512]{2,1,0:T(8,128)(2,1)S(1)} %get-tuple-element.44), channel_id=1, source_target_pairs={{0,8},{1,9},{2,10},{3,11},{4,12},{5,13},{6,14},{7,15},{8,0},{9,1},... | collective-permute-start | bytes 294920 | tf_op jit(solution)/shard_map/ppermute | solution.py:40
  27.0 1.3 %collective-permute-start.5 = (bf16[3,32,512]{2,1,0:T(8,128)(2,1)S(1)}, bf16[3,32,512]{2,1,0:T(8,128)(2,1)S(1)}, u32[]{:S(2)}, u32[]{:S(2)}) collective-permute-start(bf16[3,32,512]{2,1,0:T(8,128)(2,1)S(1)} %get-tuple-element.45), channel_id=1, source_target_pairs={{0,12},{1,13},{2,14},{3,15},{4,0},{5,1},{6,2},{7,3},{8,4},{9,5},{1... | collective-permute-start | bytes 294920 | tf_op jit(solution)/shard_map/ppermute | solution.py:40
  28.4 2.3 %collective-permute-done.4.part = bf16[3,32,512]{2,1,0:T(8,128)(2,1)S(1)} collective-permute-done((bf16[3,32,512]{2,1,0:T(8,128)(2,1)S(1)}, bf16[3,32,512]{2,1,0:T(8,128)(2,1)S(1)}, u32[]{:S(2)}, u32[]{:S(2)}) %collective-permute-start.4) | collective-permute-done | bytes 98336 | tf_op jit(solution)/shard_map/ppermute | solution.py:40
  30.6 1.0 collective-permute-done.5.part
  31.6 4.1 %collective-permute-start.6 = (bf16[3,32,512]{2,1,0:T(8,128)(2,1)S(1)}, bf16[3,32,512]{2,1,0:T(8,128)(2,1)S(1)}, u32[]{:S(2)}, u32[]{:S(2)}) collective-permute-start(bf16[3,32,512]{2,1,0:T(8,128)(2,1)S(1)} %shard_map.71.own), channel_id=1, source_target_pairs={{0,48},{1,49},{2,50},{3,51},{4,52},{5,53},{6,54},{7,55},{8,56},{9,... | collective-permute-start | bytes 294920 | tf_op jit(solution)/shard_map/ppermute | solution.py:40
  35.7 1.3 collective-permute-start.8
  37.0 2.0 %collective-permute-done.6.part = bf16[3,32,512]{2,1,0:T(8,128)(2,1)S(1)} collective-permute-done((bf16[3,32,512]{2,1,0:T(8,128)(2,1)S(1)}, bf16[3,32,512]{2,1,0:T(8,128)(2,1)S(1)}, u32[]{:S(2)}, u32[]{:S(2)}) %collective-permute-start.6) | collective-permute-done | bytes 98336 | tf_op jit(solution)/shard_map/ppermute | solution.py:40
  39.0 3.0 %collective-permute-done.7.part = bf16[3,32,512]{2,1,0:T(8,128)(2,1)S(1)} collective-permute-done((bf16[3,32,512]{2,1,0:T(8,128)(2,1)S(1)}, bf16[3,32,512]{2,1,0:T(8,128)(2,1)S(1)}, u32[]{:S(2)}, u32[]{:S(2)}) %collective-permute-start.7) | collective-permute-done | bytes 98336 | tf_op jit(solution)/shard_map/ppermute | solution.py:40
  42.0 0.6 collective-permute-done.8.part
  42.6 2.6 %collective-permute-start.9 = (bf16[3,32,512]{2,1,0:T(8,128)(2,1)S(1)}, bf16[3,32,512]{2,1,0:T(8,128)(2,1)S(1)}, u32[]{:S(2)}, u32[]{:S(2)}) collective-permute-start(bf16[3,32,512]{2,1,0:T(8,128)(2,1)S(1)} %get-tuple-element.47.own), channel_id=1, source_target_pairs={{0,12},{1,13},{2,14},{3,15},{4,0},{5,1},{6,2},{7,3},{8,4},{9,5},{1... | collective-permute-start | bytes 294920 | tf_op jit(solution)/shard_map/ppermute | solution.py:40
  45.3 0.2 collective-permute-start.10
  45.4 0.8 collective-permute-start.11
  46.2 2.3 %collective-permute-done.9.part = bf16[3,32,512]{2,1,0:T(8,128)(2,1)S(1)} collective-permute-done((bf16[3,32,512]{2,1,0:T(8,128)(2,1)S(1)}, bf16[3,32,512]{2,1,0:T(8,128)(2,1)S(1)}, u32[]{:S(2)}, u32[]{:S(2)}) %collective-permute-start.9) | collective-permute-done | bytes 98336 | tf_op jit(solution)/shard_map/ppermute | solution.py:40
  48.5 3.7 %collective-permute-done.10.part = bf16[3,32,512]{2,1,0:T(8,128)(2,1)S(1)} collective-permute-done((bf16[3,32,512]{2,1,0:T(8,128)(2,1)S(1)}, bf16[3,32,512]{2,1,0:T(8,128)(2,1)S(1)}, u32[]{:S(2)}, u32[]{:S(2)}) %collective-permute-start.10) | collective-permute-done | bytes 98336 | tf_op jit(solution)/shard_map/ppermute | solution.py:40
  52.2 4.7 %collective-permute-done.11.part = bf16[3,32,512]{2,1,0:T(8,128)(2,1)S(1)} collective-permute-done((bf16[3,32,512]{2,1,0:T(8,128)(2,1)S(1)}, bf16[3,32,512]{2,1,0:T(8,128)(2,1)S(1)}, u32[]{:S(2)}, u32[]{:S(2)}) %collective-permute-start.11) | collective-permute-done | bytes 98336 | tf_op jit(solution)/shard_map/ppermute | solution.py:40
  56.9 1.9 %collective-permute-start.12 = (bf16[4,3,32,512]{3,2,1,0:T(8,128)(2,1)S(1)}, bf16[4,3,32,512]{3,2,1,0:T(8,128)(2,1)S(1)}, u32[]{:S(2)}, u32[]{:S(2)}) collective-permute-start(bf16[4,3,32,512]{3,2,1,0:T(8,128)(2,1)S(1)} %shard_map.77.refs_0_), channel_id=1, source_target_pairs={{0,2},{1,3},{2,0},{3,1},{4,6},{5,7},{6,4},{7,5},{8,10},{9,11},{10,... | collective-permute-start | bytes 1179656 | tf_op jit(solution)/shard_map/ppermute | solution.py:40
  58.8 0.3 collective-permute-start.14
  59.2 1.7 %collective-permute-start.15 = (bf16[4,3,32,512]{3,2,1,0:T(8,128)(2,1)S(1)}, bf16[4,3,32,512]{3,2,1,0:T(8,128)(2,1)S(1)}, u32[]{:S(2)}, u32[]{:S(2)}) collective-permute-start(bf16[4,3,32,512]{3,2,1,0:T(8,128)(2,1)S(1)} %shard_map.77.refs_0_), channel_id=1, source_target_pairs={{0,1},{1,2},{2,3},{3,0},{4,5},{5,6},{6,7},{7,4},{8,9},{9,10},{10,1... | collective-permute-start | bytes 1179656 | tf_op jit(solution)/shard_map/ppermute | solution.py:40
  60.9 2.3 %shard_map.78.own = f32[4,3,32,512]{3,2,1,0:T(8,128)S(1)} custom-call(bf16[4,3,32,512]{3,2,1,0:T(8,128)(2,1)S(1)} %shard_map.77.refs_0_, bf16[2048,512]{1,0:T(8,128)(2,1)S(1)} %get-tuple-element.50.refs_1_.refs_2_, bf16[2048,512]{1,0:T(8,128)(2,1)S(1)} %get-tuple-element.35.refs_2_.refs_3_, f32[1,2048]{1,0:T(1,128)S(1)} %get-tuple-element.36.refs_3_.refs_4_), custom_call_target="tpu_custom_call" | custom-call | flops 1610612736 | bytes 4194304 | tf_op jit(solution)/shard_map/pallas_call | solution.py:49
  63.2 3.1 %collective-permute-done.12.refs_0_ = bf16[4,3,32,512]{3,2,1,0:T(8,128)(2,1)S(1)} collective-permute-done((bf16[4,3,32,512]{3,2,1,0:T(8,128)(2,1)S(1)}, bf16[4,3,32,512]{3,2,1,0:T(8,128)(2,1)S(1)}, u32[]{:S(2)}, u32[]{:S(2)}) %collective-permute-start.12) | collective-permute-done | bytes 393248 | tf_op jit(solution)/shard_map/ppermute | solution.py:40
  66.3 2.3 %shard_map.79 = bf16[4,3,32,512]{3,2,1,0:T(8,128)(2,1)S(1)} custom-call(bf16[4,3,32,512]{3,2,1,0:T(8,128)(2,1)S(1)} %collective-permute-done.12.refs_0_, bf16[2048,512]{1,0:T(8,128)(2,1)S(1)} %get-tuple-element.50.refs_1_.refs_2_, bf16[2048,512]{1,0:T(8,128)(2,1)S(1)} %get-tuple-element.35.refs_2_.refs_3_, f32[1,2048]{1,0:T(1,128)S(1)} %get-tuple-element.36.refs_3_.refs_4_), custom_call_target="tpu_custom_call" | custom-call | flops 1610612736 | bytes 4194304 | tf_op jit(solution)/shard_map/pallas_call | solution.py:49
  68.7 2.0 %collective-permute-start.13 = (bf16[4,3,32,512]{3,2,1,0:T(8,128)(2,1)S(1)}, bf16[4,3,32,512]{3,2,1,0:T(8,128)(2,1)S(1)}, u32[]{:S(2)}, u32[]{:S(2)}) collective-permute-start(bf16[4,3,32,512]{3,2,1,0:T(8,128)(2,1)S(1)} %shard_map.79), channel_id=1, source_target_pairs={{0,2},{1,3},{2,0},{3,1},{4,6},{5,7},{6,4},{7,5},{8,10},{9,11},{10,... | collective-permute-start | bytes 1179656 | tf_op jit(solution)/shard_map/ppermute | solution.py:40
  70.6 3.7 %shard_map.81 = (bf16[4,3,32,512]{3,2,1,0:T(8,128)(2,1)S(1)}, bf16[4,3,32,512]{3,2,1,0:T(8,128)(2,1)S(1)}) custom-call(bf16[4,3,32,512]{3,2,1,0:T(8,128)(2,1)S(1)} %collective-permute-done.14.refs_0_, bf16[4,3,32,512]{3,2,1,0:T(8,128)(2,1)S(1)} %collective-permute-done.15.refs_1_, bf16[2048,512]{1,0:T(8,128)(2,1)S(1)} %get-tuple-element.50.refs_1_.refs_2_, ...), custom_call_target="tpu_custom_call" | custom-call | flops 3221225472 | bytes 4194304 | tf_op jit(solution)/shard_map/pallas_call | solution.py:49
  74.4 0.9 collective-permute-start.16
  75.2 2.4 %collective-permute-start.17 = (bf16[4,3,32,512]{3,2,1,0:T(8,128)(2,1)S(1)}, bf16[4,3,32,512]{3,2,1,0:T(8,128)(2,1)S(1)}, u32[]{:S(2)}, u32[]{:S(2)}) collective-permute-start(bf16[4,3,32,512]{3,2,1,0:T(8,128)(2,1)S(1)} %get-tuple-element.52), channel_id=1, source_target_pairs={{0,3},{1,0},{2,1},{3,2},{4,7},{5,4},{6,5},{7,6},{8,11},{9,8},{10,9... | collective-permute-start | bytes 1179656 | tf_op jit(solution)/shard_map/ppermute | solution.py:40
  77.7 2.6 %collective-permute-done.13.r2 = bf16[4,3,32,512]{3,2,1,0:T(8,128)(2,1)S(1)} collective-permute-done((bf16[4,3,32,512]{3,2,1,0:T(8,128)(2,1)S(1)}, bf16[4,3,32,512]{3,2,1,0:T(8,128)(2,1)S(1)}, u32[]{:S(2)}, u32[]{:S(2)}) %collective-permute-start.13) | collective-permute-done | bytes 393248 | tf_op jit(solution)/shard_map/ppermute | solution.py:40
  80.3 4.3 %collective-permute-done.16.r1 = bf16[4,3,32,512]{3,2,1,0:T(8,128)(2,1)S(1)} collective-permute-done((bf16[4,3,32,512]{3,2,1,0:T(8,128)(2,1)S(1)}, bf16[4,3,32,512]{3,2,1,0:T(8,128)(2,1)S(1)}, u32[]{:S(2)}, u32[]{:S(2)}) %collective-permute-start.16) | collective-permute-done | bytes 393248 | tf_op jit(solution)/shard_map/ppermute | solution.py:40
  84.9 3.1 %collective-permute-start.19 = (bf16[3,32,512]{2,1,0:T(8,128)(2,1)S(1)}, bf16[3,32,512]{2,1,0:T(8,128)(2,1)S(1)}, u32[]{:S(2)}, u32[]{:S(2)}) collective-permute-start(bf16[3,32,512]{2,1,0:T(8,128)(2,1)S(1)} %get-tuple-element.55), channel_id=1, source_target_pairs={{0,8},{1,9},{2,10},{3,11},{4,12},{5,13},{6,14},{7,15},{8,0},{9,1},... | collective-permute-start | bytes 294920 | tf_op jit(solution)/shard_map/ppermute | solution.py:40
  88.0 0.4 collective-permute-start.20
  88.4 2.3 %collective-permute-done.18.part = bf16[3,32,512]{2,1,0:T(8,128)(2,1)S(1)} collective-permute-done((bf16[3,32,512]{2,1,0:T(8,128)(2,1)S(1)}, bf16[3,32,512]{2,1,0:T(8,128)(2,1)S(1)}, u32[]{:S(2)}, u32[]{:S(2)}) %collective-permute-start.18) | collective-permute-done | bytes 98336 | tf_op jit(solution)/shard_map/ppermute | solution.py:40
  90.7 1.0 collective-permute-done.19.part
  91.8 0.9 collective-permute-done.20.part
  92.7 1.0 collective-permute-start.21
  93.6 0.7 collective-permute-start.22
  94.3 1.3 %collective-permute-start.23 = (bf16[3,32,512]{2,1,0:T(8,128)(2,1)S(1)}, bf16[3,32,512]{2,1,0:T(8,128)(2,1)S(1)}, u32[]{:S(2)}, u32[]{:S(2)}) collective-permute-start(bf16[3,32,512]{2,1,0:T(8,128)(2,1)S(1)} %shard_map.85.own), channel_id=1, source_target_pairs={{0,16},{1,17},{2,18},{3,19},{4,20},{5,21},{6,22},{7,23},{8,24},{9,... | collective-permute-start | bytes 294920 | tf_op jit(solution)/shard_map/ppermute | solution.py:40
  95.6 1.7 %collective-permute-done.21.part = bf16[3,32,512]{2,1,0:T(8,128)(2,1)S(1)} collective-permute-done((bf16[3,32,512]{2,1,0:T(8,128)(2,1)S(1)}, bf16[3,32,512]{2,1,0:T(8,128)(2,1)S(1)}, u32[]{:S(2)}, u32[]{:S(2)}) %collective-permute-start.21) | collective-permute-done | bytes 98336 | tf_op jit(solution)/shard_map/ppermute | solution.py:40
  97.4 2.4 %collective-permute-done.22.part = bf16[3,32,512]{2,1,0:T(8,128)(2,1)S(1)} collective-permute-done((bf16[3,32,512]{2,1,0:T(8,128)(2,1)S(1)}, bf16[3,32,512]{2,1,0:T(8,128)(2,1)S(1)}, u32[]{:S(2)}, u32[]{:S(2)}) %collective-permute-start.22) | collective-permute-done | bytes 98336 | tf_op jit(solution)/shard_map/ppermute | solution.py:40
  99.9 1.0 collective-permute-done.23.part
  100.9 1.3 collective-permute-start.24
  102.2 0.9 collective-permute-done.24.earlier
  103.1 2.7 %collective-permute-start.25 = (bf16[3,32,512]{2,1,0:T(8,128)(2,1)S(1)}, bf16[3,32,512]{2,1,0:T(8,128)(2,1)S(1)}, u32[]{:S(2)}, u32[]{:S(2)}) collective-permute-start(bf16[3,32,512]{2,1,0:T(8,128)(2,1)S(1)} %shard_map.89.own), channel_id=1, source_target_pairs={{0,12},{1,13},{2,14},{3,15},{4,0},{5,1},{6,2},{7,3},{8,4},{9,5},{1... | collective-permute-start | bytes 294920 | tf_op jit(solution)/shard_map/ppermute | solution.py:40
  105.8 0.4 collective-permute-start.26
  106.2 0.5 collective-permute-start.27
  106.7 2.3 %collective-permute-done.25.part = bf16[3,32,512]{2,1,0:T(8,128)(2,1)S(1)} collective-permute-done((bf16[3,32,512]{2,1,0:T(8,128)(2,1)S(1)}, bf16[3,32,512]{2,1,0:T(8,128)(2,1)S(1)}, u32[]{:S(2)}, u32[]{:S(2)}) %collective-permute-start.25) | collective-permute-done | bytes 98336 | tf_op jit(solution)/shard_map/ppermute | solution.py:40
  109.0 3.0 %collective-permute-done.26.part = bf16[3,32,512]{2,1,0:T(8,128)(2,1)S(1)} collective-permute-done((bf16[3,32,512]{2,1,0:T(8,128)(2,1)S(1)}, bf16[3,32,512]{2,1,0:T(8,128)(2,1)S(1)}, u32[]{:S(2)}, u32[]{:S(2)}) %collective-permute-start.26) | collective-permute-done | bytes 98336 | tf_op jit(solution)/shard_map/ppermute | solution.py:40
  112.0 0.9 collective-permute-done.27.part
  113.0 1.6 %collective-permute-start.30 = (bf16[4,3,32,512]{3,2,1,0:T(8,128)(2,1)S(1)}, bf16[4,3,32,512]{3,2,1,0:T(8,128)(2,1)S(1)}, u32[]{:S(2)}, u32[]{:S(2)}) collective-permute-start(bf16[4,3,32,512]{3,2,1,0:T(8,128)(2,1)S(1)} %shard_map.92.refs_0_), channel_id=1, source_target_pairs={{0,2},{1,3},{2,0},{3,1},{4,6},{5,7},{6,4},{7,5},{8,10},{9,11},{10,... | collective-permute-start | bytes 1179656 | tf_op jit(solution)/shard_map/ppermute | solution.py:40
  114.5 1.4 %collective-permute-start.28 = (bf16[4,3,32,512]{3,2,1,0:T(8,128)(2,1)S(1)}, bf16[4,3,32,512]{3,2,1,0:T(8,128)(2,1)S(1)}, u32[]{:S(2)}, u32[]{:S(2)}) collective-permute-start(bf16[4,3,32,512]{3,2,1,0:T(8,128)(2,1)S(1)} %shard_map.92.refs_0_), channel_id=1, source_target_pairs={{0,3},{1,0},{2,1},{3,2},{4,7},{5,4},{6,5},{7,6},{8,11},{9,8},{10,9... | collective-permute-start | bytes 1179656 | tf_op jit(solution)/shard_map/ppermute | solution.py:40
  115.9 0.7 collective-permute-start.29
  116.6 1.6 %shard_map.93.refs_2_ = f32[2048,512]{1,0:T(8,128)S(1)} custom-call(bf16[4,3,32,512]{3,2,1,0:T(8,128)(2,1)S(1)} %shard_map.92.refs_0_, bf16[2048,512]{1,0:T(8,128)(2,1)S(1)} %copy-done), custom_call_target="tpu_custom_call" | custom-call | flops 805306368 | bytes 6291456 | tf_op jit(solution)/shard_map/pallas_call | solution.py:49
  118.2 4.2 %collective-permute-done.30.refs_0_ = bf16[4,3,32,512]{3,2,1,0:T(8,128)(2,1)S(1)} collective-permute-done((bf16[4,3,32,512]{3,2,1,0:T(8,128)(2,1)S(1)}, bf16[4,3,32,512]{3,2,1,0:T(8,128)(2,1)S(1)}, u32[]{:S(2)}, u32[]{:S(2)}) %collective-permute-start.30) | collective-permute-done | bytes 393248 | tf_op jit(solution)/shard_map/ppermute | solution.py:40
  122.4 1.6 %shard_map.94.refs_4_ = f32[2048,512]{1,0:T(8,128)S(1)} custom-call(bf16[4,3,32,512]{3,2,1,0:T(8,128)(2,1)S(1)} %collective-permute-done.30.refs_0_, bf16[2048,512]{1,0:T(8,128)(2,1)S(1)} %copy-done, f32[2048,512]{1,0:T(8,128)S(1)} %shard_map.93.refs_2_), custom_call_target="tpu_custom_call" | custom-call | flops 805306368 | bytes 6291456 | tf_op jit(solution)/shard_map/pallas_call | solution.py:49
  124.1 2.0 %collective-permute-done.28.refs_0_ = bf16[4,3,32,512]{3,2,1,0:T(8,128)(2,1)S(1)} collective-permute-done((bf16[4,3,32,512]{3,2,1,0:T(8,128)(2,1)S(1)}, bf16[4,3,32,512]{3,2,1,0:T(8,128)(2,1)S(1)}, u32[]{:S(2)}, u32[]{:S(2)}) %collective-permute-start.28) | collective-permute-done | bytes 393248 | tf_op jit(solution)/shard_map/ppermute | solution.py:40
  126.1 0.4 collective-permute-done.29.refs_1_
  126.5 3.5 %shard_map.95 = bf16[2048,512]{1,0:T(8,128)(2,1)} custom-call(bf16[4,3,32,512]{3,2,1,0:T(8,128)(2,1)S(1)} %collective-permute-done.28.refs_0_, bf16[4,3,32,512]{3,2,1,0:T(8,128)(2,1)S(1)} %collective-permute-done.29.refs_1_, bf16[2048,512]{1,0:T(8,128)(2,1)S(1)} %copy-done, f32[1,512]{1,0:T(1,128)S(1)} %bitcast.2, f32[2048,512]{1,0:T(8,128)S(1)} %shard_map.94.refs_4_), custom_call_target="tpu_custom_call" | custom-call | flops 1610612736 | bytes 6291456 | tf_op jit(solution)/shard_map/pallas_call | solution.py:49
  (38 shorter events, 0.9 us)
Async XLA Ops:
  6.3 12.5 %collective-permute-start = (bf16[4,3,32,512]{3,2,1,0:T(8,128)(2,1)S(1)}, bf16[4,3,32,512]{3,2,1,0:T(8,128)(2,1)S(1)}, u32[]{:S(2)}, u32[]{:S(2)}) collective-permute-start(bf16[4,3,32,512]{3,2,1,0:T(8,128)(2,1)S(1)} %get-tuple-element.37), channel_id=1, source_target_pairs={{0,2},{1,3},{2,0},{3,1},{4,6},{5,7},{6,4},{7,5},{8,10},{9,11},{10,... | collective-permute-start | bytes 1179656 | tf_op jit(solution)/shard_map/ppermute | solution.py:40
  13.2 9.1 %collective-permute-start.1 = (bf16[4,3,32,512]{3,2,1,0:T(8,128)(2,1)S(1)}, bf16[4,3,32,512]{3,2,1,0:T(8,128)(2,1)S(1)}, u32[]{:S(2)}, u32[]{:S(2)}) collective-permute-start(bf16[4,3,32,512]{3,2,1,0:T(8,128)(2,1)S(1)} %get-tuple-element.40), channel_id=1, source_target_pairs={{0,1},{1,2},{2,3},{3,0},{4,5},{5,6},{6,7},{7,4},{8,9},{9,10},{10,1... | collective-permute-start | bytes 1179656 | tf_op jit(solution)/shard_map/ppermute | solution.py:40
  13.9 8.4 %collective-permute-start.2 = (bf16[4,3,32,512]{3,2,1,0:T(8,128)(2,1)S(1)}, bf16[4,3,32,512]{3,2,1,0:T(8,128)(2,1)S(1)}, u32[]{:S(2)}, u32[]{:S(2)}) collective-permute-start(bf16[4,3,32,512]{3,2,1,0:T(8,128)(2,1)S(1)} %get-tuple-element.41), channel_id=1, source_target_pairs={{0,3},{1,0},{2,1},{3,2},{4,7},{5,4},{6,5},{7,6},{8,11},{9,8},{10,9... | collective-permute-start | bytes 1179656 | tf_op jit(solution)/shard_map/ppermute | solution.py:40
  22.4 5.9 %collective-permute-start.3 = (bf16[3,32,512]{2,1,0:T(8,128)(2,1)S(1)}, bf16[3,32,512]{2,1,0:T(8,128)(2,1)S(1)}, u32[]{:S(2)}, u32[]{:S(2)}) collective-permute-start(bf16[3,32,512]{2,1,0:T(8,128)(2,1)S(1)} %get-tuple-element.43), channel_id=1, source_target_pairs={{0,4},{1,5},{2,6},{3,7},{4,8},{5,9},{6,10},{7,11},{8,12},{9,13},{1... | collective-permute-start | bytes 294920 | tf_op jit(solution)/shard_map/ppermute | solution.py:40
  24.1 6.5 %collective-permute-start.4 = (bf16[3,32,512]{2,1,0:T(8,128)(2,1)S(1)}, bf16[3,32,512]{2,1,0:T(8,128)(2,1)S(1)}, u32[]{:S(2)}, u32[]{:S(2)}) collective-permute-start(bf16[3,32,512]{2,1,0:T(8,128)(2,1)S(1)} %get-tuple-element.44), channel_id=1, source_target_pairs={{0,8},{1,9},{2,10},{3,11},{4,12},{5,13},{6,14},{7,15},{8,0},{9,1},... | collective-permute-start | bytes 294920 | tf_op jit(solution)/shard_map/ppermute | solution.py:40
  27.0 4.6 %collective-permute-start.5 = (bf16[3,32,512]{2,1,0:T(8,128)(2,1)S(1)}, bf16[3,32,512]{2,1,0:T(8,128)(2,1)S(1)}, u32[]{:S(2)}, u32[]{:S(2)}) collective-permute-start(bf16[3,32,512]{2,1,0:T(8,128)(2,1)S(1)} %get-tuple-element.45), channel_id=1, source_target_pairs={{0,12},{1,13},{2,14},{3,15},{4,0},{5,1},{6,2},{7,3},{8,4},{9,5},{1... | collective-permute-start | bytes 294920 | tf_op jit(solution)/shard_map/ppermute | solution.py:40
  31.6 7.3 %collective-permute-start.6 = (bf16[3,32,512]{2,1,0:T(8,128)(2,1)S(1)}, bf16[3,32,512]{2,1,0:T(8,128)(2,1)S(1)}, u32[]{:S(2)}, u32[]{:S(2)}) collective-permute-start(bf16[3,32,512]{2,1,0:T(8,128)(2,1)S(1)} %shard_map.71.own), channel_id=1, source_target_pairs={{0,48},{1,49},{2,50},{3,51},{4,52},{5,53},{6,54},{7,55},{8,56},{9,... | collective-permute-start | bytes 294920 | tf_op jit(solution)/shard_map/ppermute | solution.py:40
  35.7 6.2 %collective-permute-start.7 = (bf16[3,32,512]{2,1,0:T(8,128)(2,1)S(1)}, bf16[3,32,512]{2,1,0:T(8,128)(2,1)S(1)}, u32[]{:S(2)}, u32[]{:S(2)}) collective-permute-start(bf16[3,32,512]{2,1,0:T(8,128)(2,1)S(1)} %shard_map.71.own), channel_id=1, source_target_pairs={{0,32},{1,33},{2,34},{3,35},{4,36},{5,37},{6,38},{7,39},{8,40},{9,... | collective-permute-start | bytes 294920 | tf_op jit(solution)/shard_map/ppermute | solution.py:40
  35.7 6.9 %collective-permute-start.8 = (bf16[3,32,512]{2,1,0:T(8,128)(2,1)S(1)}, bf16[3,32,512]{2,1,0:T(8,128)(2,1)S(1)}, u32[]{:S(2)}, u32[]{:S(2)}) collective-permute-start(bf16[3,32,512]{2,1,0:T(8,128)(2,1)S(1)} %shard_map.71.own), channel_id=1, source_target_pairs={{0,16},{1,17},{2,18},{3,19},{4,20},{5,21},{6,22},{7,23},{8,24},{9,... | collective-permute-start | bytes 294920 | tf_op jit(solution)/shard_map/ppermute | solution.py:40
  42.6 5.8 %collective-permute-start.9 = (bf16[3,32,512]{2,1,0:T(8,128)(2,1)S(1)}, bf16[3,32,512]{2,1,0:T(8,128)(2,1)S(1)}, u32[]{:S(2)}, u32[]{:S(2)}) collective-permute-start(bf16[3,32,512]{2,1,0:T(8,128)(2,1)S(1)} %get-tuple-element.47.own), channel_id=1, source_target_pairs={{0,12},{1,13},{2,14},{3,15},{4,0},{5,1},{6,2},{7,3},{8,4},{9,5},{1... | collective-permute-start | bytes 294920 | tf_op jit(solution)/shard_map/ppermute | solution.py:40
  45.3 6.9 %collective-permute-start.10 = (bf16[3,32,512]{2,1,0:T(8,128)(2,1)S(1)}, bf16[3,32,512]{2,1,0:T(8,128)(2,1)S(1)}, u32[]{:S(2)}, u32[]{:S(2)}) collective-permute-start(bf16[3,32,512]{2,1,0:T(8,128)(2,1)S(1)} %get-tuple-element.47.own), channel_id=1, source_target_pairs={{0,8},{1,9},{2,10},{3,11},{4,12},{5,13},{6,14},{7,15},{8,0},{9,1},... | collective-permute-start | bytes 294920 | tf_op jit(solution)/shard_map/ppermute | solution.py:40
  45.4 11.4 %collective-permute-start.11 = (bf16[3,32,512]{2,1,0:T(8,128)(2,1)S(1)}, bf16[3,32,512]{2,1,0:T(8,128)(2,1)S(1)}, u32[]{:S(2)}, u32[]{:S(2)}) collective-permute-start(bf16[3,32,512]{2,1,0:T(8,128)(2,1)S(1)} %get-tuple-element.47.own), channel_id=1, source_target_pairs={{0,4},{1,5},{2,6},{3,7},{4,8},{5,9},{6,10},{7,11},{8,12},{9,13},{1... | collective-permute-start | bytes 294920 | tf_op jit(solution)/shard_map/ppermute | solution.py:40
  56.9 9.5 %collective-permute-start.12 = (bf16[4,3,32,512]{3,2,1,0:T(8,128)(2,1)S(1)}, bf16[4,3,32,512]{3,2,1,0:T(8,128)(2,1)S(1)}, u32[]{:S(2)}, u32[]{:S(2)}) collective-permute-start(bf16[4,3,32,512]{3,2,1,0:T(8,128)(2,1)S(1)} %shard_map.77.refs_0_), channel_id=1, source_target_pairs={{0,2},{1,3},{2,0},{3,1},{4,6},{5,7},{6,4},{7,5},{8,10},{9,11},{10,... | collective-permute-start | bytes 1179656 | tf_op jit(solution)/shard_map/ppermute | solution.py:40
  58.8 11.8 %collective-permute-start.14 = (bf16[4,3,32,512]{3,2,1,0:T(8,128)(2,1)S(1)}, bf16[4,3,32,512]{3,2,1,0:T(8,128)(2,1)S(1)}, u32[]{:S(2)}, u32[]{:S(2)}) collective-permute-start(bf16[4,3,32,512]{3,2,1,0:T(8,128)(2,1)S(1)} %shard_map.77.refs_0_), channel_id=1, source_target_pairs={{0,3},{1,0},{2,1},{3,2},{4,7},{5,4},{6,5},{7,6},{8,11},{9,8},{10,9... | collective-permute-start | bytes 1179656 | tf_op jit(solution)/shard_map/ppermute | solution.py:40
  59.2 11.5 %collective-permute-start.15 = (bf16[4,3,32,512]{3,2,1,0:T(8,128)(2,1)S(1)}, bf16[4,3,32,512]{3,2,1,0:T(8,128)(2,1)S(1)}, u32[]{:S(2)}, u32[]{:S(2)}) collective-permute-start(bf16[4,3,32,512]{3,2,1,0:T(8,128)(2,1)S(1)} %shard_map.77.refs_0_), channel_id=1, source_target_pairs={{0,1},{1,2},{2,3},{3,0},{4,5},{5,6},{6,7},{7,4},{8,9},{9,10},{10,1... | collective-permute-start | bytes 1179656 | tf_op jit(solution)/shard_map/ppermute | solution.py:40
  68.7 11.6 %collective-permute-start.13 = (bf16[4,3,32,512]{3,2,1,0:T(8,128)(2,1)S(1)}, bf16[4,3,32,512]{3,2,1,0:T(8,128)(2,1)S(1)}, u32[]{:S(2)}, u32[]{:S(2)}) collective-permute-start(bf16[4,3,32,512]{3,2,1,0:T(8,128)(2,1)S(1)} %shard_map.79), channel_id=1, source_target_pairs={{0,2},{1,3},{2,0},{3,1},{4,6},{5,7},{6,4},{7,5},{8,10},{9,11},{10,... | collective-permute-start | bytes 1179656 | tf_op jit(solution)/shard_map/ppermute | solution.py:40
  74.4 10.3 %collective-permute-start.16 = (bf16[4,3,32,512]{3,2,1,0:T(8,128)(2,1)S(1)}, bf16[4,3,32,512]{3,2,1,0:T(8,128)(2,1)S(1)}, u32[]{:S(2)}, u32[]{:S(2)}) collective-permute-start(bf16[4,3,32,512]{3,2,1,0:T(8,128)(2,1)S(1)} %get-tuple-element.51), channel_id=1, source_target_pairs={{0,1},{1,2},{2,3},{3,0},{4,5},{5,6},{6,7},{7,4},{8,9},{9,10},{10,1... | collective-permute-start | bytes 1179656 | tf_op jit(solution)/shard_map/ppermute | solution.py:40
  75.2 9.4 %collective-permute-start.17 = (bf16[4,3,32,512]{3,2,1,0:T(8,128)(2,1)S(1)}, bf16[4,3,32,512]{3,2,1,0:T(8,128)(2,1)S(1)}, u32[]{:S(2)}, u32[]{:S(2)}) collective-permute-start(bf16[4,3,32,512]{3,2,1,0:T(8,128)(2,1)S(1)} %get-tuple-element.52), channel_id=1, source_target_pairs={{0,3},{1,0},{2,1},{3,2},{4,7},{5,4},{6,5},{7,6},{8,11},{9,8},{10,9... | collective-permute-start | bytes 1179656 | tf_op jit(solution)/shard_map/ppermute | solution.py:40
  84.8 5.9 %collective-permute-start.18 = (bf16[3,32,512]{2,1,0:T(8,128)(2,1)S(1)}, bf16[3,32,512]{2,1,0:T(8,128)(2,1)S(1)}, u32[]{:S(2)}, u32[]{:S(2)}) collective-permute-start(bf16[3,32,512]{2,1,0:T(8,128)(2,1)S(1)} %get-tuple-element.54), channel_id=1, source_target_pairs={{0,4},{1,5},{2,6},{3,7},{4,8},{5,9},{6,10},{7,11},{8,12},{9,13},{1... | collective-permute-start | bytes 294920 | tf_op jit(solution)/shard_map/ppermute | solution.py:40
  84.9 6.9 %collective-permute-start.19 = (bf16[3,32,512]{2,1,0:T(8,128)(2,1)S(1)}, bf16[3,32,512]{2,1,0:T(8,128)(2,1)S(1)}, u32[]{:S(2)}, u32[]{:S(2)}) collective-permute-start(bf16[3,32,512]{2,1,0:T(8,128)(2,1)S(1)} %get-tuple-element.55), channel_id=1, source_target_pairs={{0,8},{1,9},{2,10},{3,11},{4,12},{5,13},{6,14},{7,15},{8,0},{9,1},... | collective-permute-start | bytes 294920 | tf_op jit(solution)/shard_map/ppermute | solution.py:40
  88.0 4.6 %collective-permute-start.20 = (bf16[3,32,512]{2,1,0:T(8,128)(2,1)S(1)}, bf16[3,32,512]{2,1,0:T(8,128)(2,1)S(1)}, u32[]{:S(2)}, u32[]{:S(2)}) collective-permute-start(bf16[3,32,512]{2,1,0:T(8,128)(2,1)S(1)} %get-tuple-element.56), channel_id=1, source_target_pairs={{0,12},{1,13},{2,14},{3,15},{4,0},{5,1},{6,2},{7,3},{8,4},{9,5},{1... | collective-permute-start | bytes 294920 | tf_op jit(solution)/shard_map/ppermute | solution.py:40
  92.7 4.7 %collective-permute-start.21 = (bf16[3,32,512]{2,1,0:T(8,128)(2,1)S(1)}, bf16[3,32,512]{2,1,0:T(8,128)(2,1)S(1)}, u32[]{:S(2)}, u32[]{:S(2)}) collective-permute-start(bf16[3,32,512]{2,1,0:T(8,128)(2,1)S(1)} %shard_map.85.own), channel_id=1, source_target_pairs={{0,48},{1,49},{2,50},{3,51},{4,52},{5,53},{6,54},{7,55},{8,56},{9,... | collective-permute-start | bytes 294920 | tf_op jit(solution)/shard_map/ppermute | solution.py:40
  93.6 6.2 %collective-permute-start.22 = (bf16[3,32,512]{2,1,0:T(8,128)(2,1)S(1)}, bf16[3,32,512]{2,1,0:T(8,128)(2,1)S(1)}, u32[]{:S(2)}, u32[]{:S(2)}) collective-permute-start(bf16[3,32,512]{2,1,0:T(8,128)(2,1)S(1)} %shard_map.85.own), channel_id=1, source_target_pairs={{0,32},{1,33},{2,34},{3,35},{4,36},{5,37},{6,38},{7,39},{8,40},{9,... | collective-permute-start | bytes 294920 | tf_op jit(solution)/shard_map/ppermute | solution.py:40
  94.3 6.5 %collective-permute-start.23 = (bf16[3,32,512]{2,1,0:T(8,128)(2,1)S(1)}, bf16[3,32,512]{2,1,0:T(8,128)(2,1)S(1)}, u32[]{:S(2)}, u32[]{:S(2)}) collective-permute-start(bf16[3,32,512]{2,1,0:T(8,128)(2,1)S(1)} %shard_map.85.own), channel_id=1, source_target_pairs={{0,16},{1,17},{2,18},{3,19},{4,20},{5,21},{6,22},{7,23},{8,24},{9,... | collective-permute-start | bytes 294920 | tf_op jit(solution)/shard_map/ppermute | solution.py:40
  97.4 19.2 %copy-start = (bf16[2048,512]{1,0:T(8,128)(2,1)S(1)}, bf16[2048,512]{1,0:T(8,128)(2,1)}, u32[]{:S(2)}) copy-start(bf16[2048,512]{1,0:T(8,128)(2,1)} %refs_2_.3) | copy-start | bytes 6291460
  100.9 2.2 %collective-permute-start.24 = (bf16[3,32,512]{2,1,0:T(8,128)(2,1)S(1)}, bf16[3,32,512]{2,1,0:T(8,128)(2,1)S(1)}, u32[]{:S(2)}, u32[]{:S(2)}) collective-permute-start(bf16[3,32,512]{2,1,0:T(8,128)(2,1)S(1)} %get-tuple-element.57), channel_id=1, source_target_pairs={{0,64},{1,65},{2,66},{3,67},{4,68},{5,69},{6,70},{7,71},{8,72},{9,... | collective-permute-start | bytes 294920 | tf_op jit(solution)/shard_map/ppermute | solution.py:369
  103.1 5.9 %collective-permute-start.25 = (bf16[3,32,512]{2,1,0:T(8,128)(2,1)S(1)}, bf16[3,32,512]{2,1,0:T(8,128)(2,1)S(1)}, u32[]{:S(2)}, u32[]{:S(2)}) collective-permute-start(bf16[3,32,512]{2,1,0:T(8,128)(2,1)S(1)} %shard_map.89.own), channel_id=1, source_target_pairs={{0,12},{1,13},{2,14},{3,15},{4,0},{5,1},{6,2},{7,3},{8,4},{9,5},{1... | collective-permute-start | bytes 294920 | tf_op jit(solution)/shard_map/ppermute | solution.py:40
  105.8 6.2 %collective-permute-start.26 = (bf16[3,32,512]{2,1,0:T(8,128)(2,1)S(1)}, bf16[3,32,512]{2,1,0:T(8,128)(2,1)S(1)}, u32[]{:S(2)}, u32[]{:S(2)}) collective-permute-start(bf16[3,32,512]{2,1,0:T(8,128)(2,1)S(1)} %shard_map.89.own), channel_id=1, source_target_pairs={{0,8},{1,9},{2,10},{3,11},{4,12},{5,13},{6,14},{7,15},{8,0},{9,1},... | collective-permute-start | bytes 294920 | tf_op jit(solution)/shard_map/ppermute | solution.py:40
  106.2 6.8 %collective-permute-start.27 = (bf16[3,32,512]{2,1,0:T(8,128)(2,1)S(1)}, bf16[3,32,512]{2,1,0:T(8,128)(2,1)S(1)}, u32[]{:S(2)}, u32[]{:S(2)}) collective-permute-start(bf16[3,32,512]{2,1,0:T(8,128)(2,1)S(1)} %shard_map.89.own), channel_id=1, source_target_pairs={{0,4},{1,5},{2,6},{3,7},{4,8},{5,9},{6,10},{7,11},{8,12},{9,13},{1... | collective-permute-start | bytes 294920 | tf_op jit(solution)/shard_map/ppermute | solution.py:40
  113.0 9.5 %collective-permute-start.30 = (bf16[4,3,32,512]{3,2,1,0:T(8,128)(2,1)S(1)}, bf16[4,3,32,512]{3,2,1,0:T(8,128)(2,1)S(1)}, u32[]{:S(2)}, u32[]{:S(2)}) collective-permute-start(bf16[4,3,32,512]{3,2,1,0:T(8,128)(2,1)S(1)} %shard_map.92.refs_0_), channel_id=1, source_target_pairs={{0,2},{1,3},{2,0},{3,1},{4,6},{5,7},{6,4},{7,5},{8,10},{9,11},{10,... | collective-permute-start | bytes 1179656 | tf_op jit(solution)/shard_map/ppermute | solution.py:40
  114.5 11.6 %collective-permute-start.28 = (bf16[4,3,32,512]{3,2,1,0:T(8,128)(2,1)S(1)}, bf16[4,3,32,512]{3,2,1,0:T(8,128)(2,1)S(1)}, u32[]{:S(2)}, u32[]{:S(2)}) collective-permute-start(bf16[4,3,32,512]{3,2,1,0:T(8,128)(2,1)S(1)} %shard_map.92.refs_0_), channel_id=1, source_target_pairs={{0,3},{1,0},{2,1},{3,2},{4,7},{5,4},{6,5},{7,6},{8,11},{9,8},{10,9... | collective-permute-start | bytes 1179656 | tf_op jit(solution)/shard_map/ppermute | solution.py:40
  115.9 10.6 %collective-permute-start.29 = (bf16[4,3,32,512]{3,2,1,0:T(8,128)(2,1)S(1)}, bf16[4,3,32,512]{3,2,1,0:T(8,128)(2,1)S(1)}, u32[]{:S(2)}, u32[]{:S(2)}) collective-permute-start(bf16[4,3,32,512]{3,2,1,0:T(8,128)(2,1)S(1)} %shard_map.92.refs_0_), channel_id=1, source_target_pairs={{0,1},{1,2},{2,3},{3,0},{4,5},{5,6},{6,7},{7,4},{8,9},{9,10},{10,1... | collective-permute-start | bytes 1179656 | tf_op jit(solution)/shard_map/ppermute | solution.py:40
  118.2 8.3 %copy-start.1 = (f32[512]{0:T(512)S(1)}, f32[512]{0:T(512)}, u32[]{:S(2)}) copy-start(f32[512]{0:T(512)} %param.11) | copy-start | bytes 6148

commit v5 on v4

--- a/solution.py
+++ b/solution.py
@@ -155,22 +155,22 @@
         out[...] = (far[s] + r1[s].astype(F32) + r3[s].astype(F32)).astype(out.dtype)
 
 
-def grow_kernel(own, part, out):
-    out[...] = own[...].astype(F32) + part[...].astype(F32)
-
-
-def add_kernel(own, part, out):
-    out[...] = (own[...] + part[...].astype(F32)).astype(out.dtype)
-
-
-def update_kernel(weights, own, part, new, new_bf):
-    value = weights[...] - (own[...] + part[...].astype(F32))
+def total_of(own, r1, r2, r3):
+    return (own[...].astype(F32) + r1[...].astype(F32)) + (r2[...].astype(F32) + r3[...].astype(F32))
+
+
+def add_kernel(own, r1, r2, r3, out):
+    out[...] = total_of(own, r1, r2, r3).astype(out.dtype)
+
+
+def update_kernel(weights, own, r1, r2, r3, new, new_bf):
+    value = weights[...] - total_of(own, r1, r2, r3)
     new[...] = value
     new_bf[...] = value.astype(BF)
 
 
-def change_kernel(start, weights, own, part, change, change_bf):
-    value = (weights[...] - (own[...] + part[...].astype(F32))) - start[...]
+def change_kernel(start, weights, own, r1, r2, r3, change, change_bf):
+    value = (weights[...] - total_of(own, r1, r2, r3)) - start[...]
     change[...] = value
     change_bf[...] = value.astype(BF)
 
@@ -179,14 +179,19 @@
     out[...] = ((start[...] + earlier[...].astype(F32)) + change[...]).astype(BF)
 
 
-def join_kernel(slot, joined, part, out):
-    del joined
-    out[slot] = part[...]
-
-
-def join_first_kernel(own, part, out):
+def join_all_kernel(own, r1, r2, r3, out):
+    for s, part in enumerate((own, r1, r2, r3)):
+        out[s] = part[...]
+
+
+def join_first_kernel(own, part, out, token):
     out[0] = own[...]
     out[1] = part[...]
+    token[...] = own[0, : token.shape[0], : token.shape[1]]
+
+
+def join_kernel(slot, joined, part, *rest):
+    rest[-1][slot] = part[...]
 
 
 def apply_kernel(tile, count, first, last, *refs):
@@ -249,13 +254,6 @@
     return [hop(x, level, -r) for r in range(1, SIDE)]
 
 
-def grown(total, parts):
-    size = total.size
-    for part in parts:
-        total = call(grow_kernel, arr(total.shape, F32), None, (total, part), (size, 8 * size))
-    return total
-
-
 def combined(own, sent):
     shard = own.shape[1:]
     size = own.size
@@ -268,9 +266,8 @@
         (2 * size, 10 * size),
     )
     got = [hop(x, 1, r + 1) for r, x in enumerate(out)]
-    part = call(add_kernel, arr(shard, BF), None, (grown(keep, got[:2]), got[2]), (size, 3 * size))
-    got = ring_parts(part, 2)
-    return grown(part, got[:2]), got[2]
+    part = call(add_kernel, arr(shard, BF), None, (keep, *got), (size, 3 * size))
+    return [part] + ring_parts(part, 2)
 
 
 def first_totals(place, weights, keys, values, rates, factor, tile=256):
@@ -305,19 +302,28 @@
     return start, (keys, values, rates), combined(own, sent)
 
 
-def gathered(shard):
+def order_pairs():
+    return [(flat(0, *c), flat(1, *c)) for c in itertools.product(*[range(SIDE)] * 3)]
+
+
+def gathered(shard, in_step):
     parts = ring_parts(shard, 1)
     block = arr((SIDE, *shard.shape), BF)
     cost = (0, 4 * shard.size)
-    joined = call(join_first_kernel, block, None, (shard, parts[0]), cost)
+    if not in_step:
+        return call(join_all_kernel, block, None, (shard, *parts), cost)
+    outs = [block, arr((16, 128), BF)]
+    joined, token = call(join_first_kernel, outs, None, (shard, parts[0]), cost)
+    more = [[], [lax.ppermute(token, AXES, order_pairs())]]
     for r in (2, 3):
         kernel = functools.partial(join_kernel, r)
-        joined = call(kernel, block, None, (joined, parts[r - 1]), cost, aliases={0: 0})
+        args = (joined, parts[r - 1], *more[r - 2])
+        joined = call(kernel, block, None, args, cost, aliases={0: 0})
     return joined
 
 
 def second_totals(shard, keys, values, rates, factor):
-    block = gathered(shard)
+    block = gathered(shard, True)
     b2, b1, b3 = hop(block, 0, -2), hop(block, 0, -1), hop(block, 0, -3)
     (own,) = gradient_blocks([block], keys, values, rates, factor, F32)
     own, keys = in_turn(own, keys)
@@ -330,7 +336,7 @@
 
 
 def applied(shard, queries, gain):
-    block = gathered(shard)
+    block = gathered(shard, False)
     b2, b1, b3 = hop(block, 0, -2), hop(block, 0, -1), hop(block, 0, -3)
     result = apply_blocks([block], queries, None, None)
     result = apply_blocks([b2], queries, result, None)
@@ -365,8 +371,7 @@
         (start, first_step, *parts),
         (size, 8 * size),
     )
-    pairs = [(flat(0, *c), flat(1, *c)) for c in itertools.product(*[range(SIDE)] * 3)]
-    earlier = lax.ppermute(change_bf, AXES, pairs)
+    earlier = lax.ppermute(change_bf, AXES, order_pairs())
     closing = call(closing_kernel, arr(shard, BF), None, (start, earlier, change), (size, 8 * size))
     return applied(closing, queries, gain)
 

time: 130 us -> 126 us (0.969)
  waiting for transfers between devices: 56 us -> 49.7 us
  starting transfers between devices: 45.6 us -> 47.3 us
    ppermute x30, waiting for transfers between devices: 55 us -> 48.8 us  [hop(): return lax.ppermute(x, AXES, hop_pairs(level, step % SIDE))]
    pallas_call x32 -> x22, Pallas kernels: 28.1 us -> 28 us  [call(): pl.pallas_call(kernel, out_shape=outs, in_specs=specs or [VMEM] * len(arg...]
  transfers between devices with their start and end apart: 31 -> 32, of which waited for: 25 -> 25; matrix products, arithmetic and copies ran while one was open for 0% -> 0% of each run, Pallas kernels for 14% -> 14%
where the time goes in v5:
time: 126 us
  waiting for transfers between devices  49.7 us (39%)
  starting transfers between devices  47.3 us (38%)
  Pallas kernels  28 us (22%)
    ppermute x30, waiting for transfers between devices, hop(): return lax.ppermute(x, AXES, hop_pairs(level, step % SIDE))  48.8 us
    ppermute x30, starting transfers between devices, hop(): return lax.ppermute(x, AXES, hop_pairs(level, step % SIDE))  44.7 us
    pallas_call x22, Pallas kernels, call(): pl.pallas_call(kernel, out_shape=outs, in_specs=specs or [VMEM] * len(arg...  28 us
  transfers between devices with their start and end apart: 32, of which 25 were waited for; matrix products, arithmetic and copies ran while one was open for 0% of the time, Pallas kernels for 14%

profile of v5, /device:TPU:0, one launch (start us, length us, event | category | flops | bytes accessed | tf_op | source)
XLA Modules:
  0.0 125.6 jit_solution(13898282587340035048)
XLA Ops:
  0.2 6.1 %shard_map.64 = (bf16[2048,512]{1,0:T(8,128)(2,1)S(1)}, bf16[2048,512]{1,0:T(8,128)(2,1)S(1)}, f32[1,2048]{1,0:T(1,128)S(1)}, bf16[4,3,32,512]{3,2,1,0:T(8,128)(...) custom-call(s32[16]{0:T(128)S(1)} %fusion.place, ...), custom_call_target="tpu_custom_call" | custom-call | flops 1610612736 | bytes 4194304 | tf_op jit(solution)/shard_map/pallas_call | solution.py:49
  6.3 3.2 %collective-permute-start = (bf16[4,3,32,512]{3,2,1,0:T(8,128)(2,1)S(1)}, bf16[4,3,32,512]{3,2,1,0:T(8,128)(2,1)S(1)}, u32[]{:S(2)}, u32[]{:S(2)}) collective-permute-start(bf16[4,3,32,512]{3,2,1,0:T(8,128)(2,1)S(1)} %get-tuple-element.39), channel_id=1, source_target_pairs={{0,2},{1,3},{2,0},{3,1},{4,6},{5,7},{6,4},{7,5},{8,10},{9,11},{10,... | collective-permute-start | bytes 1179656 | tf_op jit(solution)/shard_map/ppermute | solution.py:40
  9.5 3.7 %shard_map.67 = (bf16[4,3,32,512]{3,2,1,0:T(8,128)(2,1)S(1)}, bf16[4,3,32,512]{3,2,1,0:T(8,128)(2,1)S(1)}) custom-call(bf16[4,3,32,512]{3,2,1,0:T(8,128)(2,1)S(1)} %get-tuple-element.40.refs_0_, bf16[4,3,32,512]{3,2,1,0:T(8,128)(2,1)S(1)} %get-tuple-element.41.refs_1_, bf16[2048,512]{1,0:T(8,128)(2,1)S(1)} %get-tuple-element.54.refs_1_.refs_2_, ...), custom_call_target="tpu_custom_call" | custom-call | flops 3221225472 | bytes 4194304 | tf_op jit(solution)/shard_map/pallas_call | solution.py:49
  13.2 0.7 collective-permute-start.1
  13.9 2.6 %collective-permute-start.2 = (bf16[4,3,32,512]{3,2,1,0:T(8,128)(2,1)S(1)}, bf16[4,3,32,512]{3,2,1,0:T(8,128)(2,1)S(1)}, u32[]{:S(2)}, u32[]{:S(2)}) collective-permute-start(bf16[4,3,32,512]{3,2,1,0:T(8,128)(2,1)S(1)} %get-tuple-element.43), channel_id=1, source_target_pairs={{0,3},{1,0},{2,1},{3,2},{4,7},{5,4},{6,5},{7,6},{8,11},{9,8},{10,9... | collective-permute-start | bytes 1179656 | tf_op jit(solution)/shard_map/ppermute | solution.py:40
  16.5 2.3 %shard_map.65.own = f32[4,3,32,512]{3,2,1,0:T(8,128)S(1)} custom-call(bf16[4,3,32,512]{3,2,1,0:T(8,128)(2,1)S(1)} %get-tuple-element.35.refs_0_, bf16[2048,512]{1,0:T(8,128)(2,1)S(1)} %get-tuple-element.54.refs_1_.refs_2_, bf16[2048,512]{1,0:T(8,128)(2,1)S(1)} %get-tuple-element.37.refs_2_.refs_3_, f32[1,2048]{1,0:T(1,128)S(1)} %get-tuple-element.38.refs_3_.refs_4_), custom_call_target="tpu_custom_call" | custom-call | flops 1610612736 | bytes 4194304 | tf_op jit(solution)/shard_map/pallas_call | solution.py:49
  18.9 3.4 %collective-permute-done.1.r1 = bf16[4,3,32,512]{3,2,1,0:T(8,128)(2,1)S(1)} collective-permute-done((bf16[4,3,32,512]{3,2,1,0:T(8,128)(2,1)S(1)}, bf16[4,3,32,512]{3,2,1,0:T(8,128)(2,1)S(1)}, u32[]{:S(2)}, u32[]{:S(2)}) %collective-permute-start.1) | collective-permute-done | bytes 393248 | tf_op jit(solution)/shard_map/ppermute | solution.py:40
  22.4 1.7 %collective-permute-start.3 = (bf16[3,32,512]{2,1,0:T(8,128)(2,1)S(1)}, bf16[3,32,512]{2,1,0:T(8,128)(2,1)S(1)}, u32[]{:S(2)}, u32[]{:S(2)}) collective-permute-start(bf16[3,32,512]{2,1,0:T(8,128)(2,1)S(1)} %get-tuple-element.45), channel_id=1, source_target_pairs={{0,4},{1,5},{2,6},{3,7},{4,8},{5,9},{6,10},{7,11},{8,12},{9,13},{1... | collective-permute-start | bytes 294920 | tf_op jit(solution)/shard_map/ppermute | solution.py:40
  24.1 2.9 %collective-permute-start.4 = (bf16[3,32,512]{2,1,0:T(8,128)(2,1)S(1)}, bf16[3,32,512]{2,1,0:T(8,128)(2,1)S(1)}, u32[]{:S(2)}, u32[]{:S(2)}) collective-permute-start(bf16[3,32,512]{2,1,0:T(8,128)(2,1)S(1)} %get-tuple-element.46), channel_id=1, source_target_pairs={{0,8},{1,9},{2,10},{3,11},{4,12},{5,13},{6,14},{7,15},{8,0},{9,1},... | collective-permute-start | bytes 294920 | tf_op jit(solution)/shard_map/ppermute | solution.py:40
  27.0 1.3 %collective-permute-start.5 = (bf16[3,32,512]{2,1,0:T(8,128)(2,1)S(1)}, bf16[3,32,512]{2,1,0:T(8,128)(2,1)S(1)}, u32[]{:S(2)}, u32[]{:S(2)}) collective-permute-start(bf16[3,32,512]{2,1,0:T(8,128)(2,1)S(1)} %get-tuple-element.47), channel_id=1, source_target_pairs={{0,12},{1,13},{2,14},{3,15},{4,0},{5,1},{6,2},{7,3},{8,4},{9,5},{1... | collective-permute-start | bytes 294920 | tf_op jit(solution)/shard_map/ppermute | solution.py:40
  28.3 2.3 %collective-permute-done.4.r2 = bf16[3,32,512]{2,1,0:T(8,128)(2,1)S(1)} collective-permute-done((bf16[3,32,512]{2,1,0:T(8,128)(2,1)S(1)}, bf16[3,32,512]{2,1,0:T(8,128)(2,1)S(1)}, u32[]{:S(2)}, u32[]{:S(2)}) %collective-permute-start.4) | collective-permute-done | bytes 98336 | tf_op jit(solution)/shard_map/ppermute | solution.py:40
  30.6 1.0 collective-permute-done.5.r3
  31.6 4.1 %collective-permute-start.6 = (bf16[3,32,512]{2,1,0:T(8,128)(2,1)S(1)}, bf16[3,32,512]{2,1,0:T(8,128)(2,1)S(1)}, u32[]{:S(2)}, u32[]{:S(2)}) collective-permute-start(bf16[3,32,512]{2,1,0:T(8,128)(2,1)S(1)} %shard_map.69.own), channel_id=1, source_target_pairs={{0,48},{1,49},{2,50},{3,51},{4,52},{5,53},{6,54},{7,55},{8,56},{9,... | collective-permute-start | bytes 294920 | tf_op jit(solution)/shard_map/ppermute | solution.py:40
  35.7 1.3 %collective-permute-start.8 = (bf16[3,32,512]{2,1,0:T(8,128)(2,1)S(1)}, bf16[3,32,512]{2,1,0:T(8,128)(2,1)S(1)}, u32[]{:S(2)}, u32[]{:S(2)}) collective-permute-start(bf16[3,32,512]{2,1,0:T(8,128)(2,1)S(1)} %shard_map.69.own), channel_id=1, source_target_pairs={{0,16},{1,17},{2,18},{3,19},{4,20},{5,21},{6,22},{7,23},{8,24},{9,... | collective-permute-start | bytes 294920 | tf_op jit(solution)/shard_map/ppermute | solution.py:40
  37.0 2.0 %collective-permute-done.6.r1 = bf16[3,32,512]{2,1,0:T(8,128)(2,1)S(1)} collective-permute-done((bf16[3,32,512]{2,1,0:T(8,128)(2,1)S(1)}, bf16[3,32,512]{2,1,0:T(8,128)(2,1)S(1)}, u32[]{:S(2)}, u32[]{:S(2)}) %collective-permute-start.6) | collective-permute-done | bytes 98336 | tf_op jit(solution)/shard_map/ppermute | solution.py:40
  39.0 3.0 %collective-permute-done.7.r2 = bf16[3,32,512]{2,1,0:T(8,128)(2,1)S(1)} collective-permute-done((bf16[3,32,512]{2,1,0:T(8,128)(2,1)S(1)}, bf16[3,32,512]{2,1,0:T(8,128)(2,1)S(1)}, u32[]{:S(2)}, u32[]{:S(2)}) %collective-permute-start.7) | collective-permute-done | bytes 98336 | tf_op jit(solution)/shard_map/ppermute | solution.py:40
  42.0 0.7 collective-permute-done.8.r3
  42.7 2.6 %collective-permute-start.9 = (bf16[3,32,512]{2,1,0:T(8,128)(2,1)S(1)}, bf16[3,32,512]{2,1,0:T(8,128)(2,1)S(1)}, u32[]{:S(2)}, u32[]{:S(2)}) collective-permute-start(bf16[3,32,512]{2,1,0:T(8,128)(2,1)S(1)} %get-tuple-element.49.own), channel_id=1, source_target_pairs={{0,12},{1,13},{2,14},{3,15},{4,0},{5,1},{6,2},{7,3},{8,4},{9,5},{1... | collective-permute-start | bytes 294920 | tf_op jit(solution)/shard_map/ppermute | solution.py:40
  45.3 0.2 collective-permute-start.10
  45.5 0.8 collective-permute-start.11
  46.3 2.3 %collective-permute-done.9.part = bf16[3,32,512]{2,1,0:T(8,128)(2,1)S(1)} collective-permute-done((bf16[3,32,512]{2,1,0:T(8,128)(2,1)S(1)}, bf16[3,32,512]{2,1,0:T(8,128)(2,1)S(1)}, u32[]{:S(2)}, u32[]{:S(2)}) %collective-permute-start.9) | collective-permute-done | bytes 98336 | tf_op jit(solution)/shard_map/ppermute | solution.py:40
  48.6 1.3 %collective-permute-start.12 = (bf16[16,128]{1,0:T(8,128)(2,1)S(1)}, bf16[16,128]{1,0:T(8,128)(2,1)S(1)}, u32[]{:S(2)}, u32[]{:S(2)}) collective-permute-start(bf16[16,128]{1,0:T(8,128)(2,1)S(1)} %get-tuple-element.51), channel_id=1, source_target_pairs={{0,64},{1,65},{2,66},{3,67},{4,68},{5,69},{6,70},{7,71},{8,72},{9,... | collective-permute-start | bytes 12296 | tf_op jit(solution)/shard_map/ppermute | solution.py:317
  49.9 1.7 %collective-permute-done.10.part = bf16[3,32,512]{2,1,0:T(8,128)(2,1)S(1)} collective-permute-done((bf16[3,32,512]{2,1,0:T(8,128)(2,1)S(1)}, bf16[3,32,512]{2,1,0:T(8,128)(2,1)S(1)}, u32[]{:S(2)}, u32[]{:S(2)}) %collective-permute-start.10) | collective-permute-done | bytes 98336 | tf_op jit(solution)/shard_map/ppermute | solution.py:40
  51.6 0.8 collective-permute-done.11.part
  52.4 1.5 %collective-permute-start.13 = (bf16[4,3,32,512]{3,2,1,0:T(8,128)(2,1)S(1)}, bf16[4,3,32,512]{3,2,1,0:T(8,128)(2,1)S(1)}, u32[]{:S(2)}, u32[]{:S(2)}) collective-permute-start(bf16[4,3,32,512]{3,2,1,0:T(8,128)(2,1)S(1)} %shard_map.73.refs_0_), channel_id=1, source_target_pairs={{0,2},{1,3},{2,0},{3,1},{4,6},{5,7},{6,4},{7,5},{8,10},{9,11},{10,... | collective-permute-start | bytes 1179656 | tf_op jit(solution)/shard_map/ppermute | solution.py:40
  53.9 2.0 %collective-permute-start.15 = (bf16[4,3,32,512]{3,2,1,0:T(8,128)(2,1)S(1)}, bf16[4,3,32,512]{3,2,1,0:T(8,128)(2,1)S(1)}, u32[]{:S(2)}, u32[]{:S(2)}) collective-permute-start(bf16[4,3,32,512]{3,2,1,0:T(8,128)(2,1)S(1)} %shard_map.73.refs_0_), channel_id=1, source_target_pairs={{0,3},{1,0},{2,1},{3,2},{4,7},{5,4},{6,5},{7,6},{8,11},{9,8},{10,9... | collective-permute-start | bytes 1179656 | tf_op jit(solution)/shard_map/ppermute | solution.py:40
  56.0 0.6 collective-permute-start.16
  56.6 2.3 %shard_map.74.own = f32[4,3,32,512]{3,2,1,0:T(8,128)S(1)} custom-call(bf16[4,3,32,512]{3,2,1,0:T(8,128)(2,1)S(1)} %shard_map.73.refs_0_, bf16[2048,512]{1,0:T(8,128)(2,1)S(1)} %get-tuple-element.54.refs_1_.refs_2_, bf16[2048,512]{1,0:T(8,128)(2,1)S(1)} %get-tuple-element.37.refs_2_.refs_3_, f32[1,2048]{1,0:T(1,128)S(1)} %get-tuple-element.38.refs_3_.refs_4_), custom_call_target="tpu_custom_call" | custom-call | flops 1610612736 | bytes 4194304 | tf_op jit(solution)/shard_map/pallas_call | solution.py:49
  58.9 2.9 %collective-permute-done.13.refs_0_ = bf16[4,3,32,512]{3,2,1,0:T(8,128)(2,1)S(1)} collective-permute-done((bf16[4,3,32,512]{3,2,1,0:T(8,128)(2,1)S(1)}, bf16[4,3,32,512]{3,2,1,0:T(8,128)(2,1)S(1)}, u32[]{:S(2)}, u32[]{:S(2)}) %collective-permute-start.13) | collective-permute-done | bytes 393248 | tf_op jit(solution)/shard_map/ppermute | solution.py:40
  61.9 2.3 %shard_map.75 = bf16[4,3,32,512]{3,2,1,0:T(8,128)(2,1)S(1)} custom-call(bf16[4,3,32,512]{3,2,1,0:T(8,128)(2,1)S(1)} %collective-permute-done.13.refs_0_, bf16[2048,512]{1,0:T(8,128)(2,1)S(1)} %get-tuple-element.54.refs_1_.refs_2_, bf16[2048,512]{1,0:T(8,128)(2,1)S(1)} %get-tuple-element.37.refs_2_.refs_3_, f32[1,2048]{1,0:T(1,128)S(1)} %get-tuple-element.38.refs_3_.refs_4_), custom_call_target="tpu_custom_call" | custom-call | flops 1610612736 | bytes 4194304 | tf_op jit(solution)/shard_map/pallas_call | solution.py:49
  64.2 1.5 %collective-permute-start.14 = (bf16[4,3,32,512]{3,2,1,0:T(8,128)(2,1)S(1)}, bf16[4,3,32,512]{3,2,1,0:T(8,128)(2,1)S(1)}, u32[]{:S(2)}, u32[]{:S(2)}) collective-permute-start(bf16[4,3,32,512]{3,2,1,0:T(8,128)(2,1)S(1)} %shard_map.75), channel_id=1, source_target_pairs={{0,2},{1,3},{2,0},{3,1},{4,6},{5,7},{6,4},{7,5},{8,10},{9,11},{10,... | collective-permute-start | bytes 1179656 | tf_op jit(solution)/shard_map/ppermute | solution.py:40
  65.7 0.8 collective-permute-done.15.refs_0_
  66.6 3.7 %shard_map.77 = (bf16[4,3,32,512]{3,2,1,0:T(8,128)(2,1)S(1)}, bf16[4,3,32,512]{3,2,1,0:T(8,128)(2,1)S(1)}) custom-call(bf16[4,3,32,512]{3,2,1,0:T(8,128)(2,1)S(1)} %collective-permute-done.15.refs_0_, bf16[4,3,32,512]{3,2,1,0:T(8,128)(2,1)S(1)} %collective-permute-done.16.refs_1_, bf16[2048,512]{1,0:T(8,128)(2,1)S(1)} %get-tuple-element.54.refs_1_.refs_2_, ...), custom_call_target="tpu_custom_call" | custom-call | flops 3221225472 | bytes 4194304 | tf_op jit(solution)/shard_map/pallas_call | solution.py:49
  70.3 1.9 %collective-permute-start.17 = (bf16[4,3,32,512]{3,2,1,0:T(8,128)(2,1)S(1)}, bf16[4,3,32,512]{3,2,1,0:T(8,128)(2,1)S(1)}, u32[]{:S(2)}, u32[]{:S(2)}) collective-permute-start(bf16[4,3,32,512]{3,2,1,0:T(8,128)(2,1)S(1)} %get-tuple-element.55), channel_id=1, source_target_pairs={{0,1},{1,2},{2,3},{3,0},{4,5},{5,6},{6,7},{7,4},{8,9},{9,10},{10,1... | collective-permute-start | bytes 1179656 | tf_op jit(solution)/shard_map/ppermute | solution.py:40
  72.1 1.4 %collective-permute-start.18 = (bf16[4,3,32,512]{3,2,1,0:T(8,128)(2,1)S(1)}, bf16[4,3,32,512]{3,2,1,0:T(8,128)(2,1)S(1)}, u32[]{:S(2)}, u32[]{:S(2)}) collective-permute-start(bf16[4,3,32,512]{3,2,1,0:T(8,128)(2,1)S(1)} %get-tuple-element.56), channel_id=1, source_target_pairs={{0,3},{1,0},{2,1},{3,2},{4,7},{5,4},{6,5},{7,6},{8,11},{9,8},{10,9... | collective-permute-start | bytes 1179656 | tf_op jit(solution)/shard_map/ppermute | solution.py:40
  73.7 5.7 %collective-permute-done.17.r1 = bf16[4,3,32,512]{3,2,1,0:T(8,128)(2,1)S(1)} collective-permute-done((bf16[4,3,32,512]{3,2,1,0:T(8,128)(2,1)S(1)}, bf16[4,3,32,512]{3,2,1,0:T(8,128)(2,1)S(1)}, u32[]{:S(2)}, u32[]{:S(2)}) %collective-permute-start.17) | collective-permute-done | bytes 393248 | tf_op jit(solution)/shard_map/ppermute | solution.py:40
  79.3 0.6 collective-permute-done.18.r3
  80.1 3.3 %collective-permute-start.20 = (bf16[3,32,512]{2,1,0:T(8,128)(2,1)S(1)}, bf16[3,32,512]{2,1,0:T(8,128)(2,1)S(1)}, u32[]{:S(2)}, u32[]{:S(2)}) collective-permute-start(bf16[3,32,512]{2,1,0:T(8,128)(2,1)S(1)} %get-tuple-element.59), channel_id=1, source_target_pairs={{0,8},{1,9},{2,10},{3,11},{4,12},{5,13},{6,14},{7,15},{8,0},{9,1},... | collective-permute-start | bytes 294920 | tf_op jit(solution)/shard_map/ppermute | solution.py:40
  83.4 0.4 collective-permute-start.21
  83.8 2.1 %collective-permute-done.19.r1 = bf16[3,32,512]{2,1,0:T(8,128)(2,1)S(1)} collective-permute-done((bf16[3,32,512]{2,1,0:T(8,128)(2,1)S(1)}, bf16[3,32,512]{2,1,0:T(8,128)(2,1)S(1)}, u32[]{:S(2)}, u32[]{:S(2)}) %collective-permute-start.19) | collective-permute-done | bytes 98336 | tf_op jit(solution)/shard_map/ppermute | solution.py:40
  85.9 1.1 collective-permute-done.20.r2
  87.1 1.0 collective-permute-done.21.r3
  88.1 1.0 collective-permute-start.22
  89.1 0.5 collective-permute-start.23
  89.5 1.3 %collective-permute-start.24 = (bf16[3,32,512]{2,1,0:T(8,128)(2,1)S(1)}, bf16[3,32,512]{2,1,0:T(8,128)(2,1)S(1)}, u32[]{:S(2)}, u32[]{:S(2)}) collective-permute-start(bf16[3,32,512]{2,1,0:T(8,128)(2,1)S(1)} %shard_map.79.own), channel_id=1, source_target_pairs={{0,16},{1,17},{2,18},{3,19},{4,20},{5,21},{6,22},{7,23},{8,24},{9,... | collective-permute-start | bytes 294920 | tf_op jit(solution)/shard_map/ppermute | solution.py:40
  90.8 1.9 %collective-permute-done.22.r1 = bf16[3,32,512]{2,1,0:T(8,128)(2,1)S(1)} collective-permute-done((bf16[3,32,512]{2,1,0:T(8,128)(2,1)S(1)}, bf16[3,32,512]{2,1,0:T(8,128)(2,1)S(1)}, u32[]{:S(2)}, u32[]{:S(2)}) %collective-permute-start.22) | collective-permute-done | bytes 98336 | tf_op jit(solution)/shard_map/ppermute | solution.py:40
  92.8 2.5 %collective-permute-done.23.r2 = bf16[3,32,512]{2,1,0:T(8,128)(2,1)S(1)} collective-permute-done((bf16[3,32,512]{2,1,0:T(8,128)(2,1)S(1)}, bf16[3,32,512]{2,1,0:T(8,128)(2,1)S(1)}, u32[]{:S(2)}, u32[]{:S(2)}) %collective-permute-start.23) | collective-permute-done | bytes 98336 | tf_op jit(solution)/shard_map/ppermute | solution.py:40
  95.3 1.0 collective-permute-done.24.r3
  96.3 1.3 %collective-permute-start.25 = (bf16[3,32,512]{2,1,0:T(8,128)(2,1)S(1)}, bf16[3,32,512]{2,1,0:T(8,128)(2,1)S(1)}, u32[]{:S(2)}, u32[]{:S(2)}) collective-permute-start(bf16[3,32,512]{2,1,0:T(8,128)(2,1)S(1)} %get-tuple-element.61), channel_id=1, source_target_pairs={{0,64},{1,65},{2,66},{3,67},{4,68},{5,69},{6,70},{7,71},{8,72},{9,... | collective-permute-start | bytes 294920 | tf_op jit(solution)/shard_map/ppermute | solution.py:374
  97.6 0.9 collective-permute-done.25.earlier
  98.6 2.5 %collective-permute-start.26 = (bf16[3,32,512]{2,1,0:T(8,128)(2,1)S(1)}, bf16[3,32,512]{2,1,0:T(8,128)(2,1)S(1)}, u32[]{:S(2)}, u32[]{:S(2)}) collective-permute-start(bf16[3,32,512]{2,1,0:T(8,128)(2,1)S(1)} %shard_map.81.own), channel_id=1, source_target_pairs={{0,12},{1,13},{2,14},{3,15},{4,0},{5,1},{6,2},{7,3},{8,4},{9,5},{1... | collective-permute-start | bytes 294920 | tf_op jit(solution)/shard_map/ppermute | solution.py:40
  101.1 0.4 collective-permute-start.27
  101.5 0.6 collective-permute-start.28
  102.1 2.3 %collective-permute-done.26.r1 = bf16[3,32,512]{2,1,0:T(8,128)(2,1)S(1)} collective-permute-done((bf16[3,32,512]{2,1,0:T(8,128)(2,1)S(1)}, bf16[3,32,512]{2,1,0:T(8,128)(2,1)S(1)}, u32[]{:S(2)}, u32[]{:S(2)}) %collective-permute-start.26) | collective-permute-done | bytes 98336 | tf_op jit(solution)/shard_map/ppermute | solution.py:40
  104.3 3.0 %collective-permute-done.27.r2 = bf16[3,32,512]{2,1,0:T(8,128)(2,1)S(1)} collective-permute-done((bf16[3,32,512]{2,1,0:T(8,128)(2,1)S(1)}, bf16[3,32,512]{2,1,0:T(8,128)(2,1)S(1)}, u32[]{:S(2)}, u32[]{:S(2)}) %collective-permute-start.27) | collective-permute-done | bytes 98336 | tf_op jit(solution)/shard_map/ppermute | solution.py:40
  107.3 0.9 collective-permute-done.28.r3
  108.3 2.3 %collective-permute-start.31 = (bf16[4,3,32,512]{3,2,1,0:T(8,128)(2,1)S(1)}, bf16[4,3,32,512]{3,2,1,0:T(8,128)(2,1)S(1)}, u32[]{:S(2)}, u32[]{:S(2)}) collective-permute-start(bf16[4,3,32,512]{3,2,1,0:T(8,128)(2,1)S(1)} %shard_map.82.refs_0_), channel_id=1, source_target_pairs={{0,2},{1,3},{2,0},{3,1},{4,6},{5,7},{6,4},{7,5},{8,10},{9,11},{10,... | collective-permute-start | bytes 1179656 | tf_op jit(solution)/shard_map/ppermute | solution.py:40
  110.7 0.6 collective-permute-start.29
  111.3 1.4 %collective-permute-start.30 = (bf16[4,3,32,512]{3,2,1,0:T(8,128)(2,1)S(1)}, bf16[4,3,32,512]{3,2,1,0:T(8,128)(2,1)S(1)}, u32[]{:S(2)}, u32[]{:S(2)}) collective-permute-start(bf16[4,3,32,512]{3,2,1,0:T(8,128)(2,1)S(1)} %shard_map.82.refs_0_), channel_id=1, source_target_pairs={{0,1},{1,2},{2,3},{3,0},{4,5},{5,6},{6,7},{7,4},{8,9},{9,10},{10,1... | collective-permute-start | bytes 1179656 | tf_op jit(solution)/shard_map/ppermute | solution.py:40
  112.7 1.6 %shard_map.83.refs_2_ = f32[2048,512]{1,0:T(8,128)S(1)} custom-call(bf16[4,3,32,512]{3,2,1,0:T(8,128)(2,1)S(1)} %shard_map.82.refs_0_, bf16[2048,512]{1,0:T(8,128)(2,1)S(1)} %copy-done), custom_call_target="tpu_custom_call" | custom-call | flops 805306368 | bytes 6291456 | tf_op jit(solution)/shard_map/pallas_call | solution.py:49
  114.3 3.4 %collective-permute-done.31.refs_0_ = bf16[4,3,32,512]{3,2,1,0:T(8,128)(2,1)S(1)} collective-permute-done((bf16[4,3,32,512]{3,2,1,0:T(8,128)(2,1)S(1)}, bf16[4,3,32,512]{3,2,1,0:T(8,128)(2,1)S(1)}, u32[]{:S(2)}, u32[]{:S(2)}) %collective-permute-start.31) | collective-permute-done | bytes 393248 | tf_op jit(solution)/shard_map/ppermute | solution.py:40
  117.8 1.6 %shard_map.84.refs_4_ = f32[2048,512]{1,0:T(8,128)S(1)} custom-call(bf16[4,3,32,512]{3,2,1,0:T(8,128)(2,1)S(1)} %collective-permute-done.31.refs_0_, bf16[2048,512]{1,0:T(8,128)(2,1)S(1)} %copy-done, f32[2048,512]{1,0:T(8,128)S(1)} %shard_map.83.refs_2_), custom_call_target="tpu_custom_call" | custom-call | flops 805306368 | bytes 6291456 | tf_op jit(solution)/shard_map/pallas_call | solution.py:49
  119.4 2.5 %collective-permute-done.29.refs_0_ = bf16[4,3,32,512]{3,2,1,0:T(8,128)(2,1)S(1)} collective-permute-done((bf16[4,3,32,512]{3,2,1,0:T(8,128)(2,1)S(1)}, bf16[4,3,32,512]{3,2,1,0:T(8,128)(2,1)S(1)}, u32[]{:S(2)}, u32[]{:S(2)}) %collective-permute-start.29) | collective-permute-done | bytes 393248 | tf_op jit(solution)/shard_map/ppermute | solution.py:40
  121.9 3.5 %shard_map.85 = bf16[2048,512]{1,0:T(8,128)(2,1)} custom-call(bf16[4,3,32,512]{3,2,1,0:T(8,128)(2,1)S(1)} %collective-permute-done.29.refs_0_, bf16[4,3,32,512]{3,2,1,0:T(8,128)(2,1)S(1)} %collective-permute-done.30.refs_1_, bf16[2048,512]{1,0:T(8,128)(2,1)S(1)} %copy-done, f32[1,512]{1,0:T(1,128)S(1)} %bitcast.2, f32[2048,512]{1,0:T(8,128)S(1)} %shard_map.84.refs_4_), custom_call_target="tpu_custom_call" | custom-call | flops 1610612736 | bytes 6291456 | tf_op jit(solution)/shard_map/pallas_call | solution.py:49
  (30 shorter events, 1.0 us)
Async XLA Ops:
  6.3 12.5 %collective-permute-start = (bf16[4,3,32,512]{3,2,1,0:T(8,128)(2,1)S(1)}, bf16[4,3,32,512]{3,2,1,0:T(8,128)(2,1)S(1)}, u32[]{:S(2)}, u32[]{:S(2)}) collective-permute-start(bf16[4,3,32,512]{3,2,1,0:T(8,128)(2,1)S(1)} %get-tuple-element.39), channel_id=1, source_target_pairs={{0,2},{1,3},{2,0},{3,1},{4,6},{5,7},{6,4},{7,5},{8,10},{9,11},{10,... | collective-permute-start | bytes 1179656 | tf_op jit(solution)/shard_map/ppermute | solution.py:40
  13.2 9.1 %collective-permute-start.1 = (bf16[4,3,32,512]{3,2,1,0:T(8,128)(2,1)S(1)}, bf16[4,3,32,512]{3,2,1,0:T(8,128)(2,1)S(1)}, u32[]{:S(2)}, u32[]{:S(2)}) collective-permute-start(bf16[4,3,32,512]{3,2,1,0:T(8,128)(2,1)S(1)} %get-tuple-element.42), channel_id=1, source_target_pairs={{0,1},{1,2},{2,3},{3,0},{4,5},{5,6},{6,7},{7,4},{8,9},{9,10},{10,1... | collective-permute-start | bytes 1179656 | tf_op jit(solution)/shard_map/ppermute | solution.py:40
  13.9 8.4 %collective-permute-start.2 = (bf16[4,3,32,512]{3,2,1,0:T(8,128)(2,1)S(1)}, bf16[4,3,32,512]{3,2,1,0:T(8,128)(2,1)S(1)}, u32[]{:S(2)}, u32[]{:S(2)}) collective-permute-start(bf16[4,3,32,512]{3,2,1,0:T(8,128)(2,1)S(1)} %get-tuple-element.43), channel_id=1, source_target_pairs={{0,3},{1,0},{2,1},{3,2},{4,7},{5,4},{6,5},{7,6},{8,11},{9,8},{10,9... | collective-permute-start | bytes 1179656 | tf_op jit(solution)/shard_map/ppermute | solution.py:40
  22.4 5.9 %collective-permute-start.3 = (bf16[3,32,512]{2,1,0:T(8,128)(2,1)S(1)}, bf16[3,32,512]{2,1,0:T(8,128)(2,1)S(1)}, u32[]{:S(2)}, u32[]{:S(2)}) collective-permute-start(bf16[3,32,512]{2,1,0:T(8,128)(2,1)S(1)} %get-tuple-element.45), channel_id=1, source_target_pairs={{0,4},{1,5},{2,6},{3,7},{4,8},{5,9},{6,10},{7,11},{8,12},{9,13},{1... | collective-permute-start | bytes 294920 | tf_op jit(solution)/shard_map/ppermute | solution.py:40
  24.1 6.5 %collective-permute-start.4 = (bf16[3,32,512]{2,1,0:T(8,128)(2,1)S(1)}, bf16[3,32,512]{2,1,0:T(8,128)(2,1)S(1)}, u32[]{:S(2)}, u32[]{:S(2)}) collective-permute-start(bf16[3,32,512]{2,1,0:T(8,128)(2,1)S(1)} %get-tuple-element.46), channel_id=1, source_target_pairs={{0,8},{1,9},{2,10},{3,11},{4,12},{5,13},{6,14},{7,15},{8,0},{9,1},... | collective-permute-start | bytes 294920 | tf_op jit(solution)/shard_map/ppermute | solution.py:40
  27.0 4.6 %collective-permute-start.5 = (bf16[3,32,512]{2,1,0:T(8,128)(2,1)S(1)}, bf16[3,32,512]{2,1,0:T(8,128)(2,1)S(1)}, u32[]{:S(2)}, u32[]{:S(2)}) collective-permute-start(bf16[3,32,512]{2,1,0:T(8,128)(2,1)S(1)} %get-tuple-element.47), channel_id=1, source_target_pairs={{0,12},{1,13},{2,14},{3,15},{4,0},{5,1},{6,2},{7,3},{8,4},{9,5},{1... | collective-permute-start | bytes 294920 | tf_op jit(solution)/shard_map/ppermute | solution.py:40
  31.6 7.3 %collective-permute-start.6 = (bf16[3,32,512]{2,1,0:T(8,128)(2,1)S(1)}, bf16[3,32,512]{2,1,0:T(8,128)(2,1)S(1)}, u32[]{:S(2)}, u32[]{:S(2)}) collective-permute-start(bf16[3,32,512]{2,1,0:T(8,128)(2,1)S(1)} %shard_map.69.own), channel_id=1, source_target_pairs={{0,48},{1,49},{2,50},{3,51},{4,52},{5,53},{6,54},{7,55},{8,56},{9,... | collective-permute-start | bytes 294920 | tf_op jit(solution)/shard_map/ppermute | solution.py:40
  35.7 6.2 %collective-permute-start.7 = (bf16[3,32,512]{2,1,0:T(8,128)(2,1)S(1)}, bf16[3,32,512]{2,1,0:T(8,128)(2,1)S(1)}, u32[]{:S(2)}, u32[]{:S(2)}) collective-permute-start(bf16[3,32,512]{2,1,0:T(8,128)(2,1)S(1)} %shard_map.69.own), channel_id=1, source_target_pairs={{0,32},{1,33},{2,34},{3,35},{4,36},{5,37},{6,38},{7,39},{8,40},{9,... | collective-permute-start | bytes 294920 | tf_op jit(solution)/shard_map/ppermute | solution.py:40
  35.7 6.9 %collective-permute-start.8 = (bf16[3,32,512]{2,1,0:T(8,128)(2,1)S(1)}, bf16[3,32,512]{2,1,0:T(8,128)(2,1)S(1)}, u32[]{:S(2)}, u32[]{:S(2)}) collective-permute-start(bf16[3,32,512]{2,1,0:T(8,128)(2,1)S(1)} %shard_map.69.own), channel_id=1, source_target_pairs={{0,16},{1,17},{2,18},{3,19},{4,20},{5,21},{6,22},{7,23},{8,24},{9,... | collective-permute-start | bytes 294920 | tf_op jit(solution)/shard_map/ppermute | solution.py:40
  42.7 5.8 %collective-permute-start.9 = (bf16[3,32,512]{2,1,0:T(8,128)(2,1)S(1)}, bf16[3,32,512]{2,1,0:T(8,128)(2,1)S(1)}, u32[]{:S(2)}, u32[]{:S(2)}) collective-permute-start(bf16[3,32,512]{2,1,0:T(8,128)(2,1)S(1)} %get-tuple-element.49.own), channel_id=1, source_target_pairs={{0,12},{1,13},{2,14},{3,15},{4,0},{5,1},{6,2},{7,3},{8,4},{9,5},{1... | collective-permute-start | bytes 294920 | tf_op jit(solution)/shard_map/ppermute | solution.py:40
  45.3 6.2 %collective-permute-start.10 = (bf16[3,32,512]{2,1,0:T(8,128)(2,1)S(1)}, bf16[3,32,512]{2,1,0:T(8,128)(2,1)S(1)}, u32[]{:S(2)}, u32[]{:S(2)}) collective-permute-start(bf16[3,32,512]{2,1,0:T(8,128)(2,1)S(1)} %get-tuple-element.49.own), channel_id=1, source_target_pairs={{0,8},{1,9},{2,10},{3,11},{4,12},{5,13},{6,14},{7,15},{8,0},{9,1},... | collective-permute-start | bytes 294920 | tf_op jit(solution)/shard_map/ppermute | solution.py:40
  45.5 6.9 %collective-permute-start.11 = (bf16[3,32,512]{2,1,0:T(8,128)(2,1)S(1)}, bf16[3,32,512]{2,1,0:T(8,128)(2,1)S(1)}, u32[]{:S(2)}, u32[]{:S(2)}) collective-permute-start(bf16[3,32,512]{2,1,0:T(8,128)(2,1)S(1)} %get-tuple-element.49.own), channel_id=1, source_target_pairs={{0,4},{1,5},{2,6},{3,7},{4,8},{5,9},{6,10},{7,11},{8,12},{9,13},{1... | collective-permute-start | bytes 294920 | tf_op jit(solution)/shard_map/ppermute | solution.py:40
  48.6 3.8 %collective-permute-start.12 = (bf16[16,128]{1,0:T(8,128)(2,1)S(1)}, bf16[16,128]{1,0:T(8,128)(2,1)S(1)}, u32[]{:S(2)}, u32[]{:S(2)}) collective-permute-start(bf16[16,128]{1,0:T(8,128)(2,1)S(1)} %get-tuple-element.51), channel_id=1, source_target_pairs={{0,64},{1,65},{2,66},{3,67},{4,68},{5,69},{6,70},{7,71},{8,72},{9,... | collective-permute-start | bytes 12296 | tf_op jit(solution)/shard_map/ppermute | solution.py:317
  52.4 9.5 %collective-permute-start.13 = (bf16[4,3,32,512]{3,2,1,0:T(8,128)(2,1)S(1)}, bf16[4,3,32,512]{3,2,1,0:T(8,128)(2,1)S(1)}, u32[]{:S(2)}, u32[]{:S(2)}) collective-permute-start(bf16[4,3,32,512]{3,2,1,0:T(8,128)(2,1)S(1)} %shard_map.73.refs_0_), channel_id=1, source_target_pairs={{0,2},{1,3},{2,0},{3,1},{4,6},{5,7},{6,4},{7,5},{8,10},{9,11},{10,... | collective-permute-start | bytes 1179656 | tf_op jit(solution)/shard_map/ppermute | solution.py:40
  53.9 12.6 %collective-permute-start.15 = (bf16[4,3,32,512]{3,2,1,0:T(8,128)(2,1)S(1)}, bf16[4,3,32,512]{3,2,1,0:T(8,128)(2,1)S(1)}, u32[]{:S(2)}, u32[]{:S(2)}) collective-permute-start(bf16[4,3,32,512]{3,2,1,0:T(8,128)(2,1)S(1)} %shard_map.73.refs_0_), channel_id=1, source_target_pairs={{0,3},{1,0},{2,1},{3,2},{4,7},{5,4},{6,5},{7,6},{8,11},{9,8},{10,9... | collective-permute-start | bytes 1179656 | tf_op jit(solution)/shard_map/ppermute | solution.py:40
  56.0 10.6 %collective-permute-start.16 = (bf16[4,3,32,512]{3,2,1,0:T(8,128)(2,1)S(1)}, bf16[4,3,32,512]{3,2,1,0:T(8,128)(2,1)S(1)}, u32[]{:S(2)}, u32[]{:S(2)}) collective-permute-start(bf16[4,3,32,512]{3,2,1,0:T(8,128)(2,1)S(1)} %shard_map.73.refs_0_), channel_id=1, source_target_pairs={{0,1},{1,2},{2,3},{3,0},{4,5},{5,6},{6,7},{7,4},{8,9},{9,10},{10,1... | collective-permute-start | bytes 1179656 | tf_op jit(solution)/shard_map/ppermute | solution.py:40
  64.2 9.4 %collective-permute-start.14 = (bf16[4,3,32,512]{3,2,1,0:T(8,128)(2,1)S(1)}, bf16[4,3,32,512]{3,2,1,0:T(8,128)(2,1)S(1)}, u32[]{:S(2)}, u32[]{:S(2)}) collective-permute-start(bf16[4,3,32,512]{3,2,1,0:T(8,128)(2,1)S(1)} %shard_map.75), channel_id=1, source_target_pairs={{0,2},{1,3},{2,0},{3,1},{4,6},{5,7},{6,4},{7,5},{8,10},{9,11},{10,... | collective-permute-start | bytes 1179656 | tf_op jit(solution)/shard_map/ppermute | solution.py:40
  70.3 9.1 %collective-permute-start.17 = (bf16[4,3,32,512]{3,2,1,0:T(8,128)(2,1)S(1)}, bf16[4,3,32,512]{3,2,1,0:T(8,128)(2,1)S(1)}, u32[]{:S(2)}, u32[]{:S(2)}) collective-permute-start(bf16[4,3,32,512]{3,2,1,0:T(8,128)(2,1)S(1)} %get-tuple-element.55), channel_id=1, source_target_pairs={{0,1},{1,2},{2,3},{3,0},{4,5},{5,6},{6,7},{7,4},{8,9},{9,10},{10,1... | collective-permute-start | bytes 1179656 | tf_op jit(solution)/shard_map/ppermute | solution.py:40
  72.1 7.8 %collective-permute-start.18 = (bf16[4,3,32,512]{3,2,1,0:T(8,128)(2,1)S(1)}, bf16[4,3,32,512]{3,2,1,0:T(8,128)(2,1)S(1)}, u32[]{:S(2)}, u32[]{:S(2)}) collective-permute-start(bf16[4,3,32,512]{3,2,1,0:T(8,128)(2,1)S(1)} %get-tuple-element.56), channel_id=1, source_target_pairs={{0,3},{1,0},{2,1},{3,2},{4,7},{5,4},{6,5},{7,6},{8,11},{9,8},{10,9... | collective-permute-start | bytes 1179656 | tf_op jit(solution)/shard_map/ppermute | solution.py:40
  73.7 39.0 %copy-start = (bf16[2048,512]{1,0:T(8,128)(2,1)S(1)}, bf16[2048,512]{1,0:T(8,128)(2,1)}, u32[]{:S(2)}) copy-start(bf16[2048,512]{1,0:T(8,128)(2,1)} %refs_2_.3) | copy-start | bytes 6291460
  80.0 5.9 %collective-permute-start.19 = (bf16[3,32,512]{2,1,0:T(8,128)(2,1)S(1)}, bf16[3,32,512]{2,1,0:T(8,128)(2,1)S(1)}, u32[]{:S(2)}, u32[]{:S(2)}) collective-permute-start(bf16[3,32,512]{2,1,0:T(8,128)(2,1)S(1)} %get-tuple-element.58), channel_id=1, source_target_pairs={{0,4},{1,5},{2,6},{3,7},{4,8},{5,9},{6,10},{7,11},{8,12},{9,13},{1... | collective-permute-start | bytes 294920 | tf_op jit(solution)/shard_map/ppermute | solution.py:40
  80.1 7.0 %collective-permute-start.20 = (bf16[3,32,512]{2,1,0:T(8,128)(2,1)S(1)}, bf16[3,32,512]{2,1,0:T(8,128)(2,1)S(1)}, u32[]{:S(2)}, u32[]{:S(2)}) collective-permute-start(bf16[3,32,512]{2,1,0:T(8,128)(2,1)S(1)} %get-tuple-element.59), channel_id=1, source_target_pairs={{0,8},{1,9},{2,10},{3,11},{4,12},{5,13},{6,14},{7,15},{8,0},{9,1},... | collective-permute-start | bytes 294920 | tf_op jit(solution)/shard_map/ppermute | solution.py:40
  83.4 4.6 %collective-permute-start.21 = (bf16[3,32,512]{2,1,0:T(8,128)(2,1)S(1)}, bf16[3,32,512]{2,1,0:T(8,128)(2,1)S(1)}, u32[]{:S(2)}, u32[]{:S(2)}) collective-permute-start(bf16[3,32,512]{2,1,0:T(8,128)(2,1)S(1)} %get-tuple-element.60), channel_id=1, source_target_pairs={{0,12},{1,13},{2,14},{3,15},{4,0},{5,1},{6,2},{7,3},{8,4},{9,5},{1... | collective-permute-start | bytes 294920 | tf_op jit(solution)/shard_map/ppermute | solution.py:40
  88.1 4.7 %collective-permute-start.22 = (bf16[3,32,512]{2,1,0:T(8,128)(2,1)S(1)}, bf16[3,32,512]{2,1,0:T(8,128)(2,1)S(1)}, u32[]{:S(2)}, u32[]{:S(2)}) collective-permute-start(bf16[3,32,512]{2,1,0:T(8,128)(2,1)S(1)} %shard_map.79.own), channel_id=1, source_target_pairs={{0,48},{1,49},{2,50},{3,51},{4,52},{5,53},{6,54},{7,55},{8,56},{9,... | collective-permute-start | bytes 294920 | tf_op jit(solution)/shard_map/ppermute | solution.py:40
  89.1 6.2 %collective-permute-start.23 = (bf16[3,32,512]{2,1,0:T(8,128)(2,1)S(1)}, bf16[3,32,512]{2,1,0:T(8,128)(2,1)S(1)}, u32[]{:S(2)}, u32[]{:S(2)}) collective-permute-start(bf16[3,32,512]{2,1,0:T(8,128)(2,1)S(1)} %shard_map.79.own), channel_id=1, source_target_pairs={{0,32},{1,33},{2,34},{3,35},{4,36},{5,37},{6,38},{7,39},{8,40},{9,... | collective-permute-start | bytes 294920 | tf_op jit(solution)/shard_map/ppermute | solution.py:40
  89.5 6.7 %collective-permute-start.24 = (bf16[3,32,512]{2,1,0:T(8,128)(2,1)S(1)}, bf16[3,32,512]{2,1,0:T(8,128)(2,1)S(1)}, u32[]{:S(2)}, u32[]{:S(2)}) collective-permute-start(bf16[3,32,512]{2,1,0:T(8,128)(2,1)S(1)} %shard_map.79.own), channel_id=1, source_target_pairs={{0,16},{1,17},{2,18},{3,19},{4,20},{5,21},{6,22},{7,23},{8,24},{9,... | collective-permute-start | bytes 294920 | tf_op jit(solution)/shard_map/ppermute | solution.py:40
  96.3 2.2 %collective-permute-start.25 = (bf16[3,32,512]{2,1,0:T(8,128)(2,1)S(1)}, bf16[3,32,512]{2,1,0:T(8,128)(2,1)S(1)}, u32[]{:S(2)}, u32[]{:S(2)}) collective-permute-start(bf16[3,32,512]{2,1,0:T(8,128)(2,1)S(1)} %get-tuple-element.61), channel_id=1, source_target_pairs={{0,64},{1,65},{2,66},{3,67},{4,68},{5,69},{6,70},{7,71},{8,72},{9,... | collective-permute-start | bytes 294920 | tf_op jit(solution)/shard_map/ppermute | solution.py:374
  98.6 5.8 %collective-permute-start.26 = (bf16[3,32,512]{2,1,0:T(8,128)(2,1)S(1)}, bf16[3,32,512]{2,1,0:T(8,128)(2,1)S(1)}, u32[]{:S(2)}, u32[]{:S(2)}) collective-permute-start(bf16[3,32,512]{2,1,0:T(8,128)(2,1)S(1)} %shard_map.81.own), channel_id=1, source_target_pairs={{0,12},{1,13},{2,14},{3,15},{4,0},{5,1},{6,2},{7,3},{8,4},{9,5},{1... | collective-permute-start | bytes 294920 | tf_op jit(solution)/shard_map/ppermute | solution.py:40
  101.1 6.2 %collective-permute-start.27 = (bf16[3,32,512]{2,1,0:T(8,128)(2,1)S(1)}, bf16[3,32,512]{2,1,0:T(8,128)(2,1)S(1)}, u32[]{:S(2)}, u32[]{:S(2)}) collective-permute-start(bf16[3,32,512]{2,1,0:T(8,128)(2,1)S(1)} %shard_map.81.own), channel_id=1, source_target_pairs={{0,8},{1,9},{2,10},{3,11},{4,12},{5,13},{6,14},{7,15},{8,0},{9,1},... | collective-permute-start | bytes 294920 | tf_op jit(solution)/shard_map/ppermute | solution.py:40
  101.5 6.8 %collective-permute-start.28 = (bf16[3,32,512]{2,1,0:T(8,128)(2,1)S(1)}, bf16[3,32,512]{2,1,0:T(8,128)(2,1)S(1)}, u32[]{:S(2)}, u32[]{:S(2)}) collective-permute-start(bf16[3,32,512]{2,1,0:T(8,128)(2,1)S(1)} %shard_map.81.own), channel_id=1, source_target_pairs={{0,4},{1,5},{2,6},{3,7},{4,8},{5,9},{6,10},{7,11},{8,12},{9,13},{1... | collective-permute-start | bytes 294920 | tf_op jit(solution)/shard_map/ppermute | solution.py:40
  108.3 9.5 %collective-permute-start.31 = (bf16[4,3,32,512]{3,2,1,0:T(8,128)(2,1)S(1)}, bf16[4,3,32,512]{3,2,1,0:T(8,128)(2,1)S(1)}, u32[]{:S(2)}, u32[]{:S(2)}) collective-permute-start(bf16[4,3,32,512]{3,2,1,0:T(8,128)(2,1)S(1)} %shard_map.82.refs_0_), channel_id=1, source_target_pairs={{0,2},{1,3},{2,0},{3,1},{4,6},{5,7},{6,4},{7,5},{8,10},{9,11},{10,... | collective-permute-start | bytes 1179656 | tf_op jit(solution)/shard_map/ppermute | solution.py:40
  110.7 11.2 %collective-permute-start.29 = (bf16[4,3,32,512]{3,2,1,0:T(8,128)(2,1)S(1)}, bf16[4,3,32,512]{3,2,1,0:T(8,128)(2,1)S(1)}, u32[]{:S(2)}, u32[]{:S(2)}) collective-permute-start(bf16[4,3,32,512]{3,2,1,0:T(8,128)(2,1)S(1)} %shard_map.82.refs_0_), channel_id=1, source_target_pairs={{0,3},{1,0},{2,1},{3,2},{4,7},{5,4},{6,5},{7,6},{8,11},{9,8},{10,9... | collective-permute-start | bytes 1179656 | tf_op jit(solution)/shard_map/ppermute | solution.py:40
  111.3 10.6 %collective-permute-start.30 = (bf16[4,3,32,512]{3,2,1,0:T(8,128)(2,1)S(1)}, bf16[4,3,32,512]{3,2,1,0:T(8,128)(2,1)S(1)}, u32[]{:S(2)}, u32[]{:S(2)}) collective-permute-start(bf16[4,3,32,512]{3,2,1,0:T(8,128)(2,1)S(1)} %shard_map.82.refs_0_), channel_id=1, source_target_pairs={{0,1},{1,2},{2,3},{3,0},{4,5},{5,6},{6,7},{7,4},{8,9},{9,10},{10,1... | collective-permute-start | bytes 1179656 | tf_op jit(solution)/shard_map/ppermute | solution.py:40
  114.3 7.6 %copy-start.1 = (f32[512]{0:T(512)S(1)}, f32[512]{0:T(512)}, u32[]{:S(2)}) copy-start(f32[512]{0:T(512)} %param.11) | copy-start | bytes 6148

commit v6 on v5

--- a/solution.py
+++ b/solution.py
@@ -75,14 +75,17 @@
             sem = sems.at[len(copies) // sems.shape[1], j]
             copies.append(pltpu.make_async_copy(src.at[part], dst.at[part], sem))
             copies[-1].start()
-    for copy in copies[: sems.shape[1]]:
-        copy.wait()
     width = w_ref.shape[0]
     lines = width // (SIDE * SIDE)
-    for m in range(2):
-        part = w_ref[:, m * width : (m + 1) * width].astype(BF)
-        turned[m] = part.T.reshape(SIDE * SIDE, lines, width)
-    turned[2] = w_ref[:, 2 * width :].astype(BF).reshape(SIDE * SIDE, lines, width)
+    rows = width // sems.shape[1]
+    for j, copy in enumerate(copies[: sems.shape[1]]):
+        copy.wait()
+        part = slice(j * rows, (j + 1) * rows)
+        for m in range(2):
+            piece = w_ref[part, m * width : (m + 1) * width].astype(BF)
+            turned[m, :, :, part] = piece.T.reshape(SIDE * SIDE, lines, rows)
+        piece = w_ref[part, 2 * width :].astype(BF)
+        turned[2, j * rows // lines : (j + 1) * rows // lines] = piece.reshape(-1, lines, width)
     for r, block in enumerate((b0, b1, b2, b3)):
         for s in range(SIDE):
             group = place[r * SIDE + s]
@@ -175,8 +178,9 @@
     change_bf[...] = value.astype(BF)
 
 
-def closing_kernel(start, earlier, change, out):
-    out[...] = ((start[...] + earlier[...].astype(F32)) + change[...]).astype(BF)
+def closing_kernel(group, start, other, change, out):
+    earlier = jnp.where(group[0] > 0, other[...].astype(F32), 0.0)
+    out[...] = ((start[...] + earlier) + change[...]).astype(BF)
 
 
 def join_all_kernel(own, r1, r2, r3, out):
@@ -226,7 +230,7 @@
         copy.wait()
 
 
-def apply_blocks(weights, queries, so_far, gain, tile=256):
+def apply_blocks(weights, queries, so_far, gain, tile=512):
     count = len(weights)
     units = count * weights[0].shape[0] * weights[0].shape[2]
     tokens, width = queries.shape
@@ -303,7 +307,8 @@
 
 
 def order_pairs():
-    return [(flat(0, *c), flat(1, *c)) for c in itertools.product(*[range(SIDE)] * 3)]
+    places = list(itertools.product(range(2), *[range(SIDE)] * 3))
+    return [(flat(core, *c), flat(1 - core, *c)) for core, *c in places]
 
 
 def gathered(shard, in_step):
@@ -371,8 +376,15 @@
         (start, first_step, *parts),
         (size, 8 * size),
     )
-    earlier = lax.ppermute(change_bf, AXES, order_pairs())
-    closing = call(closing_kernel, arr(shard, BF), None, (start, earlier, change), (size, 8 * size))
+    other = lax.ppermute(change_bf, AXES, order_pairs())
+    group = core.reshape(1).astype(jnp.int32)
+    closing = call(
+        closing_kernel,
+        arr(shard, BF),
+        [SMEM] + [VMEM] * 3,
+        (group, start, other, change),
+        (size, 8 * size),
+    )
     return applied(closing, queries, gain)
 
 

time: 126 us -> 125 us (level)
  starting transfers between devices: 47.3 us -> 45.6 us
  transfers between devices with their start and end apart: 32 -> 32, of which waited for: 25 -> 24; matrix products, arithmetic and copies ran while one was open for 0% -> 0% of each run, Pallas kernels for 14% -> 15%
where the time goes in v6:
time: 125 us; the launch traced here: 124 us
  waiting for transfers between devices  50.8 us (41%)
  starting transfers between devices  45.6 us (36%)
  Pallas kernels  27.5 us (22%)
    ppermute x30, waiting for transfers between devices, hop(): return lax.ppermute(x, AXES, hop_pairs(level, step % SIDE))  49.5 us
    ppermute x30, starting transfers between devices, hop(): return lax.ppermute(x, AXES, hop_pairs(level, step % SIDE))  45.4 us
    pallas_call x22, Pallas kernels, call(): pl.pallas_call(kernel, out_shape=outs, in_specs=specs or [VMEM] * len(arg...  27.5 us
  transfers between devices with their start and end apart: 32, of which 24 were waited for; matrix products, arithmetic and copies ran while one was open for 0% of the time, Pallas kernels for 15%

profile of v6, /device:TPU:0, one launch (start us, length us, event | category | flops | bytes accessed | tf_op | source)
XLA Modules:
  0.0 124.5 jit_solution(16660892277002242759)
XLA Ops:
  0.2 6.1 %shard_map.64 = (bf16[2048,512]{1,0:T(8,128)(2,1)S(1)}, bf16[2048,512]{1,0:T(8,128)(2,1)S(1)}, f32[1,2048]{1,0:T(1,128)S(1)}, bf16[4,3,32,512]{3,2,1,0:T(8,128)(...) custom-call(s32[16]{0:T(128)S(1)} %fusion.place, ...), custom_call_target="tpu_custom_call" | custom-call | flops 1610612736 | bytes 4194304 | tf_op jit(solution)/shard_map/pallas_call | solution.py:49
  6.3 3.2 %collective-permute-start = (bf16[4,3,32,512]{3,2,1,0:T(8,128)(2,1)S(1)}, bf16[4,3,32,512]{3,2,1,0:T(8,128)(2,1)S(1)}, u32[]{:S(2)}, u32[]{:S(2)}) collective-permute-start(bf16[4,3,32,512]{3,2,1,0:T(8,128)(2,1)S(1)} %get-tuple-element.39), channel_id=1, source_target_pairs={{0,2},{1,3},{2,0},{3,1},{4,6},{5,7},{6,4},{7,5},{8,10},{9,11},{10,... | collective-permute-start | bytes 1179656 | tf_op jit(solution)/shard_map/ppermute | solution.py:40
  9.5 3.7 %shard_map.67 = (bf16[4,3,32,512]{3,2,1,0:T(8,128)(2,1)S(1)}, bf16[4,3,32,512]{3,2,1,0:T(8,128)(2,1)S(1)}) custom-call(bf16[4,3,32,512]{3,2,1,0:T(8,128)(2,1)S(1)} %get-tuple-element.40.refs_0_, bf16[4,3,32,512]{3,2,1,0:T(8,128)(2,1)S(1)} %get-tuple-element.41.refs_1_, bf16[2048,512]{1,0:T(8,128)(2,1)S(1)} %get-tuple-element.54.refs_1_.refs_2_, ...), custom_call_target="tpu_custom_call" | custom-call | flops 3221225472 | bytes 4194304 | tf_op jit(solution)/shard_map/pallas_call | solution.py:49
  13.2 0.7 collective-permute-start.1
  13.9 2.6 %collective-permute-start.2 = (bf16[4,3,32,512]{3,2,1,0:T(8,128)(2,1)S(1)}, bf16[4,3,32,512]{3,2,1,0:T(8,128)(2,1)S(1)}, u32[]{:S(2)}, u32[]{:S(2)}) collective-permute-start(bf16[4,3,32,512]{3,2,1,0:T(8,128)(2,1)S(1)} %get-tuple-element.43), channel_id=1, source_target_pairs={{0,3},{1,0},{2,1},{3,2},{4,7},{5,4},{6,5},{7,6},{8,11},{9,8},{10,9... | collective-permute-start | bytes 1179656 | tf_op jit(solution)/shard_map/ppermute | solution.py:40
  16.5 2.3 %shard_map.65.own = f32[4,3,32,512]{3,2,1,0:T(8,128)S(1)} custom-call(bf16[4,3,32,512]{3,2,1,0:T(8,128)(2,1)S(1)} %get-tuple-element.35.refs_0_, bf16[2048,512]{1,0:T(8,128)(2,1)S(1)} %get-tuple-element.54.refs_1_.refs_2_, bf16[2048,512]{1,0:T(8,128)(2,1)S(1)} %get-tuple-element.37.refs_2_.refs_3_, f32[1,2048]{1,0:T(1,128)S(1)} %get-tuple-element.38.refs_3_.refs_4_), custom_call_target="tpu_custom_call" | custom-call | flops 1610612736 | bytes 4194304 | tf_op jit(solution)/shard_map/pallas_call | solution.py:49
  18.9 3.4 %collective-permute-done.1.r1 = bf16[4,3,32,512]{3,2,1,0:T(8,128)(2,1)S(1)} collective-permute-done((bf16[4,3,32,512]{3,2,1,0:T(8,128)(2,1)S(1)}, bf16[4,3,32,512]{3,2,1,0:T(8,128)(2,1)S(1)}, u32[]{:S(2)}, u32[]{:S(2)}) %collective-permute-start.1) | collective-permute-done | bytes 393248 | tf_op jit(solution)/shard_map/ppermute | solution.py:40
  22.3 0.1 shard_map.68
  22.4 1.7 %collective-permute-start.3 = (bf16[3,32,512]{2,1,0:T(8,128)(2,1)S(1)}, bf16[3,32,512]{2,1,0:T(8,128)(2,1)S(1)}, u32[]{:S(2)}, u32[]{:S(2)}) collective-permute-start(bf16[3,32,512]{2,1,0:T(8,128)(2,1)S(1)} %get-tuple-element.45), channel_id=1, source_target_pairs={{0,4},{1,5},{2,6},{3,7},{4,8},{5,9},{6,10},{7,11},{8,12},{9,13},{1... | collective-permute-start | bytes 294920 | tf_op jit(solution)/shard_map/ppermute | solution.py:40
  24.1 2.9 %collective-permute-start.4 = (bf16[3,32,512]{2,1,0:T(8,128)(2,1)S(1)}, bf16[3,32,512]{2,1,0:T(8,128)(2,1)S(1)}, u32[]{:S(2)}, u32[]{:S(2)}) collective-permute-start(bf16[3,32,512]{2,1,0:T(8,128)(2,1)S(1)} %get-tuple-element.46), channel_id=1, source_target_pairs={{0,8},{1,9},{2,10},{3,11},{4,12},{5,13},{6,14},{7,15},{8,0},{9,1},... | collective-permute-start | bytes 294920 | tf_op jit(solution)/shard_map/ppermute | solution.py:40
  27.0 1.3 %collective-permute-start.5 = (bf16[3,32,512]{2,1,0:T(8,128)(2,1)S(1)}, bf16[3,32,512]{2,1,0:T(8,128)(2,1)S(1)}, u32[]{:S(2)}, u32[]{:S(2)}) collective-permute-start(bf16[3,32,512]{2,1,0:T(8,128)(2,1)S(1)} %get-tuple-element.47), channel_id=1, source_target_pairs={{0,12},{1,13},{2,14},{3,15},{4,0},{5,1},{6,2},{7,3},{8,4},{9,5},{1... | collective-permute-start | bytes 294920 | tf_op jit(solution)/shard_map/ppermute | solution.py:40
  28.3 2.3 %collective-permute-done.4.r2 = bf16[3,32,512]{2,1,0:T(8,128)(2,1)S(1)} collective-permute-done((bf16[3,32,512]{2,1,0:T(8,128)(2,1)S(1)}, bf16[3,32,512]{2,1,0:T(8,128)(2,1)S(1)}, u32[]{:S(2)}, u32[]{:S(2)}) %collective-permute-start.4) | collective-permute-done | bytes 98336 | tf_op jit(solution)/shard_map/ppermute | solution.py:40
  30.6 1.0 collective-permute-done.5.r3
  31.6 4.1 %collective-permute-start.6 = (bf16[3,32,512]{2,1,0:T(8,128)(2,1)S(1)}, bf16[3,32,512]{2,1,0:T(8,128)(2,1)S(1)}, u32[]{:S(2)}, u32[]{:S(2)}) collective-permute-start(bf16[3,32,512]{2,1,0:T(8,128)(2,1)S(1)} %shard_map.69.own), channel_id=1, source_target_pairs={{0,48},{1,49},{2,50},{3,51},{4,52},{5,53},{6,54},{7,55},{8,56},{9,... | collective-permute-start | bytes 294920 | tf_op jit(solution)/shard_map/ppermute | solution.py:40
  35.7 1.3 %collective-permute-start.8 = (bf16[3,32,512]{2,1,0:T(8,128)(2,1)S(1)}, bf16[3,32,512]{2,1,0:T(8,128)(2,1)S(1)}, u32[]{:S(2)}, u32[]{:S(2)}) collective-permute-start(bf16[3,32,512]{2,1,0:T(8,128)(2,1)S(1)} %shard_map.69.own), channel_id=1, source_target_pairs={{0,16},{1,17},{2,18},{3,19},{4,20},{5,21},{6,22},{7,23},{8,24},{9,... | collective-permute-start | bytes 294920 | tf_op jit(solution)/shard_map/ppermute | solution.py:40
  37.0 2.0 %collective-permute-done.6.r1 = bf16[3,32,512]{2,1,0:T(8,128)(2,1)S(1)} collective-permute-done((bf16[3,32,512]{2,1,0:T(8,128)(2,1)S(1)}, bf16[3,32,512]{2,1,0:T(8,128)(2,1)S(1)}, u32[]{:S(2)}, u32[]{:S(2)}) %collective-permute-start.6) | collective-permute-done | bytes 98336 | tf_op jit(solution)/shard_map/ppermute | solution.py:40
  39.0 3.0 %collective-permute-done.7.r2 = bf16[3,32,512]{2,1,0:T(8,128)(2,1)S(1)} collective-permute-done((bf16[3,32,512]{2,1,0:T(8,128)(2,1)S(1)}, bf16[3,32,512]{2,1,0:T(8,128)(2,1)S(1)}, u32[]{:S(2)}, u32[]{:S(2)}) %collective-permute-start.7) | collective-permute-done | bytes 98336 | tf_op jit(solution)/shard_map/ppermute | solution.py:40
  42.0 0.7 collective-permute-done.8.r3
  42.7 2.6 %collective-permute-start.9 = (bf16[3,32,512]{2,1,0:T(8,128)(2,1)S(1)}, bf16[3,32,512]{2,1,0:T(8,128)(2,1)S(1)}, u32[]{:S(2)}, u32[]{:S(2)}) collective-permute-start(bf16[3,32,512]{2,1,0:T(8,128)(2,1)S(1)} %get-tuple-element.49.own), channel_id=1, source_target_pairs={{0,12},{1,13},{2,14},{3,15},{4,0},{5,1},{6,2},{7,3},{8,4},{9,5},{1... | collective-permute-start | bytes 294920 | tf_op jit(solution)/shard_map/ppermute | solution.py:40
  45.3 0.2 collective-permute-start.10
  45.5 0.8 collective-permute-start.11
  46.3 2.3 %collective-permute-done.9.part = bf16[3,32,512]{2,1,0:T(8,128)(2,1)S(1)} collective-permute-done((bf16[3,32,512]{2,1,0:T(8,128)(2,1)S(1)}, bf16[3,32,512]{2,1,0:T(8,128)(2,1)S(1)}, u32[]{:S(2)}, u32[]{:S(2)}) %collective-permute-start.9) | collective-permute-done | bytes 98336 | tf_op jit(solution)/shard_map/ppermute | solution.py:40
  48.6 0.1 collective-permute-start.12
  48.7 2.9 %collective-permute-done.10.part = bf16[3,32,512]{2,1,0:T(8,128)(2,1)S(1)} collective-permute-done((bf16[3,32,512]{2,1,0:T(8,128)(2,1)S(1)}, bf16[3,32,512]{2,1,0:T(8,128)(2,1)S(1)}, u32[]{:S(2)}, u32[]{:S(2)}) %collective-permute-start.10) | collective-permute-done | bytes 98336 | tf_op jit(solution)/shard_map/ppermute | solution.py:40
  51.6 0.8 collective-permute-done.11.part
  52.4 1.7 %collective-permute-start.13 = (bf16[4,3,32,512]{3,2,1,0:T(8,128)(2,1)S(1)}, bf16[4,3,32,512]{3,2,1,0:T(8,128)(2,1)S(1)}, u32[]{:S(2)}, u32[]{:S(2)}) collective-permute-start(bf16[4,3,32,512]{3,2,1,0:T(8,128)(2,1)S(1)} %shard_map.73.refs_0_), channel_id=1, source_target_pairs={{0,2},{1,3},{2,0},{3,1},{4,6},{5,7},{6,4},{7,5},{8,10},{9,11},{10,... | collective-permute-start | bytes 1179656 | tf_op jit(solution)/shard_map/ppermute | solution.py:40
  54.1 1.9 %collective-permute-start.15 = (bf16[4,3,32,512]{3,2,1,0:T(8,128)(2,1)S(1)}, bf16[4,3,32,512]{3,2,1,0:T(8,128)(2,1)S(1)}, u32[]{:S(2)}, u32[]{:S(2)}) collective-permute-start(bf16[4,3,32,512]{3,2,1,0:T(8,128)(2,1)S(1)} %shard_map.73.refs_0_), channel_id=1, source_target_pairs={{0,3},{1,0},{2,1},{3,2},{4,7},{5,4},{6,5},{7,6},{8,11},{9,8},{10,9... | collective-permute-start | bytes 1179656 | tf_op jit(solution)/shard_map/ppermute | solution.py:40
  56.0 0.8 collective-permute-start.16
  56.8 2.3 %shard_map.74.own = f32[4,3,32,512]{3,2,1,0:T(8,128)S(1)} custom-call(bf16[4,3,32,512]{3,2,1,0:T(8,128)(2,1)S(1)} %shard_map.73.refs_0_, bf16[2048,512]{1,0:T(8,128)(2,1)S(1)} %get-tuple-element.54.refs_1_.refs_2_, bf16[2048,512]{1,0:T(8,128)(2,1)S(1)} %get-tuple-element.37.refs_2_.refs_3_, f32[1,2048]{1,0:T(1,128)S(1)} %get-tuple-element.38.refs_3_.refs_4_), custom_call_target="tpu_custom_call" | custom-call | flops 1610612736 | bytes 4194304 | tf_op jit(solution)/shard_map/pallas_call | solution.py:49
  59.1 2.9 %collective-permute-done.13.refs_0_ = bf16[4,3,32,512]{3,2,1,0:T(8,128)(2,1)S(1)} collective-permute-done((bf16[4,3,32,512]{3,2,1,0:T(8,128)(2,1)S(1)}, bf16[4,3,32,512]{3,2,1,0:T(8,128)(2,1)S(1)}, u32[]{:S(2)}, u32[]{:S(2)}) %collective-permute-start.13) | collective-permute-done | bytes 393248 | tf_op jit(solution)/shard_map/ppermute | solution.py:40
  62.0 2.3 %shard_map.75 = bf16[4,3,32,512]{3,2,1,0:T(8,128)(2,1)S(1)} custom-call(bf16[4,3,32,512]{3,2,1,0:T(8,128)(2,1)S(1)} %collective-permute-done.13.refs_0_, bf16[2048,512]{1,0:T(8,128)(2,1)S(1)} %get-tuple-element.54.refs_1_.refs_2_, bf16[2048,512]{1,0:T(8,128)(2,1)S(1)} %get-tuple-element.37.refs_2_.refs_3_, f32[1,2048]{1,0:T(1,128)S(1)} %get-tuple-element.38.refs_3_.refs_4_), custom_call_target="tpu_custom_call" | custom-call | flops 1610612736 | bytes 4194304 | tf_op jit(solution)/shard_map/pallas_call | solution.py:49
  64.4 1.5 %collective-permute-start.14 = (bf16[4,3,32,512]{3,2,1,0:T(8,128)(2,1)S(1)}, bf16[4,3,32,512]{3,2,1,0:T(8,128)(2,1)S(1)}, u32[]{:S(2)}, u32[]{:S(2)}) collective-permute-start(bf16[4,3,32,512]{3,2,1,0:T(8,128)(2,1)S(1)} %shard_map.75), channel_id=1, source_target_pairs={{0,2},{1,3},{2,0},{3,1},{4,6},{5,7},{6,4},{7,5},{8,10},{9,11},{10,... | collective-permute-start | bytes 1179656 | tf_op jit(solution)/shard_map/ppermute | solution.py:40
  65.9 0.8 collective-permute-done.15.refs_0_
  66.8 3.7 %shard_map.77 = (bf16[4,3,32,512]{3,2,1,0:T(8,128)(2,1)S(1)}, bf16[4,3,32,512]{3,2,1,0:T(8,128)(2,1)S(1)}) custom-call(bf16[4,3,32,512]{3,2,1,0:T(8,128)(2,1)S(1)} %collective-permute-done.15.refs_0_, bf16[4,3,32,512]{3,2,1,0:T(8,128)(2,1)S(1)} %collective-permute-done.16.refs_1_, bf16[2048,512]{1,0:T(8,128)(2,1)S(1)} %get-tuple-element.54.refs_1_.refs_2_, ...), custom_call_target="tpu_custom_call" | custom-call | flops 3221225472 | bytes 4194304 | tf_op jit(solution)/shard_map/pallas_call | solution.py:49
  70.5 1.9 %collective-permute-start.17 = (bf16[4,3,32,512]{3,2,1,0:T(8,128)(2,1)S(1)}, bf16[4,3,32,512]{3,2,1,0:T(8,128)(2,1)S(1)}, u32[]{:S(2)}, u32[]{:S(2)}) collective-permute-start(bf16[4,3,32,512]{3,2,1,0:T(8,128)(2,1)S(1)} %get-tuple-element.55), channel_id=1, source_target_pairs={{0,1},{1,2},{2,3},{3,0},{4,5},{5,6},{6,7},{7,4},{8,9},{9,10},{10,1... | collective-permute-start | bytes 1179656 | tf_op jit(solution)/shard_map/ppermute | solution.py:40
  72.3 1.4 %collective-permute-start.18 = (bf16[4,3,32,512]{3,2,1,0:T(8,128)(2,1)S(1)}, bf16[4,3,32,512]{3,2,1,0:T(8,128)(2,1)S(1)}, u32[]{:S(2)}, u32[]{:S(2)}) collective-permute-start(bf16[4,3,32,512]{3,2,1,0:T(8,128)(2,1)S(1)} %get-tuple-element.56), channel_id=1, source_target_pairs={{0,3},{1,0},{2,1},{3,2},{4,7},{5,4},{6,5},{7,6},{8,11},{9,8},{10,9... | collective-permute-start | bytes 1179656 | tf_op jit(solution)/shard_map/ppermute | solution.py:40
  73.8 5.7 %collective-permute-done.17.r1 = bf16[4,3,32,512]{3,2,1,0:T(8,128)(2,1)S(1)} collective-permute-done((bf16[4,3,32,512]{3,2,1,0:T(8,128)(2,1)S(1)}, bf16[4,3,32,512]{3,2,1,0:T(8,128)(2,1)S(1)}, u32[]{:S(2)}, u32[]{:S(2)}) %collective-permute-start.17) | collective-permute-done | bytes 393248 | tf_op jit(solution)/shard_map/ppermute | solution.py:40
  79.5 0.6 collective-permute-done.18.r3
  80.1 0.1 shard_map.78
  80.3 2.5 %collective-permute-start.20 = (bf16[3,32,512]{2,1,0:T(8,128)(2,1)S(1)}, bf16[3,32,512]{2,1,0:T(8,128)(2,1)S(1)}, u32[]{:S(2)}, u32[]{:S(2)}) collective-permute-start(bf16[3,32,512]{2,1,0:T(8,128)(2,1)S(1)} %get-tuple-element.59), channel_id=1, source_target_pairs={{0,8},{1,9},{2,10},{3,11},{4,12},{5,13},{6,14},{7,15},{8,0},{9,1},... | collective-permute-start | bytes 294920 | tf_op jit(solution)/shard_map/ppermute | solution.py:40
  82.8 1.2 collective-permute-start.21
  84.0 3.2 %collective-permute-done.19.r1 = bf16[3,32,512]{2,1,0:T(8,128)(2,1)S(1)} collective-permute-done((bf16[3,32,512]{2,1,0:T(8,128)(2,1)S(1)}, bf16[3,32,512]{2,1,0:T(8,128)(2,1)S(1)}, u32[]{:S(2)}, u32[]{:S(2)}) %collective-permute-start.19) | collective-permute-done | bytes 98336 | tf_op jit(solution)/shard_map/ppermute | solution.py:40
  87.2 0.9 collective-permute-done.21.r3
  88.1 1.0 collective-permute-start.22
  89.0 0.5 collective-permute-start.23
  89.5 1.3 %collective-permute-start.24 = (bf16[3,32,512]{2,1,0:T(8,128)(2,1)S(1)}, bf16[3,32,512]{2,1,0:T(8,128)(2,1)S(1)}, u32[]{:S(2)}, u32[]{:S(2)}) collective-permute-start(bf16[3,32,512]{2,1,0:T(8,128)(2,1)S(1)} %shard_map.79.own), channel_id=1, source_target_pairs={{0,16},{1,17},{2,18},{3,19},{4,20},{5,21},{6,22},{7,23},{8,24},{9,... | collective-permute-start | bytes 294920 | tf_op jit(solution)/shard_map/ppermute | solution.py:40
  90.8 1.9 %collective-permute-done.22.r1 = bf16[3,32,512]{2,1,0:T(8,128)(2,1)S(1)} collective-permute-done((bf16[3,32,512]{2,1,0:T(8,128)(2,1)S(1)}, bf16[3,32,512]{2,1,0:T(8,128)(2,1)S(1)}, u32[]{:S(2)}, u32[]{:S(2)}) %collective-permute-start.22) | collective-permute-done | bytes 98336 | tf_op jit(solution)/shard_map/ppermute | solution.py:40
  92.8 2.5 %collective-permute-done.23.r2 = bf16[3,32,512]{2,1,0:T(8,128)(2,1)S(1)} collective-permute-done((bf16[3,32,512]{2,1,0:T(8,128)(2,1)S(1)}, bf16[3,32,512]{2,1,0:T(8,128)(2,1)S(1)}, u32[]{:S(2)}, u32[]{:S(2)}) %collective-permute-start.23) | collective-permute-done | bytes 98336 | tf_op jit(solution)/shard_map/ppermute | solution.py:40
  95.2 1.0 collective-permute-done.24.r3
  96.4 1.3 %collective-permute-done.25.other = bf16[3,32,512]{2,1,0:T(8,128)(2,1)S(1)} collective-permute-done((bf16[3,32,512]{2,1,0:T(8,128)(2,1)S(1)}, bf16[3,32,512]{2,1,0:T(8,128)(2,1)S(1)}, u32[]{:S(2)}, u32[]{:S(2)}) %collective-permute-start.25) | collective-permute-done | bytes 98336 | tf_op jit(solution)/shard_map/ppermute | solution.py:379
  97.7 2.7 %collective-permute-start.26 = (bf16[3,32,512]{2,1,0:T(8,128)(2,1)S(1)}, bf16[3,32,512]{2,1,0:T(8,128)(2,1)S(1)}, u32[]{:S(2)}, u32[]{:S(2)}) collective-permute-start(bf16[3,32,512]{2,1,0:T(8,128)(2,1)S(1)} %shard_map.81.own), channel_id=1, source_target_pairs={{0,12},{1,13},{2,14},{3,15},{4,0},{5,1},{6,2},{7,3},{8,4},{9,5},{1... | collective-permute-start | bytes 294920 | tf_op jit(solution)/shard_map/ppermute | solution.py:40
  100.5 0.4 collective-permute-start.27
  100.8 0.6 collective-permute-start.28
  101.4 2.3 %collective-permute-done.26.r1 = bf16[3,32,512]{2,1,0:T(8,128)(2,1)S(1)} collective-permute-done((bf16[3,32,512]{2,1,0:T(8,128)(2,1)S(1)}, bf16[3,32,512]{2,1,0:T(8,128)(2,1)S(1)}, u32[]{:S(2)}, u32[]{:S(2)}) %collective-permute-start.26) | collective-permute-done | bytes 98336 | tf_op jit(solution)/shard_map/ppermute | solution.py:40
  103.7 3.0 %collective-permute-done.27.r2 = bf16[3,32,512]{2,1,0:T(8,128)(2,1)S(1)} collective-permute-done((bf16[3,32,512]{2,1,0:T(8,128)(2,1)S(1)}, bf16[3,32,512]{2,1,0:T(8,128)(2,1)S(1)}, u32[]{:S(2)}, u32[]{:S(2)}) %collective-permute-start.27) | collective-permute-done | bytes 98336 | tf_op jit(solution)/shard_map/ppermute | solution.py:40
  106.7 0.9 collective-permute-done.28.r3
  107.7 2.6 %collective-permute-start.31 = (bf16[4,3,32,512]{3,2,1,0:T(8,128)(2,1)S(1)}, bf16[4,3,32,512]{3,2,1,0:T(8,128)(2,1)S(1)}, u32[]{:S(2)}, u32[]{:S(2)}) collective-permute-start(bf16[4,3,32,512]{3,2,1,0:T(8,128)(2,1)S(1)} %shard_map.82.refs_0_), channel_id=1, source_target_pairs={{0,2},{1,3},{2,0},{3,1},{4,6},{5,7},{6,4},{7,5},{8,10},{9,11},{10,... | collective-permute-start | bytes 1179656 | tf_op jit(solution)/shard_map/ppermute | solution.py:40
  110.3 1.1 collective-permute-start.29
  111.4 0.9 collective-permute-start.30
  112.3 1.8 %shard_map.83.refs_2_ = f32[2048,512]{1,0:T(8,128)S(1)} custom-call(bf16[4,3,32,512]{3,2,1,0:T(8,128)(2,1)S(1)} %shard_map.82.refs_0_, bf16[2048,512]{1,0:T(8,128)(2,1)S(1)} %copy-done), custom_call_target="tpu_custom_call" | custom-call | flops 805306368 | bytes 6291456 | tf_op jit(solution)/shard_map/pallas_call | solution.py:49
  114.1 3.3 %collective-permute-done.31.refs_0_ = bf16[4,3,32,512]{3,2,1,0:T(8,128)(2,1)S(1)} collective-permute-done((bf16[4,3,32,512]{3,2,1,0:T(8,128)(2,1)S(1)}, bf16[4,3,32,512]{3,2,1,0:T(8,128)(2,1)S(1)}, u32[]{:S(2)}, u32[]{:S(2)}) %collective-permute-start.31) | collective-permute-done | bytes 393248 | tf_op jit(solution)/shard_map/ppermute | solution.py:40
  117.4 1.8 %shard_map.84.refs_4_ = f32[2048,512]{1,0:T(8,128)S(1)} custom-call(bf16[4,3,32,512]{3,2,1,0:T(8,128)(2,1)S(1)} %collective-permute-done.31.refs_0_, bf16[2048,512]{1,0:T(8,128)(2,1)S(1)} %copy-done, f32[2048,512]{1,0:T(8,128)S(1)} %shard_map.83.refs_2_), custom_call_target="tpu_custom_call" | custom-call | flops 805306368 | bytes 6291456 | tf_op jit(solution)/shard_map/pallas_call | solution.py:49
  119.1 2.3 %collective-permute-done.29.refs_0_ = bf16[4,3,32,512]{3,2,1,0:T(8,128)(2,1)S(1)} collective-permute-done((bf16[4,3,32,512]{3,2,1,0:T(8,128)(2,1)S(1)}, bf16[4,3,32,512]{3,2,1,0:T(8,128)(2,1)S(1)}, u32[]{:S(2)}, u32[]{:S(2)}) %collective-permute-start.29) | collective-permute-done | bytes 393248 | tf_op jit(solution)/shard_map/ppermute | solution.py:40
  121.5 2.8 %shard_map.85 = bf16[2048,512]{1,0:T(8,128)(2,1)} custom-call(bf16[4,3,32,512]{3,2,1,0:T(8,128)(2,1)S(1)} %collective-permute-done.29.refs_0_, bf16[4,3,32,512]{3,2,1,0:T(8,128)(2,1)S(1)} %collective-permute-done.30.refs_1_, bf16[2048,512]{1,0:T(8,128)(2,1)S(1)} %copy-done, f32[1,512]{1,0:T(1,128)S(1)} %bitcast.3, f32[2048,512]{1,0:T(8,128)S(1)} %shard_map.84.refs_4_), custom_call_target="tpu_custom_call" | custom-call | flops 1610612736 | bytes 6291456 | tf_op jit(solution)/shard_map/pallas_call | solution.py:49
  (30 shorter events, 0.8 us)
Async XLA Ops:
  6.3 12.5 %collective-permute-start = (bf16[4,3,32,512]{3,2,1,0:T(8,128)(2,1)S(1)}, bf16[4,3,32,512]{3,2,1,0:T(8,128)(2,1)S(1)}, u32[]{:S(2)}, u32[]{:S(2)}) collective-permute-start(bf16[4,3,32,512]{3,2,1,0:T(8,128)(2,1)S(1)} %get-tuple-element.39), channel_id=1, source_target_pairs={{0,2},{1,3},{2,0},{3,1},{4,6},{5,7},{6,4},{7,5},{8,10},{9,11},{10,... | collective-permute-start | bytes 1179656 | tf_op jit(solution)/shard_map/ppermute | solution.py:40
  13.2 9.1 %collective-permute-start.1 = (bf16[4,3,32,512]{3,2,1,0:T(8,128)(2,1)S(1)}, bf16[4,3,32,512]{3,2,1,0:T(8,128)(2,1)S(1)}, u32[]{:S(2)}, u32[]{:S(2)}) collective-permute-start(bf16[4,3,32,512]{3,2,1,0:T(8,128)(2,1)S(1)} %get-tuple-element.42), channel_id=1, source_target_pairs={{0,1},{1,2},{2,3},{3,0},{4,5},{5,6},{6,7},{7,4},{8,9},{9,10},{10,1... | collective-permute-start | bytes 1179656 | tf_op jit(solution)/shard_map/ppermute | solution.py:40
  13.9 8.4 %collective-permute-start.2 = (bf16[4,3,32,512]{3,2,1,0:T(8,128)(2,1)S(1)}, bf16[4,3,32,512]{3,2,1,0:T(8,128)(2,1)S(1)}, u32[]{:S(2)}, u32[]{:S(2)}) collective-permute-start(bf16[4,3,32,512]{3,2,1,0:T(8,128)(2,1)S(1)} %get-tuple-element.43), channel_id=1, source_target_pairs={{0,3},{1,0},{2,1},{3,2},{4,7},{5,4},{6,5},{7,6},{8,11},{9,8},{10,9... | collective-permute-start | bytes 1179656 | tf_op jit(solution)/shard_map/ppermute | solution.py:40
  22.4 5.9 %collective-permute-start.3 = (bf16[3,32,512]{2,1,0:T(8,128)(2,1)S(1)}, bf16[3,32,512]{2,1,0:T(8,128)(2,1)S(1)}, u32[]{:S(2)}, u32[]{:S(2)}) collective-permute-start(bf16[3,32,512]{2,1,0:T(8,128)(2,1)S(1)} %get-tuple-element.45), channel_id=1, source_target_pairs={{0,4},{1,5},{2,6},{3,7},{4,8},{5,9},{6,10},{7,11},{8,12},{9,13},{1... | collective-permute-start | bytes 294920 | tf_op jit(solution)/shard_map/ppermute | solution.py:40
  24.1 6.5 %collective-permute-start.4 = (bf16[3,32,512]{2,1,0:T(8,128)(2,1)S(1)}, bf16[3,32,512]{2,1,0:T(8,128)(2,1)S(1)}, u32[]{:S(2)}, u32[]{:S(2)}) collective-permute-start(bf16[3,32,512]{2,1,0:T(8,128)(2,1)S(1)} %get-tuple-element.46), channel_id=1, source_target_pairs={{0,8},{1,9},{2,10},{3,11},{4,12},{5,13},{6,14},{7,15},{8,0},{9,1},... | collective-permute-start | bytes 294920 | tf_op jit(solution)/shard_map/ppermute | solution.py:40
  27.0 4.6 %collective-permute-start.5 = (bf16[3,32,512]{2,1,0:T(8,128)(2,1)S(1)}, bf16[3,32,512]{2,1,0:T(8,128)(2,1)S(1)}, u32[]{:S(2)}, u32[]{:S(2)}) collective-permute-start(bf16[3,32,512]{2,1,0:T(8,128)(2,1)S(1)} %get-tuple-element.47), channel_id=1, source_target_pairs={{0,12},{1,13},{2,14},{3,15},{4,0},{5,1},{6,2},{7,3},{8,4},{9,5},{1... | collective-permute-start | bytes 294920 | tf_op jit(solution)/shard_map/ppermute | solution.py:40
  31.6 7.3 %collective-permute-start.6 = (bf16[3,32,512]{2,1,0:T(8,128)(2,1)S(1)}, bf16[3,32,512]{2,1,0:T(8,128)(2,1)S(1)}, u32[]{:S(2)}, u32[]{:S(2)}) collective-permute-start(bf16[3,32,512]{2,1,0:T(8,128)(2,1)S(1)} %shard_map.69.own), channel_id=1, source_target_pairs={{0,48},{1,49},{2,50},{3,51},{4,52},{5,53},{6,54},{7,55},{8,56},{9,... | collective-permute-start | bytes 294920 | tf_op jit(solution)/shard_map/ppermute | solution.py:40
  35.7 6.2 %collective-permute-start.7 = (bf16[3,32,512]{2,1,0:T(8,128)(2,1)S(1)}, bf16[3,32,512]{2,1,0:T(8,128)(2,1)S(1)}, u32[]{:S(2)}, u32[]{:S(2)}) collective-permute-start(bf16[3,32,512]{2,1,0:T(8,128)(2,1)S(1)} %shard_map.69.own), channel_id=1, source_target_pairs={{0,32},{1,33},{2,34},{3,35},{4,36},{5,37},{6,38},{7,39},{8,40},{9,... | collective-permute-start | bytes 294920 | tf_op jit(solution)/shard_map/ppermute | solution.py:40
  35.7 6.9 %collective-permute-start.8 = (bf16[3,32,512]{2,1,0:T(8,128)(2,1)S(1)}, bf16[3,32,512]{2,1,0:T(8,128)(2,1)S(1)}, u32[]{:S(2)}, u32[]{:S(2)}) collective-permute-start(bf16[3,32,512]{2,1,0:T(8,128)(2,1)S(1)} %shard_map.69.own), channel_id=1, source_target_pairs={{0,16},{1,17},{2,18},{3,19},{4,20},{5,21},{6,22},{7,23},{8,24},{9,... | collective-permute-start | bytes 294920 | tf_op jit(solution)/shard_map/ppermute | solution.py:40
  42.7 5.8 %collective-permute-start.9 = (bf16[3,32,512]{2,1,0:T(8,128)(2,1)S(1)}, bf16[3,32,512]{2,1,0:T(8,128)(2,1)S(1)}, u32[]{:S(2)}, u32[]{:S(2)}) collective-permute-start(bf16[3,32,512]{2,1,0:T(8,128)(2,1)S(1)} %get-tuple-element.49.own), channel_id=1, source_target_pairs={{0,12},{1,13},{2,14},{3,15},{4,0},{5,1},{6,2},{7,3},{8,4},{9,5},{1... | collective-permute-start | bytes 294920 | tf_op jit(solution)/shard_map/ppermute | solution.py:40
  45.3 6.2 %collective-permute-start.10 = (bf16[3,32,512]{2,1,0:T(8,128)(2,1)S(1)}, bf16[3,32,512]{2,1,0:T(8,128)(2,1)S(1)}, u32[]{:S(2)}, u32[]{:S(2)}) collective-permute-start(bf16[3,32,512]{2,1,0:T(8,128)(2,1)S(1)} %get-tuple-element.49.own), channel_id=1, source_target_pairs={{0,8},{1,9},{2,10},{3,11},{4,12},{5,13},{6,14},{7,15},{8,0},{9,1},... | collective-permute-start | bytes 294920 | tf_op jit(solution)/shard_map/ppermute | solution.py:40
  45.5 6.9 %collective-permute-start.11 = (bf16[3,32,512]{2,1,0:T(8,128)(2,1)S(1)}, bf16[3,32,512]{2,1,0:T(8,128)(2,1)S(1)}, u32[]{:S(2)}, u32[]{:S(2)}) collective-permute-start(bf16[3,32,512]{2,1,0:T(8,128)(2,1)S(1)} %get-tuple-element.49.own), channel_id=1, source_target_pairs={{0,4},{1,5},{2,6},{3,7},{4,8},{5,9},{6,10},{7,11},{8,12},{9,13},{1... | collective-permute-start | bytes 294920 | tf_op jit(solution)/shard_map/ppermute | solution.py:40
  48.6 3.8 %collective-permute-start.12 = (bf16[16,128]{1,0:T(8,128)(2,1)S(1)}, bf16[16,128]{1,0:T(8,128)(2,1)S(1)}, u32[]{:S(2)}, u32[]{:S(2)}) collective-permute-start(bf16[16,128]{1,0:T(8,128)(2,1)S(1)} %get-tuple-element.51), channel_id=1, source_target_pairs={{0,64},{1,65},{2,66},{3,67},{4,68},{5,69},{6,70},{7,71},{8,72},{9,... | collective-permute-start | bytes 12296 | tf_op jit(solution)/shard_map/ppermute | solution.py:322
  52.4 9.6 %collective-permute-start.13 = (bf16[4,3,32,512]{3,2,1,0:T(8,128)(2,1)S(1)}, bf16[4,3,32,512]{3,2,1,0:T(8,128)(2,1)S(1)}, u32[]{:S(2)}, u32[]{:S(2)}) collective-permute-start(bf16[4,3,32,512]{3,2,1,0:T(8,128)(2,1)S(1)} %shard_map.73.refs_0_), channel_id=1, source_target_pairs={{0,2},{1,3},{2,0},{3,1},{4,6},{5,7},{6,4},{7,5},{8,10},{9,11},{10,... | collective-permute-start | bytes 1179656 | tf_op jit(solution)/shard_map/ppermute | solution.py:40
  54.1 12.6 %collective-permute-start.15 = (bf16[4,3,32,512]{3,2,1,0:T(8,128)(2,1)S(1)}, bf16[4,3,32,512]{3,2,1,0:T(8,128)(2,1)S(1)}, u32[]{:S(2)}, u32[]{:S(2)}) collective-permute-start(bf16[4,3,32,512]{3,2,1,0:T(8,128)(2,1)S(1)} %shard_map.73.refs_0_), channel_id=1, source_target_pairs={{0,3},{1,0},{2,1},{3,2},{4,7},{5,4},{6,5},{7,6},{8,11},{9,8},{10,9... | collective-permute-start | bytes 1179656 | tf_op jit(solution)/shard_map/ppermute | solution.py:40
  56.0 10.8 %collective-permute-start.16 = (bf16[4,3,32,512]{3,2,1,0:T(8,128)(2,1)S(1)}, bf16[4,3,32,512]{3,2,1,0:T(8,128)(2,1)S(1)}, u32[]{:S(2)}, u32[]{:S(2)}) collective-permute-start(bf16[4,3,32,512]{3,2,1,0:T(8,128)(2,1)S(1)} %shard_map.73.refs_0_), channel_id=1, source_target_pairs={{0,1},{1,2},{2,3},{3,0},{4,5},{5,6},{6,7},{7,4},{8,9},{9,10},{10,1... | collective-permute-start | bytes 1179656 | tf_op jit(solution)/shard_map/ppermute | solution.py:40
  64.4 9.4 %collective-permute-start.14 = (bf16[4,3,32,512]{3,2,1,0:T(8,128)(2,1)S(1)}, bf16[4,3,32,512]{3,2,1,0:T(8,128)(2,1)S(1)}, u32[]{:S(2)}, u32[]{:S(2)}) collective-permute-start(bf16[4,3,32,512]{3,2,1,0:T(8,128)(2,1)S(1)} %shard_map.75), channel_id=1, source_target_pairs={{0,2},{1,3},{2,0},{3,1},{4,6},{5,7},{6,4},{7,5},{8,10},{9,11},{10,... | collective-permute-start | bytes 1179656 | tf_op jit(solution)/shard_map/ppermute | solution.py:40
  70.5 9.1 %collective-permute-start.17 = (bf16[4,3,32,512]{3,2,1,0:T(8,128)(2,1)S(1)}, bf16[4,3,32,512]{3,2,1,0:T(8,128)(2,1)S(1)}, u32[]{:S(2)}, u32[]{:S(2)}) collective-permute-start(bf16[4,3,32,512]{3,2,1,0:T(8,128)(2,1)S(1)} %get-tuple-element.55), channel_id=1, source_target_pairs={{0,1},{1,2},{2,3},{3,0},{4,5},{5,6},{6,7},{7,4},{8,9},{9,10},{10,1... | collective-permute-start | bytes 1179656 | tf_op jit(solution)/shard_map/ppermute | solution.py:40
  72.3 7.8 %collective-permute-start.18 = (bf16[4,3,32,512]{3,2,1,0:T(8,128)(2,1)S(1)}, bf16[4,3,32,512]{3,2,1,0:T(8,128)(2,1)S(1)}, u32[]{:S(2)}, u32[]{:S(2)}) collective-permute-start(bf16[4,3,32,512]{3,2,1,0:T(8,128)(2,1)S(1)} %get-tuple-element.56), channel_id=1, source_target_pairs={{0,3},{1,0},{2,1},{3,2},{4,7},{5,4},{6,5},{7,6},{8,11},{9,8},{10,9... | collective-permute-start | bytes 1179656 | tf_op jit(solution)/shard_map/ppermute | solution.py:40
  73.8 38.5 %copy-start = (bf16[2048,512]{1,0:T(8,128)(2,1)S(1)}, bf16[2048,512]{1,0:T(8,128)(2,1)}, u32[]{:S(2)}) copy-start(bf16[2048,512]{1,0:T(8,128)(2,1)} %refs_2_.3) | copy-start | bytes 6291460
  80.2 6.9 %collective-permute-start.19 = (bf16[3,32,512]{2,1,0:T(8,128)(2,1)S(1)}, bf16[3,32,512]{2,1,0:T(8,128)(2,1)S(1)}, u32[]{:S(2)}, u32[]{:S(2)}) collective-permute-start(bf16[3,32,512]{2,1,0:T(8,128)(2,1)S(1)} %get-tuple-element.58), channel_id=1, source_target_pairs={{0,4},{1,5},{2,6},{3,7},{4,8},{5,9},{6,10},{7,11},{8,12},{9,13},{1... | collective-permute-start | bytes 294920 | tf_op jit(solution)/shard_map/ppermute | solution.py:40
  80.3 6.9 %collective-permute-start.20 = (bf16[3,32,512]{2,1,0:T(8,128)(2,1)S(1)}, bf16[3,32,512]{2,1,0:T(8,128)(2,1)S(1)}, u32[]{:S(2)}, u32[]{:S(2)}) collective-permute-start(bf16[3,32,512]{2,1,0:T(8,128)(2,1)S(1)} %get-tuple-element.59), channel_id=1, source_target_pairs={{0,8},{1,9},{2,10},{3,11},{4,12},{5,13},{6,14},{7,15},{8,0},{9,1},... | collective-permute-start | bytes 294920 | tf_op jit(solution)/shard_map/ppermute | solution.py:40
  82.8 5.2 %collective-permute-start.21 = (bf16[3,32,512]{2,1,0:T(8,128)(2,1)S(1)}, bf16[3,32,512]{2,1,0:T(8,128)(2,1)S(1)}, u32[]{:S(2)}, u32[]{:S(2)}) collective-permute-start(bf16[3,32,512]{2,1,0:T(8,128)(2,1)S(1)} %get-tuple-element.60), channel_id=1, source_target_pairs={{0,12},{1,13},{2,14},{3,15},{4,0},{5,1},{6,2},{7,3},{8,4},{9,5},{1... | collective-permute-start | bytes 294920 | tf_op jit(solution)/shard_map/ppermute | solution.py:40
  88.1 4.7 %collective-permute-start.22 = (bf16[3,32,512]{2,1,0:T(8,128)(2,1)S(1)}, bf16[3,32,512]{2,1,0:T(8,128)(2,1)S(1)}, u32[]{:S(2)}, u32[]{:S(2)}) collective-permute-start(bf16[3,32,512]{2,1,0:T(8,128)(2,1)S(1)} %shard_map.79.own), channel_id=1, source_target_pairs={{0,48},{1,49},{2,50},{3,51},{4,52},{5,53},{6,54},{7,55},{8,56},{9,... | collective-permute-start | bytes 294920 | tf_op jit(solution)/shard_map/ppermute | solution.py:40
  89.0 6.2 %collective-permute-start.23 = (bf16[3,32,512]{2,1,0:T(8,128)(2,1)S(1)}, bf16[3,32,512]{2,1,0:T(8,128)(2,1)S(1)}, u32[]{:S(2)}, u32[]{:S(2)}) collective-permute-start(bf16[3,32,512]{2,1,0:T(8,128)(2,1)S(1)} %shard_map.79.own), channel_id=1, source_target_pairs={{0,32},{1,33},{2,34},{3,35},{4,36},{5,37},{6,38},{7,39},{8,40},{9,... | collective-permute-start | bytes 294920 | tf_op jit(solution)/shard_map/ppermute | solution.py:40
  89.5 6.7 %collective-permute-start.24 = (bf16[3,32,512]{2,1,0:T(8,128)(2,1)S(1)}, bf16[3,32,512]{2,1,0:T(8,128)(2,1)S(1)}, u32[]{:S(2)}, u32[]{:S(2)}) collective-permute-start(bf16[3,32,512]{2,1,0:T(8,128)(2,1)S(1)} %shard_map.79.own), channel_id=1, source_target_pairs={{0,16},{1,17},{2,18},{3,19},{4,20},{5,21},{6,22},{7,23},{8,24},{9,... | collective-permute-start | bytes 294920 | tf_op jit(solution)/shard_map/ppermute | solution.py:40
  96.3 1.4 %collective-permute-start.25 = (bf16[3,32,512]{2,1,0:T(8,128)(2,1)S(1)}, bf16[3,32,512]{2,1,0:T(8,128)(2,1)S(1)}, u32[]{:S(2)}, u32[]{:S(2)}) collective-permute-start(bf16[3,32,512]{2,1,0:T(8,128)(2,1)S(1)} %get-tuple-element.61), channel_id=1, source_target_pairs={{0,64},{1,65},{2,66},{3,67},{4,68},{5,69},{6,70},{7,71},{8,72},{9,... | collective-permute-start | bytes 294920 | tf_op jit(solution)/shard_map/ppermute | solution.py:379
  97.7 6.0 %collective-permute-start.26 = (bf16[3,32,512]{2,1,0:T(8,128)(2,1)S(1)}, bf16[3,32,512]{2,1,0:T(8,128)(2,1)S(1)}, u32[]{:S(2)}, u32[]{:S(2)}) collective-permute-start(bf16[3,32,512]{2,1,0:T(8,128)(2,1)S(1)} %shard_map.81.own), channel_id=1, source_target_pairs={{0,12},{1,13},{2,14},{3,15},{4,0},{5,1},{6,2},{7,3},{8,4},{9,5},{1... | collective-permute-start | bytes 294920 | tf_op jit(solution)/shard_map/ppermute | solution.py:40
  100.5 6.2 %collective-permute-start.27 = (bf16[3,32,512]{2,1,0:T(8,128)(2,1)S(1)}, bf16[3,32,512]{2,1,0:T(8,128)(2,1)S(1)}, u32[]{:S(2)}, u32[]{:S(2)}) collective-permute-start(bf16[3,32,512]{2,1,0:T(8,128)(2,1)S(1)} %shard_map.81.own), channel_id=1, source_target_pairs={{0,8},{1,9},{2,10},{3,11},{4,12},{5,13},{6,14},{7,15},{8,0},{9,1},... | collective-permute-start | bytes 294920 | tf_op jit(solution)/shard_map/ppermute | solution.py:40
  100.8 6.8 %collective-permute-start.28 = (bf16[3,32,512]{2,1,0:T(8,128)(2,1)S(1)}, bf16[3,32,512]{2,1,0:T(8,128)(2,1)S(1)}, u32[]{:S(2)}, u32[]{:S(2)}) collective-permute-start(bf16[3,32,512]{2,1,0:T(8,128)(2,1)S(1)} %shard_map.81.own), channel_id=1, source_target_pairs={{0,4},{1,5},{2,6},{3,7},{4,8},{5,9},{6,10},{7,11},{8,12},{9,13},{1... | collective-permute-start | bytes 294920 | tf_op jit(solution)/shard_map/ppermute | solution.py:40
  107.7 9.7 %collective-permute-start.31 = (bf16[4,3,32,512]{3,2,1,0:T(8,128)(2,1)S(1)}, bf16[4,3,32,512]{3,2,1,0:T(8,128)(2,1)S(1)}, u32[]{:S(2)}, u32[]{:S(2)}) collective-permute-start(bf16[4,3,32,512]{3,2,1,0:T(8,128)(2,1)S(1)} %shard_map.82.refs_0_), channel_id=1, source_target_pairs={{0,2},{1,3},{2,0},{3,1},{4,6},{5,7},{6,4},{7,5},{8,10},{9,11},{10,... | collective-permute-start | bytes 1179656 | tf_op jit(solution)/shard_map/ppermute | solution.py:40
  110.3 11.2 %collective-permute-start.29 = (bf16[4,3,32,512]{3,2,1,0:T(8,128)(2,1)S(1)}, bf16[4,3,32,512]{3,2,1,0:T(8,128)(2,1)S(1)}, u32[]{:S(2)}, u32[]{:S(2)}) collective-permute-start(bf16[4,3,32,512]{3,2,1,0:T(8,128)(2,1)S(1)} %shard_map.82.refs_0_), channel_id=1, source_target_pairs={{0,3},{1,0},{2,1},{3,2},{4,7},{5,4},{6,5},{7,6},{8,11},{9,8},{10,9... | collective-permute-start | bytes 1179656 | tf_op jit(solution)/shard_map/ppermute | solution.py:40
  111.4 10.1 %collective-permute-start.30 = (bf16[4,3,32,512]{3,2,1,0:T(8,128)(2,1)S(1)}, bf16[4,3,32,512]{3,2,1,0:T(8,128)(2,1)S(1)}, u32[]{:S(2)}, u32[]{:S(2)}) collective-permute-start(bf16[4,3,32,512]{3,2,1,0:T(8,128)(2,1)S(1)} %shard_map.82.refs_0_), channel_id=1, source_target_pairs={{0,1},{1,2},{2,3},{3,0},{4,5},{5,6},{6,7},{7,4},{8,9},{9,10},{10,1... | collective-permute-start | bytes 1179656 | tf_op jit(solution)/shard_map/ppermute | solution.py:40
  114.1 7.4 %copy-start.1 = (f32[512]{0:T(512)S(1)}, f32[512]{0:T(512)}, u32[]{:S(2)}) copy-start(f32[512]{0:T(512)} %param.11) | copy-start | bytes 6148

commit v7 on v6

--- a/solution.py
+++ b/solution.py
@@ -341,7 +341,7 @@
 
 
 def applied(shard, queries, gain):
-    block = gathered(shard, False)
+    block = gathered(shard, True)
     b2, b1, b3 = hop(block, 0, -2), hop(block, 0, -1), hop(block, 0, -3)
     result = apply_blocks([block], queries, None, None)
     result = apply_blocks([b2], queries, result, None)

time: 125 us -> 124 us (level)
    pallas_call x22 -> x24, Pallas kernels: 27.5 us -> 27.6 us  [call(): pl.pallas_call(kernel, out_shape=outs, in_specs=specs or [VMEM] * len(arg...]
  transfers between devices with their start and end apart: 32 -> 33, of which waited for: 24 -> 24; matrix products, arithmetic and copies ran while one was open for 0% -> 0% of each run, Pallas kernels for 15% -> 15%
where the time goes in v7:
time: 124 us
  waiting for transfers between devices  50.5 us (41%)
  starting transfers between devices  45.6 us (37%)
  Pallas kernels  27.6 us (22%)
    ppermute x30, waiting for transfers between devices, hop(): return lax.ppermute(x, AXES, hop_pairs(level, step % SIDE))  49.2 us
    ppermute x30, starting transfers between devices, hop(): return lax.ppermute(x, AXES, hop_pairs(level, step % SIDE))  45.2 us
    pallas_call x24, Pallas kernels, call(): pl.pallas_call(kernel, out_shape=outs, in_specs=specs or [VMEM] * len(arg...  27.6 us
  transfers between devices with their start and end apart: 33, of which 24 were waited for; matrix products, arithmetic and copies ran while one was open for 0% of the time, Pallas kernels for 15%

profile of v7, /device:TPU:0, one launch (start us, length us, event | category | flops | bytes accessed | tf_op | source)
XLA Modules:
  0.0 124.3 jit_solution(10195491885374013173)
XLA Ops:
  0.2 6.1 %shard_map.64 = (bf16[2048,512]{1,0:T(8,128)(2,1)S(1)}, bf16[2048,512]{1,0:T(8,128)(2,1)S(1)}, f32[1,2048]{1,0:T(1,128)S(1)}, bf16[4,3,32,512]{3,2,1,0:T(8,128)(...) custom-call(s32[16]{0:T(128)S(1)} %fusion.place, ...), custom_call_target="tpu_custom_call" | custom-call | flops 1610612736 | bytes 4194304 | tf_op jit(solution)/shard_map/pallas_call | solution.py:49
  6.3 3.2 %collective-permute-start = (bf16[4,3,32,512]{3,2,1,0:T(8,128)(2,1)S(1)}, bf16[4,3,32,512]{3,2,1,0:T(8,128)(2,1)S(1)}, u32[]{:S(2)}, u32[]{:S(2)}) collective-permute-start(bf16[4,3,32,512]{3,2,1,0:T(8,128)(2,1)S(1)} %get-tuple-element.41), channel_id=1, source_target_pairs={{0,2},{1,3},{2,0},{3,1},{4,6},{5,7},{6,4},{7,5},{8,10},{9,11},{10,... | collective-permute-start | bytes 1179656 | tf_op jit(solution)/shard_map/ppermute | solution.py:40
  9.5 3.7 %shard_map.67 = (bf16[4,3,32,512]{3,2,1,0:T(8,128)(2,1)S(1)}, bf16[4,3,32,512]{3,2,1,0:T(8,128)(2,1)S(1)}) custom-call(bf16[4,3,32,512]{3,2,1,0:T(8,128)(2,1)S(1)} %get-tuple-element.42.refs_0_, bf16[4,3,32,512]{3,2,1,0:T(8,128)(2,1)S(1)} %get-tuple-element.43.refs_1_, bf16[2048,512]{1,0:T(8,128)(2,1)S(1)} %get-tuple-element.56.refs_1_.refs_2_, ...), custom_call_target="tpu_custom_call" | custom-call | flops 3221225472 | bytes 4194304 | tf_op jit(solution)/shard_map/pallas_call | solution.py:49
  13.2 0.7 collective-permute-start.1
  13.9 2.6 %collective-permute-start.2 = (bf16[4,3,32,512]{3,2,1,0:T(8,128)(2,1)S(1)}, bf16[4,3,32,512]{3,2,1,0:T(8,128)(2,1)S(1)}, u32[]{:S(2)}, u32[]{:S(2)}) collective-permute-start(bf16[4,3,32,512]{3,2,1,0:T(8,128)(2,1)S(1)} %get-tuple-element.45), channel_id=1, source_target_pairs={{0,3},{1,0},{2,1},{3,2},{4,7},{5,4},{6,5},{7,6},{8,11},{9,8},{10,9... | collective-permute-start | bytes 1179656 | tf_op jit(solution)/shard_map/ppermute | solution.py:40
  16.5 2.3 %shard_map.65.own = f32[4,3,32,512]{3,2,1,0:T(8,128)S(1)} custom-call(bf16[4,3,32,512]{3,2,1,0:T(8,128)(2,1)S(1)} %get-tuple-element.37.refs_0_, bf16[2048,512]{1,0:T(8,128)(2,1)S(1)} %get-tuple-element.56.refs_1_.refs_2_, bf16[2048,512]{1,0:T(8,128)(2,1)S(1)} %get-tuple-element.39.refs_2_.refs_3_, f32[1,2048]{1,0:T(1,128)S(1)} %get-tuple-element.40.refs_3_.refs_4_), custom_call_target="tpu_custom_call" | custom-call | flops 1610612736 | bytes 4194304 | tf_op jit(solution)/shard_map/pallas_call | solution.py:49
  18.9 3.4 %collective-permute-done.1.r1 = bf16[4,3,32,512]{3,2,1,0:T(8,128)(2,1)S(1)} collective-permute-done((bf16[4,3,32,512]{3,2,1,0:T(8,128)(2,1)S(1)}, bf16[4,3,32,512]{3,2,1,0:T(8,128)(2,1)S(1)}, u32[]{:S(2)}, u32[]{:S(2)}) %collective-permute-start.1) | collective-permute-done | bytes 393248 | tf_op jit(solution)/shard_map/ppermute | solution.py:40
  22.3 0.1 shard_map.68
  22.4 1.7 %collective-permute-start.3 = (bf16[3,32,512]{2,1,0:T(8,128)(2,1)S(1)}, bf16[3,32,512]{2,1,0:T(8,128)(2,1)S(1)}, u32[]{:S(2)}, u32[]{:S(2)}) collective-permute-start(bf16[3,32,512]{2,1,0:T(8,128)(2,1)S(1)} %get-tuple-element.47), channel_id=1, source_target_pairs={{0,4},{1,5},{2,6},{3,7},{4,8},{5,9},{6,10},{7,11},{8,12},{9,13},{1... | collective-permute-start | bytes 294920 | tf_op jit(solution)/shard_map/ppermute | solution.py:40
  24.1 2.9 %collective-permute-start.4 = (bf16[3,32,512]{2,1,0:T(8,128)(2,1)S(1)}, bf16[3,32,512]{2,1,0:T(8,128)(2,1)S(1)}, u32[]{:S(2)}, u32[]{:S(2)}) collective-permute-start(bf16[3,32,512]{2,1,0:T(8,128)(2,1)S(1)} %get-tuple-element.48), channel_id=1, source_target_pairs={{0,8},{1,9},{2,10},{3,11},{4,12},{5,13},{6,14},{7,15},{8,0},{9,1},... | collective-permute-start | bytes 294920 | tf_op jit(solution)/shard_map/ppermute | solution.py:40
  27.0 1.3 %collective-permute-start.5 = (bf16[3,32,512]{2,1,0:T(8,128)(2,1)S(1)}, bf16[3,32,512]{2,1,0:T(8,128)(2,1)S(1)}, u32[]{:S(2)}, u32[]{:S(2)}) collective-permute-start(bf16[3,32,512]{2,1,0:T(8,128)(2,1)S(1)} %get-tuple-element.49), channel_id=1, source_target_pairs={{0,12},{1,13},{2,14},{3,15},{4,0},{5,1},{6,2},{7,3},{8,4},{9,5},{1... | collective-permute-start | bytes 294920 | tf_op jit(solution)/shard_map/ppermute | solution.py:40
  28.3 2.3 %collective-permute-done.4.r2 = bf16[3,32,512]{2,1,0:T(8,128)(2,1)S(1)} collective-permute-done((bf16[3,32,512]{2,1,0:T(8,128)(2,1)S(1)}, bf16[3,32,512]{2,1,0:T(8,128)(2,1)S(1)}, u32[]{:S(2)}, u32[]{:S(2)}) %collective-permute-start.4) | collective-permute-done | bytes 98336 | tf_op jit(solution)/shard_map/ppermute | solution.py:40
  30.6 1.0 collective-permute-done.5.r3
  31.6 4.1 %collective-permute-start.6 = (bf16[3,32,512]{2,1,0:T(8,128)(2,1)S(1)}, bf16[3,32,512]{2,1,0:T(8,128)(2,1)S(1)}, u32[]{:S(2)}, u32[]{:S(2)}) collective-permute-start(bf16[3,32,512]{2,1,0:T(8,128)(2,1)S(1)} %shard_map.69.own), channel_id=1, source_target_pairs={{0,48},{1,49},{2,50},{3,51},{4,52},{5,53},{6,54},{7,55},{8,56},{9,... | collective-permute-start | bytes 294920 | tf_op jit(solution)/shard_map/ppermute | solution.py:40
  35.7 1.3 %collective-permute-start.8 = (bf16[3,32,512]{2,1,0:T(8,128)(2,1)S(1)}, bf16[3,32,512]{2,1,0:T(8,128)(2,1)S(1)}, u32[]{:S(2)}, u32[]{:S(2)}) collective-permute-start(bf16[3,32,512]{2,1,0:T(8,128)(2,1)S(1)} %shard_map.69.own), channel_id=1, source_target_pairs={{0,16},{1,17},{2,18},{3,19},{4,20},{5,21},{6,22},{7,23},{8,24},{9,... | collective-permute-start | bytes 294920 | tf_op jit(solution)/shard_map/ppermute | solution.py:40
  37.0 2.0 %collective-permute-done.6.r1 = bf16[3,32,512]{2,1,0:T(8,128)(2,1)S(1)} collective-permute-done((bf16[3,32,512]{2,1,0:T(8,128)(2,1)S(1)}, bf16[3,32,512]{2,1,0:T(8,128)(2,1)S(1)}, u32[]{:S(2)}, u32[]{:S(2)}) %collective-permute-start.6) | collective-permute-done | bytes 98336 | tf_op jit(solution)/shard_map/ppermute | solution.py:40
  39.0 3.0 %collective-permute-done.7.r2 = bf16[3,32,512]{2,1,0:T(8,128)(2,1)S(1)} collective-permute-done((bf16[3,32,512]{2,1,0:T(8,128)(2,1)S(1)}, bf16[3,32,512]{2,1,0:T(8,128)(2,1)S(1)}, u32[]{:S(2)}, u32[]{:S(2)}) %collective-permute-start.7) | collective-permute-done | bytes 98336 | tf_op jit(solution)/shard_map/ppermute | solution.py:40
  42.0 0.7 collective-permute-done.8.r3
  42.7 2.6 %collective-permute-start.9 = (bf16[3,32,512]{2,1,0:T(8,128)(2,1)S(1)}, bf16[3,32,512]{2,1,0:T(8,128)(2,1)S(1)}, u32[]{:S(2)}, u32[]{:S(2)}) collective-permute-start(bf16[3,32,512]{2,1,0:T(8,128)(2,1)S(1)} %get-tuple-element.51.own), channel_id=1, source_target_pairs={{0,12},{1,13},{2,14},{3,15},{4,0},{5,1},{6,2},{7,3},{8,4},{9,5},{1... | collective-permute-start | bytes 294920 | tf_op jit(solution)/shard_map/ppermute | solution.py:40
  45.3 0.2 collective-permute-start.10
  45.5 0.8 collective-permute-start.11
  46.3 2.3 %collective-permute-done.9.part = bf16[3,32,512]{2,1,0:T(8,128)(2,1)S(1)} collective-permute-done((bf16[3,32,512]{2,1,0:T(8,128)(2,1)S(1)}, bf16[3,32,512]{2,1,0:T(8,128)(2,1)S(1)}, u32[]{:S(2)}, u32[]{:S(2)}) %collective-permute-start.9) | collective-permute-done | bytes 98336 | tf_op jit(solution)/shard_map/ppermute | solution.py:40
  48.7 2.9 %collective-permute-done.10.part = bf16[3,32,512]{2,1,0:T(8,128)(2,1)S(1)} collective-permute-done((bf16[3,32,512]{2,1,0:T(8,128)(2,1)S(1)}, bf16[3,32,512]{2,1,0:T(8,128)(2,1)S(1)}, u32[]{:S(2)}, u32[]{:S(2)}) %collective-permute-start.10) | collective-permute-done | bytes 98336 | tf_op jit(solution)/shard_map/ppermute | solution.py:40
  51.6 0.8 collective-permute-done.11.part
  52.4 1.7 %collective-permute-start.13 = (bf16[4,3,32,512]{3,2,1,0:T(8,128)(2,1)S(1)}, bf16[4,3,32,512]{3,2,1,0:T(8,128)(2,1)S(1)}, u32[]{:S(2)}, u32[]{:S(2)}) collective-permute-start(bf16[4,3,32,512]{3,2,1,0:T(8,128)(2,1)S(1)} %shard_map.73.refs_0_), channel_id=1, source_target_pairs={{0,2},{1,3},{2,0},{3,1},{4,6},{5,7},{6,4},{7,5},{8,10},{9,11},{10,... | collective-permute-start | bytes 1179656 | tf_op jit(solution)/shard_map/ppermute | solution.py:40
  54.1 1.9 %collective-permute-start.15 = (bf16[4,3,32,512]{3,2,1,0:T(8,128)(2,1)S(1)}, bf16[4,3,32,512]{3,2,1,0:T(8,128)(2,1)S(1)}, u32[]{:S(2)}, u32[]{:S(2)}) collective-permute-start(bf16[4,3,32,512]{3,2,1,0:T(8,128)(2,1)S(1)} %shard_map.73.refs_0_), channel_id=1, source_target_pairs={{0,3},{1,0},{2,1},{3,2},{4,7},{5,4},{6,5},{7,6},{8,11},{9,8},{10,9... | collective-permute-start | bytes 1179656 | tf_op jit(solution)/shard_map/ppermute | solution.py:40
  56.0 0.8 collective-permute-start.16
  56.8 2.3 %shard_map.74.own = f32[4,3,32,512]{3,2,1,0:T(8,128)S(1)} custom-call(bf16[4,3,32,512]{3,2,1,0:T(8,128)(2,1)S(1)} %shard_map.73.refs_0_, bf16[2048,512]{1,0:T(8,128)(2,1)S(1)} %get-tuple-element.56.refs_1_.refs_2_, bf16[2048,512]{1,0:T(8,128)(2,1)S(1)} %get-tuple-element.39.refs_2_.refs_3_, f32[1,2048]{1,0:T(1,128)S(1)} %get-tuple-element.40.refs_3_.refs_4_), custom_call_target="tpu_custom_call" | custom-call | flops 1610612736 | bytes 4194304 | tf_op jit(solution)/shard_map/pallas_call | solution.py:49
  59.1 2.9 %collective-permute-done.13.refs_0_ = bf16[4,3,32,512]{3,2,1,0:T(8,128)(2,1)S(1)} collective-permute-done((bf16[4,3,32,512]{3,2,1,0:T(8,128)(2,1)S(1)}, bf16[4,3,32,512]{3,2,1,0:T(8,128)(2,1)S(1)}, u32[]{:S(2)}, u32[]{:S(2)}) %collective-permute-start.13) | collective-permute-done | bytes 393248 | tf_op jit(solution)/shard_map/ppermute | solution.py:40
  62.0 2.3 %shard_map.75 = bf16[4,3,32,512]{3,2,1,0:T(8,128)(2,1)S(1)} custom-call(bf16[4,3,32,512]{3,2,1,0:T(8,128)(2,1)S(1)} %collective-permute-done.13.refs_0_, bf16[2048,512]{1,0:T(8,128)(2,1)S(1)} %get-tuple-element.56.refs_1_.refs_2_, bf16[2048,512]{1,0:T(8,128)(2,1)S(1)} %get-tuple-element.39.refs_2_.refs_3_, f32[1,2048]{1,0:T(1,128)S(1)} %get-tuple-element.40.refs_3_.refs_4_), custom_call_target="tpu_custom_call" | custom-call | flops 1610612736 | bytes 4194304 | tf_op jit(solution)/shard_map/pallas_call | solution.py:49
  64.4 1.5 %collective-permute-start.14 = (bf16[4,3,32,512]{3,2,1,0:T(8,128)(2,1)S(1)}, bf16[4,3,32,512]{3,2,1,0:T(8,128)(2,1)S(1)}, u32[]{:S(2)}, u32[]{:S(2)}) collective-permute-start(bf16[4,3,32,512]{3,2,1,0:T(8,128)(2,1)S(1)} %shard_map.75), channel_id=1, source_target_pairs={{0,2},{1,3},{2,0},{3,1},{4,6},{5,7},{6,4},{7,5},{8,10},{9,11},{10,... | collective-permute-start | bytes 1179656 | tf_op jit(solution)/shard_map/ppermute | solution.py:40
  65.9 0.8 collective-permute-done.15.refs_0_
  66.8 3.7 %shard_map.77 = (bf16[4,3,32,512]{3,2,1,0:T(8,128)(2,1)S(1)}, bf16[4,3,32,512]{3,2,1,0:T(8,128)(2,1)S(1)}) custom-call(bf16[4,3,32,512]{3,2,1,0:T(8,128)(2,1)S(1)} %collective-permute-done.15.refs_0_, bf16[4,3,32,512]{3,2,1,0:T(8,128)(2,1)S(1)} %collective-permute-done.16.refs_1_, bf16[2048,512]{1,0:T(8,128)(2,1)S(1)} %get-tuple-element.56.refs_1_.refs_2_, ...), custom_call_target="tpu_custom_call" | custom-call | flops 3221225472 | bytes 4194304 | tf_op jit(solution)/shard_map/pallas_call | solution.py:49
  70.5 1.9 %collective-permute-start.17 = (bf16[4,3,32,512]{3,2,1,0:T(8,128)(2,1)S(1)}, bf16[4,3,32,512]{3,2,1,0:T(8,128)(2,1)S(1)}, u32[]{:S(2)}, u32[]{:S(2)}) collective-permute-start(bf16[4,3,32,512]{3,2,1,0:T(8,128)(2,1)S(1)} %get-tuple-element.57), channel_id=1, source_target_pairs={{0,1},{1,2},{2,3},{3,0},{4,5},{5,6},{6,7},{7,4},{8,9},{9,10},{10,1... | collective-permute-start | bytes 1179656 | tf_op jit(solution)/shard_map/ppermute | solution.py:40
  72.3 1.4 %collective-permute-start.18 = (bf16[4,3,32,512]{3,2,1,0:T(8,128)(2,1)S(1)}, bf16[4,3,32,512]{3,2,1,0:T(8,128)(2,1)S(1)}, u32[]{:S(2)}, u32[]{:S(2)}) collective-permute-start(bf16[4,3,32,512]{3,2,1,0:T(8,128)(2,1)S(1)} %get-tuple-element.58), channel_id=1, source_target_pairs={{0,3},{1,0},{2,1},{3,2},{4,7},{5,4},{6,5},{7,6},{8,11},{9,8},{10,9... | collective-permute-start | bytes 1179656 | tf_op jit(solution)/shard_map/ppermute | solution.py:40
  73.8 5.7 %collective-permute-done.17.r1 = bf16[4,3,32,512]{3,2,1,0:T(8,128)(2,1)S(1)} collective-permute-done((bf16[4,3,32,512]{3,2,1,0:T(8,128)(2,1)S(1)}, bf16[4,3,32,512]{3,2,1,0:T(8,128)(2,1)S(1)}, u32[]{:S(2)}, u32[]{:S(2)}) %collective-permute-start.17) | collective-permute-done | bytes 393248 | tf_op jit(solution)/shard_map/ppermute | solution.py:40
  79.5 0.6 collective-permute-done.18.r3
  80.1 0.1 shard_map.78
  80.3 2.5 %collective-permute-start.20 = (bf16[3,32,512]{2,1,0:T(8,128)(2,1)S(1)}, bf16[3,32,512]{2,1,0:T(8,128)(2,1)S(1)}, u32[]{:S(2)}, u32[]{:S(2)}) collective-permute-start(bf16[3,32,512]{2,1,0:T(8,128)(2,1)S(1)} %get-tuple-element.61), channel_id=1, source_target_pairs={{0,8},{1,9},{2,10},{3,11},{4,12},{5,13},{6,14},{7,15},{8,0},{9,1},... | collective-permute-start | bytes 294920 | tf_op jit(solution)/shard_map/ppermute | solution.py:40
  82.8 1.2 collective-permute-start.21
  84.0 3.2 %collective-permute-done.19.r1 = bf16[3,32,512]{2,1,0:T(8,128)(2,1)S(1)} collective-permute-done((bf16[3,32,512]{2,1,0:T(8,128)(2,1)S(1)}, bf16[3,32,512]{2,1,0:T(8,128)(2,1)S(1)}, u32[]{:S(2)}, u32[]{:S(2)}) %collective-permute-start.19) | collective-permute-done | bytes 98336 | tf_op jit(solution)/shard_map/ppermute | solution.py:40
  87.2 0.9 collective-permute-done.21.r3
  88.1 1.0 collective-permute-start.22
  89.1 0.5 collective-permute-start.23
  89.5 1.3 %collective-permute-start.24 = (bf16[3,32,512]{2,1,0:T(8,128)(2,1)S(1)}, bf16[3,32,512]{2,1,0:T(8,128)(2,1)S(1)}, u32[]{:S(2)}, u32[]{:S(2)}) collective-permute-start(bf16[3,32,512]{2,1,0:T(8,128)(2,1)S(1)} %shard_map.79.own), channel_id=1, source_target_pairs={{0,16},{1,17},{2,18},{3,19},{4,20},{5,21},{6,22},{7,23},{8,24},{9,... | collective-permute-start | bytes 294920 | tf_op jit(solution)/shard_map/ppermute | solution.py:40
  90.9 1.9 %collective-permute-done.22.r1 = bf16[3,32,512]{2,1,0:T(8,128)(2,1)S(1)} collective-permute-done((bf16[3,32,512]{2,1,0:T(8,128)(2,1)S(1)}, bf16[3,32,512]{2,1,0:T(8,128)(2,1)S(1)}, u32[]{:S(2)}, u32[]{:S(2)}) %collective-permute-start.22) | collective-permute-done | bytes 98336 | tf_op jit(solution)/shard_map/ppermute | solution.py:40
  92.8 2.5 %collective-permute-done.23.r2 = bf16[3,32,512]{2,1,0:T(8,128)(2,1)S(1)} collective-permute-done((bf16[3,32,512]{2,1,0:T(8,128)(2,1)S(1)}, bf16[3,32,512]{2,1,0:T(8,128)(2,1)S(1)}, u32[]{:S(2)}, u32[]{:S(2)}) %collective-permute-start.23) | collective-permute-done | bytes 98336 | tf_op jit(solution)/shard_map/ppermute | solution.py:40
  95.3 1.0 collective-permute-done.24.r3
  96.4 1.3 %collective-permute-done.25.other = bf16[3,32,512]{2,1,0:T(8,128)(2,1)S(1)} collective-permute-done((bf16[3,32,512]{2,1,0:T(8,128)(2,1)S(1)}, bf16[3,32,512]{2,1,0:T(8,128)(2,1)S(1)}, u32[]{:S(2)}, u32[]{:S(2)}) %collective-permute-start.25) | collective-permute-done | bytes 98336 | tf_op jit(solution)/shard_map/ppermute | solution.py:379
  97.7 2.7 %collective-permute-start.26 = (bf16[3,32,512]{2,1,0:T(8,128)(2,1)S(1)}, bf16[3,32,512]{2,1,0:T(8,128)(2,1)S(1)}, u32[]{:S(2)}, u32[]{:S(2)}) collective-permute-start(bf16[3,32,512]{2,1,0:T(8,128)(2,1)S(1)} %shard_map.81.own), channel_id=1, source_target_pairs={{0,12},{1,13},{2,14},{3,15},{4,0},{5,1},{6,2},{7,3},{8,4},{9,5},{1... | collective-permute-start | bytes 294920 | tf_op jit(solution)/shard_map/ppermute | solution.py:40
  100.5 0.4 collective-permute-start.27
  100.8 0.6 collective-permute-start.28
  101.4 2.3 %collective-permute-done.26.part = bf16[3,32,512]{2,1,0:T(8,128)(2,1)S(1)} collective-permute-done((bf16[3,32,512]{2,1,0:T(8,128)(2,1)S(1)}, bf16[3,32,512]{2,1,0:T(8,128)(2,1)S(1)}, u32[]{:S(2)}, u32[]{:S(2)}) %collective-permute-start.26) | collective-permute-done | bytes 98336 | tf_op jit(solution)/shard_map/ppermute | solution.py:40
  103.7 0.3 collective-permute-start.29
  104.0 2.7 %collective-permute-done.27.part = bf16[3,32,512]{2,1,0:T(8,128)(2,1)S(1)} collective-permute-done((bf16[3,32,512]{2,1,0:T(8,128)(2,1)S(1)}, bf16[3,32,512]{2,1,0:T(8,128)(2,1)S(1)}, u32[]{:S(2)}, u32[]{:S(2)}) %collective-permute-start.27) | collective-permute-done | bytes 98336 | tf_op jit(solution)/shard_map/ppermute | solution.py:40
  106.7 0.9 collective-permute-done.28.part
  107.7 2.4 %collective-permute-start.32 = (bf16[4,3,32,512]{3,2,1,0:T(8,128)(2,1)S(1)}, bf16[4,3,32,512]{3,2,1,0:T(8,128)(2,1)S(1)}, u32[]{:S(2)}, u32[]{:S(2)}) collective-permute-start(bf16[4,3,32,512]{3,2,1,0:T(8,128)(2,1)S(1)} %shard_map.84.refs_0_), channel_id=1, source_target_pairs={{0,2},{1,3},{2,0},{3,1},{4,6},{5,7},{6,4},{7,5},{8,10},{9,11},{10,... | collective-permute-start | bytes 1179656 | tf_op jit(solution)/shard_map/ppermute | solution.py:40
  110.0 1.1 collective-permute-start.30
  111.2 0.9 collective-permute-start.31
  112.1 1.8 %shard_map.85.refs_2_ = f32[2048,512]{1,0:T(8,128)S(1)} custom-call(bf16[4,3,32,512]{3,2,1,0:T(8,128)(2,1)S(1)} %shard_map.84.refs_0_, bf16[2048,512]{1,0:T(8,128)(2,1)S(1)} %copy-done), custom_call_target="tpu_custom_call" | custom-call | flops 805306368 | bytes 6291456 | tf_op jit(solution)/shard_map/pallas_call | solution.py:49
  113.9 3.3 %collective-permute-done.32.refs_0_ = bf16[4,3,32,512]{3,2,1,0:T(8,128)(2,1)S(1)} collective-permute-done((bf16[4,3,32,512]{3,2,1,0:T(8,128)(2,1)S(1)}, bf16[4,3,32,512]{3,2,1,0:T(8,128)(2,1)S(1)}, u32[]{:S(2)}, u32[]{:S(2)}) %collective-permute-start.32) | collective-permute-done | bytes 393248 | tf_op jit(solution)/shard_map/ppermute | solution.py:40
  117.1 1.8 %shard_map.86.refs_4_ = f32[2048,512]{1,0:T(8,128)S(1)} custom-call(bf16[4,3,32,512]{3,2,1,0:T(8,128)(2,1)S(1)} %collective-permute-done.32.refs_0_, bf16[2048,512]{1,0:T(8,128)(2,1)S(1)} %copy-done, f32[2048,512]{1,0:T(8,128)S(1)} %shard_map.85.refs_2_), custom_call_target="tpu_custom_call" | custom-call | flops 805306368 | bytes 6291456 | tf_op jit(solution)/shard_map/pallas_call | solution.py:49
  118.9 2.3 %collective-permute-done.30.refs_0_ = bf16[4,3,32,512]{3,2,1,0:T(8,128)(2,1)S(1)} collective-permute-done((bf16[4,3,32,512]{3,2,1,0:T(8,128)(2,1)S(1)}, bf16[4,3,32,512]{3,2,1,0:T(8,128)(2,1)S(1)}, u32[]{:S(2)}, u32[]{:S(2)}) %collective-permute-start.30) | collective-permute-done | bytes 393248 | tf_op jit(solution)/shard_map/ppermute | solution.py:40
  121.3 2.8 %shard_map.87 = bf16[2048,512]{1,0:T(8,128)(2,1)} custom-call(bf16[4,3,32,512]{3,2,1,0:T(8,128)(2,1)S(1)} %collective-permute-done.30.refs_0_, bf16[4,3,32,512]{3,2,1,0:T(8,128)(2,1)S(1)} %collective-permute-done.31.refs_1_, bf16[2048,512]{1,0:T(8,128)(2,1)S(1)} %copy-done, f32[1,512]{1,0:T(1,128)S(1)} %bitcast.3, f32[2048,512]{1,0:T(8,128)S(1)} %shard_map.86.refs_4_), custom_call_target="tpu_custom_call" | custom-call | flops 1610612736 | bytes 6291456 | tf_op jit(solution)/shard_map/pallas_call | solution.py:49
  (34 shorter events, 0.9 us)
Async XLA Ops:
  6.3 12.5 %collective-permute-start = (bf16[4,3,32,512]{3,2,1,0:T(8,128)(2,1)S(1)}, bf16[4,3,32,512]{3,2,1,0:T(8,128)(2,1)S(1)}, u32[]{:S(2)}, u32[]{:S(2)}) collective-permute-start(bf16[4,3,32,512]{3,2,1,0:T(8,128)(2,1)S(1)} %get-tuple-element.41), channel_id=1, source_target_pairs={{0,2},{1,3},{2,0},{3,1},{4,6},{5,7},{6,4},{7,5},{8,10},{9,11},{10,... | collective-permute-start | bytes 1179656 | tf_op jit(solution)/shard_map/ppermute | solution.py:40
  13.2 9.1 %collective-permute-start.1 = (bf16[4,3,32,512]{3,2,1,0:T(8,128)(2,1)S(1)}, bf16[4,3,32,512]{3,2,1,0:T(8,128)(2,1)S(1)}, u32[]{:S(2)}, u32[]{:S(2)}) collective-permute-start(bf16[4,3,32,512]{3,2,1,0:T(8,128)(2,1)S(1)} %get-tuple-element.44), channel_id=1, source_target_pairs={{0,1},{1,2},{2,3},{3,0},{4,5},{5,6},{6,7},{7,4},{8,9},{9,10},{10,1... | collective-permute-start | bytes 1179656 | tf_op jit(solution)/shard_map/ppermute | solution.py:40
  13.9 8.4 %collective-permute-start.2 = (bf16[4,3,32,512]{3,2,1,0:T(8,128)(2,1)S(1)}, bf16[4,3,32,512]{3,2,1,0:T(8,128)(2,1)S(1)}, u32[]{:S(2)}, u32[]{:S(2)}) collective-permute-start(bf16[4,3,32,512]{3,2,1,0:T(8,128)(2,1)S(1)} %get-tuple-element.45), channel_id=1, source_target_pairs={{0,3},{1,0},{2,1},{3,2},{4,7},{5,4},{6,5},{7,6},{8,11},{9,8},{10,9... | collective-permute-start | bytes 1179656 | tf_op jit(solution)/shard_map/ppermute | solution.py:40
  22.4 5.9 %collective-permute-start.3 = (bf16[3,32,512]{2,1,0:T(8,128)(2,1)S(1)}, bf16[3,32,512]{2,1,0:T(8,128)(2,1)S(1)}, u32[]{:S(2)}, u32[]{:S(2)}) collective-permute-start(bf16[3,32,512]{2,1,0:T(8,128)(2,1)S(1)} %get-tuple-element.47), channel_id=1, source_target_pairs={{0,4},{1,5},{2,6},{3,7},{4,8},{5,9},{6,10},{7,11},{8,12},{9,13},{1... | collective-permute-start | bytes 294920 | tf_op jit(solution)/shard_map/ppermute | solution.py:40
  24.1 6.5 %collective-permute-start.4 = (bf16[3,32,512]{2,1,0:T(8,128)(2,1)S(1)}, bf16[3,32,512]{2,1,0:T(8,128)(2,1)S(1)}, u32[]{:S(2)}, u32[]{:S(2)}) collective-permute-start(bf16[3,32,512]{2,1,0:T(8,128)(2,1)S(1)} %get-tuple-element.48), channel_id=1, source_target_pairs={{0,8},{1,9},{2,10},{3,11},{4,12},{5,13},{6,14},{7,15},{8,0},{9,1},... | collective-permute-start | bytes 294920 | tf_op jit(solution)/shard_map/ppermute | solution.py:40
  27.0 4.6 %collective-permute-start.5 = (bf16[3,32,512]{2,1,0:T(8,128)(2,1)S(1)}, bf16[3,32,512]{2,1,0:T(8,128)(2,1)S(1)}, u32[]{:S(2)}, u32[]{:S(2)}) collective-permute-start(bf16[3,32,512]{2,1,0:T(8,128)(2,1)S(1)} %get-tuple-element.49), channel_id=1, source_target_pairs={{0,12},{1,13},{2,14},{3,15},{4,0},{5,1},{6,2},{7,3},{8,4},{9,5},{1... | collective-permute-start | bytes 294920 | tf_op jit(solution)/shard_map/ppermute | solution.py:40
  31.6 7.3 %collective-permute-start.6 = (bf16[3,32,512]{2,1,0:T(8,128)(2,1)S(1)}, bf16[3,32,512]{2,1,0:T(8,128)(2,1)S(1)}, u32[]{:S(2)}, u32[]{:S(2)}) collective-permute-start(bf16[3,32,512]{2,1,0:T(8,128)(2,1)S(1)} %shard_map.69.own), channel_id=1, source_target_pairs={{0,48},{1,49},{2,50},{3,51},{4,52},{5,53},{6,54},{7,55},{8,56},{9,... | collective-permute-start | bytes 294920 | tf_op jit(solution)/shard_map/ppermute | solution.py:40
  35.7 6.2 %collective-permute-start.7 = (bf16[3,32,512]{2,1,0:T(8,128)(2,1)S(1)}, bf16[3,32,512]{2,1,0:T(8,128)(2,1)S(1)}, u32[]{:S(2)}, u32[]{:S(2)}) collective-permute-start(bf16[3,32,512]{2,1,0:T(8,128)(2,1)S(1)} %shard_map.69.own), channel_id=1, source_target_pairs={{0,32},{1,33},{2,34},{3,35},{4,36},{5,37},{6,38},{7,39},{8,40},{9,... | collective-permute-start | bytes 294920 | tf_op jit(solution)/shard_map/ppermute | solution.py:40
  35.7 6.9 %collective-permute-start.8 = (bf16[3,32,512]{2,1,0:T(8,128)(2,1)S(1)}, bf16[3,32,512]{2,1,0:T(8,128)(2,1)S(1)}, u32[]{:S(2)}, u32[]{:S(2)}) collective-permute-start(bf16[3,32,512]{2,1,0:T(8,128)(2,1)S(1)} %shard_map.69.own), channel_id=1, source_target_pairs={{0,16},{1,17},{2,18},{3,19},{4,20},{5,21},{6,22},{7,23},{8,24},{9,... | collective-permute-start | bytes 294920 | tf_op jit(solution)/shard_map/ppermute | solution.py:40
  42.7 5.8 %collective-permute-start.9 = (bf16[3,32,512]{2,1,0:T(8,128)(2,1)S(1)}, bf16[3,32,512]{2,1,0:T(8,128)(2,1)S(1)}, u32[]{:S(2)}, u32[]{:S(2)}) collective-permute-start(bf16[3,32,512]{2,1,0:T(8,128)(2,1)S(1)} %get-tuple-element.51.own), channel_id=1, source_target_pairs={{0,12},{1,13},{2,14},{3,15},{4,0},{5,1},{6,2},{7,3},{8,4},{9,5},{1... | collective-permute-start | bytes 294920 | tf_op jit(solution)/shard_map/ppermute | solution.py:40
  45.3 6.2 %collective-permute-start.10 = (bf16[3,32,512]{2,1,0:T(8,128)(2,1)S(1)}, bf16[3,32,512]{2,1,0:T(8,128)(2,1)S(1)}, u32[]{:S(2)}, u32[]{:S(2)}) collective-permute-start(bf16[3,32,512]{2,1,0:T(8,128)(2,1)S(1)} %get-tuple-element.51.own), channel_id=1, source_target_pairs={{0,8},{1,9},{2,10},{3,11},{4,12},{5,13},{6,14},{7,15},{8,0},{9,1},... | collective-permute-start | bytes 294920 | tf_op jit(solution)/shard_map/ppermute | solution.py:40
  45.5 6.9 %collective-permute-start.11 = (bf16[3,32,512]{2,1,0:T(8,128)(2,1)S(1)}, bf16[3,32,512]{2,1,0:T(8,128)(2,1)S(1)}, u32[]{:S(2)}, u32[]{:S(2)}) collective-permute-start(bf16[3,32,512]{2,1,0:T(8,128)(2,1)S(1)} %get-tuple-element.51.own), channel_id=1, source_target_pairs={{0,4},{1,5},{2,6},{3,7},{4,8},{5,9},{6,10},{7,11},{8,12},{9,13},{1... | collective-permute-start | bytes 294920 | tf_op jit(solution)/shard_map/ppermute | solution.py:40
  48.6 3.8 %collective-permute-start.12 = (bf16[16,128]{1,0:T(8,128)(2,1)S(1)}, bf16[16,128]{1,0:T(8,128)(2,1)S(1)}, u32[]{:S(2)}, u32[]{:S(2)}) collective-permute-start(bf16[16,128]{1,0:T(8,128)(2,1)S(1)} %get-tuple-element.53), channel_id=1, source_target_pairs={{0,64},{1,65},{2,66},{3,67},{4,68},{5,69},{6,70},{7,71},{8,72},{9,... | collective-permute-start | bytes 12296 | tf_op jit(solution)/shard_map/ppermute | solution.py:322
  52.4 9.6 %collective-permute-start.13 = (bf16[4,3,32,512]{3,2,1,0:T(8,128)(2,1)S(1)}, bf16[4,3,32,512]{3,2,1,0:T(8,128)(2,1)S(1)}, u32[]{:S(2)}, u32[]{:S(2)}) collective-permute-start(bf16[4,3,32,512]{3,2,1,0:T(8,128)(2,1)S(1)} %shard_map.73.refs_0_), channel_id=1, source_target_pairs={{0,2},{1,3},{2,0},{3,1},{4,6},{5,7},{6,4},{7,5},{8,10},{9,11},{10,... | collective-permute-start | bytes 1179656 | tf_op jit(solution)/shard_map/ppermute | solution.py:40
  54.1 12.6 %collective-permute-start.15 = (bf16[4,3,32,512]{3,2,1,0:T(8,128)(2,1)S(1)}, bf16[4,3,32,512]{3,2,1,0:T(8,128)(2,1)S(1)}, u32[]{:S(2)}, u32[]{:S(2)}) collective-permute-start(bf16[4,3,32,512]{3,2,1,0:T(8,128)(2,1)S(1)} %shard_map.73.refs_0_), channel_id=1, source_target_pairs={{0,3},{1,0},{2,1},{3,2},{4,7},{5,4},{6,5},{7,6},{8,11},{9,8},{10,9... | collective-permute-start | bytes 1179656 | tf_op jit(solution)/shard_map/ppermute | solution.py:40
  56.0 10.8 %collective-permute-start.16 = (bf16[4,3,32,512]{3,2,1,0:T(8,128)(2,1)S(1)}, bf16[4,3,32,512]{3,2,1,0:T(8,128)(2,1)S(1)}, u32[]{:S(2)}, u32[]{:S(2)}) collective-permute-start(bf16[4,3,32,512]{3,2,1,0:T(8,128)(2,1)S(1)} %shard_map.73.refs_0_), channel_id=1, source_target_pairs={{0,1},{1,2},{2,3},{3,0},{4,5},{5,6},{6,7},{7,4},{8,9},{9,10},{10,1... | collective-permute-start | bytes 1179656 | tf_op jit(solution)/shard_map/ppermute | solution.py:40
  64.4 9.4 %collective-permute-start.14 = (bf16[4,3,32,512]{3,2,1,0:T(8,128)(2,1)S(1)}, bf16[4,3,32,512]{3,2,1,0:T(8,128)(2,1)S(1)}, u32[]{:S(2)}, u32[]{:S(2)}) collective-permute-start(bf16[4,3,32,512]{3,2,1,0:T(8,128)(2,1)S(1)} %shard_map.75), channel_id=1, source_target_pairs={{0,2},{1,3},{2,0},{3,1},{4,6},{5,7},{6,4},{7,5},{8,10},{9,11},{10,... | collective-permute-start | bytes 1179656 | tf_op jit(solution)/shard_map/ppermute | solution.py:40
  70.5 9.1 %collective-permute-start.17 = (bf16[4,3,32,512]{3,2,1,0:T(8,128)(2,1)S(1)}, bf16[4,3,32,512]{3,2,1,0:T(8,128)(2,1)S(1)}, u32[]{:S(2)}, u32[]{:S(2)}) collective-permute-start(bf16[4,3,32,512]{3,2,1,0:T(8,128)(2,1)S(1)} %get-tuple-element.57), channel_id=1, source_target_pairs={{0,1},{1,2},{2,3},{3,0},{4,5},{5,6},{6,7},{7,4},{8,9},{9,10},{10,1... | collective-permute-start | bytes 1179656 | tf_op jit(solution)/shard_map/ppermute | solution.py:40
  72.3 7.8 %collective-permute-start.18 = (bf16[4,3,32,512]{3,2,1,0:T(8,128)(2,1)S(1)}, bf16[4,3,32,512]{3,2,1,0:T(8,128)(2,1)S(1)}, u32[]{:S(2)}, u32[]{:S(2)}) collective-permute-start(bf16[4,3,32,512]{3,2,1,0:T(8,128)(2,1)S(1)} %get-tuple-element.58), channel_id=1, source_target_pairs={{0,3},{1,0},{2,1},{3,2},{4,7},{5,4},{6,5},{7,6},{8,11},{9,8},{10,9... | collective-permute-start | bytes 1179656 | tf_op jit(solution)/shard_map/ppermute | solution.py:40
  80.2 31.8 %copy-start = (bf16[2048,512]{1,0:T(8,128)(2,1)S(1)}, bf16[2048,512]{1,0:T(8,128)(2,1)}, u32[]{:S(2)}) copy-start(bf16[2048,512]{1,0:T(8,128)(2,1)} %refs_2_.3) | copy-start | bytes 6291460
  80.2 6.9 %collective-permute-start.19 = (bf16[3,32,512]{2,1,0:T(8,128)(2,1)S(1)}, bf16[3,32,512]{2,1,0:T(8,128)(2,1)S(1)}, u32[]{:S(2)}, u32[]{:S(2)}) collective-permute-start(bf16[3,32,512]{2,1,0:T(8,128)(2,1)S(1)} %get-tuple-element.60), channel_id=1, source_target_pairs={{0,4},{1,5},{2,6},{3,7},{4,8},{5,9},{6,10},{7,11},{8,12},{9,13},{1... | collective-permute-start | bytes 294920 | tf_op jit(solution)/shard_map/ppermute | solution.py:40
  80.3 6.9 %collective-permute-start.20 = (bf16[3,32,512]{2,1,0:T(8,128)(2,1)S(1)}, bf16[3,32,512]{2,1,0:T(8,128)(2,1)S(1)}, u32[]{:S(2)}, u32[]{:S(2)}) collective-permute-start(bf16[3,32,512]{2,1,0:T(8,128)(2,1)S(1)} %get-tuple-element.61), channel_id=1, source_target_pairs={{0,8},{1,9},{2,10},{3,11},{4,12},{5,13},{6,14},{7,15},{8,0},{9,1},... | collective-permute-start | bytes 294920 | tf_op jit(solution)/shard_map/ppermute | solution.py:40
  82.8 5.2 %collective-permute-start.21 = (bf16[3,32,512]{2,1,0:T(8,128)(2,1)S(1)}, bf16[3,32,512]{2,1,0:T(8,128)(2,1)S(1)}, u32[]{:S(2)}, u32[]{:S(2)}) collective-permute-start(bf16[3,32,512]{2,1,0:T(8,128)(2,1)S(1)} %get-tuple-element.62), channel_id=1, source_target_pairs={{0,12},{1,13},{2,14},{3,15},{4,0},{5,1},{6,2},{7,3},{8,4},{9,5},{1... | collective-permute-start | bytes 294920 | tf_op jit(solution)/shard_map/ppermute | solution.py:40
  88.1 4.7 %collective-permute-start.22 = (bf16[3,32,512]{2,1,0:T(8,128)(2,1)S(1)}, bf16[3,32,512]{2,1,0:T(8,128)(2,1)S(1)}, u32[]{:S(2)}, u32[]{:S(2)}) collective-permute-start(bf16[3,32,512]{2,1,0:T(8,128)(2,1)S(1)} %shard_map.79.own), channel_id=1, source_target_pairs={{0,48},{1,49},{2,50},{3,51},{4,52},{5,53},{6,54},{7,55},{8,56},{9,... | collective-permute-start | bytes 294920 | tf_op jit(solution)/shard_map/ppermute | solution.py:40
  89.1 6.2 %collective-permute-start.23 = (bf16[3,32,512]{2,1,0:T(8,128)(2,1)S(1)}, bf16[3,32,512]{2,1,0:T(8,128)(2,1)S(1)}, u32[]{:S(2)}, u32[]{:S(2)}) collective-permute-start(bf16[3,32,512]{2,1,0:T(8,128)(2,1)S(1)} %shard_map.79.own), channel_id=1, source_target_pairs={{0,32},{1,33},{2,34},{3,35},{4,36},{5,37},{6,38},{7,39},{8,40},{9,... | collective-permute-start | bytes 294920 | tf_op jit(solution)/shard_map/ppermute | solution.py:40
  89.5 6.7 %collective-permute-start.24 = (bf16[3,32,512]{2,1,0:T(8,128)(2,1)S(1)}, bf16[3,32,512]{2,1,0:T(8,128)(2,1)S(1)}, u32[]{:S(2)}, u32[]{:S(2)}) collective-permute-start(bf16[3,32,512]{2,1,0:T(8,128)(2,1)S(1)} %shard_map.79.own), channel_id=1, source_target_pairs={{0,16},{1,17},{2,18},{3,19},{4,20},{5,21},{6,22},{7,23},{8,24},{9,... | collective-permute-start | bytes 294920 | tf_op jit(solution)/shard_map/ppermute | solution.py:40
  96.3 1.4 %collective-permute-start.25 = (bf16[3,32,512]{2,1,0:T(8,128)(2,1)S(1)}, bf16[3,32,512]{2,1,0:T(8,128)(2,1)S(1)}, u32[]{:S(2)}, u32[]{:S(2)}) collective-permute-start(bf16[3,32,512]{2,1,0:T(8,128)(2,1)S(1)} %get-tuple-element.63), channel_id=1, source_target_pairs={{0,64},{1,65},{2,66},{3,67},{4,68},{5,69},{6,70},{7,71},{8,72},{9,... | collective-permute-start | bytes 294920 | tf_op jit(solution)/shard_map/ppermute | solution.py:379
  97.7 6.0 %collective-permute-start.26 = (bf16[3,32,512]{2,1,0:T(8,128)(2,1)S(1)}, bf16[3,32,512]{2,1,0:T(8,128)(2,1)S(1)}, u32[]{:S(2)}, u32[]{:S(2)}) collective-permute-start(bf16[3,32,512]{2,1,0:T(8,128)(2,1)S(1)} %shard_map.81.own), channel_id=1, source_target_pairs={{0,12},{1,13},{2,14},{3,15},{4,0},{5,1},{6,2},{7,3},{8,4},{9,5},{1... | collective-permute-start | bytes 294920 | tf_op jit(solution)/shard_map/ppermute | solution.py:40
  100.5 6.2 %collective-permute-start.27 = (bf16[3,32,512]{2,1,0:T(8,128)(2,1)S(1)}, bf16[3,32,512]{2,1,0:T(8,128)(2,1)S(1)}, u32[]{:S(2)}, u32[]{:S(2)}) collective-permute-start(bf16[3,32,512]{2,1,0:T(8,128)(2,1)S(1)} %shard_map.81.own), channel_id=1, source_target_pairs={{0,8},{1,9},{2,10},{3,11},{4,12},{5,13},{6,14},{7,15},{8,0},{9,1},... | collective-permute-start | bytes 294920 | tf_op jit(solution)/shard_map/ppermute | solution.py:40
  100.8 6.8 %collective-permute-start.28 = (bf16[3,32,512]{2,1,0:T(8,128)(2,1)S(1)}, bf16[3,32,512]{2,1,0:T(8,128)(2,1)S(1)}, u32[]{:S(2)}, u32[]{:S(2)}) collective-permute-start(bf16[3,32,512]{2,1,0:T(8,128)(2,1)S(1)} %shard_map.81.own), channel_id=1, source_target_pairs={{0,4},{1,5},{2,6},{3,7},{4,8},{5,9},{6,10},{7,11},{8,12},{9,13},{1... | collective-permute-start | bytes 294920 | tf_op jit(solution)/shard_map/ppermute | solution.py:40
  103.7 3.9 %collective-permute-start.29 = (bf16[16,128]{1,0:T(8,128)(2,1)S(1)}, bf16[16,128]{1,0:T(8,128)(2,1)S(1)}, u32[]{:S(2)}, u32[]{:S(2)}) collective-permute-start(bf16[16,128]{1,0:T(8,128)(2,1)S(1)} %get-tuple-element.66), channel_id=1, source_target_pairs={{0,64},{1,65},{2,66},{3,67},{4,68},{5,69},{6,70},{7,71},{8,72},{9,... | collective-permute-start | bytes 12296 | tf_op jit(solution)/shard_map/ppermute | solution.py:322
  107.7 9.5 %collective-permute-start.32 = (bf16[4,3,32,512]{3,2,1,0:T(8,128)(2,1)S(1)}, bf16[4,3,32,512]{3,2,1,0:T(8,128)(2,1)S(1)}, u32[]{:S(2)}, u32[]{:S(2)}) collective-permute-start(bf16[4,3,32,512]{3,2,1,0:T(8,128)(2,1)S(1)} %shard_map.84.refs_0_), channel_id=1, source_target_pairs={{0,2},{1,3},{2,0},{3,1},{4,6},{5,7},{6,4},{7,5},{8,10},{9,11},{10,... | collective-permute-start | bytes 1179656 | tf_op jit(solution)/shard_map/ppermute | solution.py:40
  110.0 11.2 %collective-permute-start.30 = (bf16[4,3,32,512]{3,2,1,0:T(8,128)(2,1)S(1)}, bf16[4,3,32,512]{3,2,1,0:T(8,128)(2,1)S(1)}, u32[]{:S(2)}, u32[]{:S(2)}) collective-permute-start(bf16[4,3,32,512]{3,2,1,0:T(8,128)(2,1)S(1)} %shard_map.84.refs_0_), channel_id=1, source_target_pairs={{0,3},{1,0},{2,1},{3,2},{4,7},{5,4},{6,5},{7,6},{8,11},{9,8},{10,9... | collective-permute-start | bytes 1179656 | tf_op jit(solution)/shard_map/ppermute | solution.py:40
  111.2 10.1 %collective-permute-start.31 = (bf16[4,3,32,512]{3,2,1,0:T(8,128)(2,1)S(1)}, bf16[4,3,32,512]{3,2,1,0:T(8,128)(2,1)S(1)}, u32[]{:S(2)}, u32[]{:S(2)}) collective-permute-start(bf16[4,3,32,512]{3,2,1,0:T(8,128)(2,1)S(1)} %shard_map.84.refs_0_), channel_id=1, source_target_pairs={{0,1},{1,2},{2,3},{3,0},{4,5},{5,6},{6,7},{7,4},{8,9},{9,10},{10,1... | collective-permute-start | bytes 1179656 | tf_op jit(solution)/shard_map/ppermute | solution.py:40
  113.9 7.4 %copy-start.1 = (f32[512]{0:T(512)S(1)}, f32[512]{0:T(512)}, u32[]{:S(2)}) copy-start(f32[512]{0:T(512)} %param.11) | copy-start | bytes 6148

commit v8 on v7

--- a/solution.py
+++ b/solution.py
@@ -74,7 +74,10 @@
             part = pl.ds(j * rows, rows)
             sem = sems.at[len(copies) // sems.shape[1], j]
             copies.append(pltpu.make_async_copy(src.at[part], dst.at[part], sem))
-            copies[-1].start()
+    count = sems.shape[1]
+    pairs = [copies[i * count + j] for j in range(count) for i in (1, 2)]
+    for copy in (*copies[:count], copies[3 * count], *pairs):
+        copy.start()
     width = w_ref.shape[0]
     lines = width // (SIDE * SIDE)
     rows = width // sems.shape[1]
@@ -91,15 +94,23 @@
             group = place[r * SIDE + s]
             for m in range(3):
                 block[s, m] = turned[m, group]
+    count = sems.shape[1]
+    copies[3 * count].wait()
+
+    def ready(i):
+        tiles = k_ref.shape[0] // tile // count
+        if i % tiles == 0:
+            copies[count + i // tiles].wait()
+            copies[2 * count + i // tiles].wait()
+
+    refs = (b2, k_ref, v_ref, rate_ref, g2, grads, hiddens)
+    gradient_kernel(factor, tile, 1, *refs, ready=ready)
     mine = place[0]
     for m in range(2):
         start = pl.multiple_of(m * width + (mine // SIDE) * 128, 128)
         slab[...] = w_ref[:, pl.ds(start, 128)].T.reshape(SIDE, lines, width)
         own[m] = slab[mine % SIDE]
     own[2] = w_ref[pl.ds(pl.multiple_of(mine * lines, lines), lines), 2 * width :]
-    for copy in copies[sems.shape[1] :]:
-        copy.wait()
-    gradient_kernel(factor, tile, 1, b2, k_ref, v_ref, rate_ref, g2, grads, hiddens)
 
 
 def rows_of(w_refs, m):
@@ -107,7 +118,7 @@
     return parts[0] if len(parts) == 1 else jnp.concatenate(parts, axis=0)
 
 
-def gradient_kernel(factor, tile, count, *refs):
+def gradient_kernel(factor, tile, count, *refs, ready=None):
     w_refs, (k_ref, v_ref, rate_ref) = refs[:count], refs[count : count + 3]
     outs, (grads, hiddens) = refs[count + 3 : 2 * count + 3], refs[2 * count + 3 :]
     wgu = jnp.concatenate([rows_of(w_refs, 0), rows_of(w_refs, 1)], axis=0)
@@ -115,6 +126,8 @@
     units, width = wd.shape
     for i in range(k_ref.shape[0] // tile):
         rows = slice(i * tile, (i + 1) * tile)
+        if ready is not None:
+            ready(i)
         scale = -(rate_ref[:, rows] * factor)
         gu = lax.dot_general(wgu, k_ref[rows, :], NT, preferred_element_type=F32)
         hidden_grad = lax.dot_general(wd, v_ref[rows, :], NT, preferred_element_type=F32) * scale

time: 124 us -> 124 us (level)
  no operation moved by 1% of the time
where the time goes in v8:
time: 124 us
  waiting for transfers between devices  50.3 us (41%)
  starting transfers between devices  45.6 us (37%)
  Pallas kernels  27.3 us (22%)
    ppermute x30, waiting for transfers between devices, hop(): return lax.ppermute(x, AXES, hop_pairs(level, step % SIDE))  49 us
    ppermute x30, starting transfers between devices, hop(): return lax.ppermute(x, AXES, hop_pairs(level, step % SIDE))  45 us
    pallas_call x24, Pallas kernels, call(): pl.pallas_call(kernel, out_shape=outs, in_specs=specs or [VMEM] * len(arg...  27.3 us
  transfers between devices with their start and end apart: 33, of which 24 were waited for; matrix products, arithmetic and copies ran while one was open for 0% of the time, Pallas kernels for 15%

profile of v8, /device:TPU:0, one launch (start us, length us, event | category | flops | bytes accessed | tf_op | source)
XLA Modules:
  0.0 123.8 jit_solution(8400264319232601902)
XLA Ops:
  0.2 5.7 %shard_map.64 = (bf16[2048,512]{1,0:T(8,128)(2,1)S(1)}, bf16[2048,512]{1,0:T(8,128)(2,1)S(1)}, f32[1,2048]{1,0:T(1,128)S(1)}, bf16[4,3,32,512]{3,2,1,0:T(8,128)(...) custom-call(s32[16]{0:T(128)S(1)} %fusion.place, ...), custom_call_target="tpu_custom_call" | custom-call | flops 1610612736 | bytes 4194304 | tf_op jit(solution)/shard_map/pallas_call | solution.py:49
  5.9 3.2 %collective-permute-start = (bf16[4,3,32,512]{3,2,1,0:T(8,128)(2,1)S(1)}, bf16[4,3,32,512]{3,2,1,0:T(8,128)(2,1)S(1)}, u32[]{:S(2)}, u32[]{:S(2)}) collective-permute-start(bf16[4,3,32,512]{3,2,1,0:T(8,128)(2,1)S(1)} %get-tuple-element.41), channel_id=1, source_target_pairs={{0,2},{1,3},{2,0},{3,1},{4,6},{5,7},{6,4},{7,5},{8,10},{9,11},{10,... | collective-permute-start | bytes 1179656 | tf_op jit(solution)/shard_map/ppermute | solution.py:40
  9.1 3.7 %shard_map.67 = (bf16[4,3,32,512]{3,2,1,0:T(8,128)(2,1)S(1)}, bf16[4,3,32,512]{3,2,1,0:T(8,128)(2,1)S(1)}) custom-call(bf16[4,3,32,512]{3,2,1,0:T(8,128)(2,1)S(1)} %get-tuple-element.42.refs_0_, bf16[4,3,32,512]{3,2,1,0:T(8,128)(2,1)S(1)} %get-tuple-element.43.refs_1_, bf16[2048,512]{1,0:T(8,128)(2,1)S(1)} %get-tuple-element.56.refs_1_.refs_2_, ...), custom_call_target="tpu_custom_call" | custom-call | flops 3221225472 | bytes 4194304 | tf_op jit(solution)/shard_map/pallas_call | solution.py:49
  12.9 0.6 collective-permute-start.1
  13.5 2.7 %collective-permute-start.2 = (bf16[4,3,32,512]{3,2,1,0:T(8,128)(2,1)S(1)}, bf16[4,3,32,512]{3,2,1,0:T(8,128)(2,1)S(1)}, u32[]{:S(2)}, u32[]{:S(2)}) collective-permute-start(bf16[4,3,32,512]{3,2,1,0:T(8,128)(2,1)S(1)} %get-tuple-element.45), channel_id=1, source_target_pairs={{0,3},{1,0},{2,1},{3,2},{4,7},{5,4},{6,5},{7,6},{8,11},{9,8},{10,9... | collective-permute-start | bytes 1179656 | tf_op jit(solution)/shard_map/ppermute | solution.py:40
  16.2 2.3 %shard_map.65.own = f32[4,3,32,512]{3,2,1,0:T(8,128)S(1)} custom-call(bf16[4,3,32,512]{3,2,1,0:T(8,128)(2,1)S(1)} %get-tuple-element.37.refs_0_, bf16[2048,512]{1,0:T(8,128)(2,1)S(1)} %get-tuple-element.56.refs_1_.refs_2_, bf16[2048,512]{1,0:T(8,128)(2,1)S(1)} %get-tuple-element.39.refs_2_.refs_3_, f32[1,2048]{1,0:T(1,128)S(1)} %get-tuple-element.40.refs_3_.refs_4_), custom_call_target="tpu_custom_call" | custom-call | flops 1610612736 | bytes 4194304 | tf_op jit(solution)/shard_map/pallas_call | solution.py:49
  18.6 3.4 %collective-permute-done.1.r1 = bf16[4,3,32,512]{3,2,1,0:T(8,128)(2,1)S(1)} collective-permute-done((bf16[4,3,32,512]{3,2,1,0:T(8,128)(2,1)S(1)}, bf16[4,3,32,512]{3,2,1,0:T(8,128)(2,1)S(1)}, u32[]{:S(2)}, u32[]{:S(2)}) %collective-permute-start.1) | collective-permute-done | bytes 393248 | tf_op jit(solution)/shard_map/ppermute | solution.py:40
  22.0 0.1 shard_map.68
  22.1 1.6 %collective-permute-start.3 = (bf16[3,32,512]{2,1,0:T(8,128)(2,1)S(1)}, bf16[3,32,512]{2,1,0:T(8,128)(2,1)S(1)}, u32[]{:S(2)}, u32[]{:S(2)}) collective-permute-start(bf16[3,32,512]{2,1,0:T(8,128)(2,1)S(1)} %get-tuple-element.47), channel_id=1, source_target_pairs={{0,4},{1,5},{2,6},{3,7},{4,8},{5,9},{6,10},{7,11},{8,12},{9,13},{1... | collective-permute-start | bytes 294920 | tf_op jit(solution)/shard_map/ppermute | solution.py:40
  23.8 2.9 %collective-permute-start.4 = (bf16[3,32,512]{2,1,0:T(8,128)(2,1)S(1)}, bf16[3,32,512]{2,1,0:T(8,128)(2,1)S(1)}, u32[]{:S(2)}, u32[]{:S(2)}) collective-permute-start(bf16[3,32,512]{2,1,0:T(8,128)(2,1)S(1)} %get-tuple-element.48), channel_id=1, source_target_pairs={{0,8},{1,9},{2,10},{3,11},{4,12},{5,13},{6,14},{7,15},{8,0},{9,1},... | collective-permute-start | bytes 294920 | tf_op jit(solution)/shard_map/ppermute | solution.py:40
  26.7 1.3 %collective-permute-start.5 = (bf16[3,32,512]{2,1,0:T(8,128)(2,1)S(1)}, bf16[3,32,512]{2,1,0:T(8,128)(2,1)S(1)}, u32[]{:S(2)}, u32[]{:S(2)}) collective-permute-start(bf16[3,32,512]{2,1,0:T(8,128)(2,1)S(1)} %get-tuple-element.49), channel_id=1, source_target_pairs={{0,12},{1,13},{2,14},{3,15},{4,0},{5,1},{6,2},{7,3},{8,4},{9,5},{1... | collective-permute-start | bytes 294920 | tf_op jit(solution)/shard_map/ppermute | solution.py:40
  28.0 2.3 %collective-permute-done.4.r2 = bf16[3,32,512]{2,1,0:T(8,128)(2,1)S(1)} collective-permute-done((bf16[3,32,512]{2,1,0:T(8,128)(2,1)S(1)}, bf16[3,32,512]{2,1,0:T(8,128)(2,1)S(1)}, u32[]{:S(2)}, u32[]{:S(2)}) %collective-permute-start.4) | collective-permute-done | bytes 98336 | tf_op jit(solution)/shard_map/ppermute | solution.py:40
  30.3 1.0 collective-permute-done.5.r3
  31.3 4.1 %collective-permute-start.6 = (bf16[3,32,512]{2,1,0:T(8,128)(2,1)S(1)}, bf16[3,32,512]{2,1,0:T(8,128)(2,1)S(1)}, u32[]{:S(2)}, u32[]{:S(2)}) collective-permute-start(bf16[3,32,512]{2,1,0:T(8,128)(2,1)S(1)} %shard_map.69.own), channel_id=1, source_target_pairs={{0,48},{1,49},{2,50},{3,51},{4,52},{5,53},{6,54},{7,55},{8,56},{9,... | collective-permute-start | bytes 294920 | tf_op jit(solution)/shard_map/ppermute | solution.py:40
  35.4 1.3 %collective-permute-start.8 = (bf16[3,32,512]{2,1,0:T(8,128)(2,1)S(1)}, bf16[3,32,512]{2,1,0:T(8,128)(2,1)S(1)}, u32[]{:S(2)}, u32[]{:S(2)}) collective-permute-start(bf16[3,32,512]{2,1,0:T(8,128)(2,1)S(1)} %shard_map.69.own), channel_id=1, source_target_pairs={{0,16},{1,17},{2,18},{3,19},{4,20},{5,21},{6,22},{7,23},{8,24},{9,... | collective-permute-start | bytes 294920 | tf_op jit(solution)/shard_map/ppermute | solution.py:40
  36.7 2.0 %collective-permute-done.6.r1 = bf16[3,32,512]{2,1,0:T(8,128)(2,1)S(1)} collective-permute-done((bf16[3,32,512]{2,1,0:T(8,128)(2,1)S(1)}, bf16[3,32,512]{2,1,0:T(8,128)(2,1)S(1)}, u32[]{:S(2)}, u32[]{:S(2)}) %collective-permute-start.6) | collective-permute-done | bytes 98336 | tf_op jit(solution)/shard_map/ppermute | solution.py:40
  38.6 3.0 %collective-permute-done.7.r2 = bf16[3,32,512]{2,1,0:T(8,128)(2,1)S(1)} collective-permute-done((bf16[3,32,512]{2,1,0:T(8,128)(2,1)S(1)}, bf16[3,32,512]{2,1,0:T(8,128)(2,1)S(1)}, u32[]{:S(2)}, u32[]{:S(2)}) %collective-permute-start.7) | collective-permute-done | bytes 98336 | tf_op jit(solution)/shard_map/ppermute | solution.py:40
  41.6 0.7 collective-permute-done.8.r3
  42.4 2.6 %collective-permute-start.9 = (bf16[3,32,512]{2,1,0:T(8,128)(2,1)S(1)}, bf16[3,32,512]{2,1,0:T(8,128)(2,1)S(1)}, u32[]{:S(2)}, u32[]{:S(2)}) collective-permute-start(bf16[3,32,512]{2,1,0:T(8,128)(2,1)S(1)} %get-tuple-element.51.own), channel_id=1, source_target_pairs={{0,12},{1,13},{2,14},{3,15},{4,0},{5,1},{6,2},{7,3},{8,4},{9,5},{1... | collective-permute-start | bytes 294920 | tf_op jit(solution)/shard_map/ppermute | solution.py:40
  45.0 0.2 collective-permute-start.10
  45.2 0.8 collective-permute-start.11
  46.0 2.3 %collective-permute-done.9.part = bf16[3,32,512]{2,1,0:T(8,128)(2,1)S(1)} collective-permute-done((bf16[3,32,512]{2,1,0:T(8,128)(2,1)S(1)}, bf16[3,32,512]{2,1,0:T(8,128)(2,1)S(1)}, u32[]{:S(2)}, u32[]{:S(2)}) %collective-permute-start.9) | collective-permute-done | bytes 98336 | tf_op jit(solution)/shard_map/ppermute | solution.py:40
  48.2 0.3 collective-permute-start.12
  48.5 2.7 %collective-permute-done.10.part = bf16[3,32,512]{2,1,0:T(8,128)(2,1)S(1)} collective-permute-done((bf16[3,32,512]{2,1,0:T(8,128)(2,1)S(1)}, bf16[3,32,512]{2,1,0:T(8,128)(2,1)S(1)}, u32[]{:S(2)}, u32[]{:S(2)}) %collective-permute-start.10) | collective-permute-done | bytes 98336 | tf_op jit(solution)/shard_map/ppermute | solution.py:40
  51.2 0.8 collective-permute-done.11.part
  52.1 1.5 %collective-permute-start.13 = (bf16[4,3,32,512]{3,2,1,0:T(8,128)(2,1)S(1)}, bf16[4,3,32,512]{3,2,1,0:T(8,128)(2,1)S(1)}, u32[]{:S(2)}, u32[]{:S(2)}) collective-permute-start(bf16[4,3,32,512]{3,2,1,0:T(8,128)(2,1)S(1)} %shard_map.73.refs_0_), channel_id=1, source_target_pairs={{0,2},{1,3},{2,0},{3,1},{4,6},{5,7},{6,4},{7,5},{8,10},{9,11},{10,... | collective-permute-start | bytes 1179656 | tf_op jit(solution)/shard_map/ppermute | solution.py:40
  53.6 1.9 %collective-permute-start.15 = (bf16[4,3,32,512]{3,2,1,0:T(8,128)(2,1)S(1)}, bf16[4,3,32,512]{3,2,1,0:T(8,128)(2,1)S(1)}, u32[]{:S(2)}, u32[]{:S(2)}) collective-permute-start(bf16[4,3,32,512]{3,2,1,0:T(8,128)(2,1)S(1)} %shard_map.73.refs_0_), channel_id=1, source_target_pairs={{0,3},{1,0},{2,1},{3,2},{4,7},{5,4},{6,5},{7,6},{8,11},{9,8},{10,9... | collective-permute-start | bytes 1179656 | tf_op jit(solution)/shard_map/ppermute | solution.py:40
  55.5 0.8 collective-permute-start.16
  56.2 2.3 %shard_map.74.own = f32[4,3,32,512]{3,2,1,0:T(8,128)S(1)} custom-call(bf16[4,3,32,512]{3,2,1,0:T(8,128)(2,1)S(1)} %shard_map.73.refs_0_, bf16[2048,512]{1,0:T(8,128)(2,1)S(1)} %get-tuple-element.56.refs_1_.refs_2_, bf16[2048,512]{1,0:T(8,128)(2,1)S(1)} %get-tuple-element.39.refs_2_.refs_3_, f32[1,2048]{1,0:T(1,128)S(1)} %get-tuple-element.40.refs_3_.refs_4_), custom_call_target="tpu_custom_call" | custom-call | flops 1610612736 | bytes 4194304 | tf_op jit(solution)/shard_map/pallas_call | solution.py:49
  58.6 3.0 %collective-permute-done.13.refs_0_ = bf16[4,3,32,512]{3,2,1,0:T(8,128)(2,1)S(1)} collective-permute-done((bf16[4,3,32,512]{3,2,1,0:T(8,128)(2,1)S(1)}, bf16[4,3,32,512]{3,2,1,0:T(8,128)(2,1)S(1)}, u32[]{:S(2)}, u32[]{:S(2)}) %collective-permute-start.13) | collective-permute-done | bytes 393248 | tf_op jit(solution)/shard_map/ppermute | solution.py:40
  61.5 2.3 %shard_map.75 = bf16[4,3,32,512]{3,2,1,0:T(8,128)(2,1)S(1)} custom-call(bf16[4,3,32,512]{3,2,1,0:T(8,128)(2,1)S(1)} %collective-permute-done.13.refs_0_, bf16[2048,512]{1,0:T(8,128)(2,1)S(1)} %get-tuple-element.56.refs_1_.refs_2_, bf16[2048,512]{1,0:T(8,128)(2,1)S(1)} %get-tuple-element.39.refs_2_.refs_3_, f32[1,2048]{1,0:T(1,128)S(1)} %get-tuple-element.40.refs_3_.refs_4_), custom_call_target="tpu_custom_call" | custom-call | flops 1610612736 | bytes 4194304 | tf_op jit(solution)/shard_map/pallas_call | solution.py:49
  63.9 1.5 %collective-permute-start.14 = (bf16[4,3,32,512]{3,2,1,0:T(8,128)(2,1)S(1)}, bf16[4,3,32,512]{3,2,1,0:T(8,128)(2,1)S(1)}, u32[]{:S(2)}, u32[]{:S(2)}) collective-permute-start(bf16[4,3,32,512]{3,2,1,0:T(8,128)(2,1)S(1)} %shard_map.75), channel_id=1, source_target_pairs={{0,2},{1,3},{2,0},{3,1},{4,6},{5,7},{6,4},{7,5},{8,10},{9,11},{10,... | collective-permute-start | bytes 1179656 | tf_op jit(solution)/shard_map/ppermute | solution.py:40
  65.4 0.8 collective-permute-done.15.refs_0_
  66.3 3.7 %shard_map.77 = (bf16[4,3,32,512]{3,2,1,0:T(8,128)(2,1)S(1)}, bf16[4,3,32,512]{3,2,1,0:T(8,128)(2,1)S(1)}) custom-call(bf16[4,3,32,512]{3,2,1,0:T(8,128)(2,1)S(1)} %collective-permute-done.15.refs_0_, bf16[4,3,32,512]{3,2,1,0:T(8,128)(2,1)S(1)} %collective-permute-done.16.refs_1_, bf16[2048,512]{1,0:T(8,128)(2,1)S(1)} %get-tuple-element.56.refs_1_.refs_2_, ...), custom_call_target="tpu_custom_call" | custom-call | flops 3221225472 | bytes 4194304 | tf_op jit(solution)/shard_map/pallas_call | solution.py:49
  70.0 1.9 %collective-permute-start.17 = (bf16[4,3,32,512]{3,2,1,0:T(8,128)(2,1)S(1)}, bf16[4,3,32,512]{3,2,1,0:T(8,128)(2,1)S(1)}, u32[]{:S(2)}, u32[]{:S(2)}) collective-permute-start(bf16[4,3,32,512]{3,2,1,0:T(8,128)(2,1)S(1)} %get-tuple-element.57), channel_id=1, source_target_pairs={{0,1},{1,2},{2,3},{3,0},{4,5},{5,6},{6,7},{7,4},{8,9},{9,10},{10,1... | collective-permute-start | bytes 1179656 | tf_op jit(solution)/shard_map/ppermute | solution.py:40
  71.8 1.4 %collective-permute-start.18 = (bf16[4,3,32,512]{3,2,1,0:T(8,128)(2,1)S(1)}, bf16[4,3,32,512]{3,2,1,0:T(8,128)(2,1)S(1)}, u32[]{:S(2)}, u32[]{:S(2)}) collective-permute-start(bf16[4,3,32,512]{3,2,1,0:T(8,128)(2,1)S(1)} %get-tuple-element.58), channel_id=1, source_target_pairs={{0,3},{1,0},{2,1},{3,2},{4,7},{5,4},{6,5},{7,6},{8,11},{9,8},{10,9... | collective-permute-start | bytes 1179656 | tf_op jit(solution)/shard_map/ppermute | solution.py:40
  73.3 5.7 %collective-permute-done.17.r1 = bf16[4,3,32,512]{3,2,1,0:T(8,128)(2,1)S(1)} collective-permute-done((bf16[4,3,32,512]{3,2,1,0:T(8,128)(2,1)S(1)}, bf16[4,3,32,512]{3,2,1,0:T(8,128)(2,1)S(1)}, u32[]{:S(2)}, u32[]{:S(2)}) %collective-permute-start.17) | collective-permute-done | bytes 393248 | tf_op jit(solution)/shard_map/ppermute | solution.py:40
  79.0 0.6 collective-permute-done.18.r3
  79.8 2.7 %collective-permute-start.20 = (bf16[3,32,512]{2,1,0:T(8,128)(2,1)S(1)}, bf16[3,32,512]{2,1,0:T(8,128)(2,1)S(1)}, u32[]{:S(2)}, u32[]{:S(2)}) collective-permute-start(bf16[3,32,512]{2,1,0:T(8,128)(2,1)S(1)} %get-tuple-element.61), channel_id=1, source_target_pairs={{0,8},{1,9},{2,10},{3,11},{4,12},{5,13},{6,14},{7,15},{8,0},{9,1},... | collective-permute-start | bytes 294920 | tf_op jit(solution)/shard_map/ppermute | solution.py:40
  82.5 1.0 collective-permute-start.21
  83.5 3.2 %collective-permute-done.19.r1 = bf16[3,32,512]{2,1,0:T(8,128)(2,1)S(1)} collective-permute-done((bf16[3,32,512]{2,1,0:T(8,128)(2,1)S(1)}, bf16[3,32,512]{2,1,0:T(8,128)(2,1)S(1)}, u32[]{:S(2)}, u32[]{:S(2)}) %collective-permute-start.19) | collective-permute-done | bytes 98336 | tf_op jit(solution)/shard_map/ppermute | solution.py:40
  86.7 0.9 collective-permute-done.21.r3
  87.6 1.0 collective-permute-start.22
  88.6 0.5 collective-permute-start.23
  89.0 1.3 %collective-permute-start.24 = (bf16[3,32,512]{2,1,0:T(8,128)(2,1)S(1)}, bf16[3,32,512]{2,1,0:T(8,128)(2,1)S(1)}, u32[]{:S(2)}, u32[]{:S(2)}) collective-permute-start(bf16[3,32,512]{2,1,0:T(8,128)(2,1)S(1)} %shard_map.79.own), channel_id=1, source_target_pairs={{0,16},{1,17},{2,18},{3,19},{4,20},{5,21},{6,22},{7,23},{8,24},{9,... | collective-permute-start | bytes 294920 | tf_op jit(solution)/shard_map/ppermute | solution.py:40
  90.3 1.9 %collective-permute-done.22.r1 = bf16[3,32,512]{2,1,0:T(8,128)(2,1)S(1)} collective-permute-done((bf16[3,32,512]{2,1,0:T(8,128)(2,1)S(1)}, bf16[3,32,512]{2,1,0:T(8,128)(2,1)S(1)}, u32[]{:S(2)}, u32[]{:S(2)}) %collective-permute-start.22) | collective-permute-done | bytes 98336 | tf_op jit(solution)/shard_map/ppermute | solution.py:40
  92.3 2.5 %collective-permute-done.23.r2 = bf16[3,32,512]{2,1,0:T(8,128)(2,1)S(1)} collective-permute-done((bf16[3,32,512]{2,1,0:T(8,128)(2,1)S(1)}, bf16[3,32,512]{2,1,0:T(8,128)(2,1)S(1)}, u32[]{:S(2)}, u32[]{:S(2)}) %collective-permute-start.23) | collective-permute-done | bytes 98336 | tf_op jit(solution)/shard_map/ppermute | solution.py:40
  94.8 1.0 collective-permute-done.24.r3
  95.9 1.3 %collective-permute-done.25.other = bf16[3,32,512]{2,1,0:T(8,128)(2,1)S(1)} collective-permute-done((bf16[3,32,512]{2,1,0:T(8,128)(2,1)S(1)}, bf16[3,32,512]{2,1,0:T(8,128)(2,1)S(1)}, u32[]{:S(2)}, u32[]{:S(2)}) %collective-permute-start.25) | collective-permute-done | bytes 98336 | tf_op jit(solution)/shard_map/ppermute | solution.py:392
  97.2 2.7 %collective-permute-start.26 = (bf16[3,32,512]{2,1,0:T(8,128)(2,1)S(1)}, bf16[3,32,512]{2,1,0:T(8,128)(2,1)S(1)}, u32[]{:S(2)}, u32[]{:S(2)}) collective-permute-start(bf16[3,32,512]{2,1,0:T(8,128)(2,1)S(1)} %shard_map.81.own), channel_id=1, source_target_pairs={{0,12},{1,13},{2,14},{3,15},{4,0},{5,1},{6,2},{7,3},{8,4},{9,5},{1... | collective-permute-start | bytes 294920 | tf_op jit(solution)/shard_map/ppermute | solution.py:40
  100.0 0.4 collective-permute-start.27
  100.4 0.6 collective-permute-start.28
  100.9 2.3 %collective-permute-done.26.part = bf16[3,32,512]{2,1,0:T(8,128)(2,1)S(1)} collective-permute-done((bf16[3,32,512]{2,1,0:T(8,128)(2,1)S(1)}, bf16[3,32,512]{2,1,0:T(8,128)(2,1)S(1)}, u32[]{:S(2)}, u32[]{:S(2)}) %collective-permute-start.26) | collective-permute-done | bytes 98336 | tf_op jit(solution)/shard_map/ppermute | solution.py:40
  103.2 0.3 collective-permute-start.29
  103.5 2.7 %collective-permute-done.27.part = bf16[3,32,512]{2,1,0:T(8,128)(2,1)S(1)} collective-permute-done((bf16[3,32,512]{2,1,0:T(8,128)(2,1)S(1)}, bf16[3,32,512]{2,1,0:T(8,128)(2,1)S(1)}, u32[]{:S(2)}, u32[]{:S(2)}) %collective-permute-start.27) | collective-permute-done | bytes 98336 | tf_op jit(solution)/shard_map/ppermute | solution.py:40
  106.2 0.9 collective-permute-done.28.part
  107.2 2.3 %collective-permute-start.32 = (bf16[4,3,32,512]{3,2,1,0:T(8,128)(2,1)S(1)}, bf16[4,3,32,512]{3,2,1,0:T(8,128)(2,1)S(1)}, u32[]{:S(2)}, u32[]{:S(2)}) collective-permute-start(bf16[4,3,32,512]{3,2,1,0:T(8,128)(2,1)S(1)} %shard_map.84.refs_0_), channel_id=1, source_target_pairs={{0,2},{1,3},{2,0},{3,1},{4,6},{5,7},{6,4},{7,5},{8,10},{9,11},{10,... | collective-permute-start | bytes 1179656 | tf_op jit(solution)/shard_map/ppermute | solution.py:40
  109.5 1.1 collective-permute-start.30
  110.7 0.9 collective-permute-start.31
  111.5 1.8 %shard_map.85.refs_2_ = f32[2048,512]{1,0:T(8,128)S(1)} custom-call(bf16[4,3,32,512]{3,2,1,0:T(8,128)(2,1)S(1)} %shard_map.84.refs_0_, bf16[2048,512]{1,0:T(8,128)(2,1)S(1)} %copy-done), custom_call_target="tpu_custom_call" | custom-call | flops 805306368 | bytes 6291456 | tf_op jit(solution)/shard_map/pallas_call | solution.py:49
  113.3 3.3 %collective-permute-done.32.refs_0_ = bf16[4,3,32,512]{3,2,1,0:T(8,128)(2,1)S(1)} collective-permute-done((bf16[4,3,32,512]{3,2,1,0:T(8,128)(2,1)S(1)}, bf16[4,3,32,512]{3,2,1,0:T(8,128)(2,1)S(1)}, u32[]{:S(2)}, u32[]{:S(2)}) %collective-permute-start.32) | collective-permute-done | bytes 393248 | tf_op jit(solution)/shard_map/ppermute | solution.py:40
  116.6 1.8 %shard_map.86.refs_4_ = f32[2048,512]{1,0:T(8,128)S(1)} custom-call(bf16[4,3,32,512]{3,2,1,0:T(8,128)(2,1)S(1)} %collective-permute-done.32.refs_0_, bf16[2048,512]{1,0:T(8,128)(2,1)S(1)} %copy-done, f32[2048,512]{1,0:T(8,128)S(1)} %shard_map.85.refs_2_), custom_call_target="tpu_custom_call" | custom-call | flops 805306368 | bytes 6291456 | tf_op jit(solution)/shard_map/pallas_call | solution.py:49
  118.4 2.3 %collective-permute-done.30.refs_0_ = bf16[4,3,32,512]{3,2,1,0:T(8,128)(2,1)S(1)} collective-permute-done((bf16[4,3,32,512]{3,2,1,0:T(8,128)(2,1)S(1)}, bf16[4,3,32,512]{3,2,1,0:T(8,128)(2,1)S(1)}, u32[]{:S(2)}, u32[]{:S(2)}) %collective-permute-start.30) | collective-permute-done | bytes 393248 | tf_op jit(solution)/shard_map/ppermute | solution.py:40
  120.8 2.8 %shard_map.87 = bf16[2048,512]{1,0:T(8,128)(2,1)} custom-call(bf16[4,3,32,512]{3,2,1,0:T(8,128)(2,1)S(1)} %collective-permute-done.30.refs_0_, bf16[4,3,32,512]{3,2,1,0:T(8,128)(2,1)S(1)} %collective-permute-done.31.refs_1_, bf16[2048,512]{1,0:T(8,128)(2,1)S(1)} %copy-done, f32[1,512]{1,0:T(1,128)S(1)} %bitcast.3, f32[2048,512]{1,0:T(8,128)S(1)} %shard_map.86.refs_4_), custom_call_target="tpu_custom_call" | custom-call | flops 1610612736 | bytes 6291456 | tf_op jit(solution)/shard_map/pallas_call | solution.py:49
  (34 shorter events, 1.0 us)
Async XLA Ops:
  5.9 12.5 %collective-permute-start = (bf16[4,3,32,512]{3,2,1,0:T(8,128)(2,1)S(1)}, bf16[4,3,32,512]{3,2,1,0:T(8,128)(2,1)S(1)}, u32[]{:S(2)}, u32[]{:S(2)}) collective-permute-start(bf16[4,3,32,512]{3,2,1,0:T(8,128)(2,1)S(1)} %get-tuple-element.41), channel_id=1, source_target_pairs={{0,2},{1,3},{2,0},{3,1},{4,6},{5,7},{6,4},{7,5},{8,10},{9,11},{10,... | collective-permute-start | bytes 1179656 | tf_op jit(solution)/shard_map/ppermute | solution.py:40
  12.9 9.1 %collective-permute-start.1 = (bf16[4,3,32,512]{3,2,1,0:T(8,128)(2,1)S(1)}, bf16[4,3,32,512]{3,2,1,0:T(8,128)(2,1)S(1)}, u32[]{:S(2)}, u32[]{:S(2)}) collective-permute-start(bf16[4,3,32,512]{3,2,1,0:T(8,128)(2,1)S(1)} %get-tuple-element.44), channel_id=1, source_target_pairs={{0,1},{1,2},{2,3},{3,0},{4,5},{5,6},{6,7},{7,4},{8,9},{9,10},{10,1... | collective-permute-start | bytes 1179656 | tf_op jit(solution)/shard_map/ppermute | solution.py:40
  13.5 8.4 %collective-permute-start.2 = (bf16[4,3,32,512]{3,2,1,0:T(8,128)(2,1)S(1)}, bf16[4,3,32,512]{3,2,1,0:T(8,128)(2,1)S(1)}, u32[]{:S(2)}, u32[]{:S(2)}) collective-permute-start(bf16[4,3,32,512]{3,2,1,0:T(8,128)(2,1)S(1)} %get-tuple-element.45), channel_id=1, source_target_pairs={{0,3},{1,0},{2,1},{3,2},{4,7},{5,4},{6,5},{7,6},{8,11},{9,8},{10,9... | collective-permute-start | bytes 1179656 | tf_op jit(solution)/shard_map/ppermute | solution.py:40
  22.1 5.9 %collective-permute-start.3 = (bf16[3,32,512]{2,1,0:T(8,128)(2,1)S(1)}, bf16[3,32,512]{2,1,0:T(8,128)(2,1)S(1)}, u32[]{:S(2)}, u32[]{:S(2)}) collective-permute-start(bf16[3,32,512]{2,1,0:T(8,128)(2,1)S(1)} %get-tuple-element.47), channel_id=1, source_target_pairs={{0,4},{1,5},{2,6},{3,7},{4,8},{5,9},{6,10},{7,11},{8,12},{9,13},{1... | collective-permute-start | bytes 294920 | tf_op jit(solution)/shard_map/ppermute | solution.py:40
  23.8 6.5 %collective-permute-start.4 = (bf16[3,32,512]{2,1,0:T(8,128)(2,1)S(1)}, bf16[3,32,512]{2,1,0:T(8,128)(2,1)S(1)}, u32[]{:S(2)}, u32[]{:S(2)}) collective-permute-start(bf16[3,32,512]{2,1,0:T(8,128)(2,1)S(1)} %get-tuple-element.48), channel_id=1, source_target_pairs={{0,8},{1,9},{2,10},{3,11},{4,12},{5,13},{6,14},{7,15},{8,0},{9,1},... | collective-permute-start | bytes 294920 | tf_op jit(solution)/shard_map/ppermute | solution.py:40
  26.7 4.6 %collective-permute-start.5 = (bf16[3,32,512]{2,1,0:T(8,128)(2,1)S(1)}, bf16[3,32,512]{2,1,0:T(8,128)(2,1)S(1)}, u32[]{:S(2)}, u32[]{:S(2)}) collective-permute-start(bf16[3,32,512]{2,1,0:T(8,128)(2,1)S(1)} %get-tuple-element.49), channel_id=1, source_target_pairs={{0,12},{1,13},{2,14},{3,15},{4,0},{5,1},{6,2},{7,3},{8,4},{9,5},{1... | collective-permute-start | bytes 294920 | tf_op jit(solution)/shard_map/ppermute | solution.py:40
  31.3 7.3 %collective-permute-start.6 = (bf16[3,32,512]{2,1,0:T(8,128)(2,1)S(1)}, bf16[3,32,512]{2,1,0:T(8,128)(2,1)S(1)}, u32[]{:S(2)}, u32[]{:S(2)}) collective-permute-start(bf16[3,32,512]{2,1,0:T(8,128)(2,1)S(1)} %shard_map.69.own), channel_id=1, source_target_pairs={{0,48},{1,49},{2,50},{3,51},{4,52},{5,53},{6,54},{7,55},{8,56},{9,... | collective-permute-start | bytes 294920 | tf_op jit(solution)/shard_map/ppermute | solution.py:40
  35.4 6.2 %collective-permute-start.7 = (bf16[3,32,512]{2,1,0:T(8,128)(2,1)S(1)}, bf16[3,32,512]{2,1,0:T(8,128)(2,1)S(1)}, u32[]{:S(2)}, u32[]{:S(2)}) collective-permute-start(bf16[3,32,512]{2,1,0:T(8,128)(2,1)S(1)} %shard_map.69.own), channel_id=1, source_target_pairs={{0,32},{1,33},{2,34},{3,35},{4,36},{5,37},{6,38},{7,39},{8,40},{9,... | collective-permute-start | bytes 294920 | tf_op jit(solution)/shard_map/ppermute | solution.py:40
  35.4 6.9 %collective-permute-start.8 = (bf16[3,32,512]{2,1,0:T(8,128)(2,1)S(1)}, bf16[3,32,512]{2,1,0:T(8,128)(2,1)S(1)}, u32[]{:S(2)}, u32[]{:S(2)}) collective-permute-start(bf16[3,32,512]{2,1,0:T(8,128)(2,1)S(1)} %shard_map.69.own), channel_id=1, source_target_pairs={{0,16},{1,17},{2,18},{3,19},{4,20},{5,21},{6,22},{7,23},{8,24},{9,... | collective-permute-start | bytes 294920 | tf_op jit(solution)/shard_map/ppermute | solution.py:40
  42.4 5.8 %collective-permute-start.9 = (bf16[3,32,512]{2,1,0:T(8,128)(2,1)S(1)}, bf16[3,32,512]{2,1,0:T(8,128)(2,1)S(1)}, u32[]{:S(2)}, u32[]{:S(2)}) collective-permute-start(bf16[3,32,512]{2,1,0:T(8,128)(2,1)S(1)} %get-tuple-element.51.own), channel_id=1, source_target_pairs={{0,12},{1,13},{2,14},{3,15},{4,0},{5,1},{6,2},{7,3},{8,4},{9,5},{1... | collective-permute-start | bytes 294920 | tf_op jit(solution)/shard_map/ppermute | solution.py:40
  45.0 6.2 %collective-permute-start.10 = (bf16[3,32,512]{2,1,0:T(8,128)(2,1)S(1)}, bf16[3,32,512]{2,1,0:T(8,128)(2,1)S(1)}, u32[]{:S(2)}, u32[]{:S(2)}) collective-permute-start(bf16[3,32,512]{2,1,0:T(8,128)(2,1)S(1)} %get-tuple-element.51.own), channel_id=1, source_target_pairs={{0,8},{1,9},{2,10},{3,11},{4,12},{5,13},{6,14},{7,15},{8,0},{9,1},... | collective-permute-start | bytes 294920 | tf_op jit(solution)/shard_map/ppermute | solution.py:40
  45.2 6.9 %collective-permute-start.11 = (bf16[3,32,512]{2,1,0:T(8,128)(2,1)S(1)}, bf16[3,32,512]{2,1,0:T(8,128)(2,1)S(1)}, u32[]{:S(2)}, u32[]{:S(2)}) collective-permute-start(bf16[3,32,512]{2,1,0:T(8,128)(2,1)S(1)} %get-tuple-element.51.own), channel_id=1, source_target_pairs={{0,4},{1,5},{2,6},{3,7},{4,8},{5,9},{6,10},{7,11},{8,12},{9,13},{1... | collective-permute-start | bytes 294920 | tf_op jit(solution)/shard_map/ppermute | solution.py:40
  48.2 3.8 %collective-permute-start.12 = (bf16[16,128]{1,0:T(8,128)(2,1)S(1)}, bf16[16,128]{1,0:T(8,128)(2,1)S(1)}, u32[]{:S(2)}, u32[]{:S(2)}) collective-permute-start(bf16[16,128]{1,0:T(8,128)(2,1)S(1)} %get-tuple-element.53), channel_id=1, source_target_pairs={{0,64},{1,65},{2,66},{3,67},{4,68},{5,69},{6,70},{7,71},{8,72},{9,... | collective-permute-start | bytes 12296 | tf_op jit(solution)/shard_map/ppermute | solution.py:335
  52.1 9.5 %collective-permute-start.13 = (bf16[4,3,32,512]{3,2,1,0:T(8,128)(2,1)S(1)}, bf16[4,3,32,512]{3,2,1,0:T(8,128)(2,1)S(1)}, u32[]{:S(2)}, u32[]{:S(2)}) collective-permute-start(bf16[4,3,32,512]{3,2,1,0:T(8,128)(2,1)S(1)} %shard_map.73.refs_0_), channel_id=1, source_target_pairs={{0,2},{1,3},{2,0},{3,1},{4,6},{5,7},{6,4},{7,5},{8,10},{9,11},{10,... | collective-permute-start | bytes 1179656 | tf_op jit(solution)/shard_map/ppermute | solution.py:40
  53.6 12.6 %collective-permute-start.15 = (bf16[4,3,32,512]{3,2,1,0:T(8,128)(2,1)S(1)}, bf16[4,3,32,512]{3,2,1,0:T(8,128)(2,1)S(1)}, u32[]{:S(2)}, u32[]{:S(2)}) collective-permute-start(bf16[4,3,32,512]{3,2,1,0:T(8,128)(2,1)S(1)} %shard_map.73.refs_0_), channel_id=1, source_target_pairs={{0,3},{1,0},{2,1},{3,2},{4,7},{5,4},{6,5},{7,6},{8,11},{9,8},{10,9... | collective-permute-start | bytes 1179656 | tf_op jit(solution)/shard_map/ppermute | solution.py:40
  55.5 10.8 %collective-permute-start.16 = (bf16[4,3,32,512]{3,2,1,0:T(8,128)(2,1)S(1)}, bf16[4,3,32,512]{3,2,1,0:T(8,128)(2,1)S(1)}, u32[]{:S(2)}, u32[]{:S(2)}) collective-permute-start(bf16[4,3,32,512]{3,2,1,0:T(8,128)(2,1)S(1)} %shard_map.73.refs_0_), channel_id=1, source_target_pairs={{0,1},{1,2},{2,3},{3,0},{4,5},{5,6},{6,7},{7,4},{8,9},{9,10},{10,1... | collective-permute-start | bytes 1179656 | tf_op jit(solution)/shard_map/ppermute | solution.py:40
  63.9 9.4 %collective-permute-start.14 = (bf16[4,3,32,512]{3,2,1,0:T(8,128)(2,1)S(1)}, bf16[4,3,32,512]{3,2,1,0:T(8,128)(2,1)S(1)}, u32[]{:S(2)}, u32[]{:S(2)}) collective-permute-start(bf16[4,3,32,512]{3,2,1,0:T(8,128)(2,1)S(1)} %shard_map.75), channel_id=1, source_target_pairs={{0,2},{1,3},{2,0},{3,1},{4,6},{5,7},{6,4},{7,5},{8,10},{9,11},{10,... | collective-permute-start | bytes 1179656 | tf_op jit(solution)/shard_map/ppermute | solution.py:40
  70.0 9.1 %collective-permute-start.17 = (bf16[4,3,32,512]{3,2,1,0:T(8,128)(2,1)S(1)}, bf16[4,3,32,512]{3,2,1,0:T(8,128)(2,1)S(1)}, u32[]{:S(2)}, u32[]{:S(2)}) collective-permute-start(bf16[4,3,32,512]{3,2,1,0:T(8,128)(2,1)S(1)} %get-tuple-element.57), channel_id=1, source_target_pairs={{0,1},{1,2},{2,3},{3,0},{4,5},{5,6},{6,7},{7,4},{8,9},{9,10},{10,1... | collective-permute-start | bytes 1179656 | tf_op jit(solution)/shard_map/ppermute | solution.py:40
  71.8 7.8 %collective-permute-start.18 = (bf16[4,3,32,512]{3,2,1,0:T(8,128)(2,1)S(1)}, bf16[4,3,32,512]{3,2,1,0:T(8,128)(2,1)S(1)}, u32[]{:S(2)}, u32[]{:S(2)}) collective-permute-start(bf16[4,3,32,512]{3,2,1,0:T(8,128)(2,1)S(1)} %get-tuple-element.58), channel_id=1, source_target_pairs={{0,3},{1,0},{2,1},{3,2},{4,7},{5,4},{6,5},{7,6},{8,11},{9,8},{10,9... | collective-permute-start | bytes 1179656 | tf_op jit(solution)/shard_map/ppermute | solution.py:40
  79.7 31.8 %copy-start = (bf16[2048,512]{1,0:T(8,128)(2,1)S(1)}, bf16[2048,512]{1,0:T(8,128)(2,1)}, u32[]{:S(2)}) copy-start(bf16[2048,512]{1,0:T(8,128)(2,1)} %refs_2_.3) | copy-start | bytes 6291460
  79.7 6.9 %collective-permute-start.19 = (bf16[3,32,512]{2,1,0:T(8,128)(2,1)S(1)}, bf16[3,32,512]{2,1,0:T(8,128)(2,1)S(1)}, u32[]{:S(2)}, u32[]{:S(2)}) collective-permute-start(bf16[3,32,512]{2,1,0:T(8,128)(2,1)S(1)} %get-tuple-element.60), channel_id=1, source_target_pairs={{0,4},{1,5},{2,6},{3,7},{4,8},{5,9},{6,10},{7,11},{8,12},{9,13},{1... | collective-permute-start | bytes 294920 | tf_op jit(solution)/shard_map/ppermute | solution.py:40
  79.8 6.9 %collective-permute-start.20 = (bf16[3,32,512]{2,1,0:T(8,128)(2,1)S(1)}, bf16[3,32,512]{2,1,0:T(8,128)(2,1)S(1)}, u32[]{:S(2)}, u32[]{:S(2)}) collective-permute-start(bf16[3,32,512]{2,1,0:T(8,128)(2,1)S(1)} %get-tuple-element.61), channel_id=1, source_target_pairs={{0,8},{1,9},{2,10},{3,11},{4,12},{5,13},{6,14},{7,15},{8,0},{9,1},... | collective-permute-start | bytes 294920 | tf_op jit(solution)/shard_map/ppermute | solution.py:40
  82.5 5.0 %collective-permute-start.21 = (bf16[3,32,512]{2,1,0:T(8,128)(2,1)S(1)}, bf16[3,32,512]{2,1,0:T(8,128)(2,1)S(1)}, u32[]{:S(2)}, u32[]{:S(2)}) collective-permute-start(bf16[3,32,512]{2,1,0:T(8,128)(2,1)S(1)} %get-tuple-element.62), channel_id=1, source_target_pairs={{0,12},{1,13},{2,14},{3,15},{4,0},{5,1},{6,2},{7,3},{8,4},{9,5},{1... | collective-permute-start | bytes 294920 | tf_op jit(solution)/shard_map/ppermute | solution.py:40
  87.6 4.7 %collective-permute-start.22 = (bf16[3,32,512]{2,1,0:T(8,128)(2,1)S(1)}, bf16[3,32,512]{2,1,0:T(8,128)(2,1)S(1)}, u32[]{:S(2)}, u32[]{:S(2)}) collective-permute-start(bf16[3,32,512]{2,1,0:T(8,128)(2,1)S(1)} %shard_map.79.own), channel_id=1, source_target_pairs={{0,48},{1,49},{2,50},{3,51},{4,52},{5,53},{6,54},{7,55},{8,56},{9,... | collective-permute-start | bytes 294920 | tf_op jit(solution)/shard_map/ppermute | solution.py:40
  88.6 6.2 %collective-permute-start.23 = (bf16[3,32,512]{2,1,0:T(8,128)(2,1)S(1)}, bf16[3,32,512]{2,1,0:T(8,128)(2,1)S(1)}, u32[]{:S(2)}, u32[]{:S(2)}) collective-permute-start(bf16[3,32,512]{2,1,0:T(8,128)(2,1)S(1)} %shard_map.79.own), channel_id=1, source_target_pairs={{0,32},{1,33},{2,34},{3,35},{4,36},{5,37},{6,38},{7,39},{8,40},{9,... | collective-permute-start | bytes 294920 | tf_op jit(solution)/shard_map/ppermute | solution.py:40
  89.0 6.7 %collective-permute-start.24 = (bf16[3,32,512]{2,1,0:T(8,128)(2,1)S(1)}, bf16[3,32,512]{2,1,0:T(8,128)(2,1)S(1)}, u32[]{:S(2)}, u32[]{:S(2)}) collective-permute-start(bf16[3,32,512]{2,1,0:T(8,128)(2,1)S(1)} %shard_map.79.own), channel_id=1, source_target_pairs={{0,16},{1,17},{2,18},{3,19},{4,20},{5,21},{6,22},{7,23},{8,24},{9,... | collective-permute-start | bytes 294920 | tf_op jit(solution)/shard_map/ppermute | solution.py:40
  95.8 1.4 %collective-permute-start.25 = (bf16[3,32,512]{2,1,0:T(8,128)(2,1)S(1)}, bf16[3,32,512]{2,1,0:T(8,128)(2,1)S(1)}, u32[]{:S(2)}, u32[]{:S(2)}) collective-permute-start(bf16[3,32,512]{2,1,0:T(8,128)(2,1)S(1)} %get-tuple-element.63), channel_id=1, source_target_pairs={{0,64},{1,65},{2,66},{3,67},{4,68},{5,69},{6,70},{7,71},{8,72},{9,... | collective-permute-start | bytes 294920 | tf_op jit(solution)/shard_map/ppermute | solution.py:392
  97.2 6.0 %collective-permute-start.26 = (bf16[3,32,512]{2,1,0:T(8,128)(2,1)S(1)}, bf16[3,32,512]{2,1,0:T(8,128)(2,1)S(1)}, u32[]{:S(2)}, u32[]{:S(2)}) collective-permute-start(bf16[3,32,512]{2,1,0:T(8,128)(2,1)S(1)} %shard_map.81.own), channel_id=1, source_target_pairs={{0,12},{1,13},{2,14},{3,15},{4,0},{5,1},{6,2},{7,3},{8,4},{9,5},{1... | collective-permute-start | bytes 294920 | tf_op jit(solution)/shard_map/ppermute | solution.py:40
  100.0 6.2 %collective-permute-start.27 = (bf16[3,32,512]{2,1,0:T(8,128)(2,1)S(1)}, bf16[3,32,512]{2,1,0:T(8,128)(2,1)S(1)}, u32[]{:S(2)}, u32[]{:S(2)}) collective-permute-start(bf16[3,32,512]{2,1,0:T(8,128)(2,1)S(1)} %shard_map.81.own), channel_id=1, source_target_pairs={{0,8},{1,9},{2,10},{3,11},{4,12},{5,13},{6,14},{7,15},{8,0},{9,1},... | collective-permute-start | bytes 294920 | tf_op jit(solution)/shard_map/ppermute | solution.py:40
  100.4 6.8 %collective-permute-start.28 = (bf16[3,32,512]{2,1,0:T(8,128)(2,1)S(1)}, bf16[3,32,512]{2,1,0:T(8,128)(2,1)S(1)}, u32[]{:S(2)}, u32[]{:S(2)}) collective-permute-start(bf16[3,32,512]{2,1,0:T(8,128)(2,1)S(1)} %shard_map.81.own), channel_id=1, source_target_pairs={{0,4},{1,5},{2,6},{3,7},{4,8},{5,9},{6,10},{7,11},{8,12},{9,13},{1... | collective-permute-start | bytes 294920 | tf_op jit(solution)/shard_map/ppermute | solution.py:40
  103.2 3.9 %collective-permute-start.29 = (bf16[16,128]{1,0:T(8,128)(2,1)S(1)}, bf16[16,128]{1,0:T(8,128)(2,1)S(1)}, u32[]{:S(2)}, u32[]{:S(2)}) collective-permute-start(bf16[16,128]{1,0:T(8,128)(2,1)S(1)} %get-tuple-element.66), channel_id=1, source_target_pairs={{0,64},{1,65},{2,66},{3,67},{4,68},{5,69},{6,70},{7,71},{8,72},{9,... | collective-permute-start | bytes 12296 | tf_op jit(solution)/shard_map/ppermute | solution.py:335
  107.2 9.5 %collective-permute-start.32 = (bf16[4,3,32,512]{3,2,1,0:T(8,128)(2,1)S(1)}, bf16[4,3,32,512]{3,2,1,0:T(8,128)(2,1)S(1)}, u32[]{:S(2)}, u32[]{:S(2)}) collective-permute-start(bf16[4,3,32,512]{3,2,1,0:T(8,128)(2,1)S(1)} %shard_map.84.refs_0_), channel_id=1, source_target_pairs={{0,2},{1,3},{2,0},{3,1},{4,6},{5,7},{6,4},{7,5},{8,10},{9,11},{10,... | collective-permute-start | bytes 1179656 | tf_op jit(solution)/shard_map/ppermute | solution.py:40
  109.5 11.2 %collective-permute-start.30 = (bf16[4,3,32,512]{3,2,1,0:T(8,128)(2,1)S(1)}, bf16[4,3,32,512]{3,2,1,0:T(8,128)(2,1)S(1)}, u32[]{:S(2)}, u32[]{:S(2)}) collective-permute-start(bf16[4,3,32,512]{3,2,1,0:T(8,128)(2,1)S(1)} %shard_map.84.refs_0_), channel_id=1, source_target_pairs={{0,3},{1,0},{2,1},{3,2},{4,7},{5,4},{6,5},{7,6},{8,11},{9,8},{10,9... | collective-permute-start | bytes 1179656 | tf_op jit(solution)/shard_map/ppermute | solution.py:40
  110.7 10.1 %collective-permute-start.31 = (bf16[4,3,32,512]{3,2,1,0:T(8,128)(2,1)S(1)}, bf16[4,3,32,512]{3,2,1,0:T(8,128)(2,1)S(1)}, u32[]{:S(2)}, u32[]{:S(2)}) collective-permute-start(bf16[4,3,32,512]{3,2,1,0:T(8,128)(2,1)S(1)} %shard_map.84.refs_0_), channel_id=1, source_target_pairs={{0,1},{1,2},{2,3},{3,0},{4,5},{5,6},{6,7},{7,4},{8,9},{9,10},{10,1... | collective-permute-start | bytes 1179656 | tf_op jit(solution)/shard_map/ppermute | solution.py:40
  113.3 7.4 %copy-start.1 = (f32[512]{0:T(512)S(1)}, f32[512]{0:T(512)}, u32[]{:S(2)}) copy-start(f32[512]{0:T(512)} %param.11) | copy-start | bytes 6148
